TPU v7x, 32 devices: a whole 2x2x4 slice. The times are simulated.
32 devices in a mesh: src: 4 (over z), tm: 8 (over y, x, core).
Axes of the slice: x: 2, y: 2, z: 4, core: 2. Of those that a mesh axis runs over, the one named last changes fastest.
Arguments:
- greens: bfloat16 [16384, 3072], P('tm', 'src')
- pairs: int32 [4, 2], P('src'), may hold values from 0 to 3, as said below
- onsets: int32 [4], replicated, may hold values from 0 to 8191
Outputs:
- gram: float32 [4, 768, 768], P('src', 'tm')
Inputs may be any that keep to these rules, and one draw needn't show every extreme that they name: `pairs`: row s names the blocks s and (s - 1) mod 4, in either order.
All inputs are finite; a program needn't handle non-finite values.
Results may differ from a plain program's by a relative error of at most 0.0003.
Values may be sent and summed in bfloat16 or wider, within the bound.
No kernel may reach another device: no remote copies, remote signals or barrier semaphores. Data moves between devices by JAX's collectives and lax.ppermute only.
A program may use at most 64 MiB of HBM per device.

v0:
```python
import functools

import jax
import jax.numpy as jnp
from jax import lax
from jax.experimental import pallas as pl
from jax.experimental.pallas import tpu as pltpu
from jax.sharding import PartitionSpec as P


PARTS = (2, 2, 1, 1)
HEAD = 8


def from_behind(value, axis, by):
    length = lax.axis_size(axis)
    return lax.ppermute(value, axis, [(i, (i + by) % length) for i in range(length)])


def swapped(value, axis, bits):
    length = lax.axis_size(axis)
    return lax.ppermute(value, axis, [(i, i ^ bits) for i in range(length)])


def summed(value, axis):
    bits = 1
    while bits < lax.axis_size(axis):
        value = value + swapped(value, axis, bits)
        bits *= 2
    return value


def split(strips, bit):
    halves = strips.reshape((strips.shape[0] // 2, 2) + strips.shape[1:])
    keep = lax.dynamic_index_in_dim(halves, bit, 1, keepdims=False)
    give = lax.dynamic_index_in_dim(halves, 1 - bit, 1, keepdims=False)
    return keep, give


def strips_arrived(keep, give, axis):
    me = lax.axis_index(axis) // 2
    bits = 1
    strips = keep + swapped(give, axis, bits)
    while strips.shape[0] > 4:
        keep, give = split(strips, me % 2)
        bits *= 2
        me = me // 2
        strips = keep + swapped(give, axis, bits)
    bits *= 2
    terms = [lax.dynamic_index_in_dim(strips, me, 0, keepdims=False)]
    for m in range(1, strips.shape[0]):
        give = lax.dynamic_index_in_dim(strips, me ^ m, 0, keepdims=False)
        terms.append(swapped(give, axis, bits * m))
    return terms


def runs_of(share):
    whole = sum(PARTS)
    if share % whole:
        return [(0, share)]
    unit = share // whole
    runs, start = [], 0
    for part in PARTS:
        runs.append((start, part * unit))
        start += part * unit
    return runs


def picker(width, share, start, run):
    picked = width // share * run
    q = lax.broadcasted_iota(jnp.int32, (width, picked), 1)
    source = lax.broadcasted_iota(jnp.int32, (width, picked), 0)
    return (q // run) * share + start + q % run == source


def picked(block, share, start, run):
    return jnp.dot(
        block,
        picker(block.shape[1], share, start, run).astype(jnp.bfloat16),
        preferred_element_type=jnp.float32,
    ).astype(jnp.bfloat16)


def gram_kernel(lane, share, run, flags, own, head, rest, keep, give, part):
    cut = head.shape[0]
    columns = rest.shape[1]
    groups = keep.shape[0] * 2
    bit = flags[1]
    product = jnp.dot(
        own[:, cut:], rest[...], preferred_element_type=jnp.float32
    ) + jnp.dot(
        own[:, :cut], head[:, lane : lane + columns], preferred_element_type=jnp.float32
    )

    @pl.when(flags[0] == 1)
    def _():
        part[...] = product
        for pair in range(groups // 2):
            for target, odd in ((keep, bit), (give, 1 - bit)):
                top = (2 * pair + odd) * share
                for piece in range(share // run):
                    rows = pl.ds(pl.multiple_of(top + piece * run, 8), run)
                    target[pair, :, piece * columns : (piece + 1) * columns] = part[rows, :]

    @pl.when(flags[0] == 0)
    def _():
        turned = product.T
        for pair in range(groups // 2):
            even = turned[2 * pair * run : (2 * pair + 1) * run, :]
            uneven = turned[(2 * pair + 1) * run : (2 * pair + 2) * run, :]
            keep[pair] = jnp.where(bit == 0, even, uneven)
            give[pair] = jnp.where(bit == 0, uneven, even)


def gram(flags, own, head, rest, share, start, run):
    width = own.shape[0]
    groups = width // share
    half = jax.ShapeDtypeStruct((groups // 2, run, width), jnp.float32)
    columns = groups * run
    return pl.pallas_call(
        functools.partial(gram_kernel, start * groups, share, run),
        out_shape=(half, half),
        in_specs=[pl.BlockSpec(memory_space=pltpu.SMEM)]
        + [pl.BlockSpec(memory_space=pltpu.VMEM)] * 3,
        out_specs=(pl.BlockSpec(memory_space=pltpu.VMEM),) * 2,
        scratch_shapes=[pltpu.VMEM((width, columns), jnp.float32)],
        cost_estimate=pl.CostEstimate(
            flops=2 * own.size * columns, bytes_accessed=2 * own.size, transcendentals=0
        ),
        compiler_params=pltpu.CompilerParams(vmem_limit_bytes=16 << 20),
        name="gram",
    )(flags, own, head, rest)


def gram_plain(flags, own, head, rest, share, start, run):
    width = own.shape[0]
    groups = width // share
    columns = groups * run
    block = jnp.concatenate([head[:, start * groups : start * groups + columns], rest], axis=0)
    product = jnp.dot(own, block, preferred_element_type=jnp.float32)
    strips = jnp.where(
        flags[0] == 1,
        product.reshape(groups, share // run, run, columns)
        .transpose(0, 2, 1, 3)
        .reshape(groups, run, width),
        product.T.reshape(groups, run, width),
    )
    return split(strips, flags[1])


def put_back(runs, share, parts):
    width = parts[0].shape[1]
    total = jnp.zeros((share, width), jnp.float32)
    for (start, run), part in zip(runs, parts):
        columns = width // share * run
        spread = (
            part.reshape(run, share // run, columns).transpose(1, 0, 2).reshape(share, columns)
        )
        total = total + lax.dot_general(
            spread,
            picker(width, share, start, run).astype(jnp.float32),
            (((1,), (1,)), ((), ())),
            precision=lax.Precision.HIGHEST,
            preferred_element_type=jnp.float32,
        )
    return total


def finish_kernel(share, start, run, flags, base, scale_rows, scale_cols, *refs):
    *terms, out = refs
    width = base.shape[1]
    columns = width // share * run
    part = terms[0][...]
    for term in terms[1:]:
        part = part + term[...]

    @pl.when(flags[0] == 1)
    def _():
        spread = jnp.concatenate(
            [part[:, n * columns : (n + 1) * columns] for n in range(share // run)], axis=0
        )
        q = lax.broadcasted_iota(jnp.int32, (columns, width), 0)
        source = lax.broadcasted_iota(jnp.int32, (columns, width), 1)
        order = (q // run) * share + start + q % run == source
        placed = jnp.dot(
            spread,
            order.astype(jnp.float32),
            precision=lax.Precision.HIGHEST,
            preferred_element_type=jnp.float32,
        )
        out[0] = (base[...] + placed) * scale_rows[...] * scale_cols[...]

    @pl.when(flags[0] == 0)
    def _():
        out[0] = base[...] * scale_rows[...] * scale_cols[...]
        out[0, start : start + run, :] = (
            part * scale_rows[start : start + run, :] * scale_cols[...]
        )


def finish(flags, base, scale_rows, scale_cols, terms, share, start, run):
    return pl.pallas_call(
        functools.partial(finish_kernel, share, start, run),
        out_shape=jax.ShapeDtypeStruct((1,) + base.shape, jnp.float32),
        in_specs=[pl.BlockSpec(memory_space=pltpu.SMEM)]
        + [pl.BlockSpec(memory_space=pltpu.VMEM)] * (3 + len(terms)),
        out_specs=pl.BlockSpec(memory_space=pltpu.VMEM),
        cost_estimate=pl.CostEstimate(
            flops=2 * base.size * 256, bytes_accessed=8 * base.size, transcendentals=0
        ),
        compiler_params=pltpu.CompilerParams(vmem_limit_bytes=8 << 20),
        name="finish",
    )(flags, base, scale_rows, scale_cols, *terms)


def on_device(greens, pairs, onsets):
    rows_dev, width = greens.shape
    groups = lax.axis_size("tm")
    share = width // groups
    row_group = lax.axis_index("tm")
    row_start = row_group * rows_dev
    owner = lax.axis_index("src")
    blocks = lax.axis_size("src")
    runs = runs_of(share)
    aligned = all(run % 8 == 0 and groups * run % 128 == 0 for _, run in runs)
    cut = rows_dev // HEAD

    owner_first = pairs[0, 0] == owner
    own_onset = onsets[owner]
    arrival = jnp.maximum(own_onset, onsets[(owner + blocks - 1) % blocks])
    row_ids = row_start + jnp.arange(rows_dev, dtype=jnp.int32)
    flags = jnp.stack([owner_first.astype(jnp.int32), row_group % 2])

    head = from_behind(greens[:cut], "src", 1)
    lower = []
    for run in runs:
        lower.append(from_behind(picked(greens[cut:], share, *run), "src", 1))
    own_f = jnp.where((row_ids >= own_onset)[:, None], greens.astype(jnp.float32), 0.0)
    norm_own = summed(jnp.sum(own_f * own_f, axis=0), "tm")
    norm_low = from_behind(norm_own, "src", 1)
    own = jnp.where((row_ids >= arrival)[:, None], greens, jnp.zeros_like(greens)).T
    head = jnp.concatenate([picked(head, share, *run) for run in runs], axis=1)

    done = []
    for step, (run, block) in enumerate(zip(runs, lower)):
        form = gram if aligned else gram_plain
        keep, give = form(flags, own, head, block, share, *run)
        terms = strips_arrived(keep, give, "tm")
        if step == len(runs) - 1:
            done.append(terms)
        else:
            done.append(functools.reduce(jnp.add, terms))

    scale_own = lax.rsqrt(norm_own + 1e-06)
    scale_low = lax.rsqrt(norm_low + 1e-06)
    scale_rows = lax.dynamic_slice_in_dim(
        jnp.where(owner_first, scale_own, scale_low), row_group * share, share, 0
    )[:, None]
    scale_cols = jnp.where(owner_first, scale_low, scale_own)[None, :]
    early, last = done[:-1], done[-1]
    if not aligned:
        early, last = early + [functools.reduce(jnp.add, last)], []
    base = lax.cond(
        owner_first,
        lambda *parts: put_back(runs, share, parts),
        lambda *parts: jnp.concatenate(
            parts + (jnp.zeros((share - sum(p.shape[0] for p in parts), width), jnp.float32),),
            axis=0,
        ),
        *early,
    )
    if aligned:
        return finish(flags, base, scale_rows, scale_cols, last, share, *runs[-1])
    return (base * scale_rows * scale_cols)[None]


def solution(mesh):
    in_specs = (P("tm", "src"), P("src", None), P())
    out_specs = P("src", "tm", None)
    return jax.shard_map(
        on_device, mesh=mesh, in_specs=in_specs, out_specs=out_specs, check_vma=False
    )
```

profile of v0, /device:TPU:0, one launch (start us, length us, event | category | flops | bytes accessed | tf_op | source)
XLA Modules:
  0.0 111.7 jit_solution(16472204657352161551)
XLA Ops:
  0.0 1.0 slice.13
  1.0 3.1 %collective-permute-start = (bf16[256,768]{1,0:T(8,128)(2,1)S(1)}, bf16[256,768]{1,0:T(8,128)(2,1)}, u32[]{:S(2)}, u32[]{:S(2)}) collective-permute-start(bf16[256,768]{1,0:T(8,128)(2,1)S(1)} %slice.13), channel_id=1, source_target_pairs={{0,8},{8,16},{16,24},{24,0},{1,9},{9,17},{17,25},{25,1},{2,10},{10... | collective-permute-start | bytes 1179656 | tf_op jit(solution)/shard_map/ppermute | solution.py:17
  4.2 0.0 copy-start.3
  4.2 3.8 %fusion.36 = bf16[1792,256]{1,0:T(8,128)(2,1)} fusion(bf16[2048,768]{1,0:T(8,128)(2,1)} %param.5, s32[256]{0:T(256)S(1)} %get-tuple-element.80, s32[256]{0:T(256)S(1)} %get-tuple-element.81, s32[256]{0:T(256)S(1)} %get-tuple-element.79, s32[256]{0:T(256)S(1)} %get-tuple-element.82, pred[256]{0:T(512)(128)(4,1)S(1)} %get-tuple-element.73, ...), kind=kOutput, calls=%fused_computation.58 | convolution fusion | flops 706084864 | bytes 3674624 | tf_op jit(solution)/shard_map/dot_general | solution.py:77
  8.0 1.6 %collective-permute-start.1 = (bf16[1792,256]{1,0:T(8,128)(2,1)}, bf16[1792,256]{1,0:T(8,128)(2,1)}, u32[]{:S(2)}, u32[]{:S(2)}) collective-permute-start(bf16[1792,256]{1,0:T(8,128)(2,1)} %fusion.36), channel_id=1, source_target_pairs={{0,8},{8,16},{16,24},{24,0},{1,9},{9,17},{17,25},{25,1},{2,10},{10... | collective-permute-start | bytes 2752520 | tf_op jit(solution)/shard_map/ppermute | solution.py:17
  9.6 1.9 %fusion.37 = bf16[1792,256]{1,0:T(8,128)(2,1)} fusion(bf16[2048,768]{1,0:T(8,128)(2,1)S(1)} %copy-done.3, s32[256]{0:T(256)S(1)} %get-tuple-element.80, s32[256]{0:T(256)S(1)} %get-tuple-element.81, s32[256]{0:T(256)S(1)} %get-tuple-element.79, s32[256]{0:T(256)S(1)} %get-tuple-element.82, pred[256]{0:T(512)(128)(4,1)S(1)} %get-tuple-element.73, ...), kind=kOutput, calls=%fused_computation.59 | convolution fusion | flops 706281472 | bytes 3675136 | tf_op jit(solution)/shard_map/dot_general | solution.py:77
  11.5 1.6 %collective-permute-start.6 = (bf16[1792,256]{1,0:T(8,128)(2,1)}, bf16[1792,256]{1,0:T(8,128)(2,1)}, u32[]{:S(2)}, u32[]{:S(2)}) collective-permute-start(bf16[1792,256]{1,0:T(8,128)(2,1)} %fusion.37), channel_id=1, source_target_pairs={{0,8},{8,16},{16,24},{24,0},{1,9},{9,17},{17,25},{25,1},{2,10},{10... | collective-permute-start | bytes 2752520 | tf_op jit(solution)/shard_map/ppermute | solution.py:17
  13.1 0.5 copy-done.16
  13.7 1.7 %fusion.38 = bf16[1792,128]{1,0:T(8,128)(2,1)} fusion(bf16[2048,768]{1,0:T(8,128)(2,1)S(1)} %copy-done.3, s32[128]{0:T(128)S(1)} %get-tuple-element.76, s32[128]{0:T(128)S(1)} %get-tuple-element.77, s32[128]{0:T(128)S(1)} %get-tuple-element.75, s32[128]{0:T(128)S(1)} %get-tuple-element.78, pred[128]{0:T(512)(128)(4,1)S(1)} %get-tuple-element.71, ...), kind=kOutput, calls=%fused_computation.62 | convolution fusion | flops 353140736 | bytes 3214336 | tf_op jit(solution)/shard_map/dot_general | solution.py:77
  15.4 0.0 collective-permute-start.11
  15.5 0.6 fusion.72
  16.1 0.6 fusion.58
  16.7 1.0 multiply_reduce_fusion
  17.8 0.1 collective-permute-start.16
  17.8 2.9 %copy.17 = bf16[2048,768]{0,1:T(8,128)(2,1)} copy(bf16[2048,768]{1,0:T(8,128)(2,1)S(1)} %copy-done.3) | data formatting | bytes 6291456 | tf_op args[0]
  22.0 0.0 copy-start.4
  22.1 2.3 %select_bitcast_fusion.own = bf16[768,2048]{1,0:T(8,128)(2,1)S(1)} fusion(bf16[2048,768]{0,1:T(8,128)(2,1)} %copy.17, pred[2048]{0:T(1024)(128)(4,1)S(1)} %fusion.59), kind=kLoop, calls=%fused_computation.55 | loop fusion | flops 1572864 | bytes 6293504 | tf_op jit(solution)/shard_map/transpose | solution.py:241
  24.4 0.0 copy-start.11
  24.4 1.7 %collective-permute-start.17 = (f32[768]{0:T(1024)S(1)}, f32[768]{0:T(1024)S(1)}, u32[]{:S(2)}, u32[]{:S(2)}) collective-permute-start(f32[768]{0:T(1024)S(1)} %add.272), channel_id=1, source_target_pairs={{0,2},{1,3},{2,0},{3,1},{4,6},{5,7},{6,4},{7,5},{8,10},{9,11},{10,... | collective-permute-start | bytes 9224 | tf_op jit(solution)/shard_map/ppermute | solution.py:22
  26.2 1.7 %fusion.39 = bf16[1792,128]{1,0:T(8,128)(2,1)} fusion(bf16[2048,768]{1,0:T(8,128)(2,1)S(1)} %copy-done.4, s32[128]{0:T(128)S(1)} %copy-done.17, s32[128]{0:T(128)S(1)} %copy-done.19, s32[128]{0:T(128)S(1)} %copy-done.15, s32[128]{0:T(128)S(1)} %copy-done.21, pred[128]{0:T(512)(128)(4,1)S(1)} %copy-done.23, pred[128]{0:T(512)(128)(4,1)S(1)} %copy-done.25), kind=kOutput, calls=%fused_computation.63 | convolution fusion | flops 353140736 | bytes 3214336 | tf_op jit(solution)/shard_map/dot_general | solution.py:77
  27.9 0.1 collective-permute-done.17
  28.1 1.7 %collective-permute-start.18 = (f32[768]{0:T(1024)S(1)}, f32[768]{0:T(1024)S(1)}, u32[]{:S(2)}, u32[]{:S(2)}) collective-permute-start(f32[768]{0:T(1024)S(1)} %add.273), channel_id=1, source_target_pairs={{0,4},{1,5},{2,6},{3,7},{4,0},{5,1},{6,2},{7,3},{8,12},{9,13},{10,... | collective-permute-start | bytes 9224 | tf_op jit(solution)/shard_map/ppermute | solution.py:22
  29.8 0.1 pad_add_fusion.flags
  29.8 1.9 %collective-permute-done.18 = f32[768]{0:T(1024)S(1)} collective-permute-done((f32[768]{0:T(1024)S(1)}, f32[768]{0:T(1024)S(1)}, u32[]{:S(2)}, u32[]{:S(2)}) %collective-permute-start.18) | collective-permute-done | bytes 3104 | tf_op jit(solution)/shard_map/ppermute | solution.py:22
  31.7 1.7 %collective-permute-start.20 = (bf16[1792,128]{1,0:T(8,128)(2,1)}, bf16[1792,128]{1,0:T(8,128)(2,1)S(1)}, u32[]{:S(2)}, u32[]{:S(2)}) collective-permute-start(bf16[1792,128]{1,0:T(8,128)(2,1)} %fusion.39), channel_id=1, source_target_pairs={{0,8},{8,16},{16,24},{24,0},{1,9},{9,17},{17,25},{25,1},{2,10},{10... | collective-permute-start | bytes 1376264 | tf_op jit(solution)/shard_map/ppermute | solution.py:17
  33.4 1.6 %collective-permute-start.19 = (f32[768]{0:T(1024)S(1)}, f32[768]{0:T(1024)S(1)}, u32[]{:S(2)}, u32[]{:S(2)}) collective-permute-start(f32[768]{0:T(1024)S(1)} %add.274), channel_id=1, source_target_pairs={{0,8},{8,16},{16,24},{24,0},{1,9},{9,17},{17,25},{25,1},{2,10},{10... | collective-permute-start | bytes 9224 | tf_op jit(solution)/shard_map/ppermute | solution.py:17
  35.0 1.4 %fusion.45 = bf16[256,256]{1,0:T(8,128)(2,1)S(1)} fusion(bf16[256,768]{1,0:T(8,128)(2,1)} %collective-permute-done, s32[256]{0:T(256)} %copy-done.8, s32[256]{0:T(256)} %copy-done.9, s32[256]{0:T(256)} %copy-done.6, s32[256]{0:T(256)} %copy-done.10, pred[256]{0:T(512)(128)(4,1)} %copy-done.12, pred[256]{0:T(512)(128)(4,1)} %copy-done.13), kind=kOutput, calls=%fused_computation.71 | convolution fusion | flops 101908480 | bytes 528896 | tf_op jit(solution)/shard_map/dot_general | solution.py:77
  36.4 1.4 %fusion.44 = bf16[256,256]{1,0:T(8,128)(2,1)S(1)} fusion(bf16[256,768]{1,0:T(8,128)(2,1)} %collective-permute-done, s32[256]{0:T(256)} %copy-done.8, s32[256]{0:T(256)} %copy-done.9, s32[256]{0:T(256)S(1)} %copy-done.7, s32[256]{0:T(256)} %copy-done.10, pred[256]{0:T(512)(128)(4,1)} %copy-done.12, pred[256]{0:T(512)(128)(4,1)} %copy-done.13), kind=kOutput, calls=%fused_computation.70 | convolution fusion | flops 101711872 | bytes 528896 | tf_op jit(solution)/shard_map/dot_general | solution.py:77
  37.8 1.3 %fusion.47 = bf16[256,128]{1,0:T(8,128)(2,1)S(1)} fusion(bf16[256,768]{1,0:T(8,128)(2,1)} %collective-permute-done, s32[128]{0:T(128)} %copy-done.16, s32[128]{0:T(128)} %copy-done.18, s32[128]{0:T(128)} %copy-done.14, s32[128]{0:T(128)} %copy-done.20, pred[128]{0:T(512)(128)(4,1)} %copy-done.22, pred[128]{0:T(512)(128)(4,1)} %copy-done.24), kind=kOutput, calls=%fused_computation.77 | convolution fusion | flops 50954240 | bytes 461056 | tf_op jit(solution)/shard_map/dot_general | solution.py:77
  39.1 1.3 %fusion.46 = bf16[256,128]{1,0:T(8,128)(2,1)S(1)} fusion(bf16[256,768]{1,0:T(8,128)(2,1)} %collective-permute-done, s32[128]{0:T(128)} %copy-done.16, s32[128]{0:T(128)} %copy-done.18, s32[128]{0:T(128)} %copy-done.14, s32[128]{0:T(128)} %copy-done.20, pred[128]{0:T(512)(128)(4,1)} %copy-done.22, pred[128]{0:T(512)(128)(4,1)} %copy-done.24), kind=kOutput, calls=%fused_computation.76 | convolution fusion | flops 50954240 | bytes 461056 | tf_op jit(solution)/shard_map/dot_general | solution.py:77
  40.4 24.9 %collective-permute-done.11.rest = bf16[1792,128]{1,0:T(8,128)(2,1)} collective-permute-done((bf16[1792,128]{1,0:T(8,128)(2,1)}, bf16[1792,128]{1,0:T(8,128)(2,1)}, u32[]{:S(2)}, u32[]{:S(2)}) %collective-permute-start.11) | collective-permute-done | bytes 458784 | tf_op jit(solution)/shard_map/ppermute | solution.py:17
  65.4 2.8 %gram.6 = (f32[4,16,768]{2,1,0:T(8,128)S(1)}, f32[4,16,768]{2,1,0:T(8,128)}) custom-call(s32[2]{0:T(128)S(1)} %pad_add_fusion.flags, bf16[768,2048]{1,0:T(8,128)(2,1)S(1)} %select_bitcast_fusion.own, bf16[256,768]{1,0:T(8,128)(2,1)S(1)} %pad_maximum_fusion.head, bf16[1792,128]{1,0:T(8,128)(2,1)} %collective-permute-done.11.rest), custom_call_target="tpu_custom_call" | custom-call | flops 402653184 | bytes 3145728 | tf_op jit(solution)/shard_map/gram/pallas_call | solution.py:120
  68.2 6.1 %collective-permute-done.19 = f32[768]{0:T(1024)S(1)} collective-permute-done((f32[768]{0:T(1024)S(1)}, f32[768]{0:T(1024)S(1)}, u32[]{:S(2)}, u32[]{:S(2)}) %collective-permute-start.19) | collective-permute-done | bytes 3104 | tf_op jit(solution)/shard_map/ppermute | solution.py:17
  74.4 2.4 %gram.7 = (f32[4,16,768]{2,1,0:T(8,128)S(1)}, f32[4,16,768]{2,1,0:T(8,128)}) custom-call(s32[2]{0:T(128)S(1)} %pad_add_fusion.flags, bf16[768,2048]{1,0:T(8,128)(2,1)S(1)} %select_bitcast_fusion.own, bf16[256,768]{1,0:T(8,128)(2,1)S(1)} %pad_maximum_fusion.head, bf16[1792,128]{1,0:T(8,128)(2,1)S(1)} %collective-permute-done.20.rest), custom_call_target="tpu_custom_call" | custom-call | flops 402653184 | bytes 3145728 | tf_op jit(solution)/shard_map/gram/pallas_call | solution.py:120
  76.7 0.7 copy-done.1
  77.4 0.1 dynamic-slice_bitcast_fusion.13
  77.5 0.7 copy.26.scale_rows
  78.2 1.0 add.268
  79.3 2.5 %collective-permute-start.15 = (f32[16,768]{1,0:T(8,128)S(1)}, f32[16,768]{1,0:T(8,128)S(1)}, u32[]{:S(2)}, u32[]{:S(2)}) collective-permute-start(f32[16,768]{1,0:T(8,128)S(1)} %get-tuple-element.65), channel_id=1, source_target_pairs={{0,6},{1,7},{2,4},{3,5},{4,2},{5,3},{6,0},{7,1},{8,14},{9,15},{10,... | collective-permute-start | bytes 147464 | tf_op jit(solution)/shard_map/ppermute | solution.py:22
  81.8 0.5 collective-permute-start.14
  82.3 0.5 collective-permute-start.13
  82.9 1.0 add.278
  83.9 2.5 %gram.4 = (f32[4,32,768]{2,1,0:T(8,128)S(1)}, f32[4,32,768]{2,1,0:T(8,128)S(1)}) custom-call(s32[2]{0:T(128)S(1)} %pad_add_fusion.flags, bf16[768,2048]{1,0:T(8,128)(2,1)S(1)} %select_bitcast_fusion.own, bf16[256,768]{1,0:T(8,128)(2,1)S(1)} %pad_maximum_fusion.head, bf16[1792,256]{1,0:T(8,128)(2,1)} %collective-permute-done.1.rest), custom_call_target="tpu_custom_call" | custom-call | flops 805306368 | bytes 3145728 | tf_op jit(solution)/shard_map/gram/pallas_call | solution.py:120
  86.4 0.1 collective-permute-start.2
  86.5 2.6 %gram.5 = (f32[4,32,768]{2,1,0:T(8,128)S(1)}, f32[4,32,768]{2,1,0:T(8,128)S(1)}) custom-call(s32[2]{0:T(128)S(1)} %pad_add_fusion.flags, bf16[768,2048]{1,0:T(8,128)(2,1)S(1)} %select_bitcast_fusion.own, bf16[256,768]{1,0:T(8,128)(2,1)S(1)} %pad_maximum_fusion.head, bf16[1792,256]{1,0:T(8,128)(2,1)} %collective-permute-done.6.rest), custom_call_target="tpu_custom_call" | custom-call | flops 805306368 | bytes 3145728 | tf_op jit(solution)/shard_map/gram/pallas_call | solution.py:120
  89.1 0.6 collective-permute-start.7
  89.7 1.6 %collective-permute-start.22 = (f32[16,768]{1,0:T(8,128)S(1)}, f32[16,768]{1,0:T(8,128)S(1)}, u32[]{:S(2)}, u32[]{:S(2)}) collective-permute-start(f32[16,768]{1,0:T(8,128)S(1)} %get-tuple-element.62), channel_id=1, source_target_pairs={{0,2},{1,3},{2,0},{3,1},{4,6},{5,7},{6,4},{7,5},{8,10},{9,11},{10,... | collective-permute-start | bytes 147464 | tf_op jit(solution)/shard_map/ppermute | solution.py:22
  91.3 1.5 %collective-permute-start.23 = (f32[16,768]{1,0:T(8,128)S(1)}, f32[16,768]{1,0:T(8,128)S(1)}, u32[]{:S(2)}, u32[]{:S(2)}) collective-permute-start(f32[16,768]{1,0:T(8,128)S(1)} %get-tuple-element.61), channel_id=1, source_target_pairs={{0,4},{1,5},{2,6},{3,7},{4,0},{5,1},{6,2},{7,3},{8,12},{9,13},{10,... | collective-permute-start | bytes 147464 | tf_op jit(solution)/shard_map/ppermute | solution.py:22
  92.9 0.5 collective-permute-start.5
  93.4 1.5 %collective-permute-start.4 = (f32[32,768]{1,0:T(8,128)S(1)}, f32[32,768]{1,0:T(8,128)S(1)}, u32[]{:S(2)}, u32[]{:S(2)}) collective-permute-start(f32[32,768]{1,0:T(8,128)S(1)} %get-tuple-element.59), channel_id=1, source_target_pairs={{0,4},{1,5},{2,6},{3,7},{4,0},{5,1},{6,2},{7,3},{8,12},{9,13},{10,... | collective-permute-start | bytes 294920 | tf_op jit(solution)/shard_map/ppermute | solution.py:22
  95.0 1.5 %collective-permute-start.3 = (f32[32,768]{1,0:T(8,128)S(1)}, f32[32,768]{1,0:T(8,128)S(1)}, u32[]{:S(2)}, u32[]{:S(2)}) collective-permute-start(f32[32,768]{1,0:T(8,128)S(1)} %get-tuple-element.57), channel_id=1, source_target_pairs={{0,2},{1,3},{2,0},{3,1},{4,6},{5,7},{6,4},{7,5},{8,10},{9,11},{10,... | collective-permute-start | bytes 294920 | tf_op jit(solution)/shard_map/ppermute | solution.py:22
  96.5 0.1 add.264
  96.6 2.6 %collective-permute-done.5 = f32[32,768]{1,0:T(8,128)S(1)} collective-permute-done((f32[32,768]{1,0:T(8,128)S(1)}, f32[32,768]{1,0:T(8,128)S(1)}, u32[]{:S(2)}, u32[]{:S(2)}) %collective-permute-start.5) | collective-permute-done | bytes 98336 | tf_op jit(solution)/shard_map/ppermute | solution.py:22
  99.1 0.4 collective-permute-done.4
  99.6 1.9 %collective-permute-start.9 = (f32[32,768]{1,0:T(8,128)S(1)}, f32[32,768]{1,0:T(8,128)S(1)}, u32[]{:S(2)}, u32[]{:S(2)}) collective-permute-start(f32[32,768]{1,0:T(8,128)S(1)} %get-tuple-element.56), channel_id=1, source_target_pairs={{0,4},{1,5},{2,6},{3,7},{4,0},{5,1},{6,2},{7,3},{8,12},{9,13},{10,... | collective-permute-start | bytes 294920 | tf_op jit(solution)/shard_map/ppermute | solution.py:22
  101.5 1.1 %collective-permute-start.8 = (f32[32,768]{1,0:T(8,128)S(1)}, f32[32,768]{1,0:T(8,128)S(1)}, u32[]{:S(2)}, u32[]{:S(2)}) collective-permute-start(f32[32,768]{1,0:T(8,128)S(1)} %get-tuple-element.54), channel_id=1, source_target_pairs={{0,2},{1,3},{2,0},{3,1},{4,6},{5,7},{6,4},{7,5},{8,10},{9,11},{10,... | collective-permute-start | bytes 294920 | tf_op jit(solution)/shard_map/ppermute | solution.py:22
  102.7 2.7 %collective-permute-done.10 = f32[32,768]{1,0:T(8,128)S(1)} collective-permute-done((f32[32,768]{1,0:T(8,128)S(1)}, f32[32,768]{1,0:T(8,128)S(1)}, u32[]{:S(2)}, u32[]{:S(2)}) %collective-permute-start.10) | collective-permute-done | bytes 98336 | tf_op jit(solution)/shard_map/ppermute | solution.py:22
  105.3 0.3 collective-permute-done.9
  105.7 1.0 collective-permute-done.8
  106.7 0.2 conditional.1
  106.8 0.1 pad.3.clone
  106.8 0.1 maximum_maximum_fusion
  107.0 3.4 %collective-permute-done.24.refs_3_ = f32[16,768]{1,0:T(8,128)S(1)} collective-permute-done((f32[16,768]{1,0:T(8,128)S(1)}, f32[16,768]{1,0:T(8,128)S(1)}, u32[]{:S(2)}, u32[]{:S(2)}) %collective-permute-start.24) | collective-permute-done | bytes 49184 | tf_op jit(solution)/shard_map/ppermute | solution.py:22
  110.3 1.4 %finish.1 = f32[1,96,768]{2,1,0:T(8,128)} custom-call(s32[2]{0:T(128)S(1)} %pad_add_fusion.flags, f32[96,768]{1,0:T(8,128)S(1)} %get-tuple-element.83.base, f32[96,1]{1,0:T(8,128)S(1)} %copy-done, f32[1,768]{1,0:T(1,128)S(1)} %broadcast_in_dim.36.scale_cols, f32[16,768]{1,0:T(8,128)S(1)} %get-tuple-element.63.refs_0_, ...), custom_call_target="tpu_custom_call" | custom-call | flops 37748736 | bytes 589824 | tf_op jit(solution)/shard_map/finish/pallas_call | solution.py:202
  (88 shorter events, 0.4 us)
Async XLA Ops:
  1.0 32.4 %collective-permute-start = (bf16[256,768]{1,0:T(8,128)(2,1)S(1)}, bf16[256,768]{1,0:T(8,128)(2,1)}, u32[]{:S(2)}, u32[]{:S(2)}) collective-permute-start(bf16[256,768]{1,0:T(8,128)(2,1)S(1)} %slice.13), channel_id=1, source_target_pairs={{0,8},{8,16},{16,24},{24,0},{1,9},{9,17},{17,25},{25,1},{2,10},{10... | collective-permute-start | bytes 1179656 | tf_op jit(solution)/shard_map/ppermute | solution.py:17
  4.1 5.5 %copy-start.6 = (s32[256]{0:T(256)}, s32[256]{0:T(256)S(1)}, u32[]{:S(2)}) copy-start(s32[256]{0:T(256)S(1)} %get-tuple-element.79) | copy-start | bytes 3076
  4.1 5.5 %copy-start.8 = (s32[256]{0:T(256)}, s32[256]{0:T(256)S(1)}, u32[]{:S(2)}) copy-start(s32[256]{0:T(256)S(1)} %get-tuple-element.80) | copy-start | bytes 3076
  4.1 5.4 %copy-start.9 = (s32[256]{0:T(256)}, s32[256]{0:T(256)S(1)}, u32[]{:S(2)}) copy-start(s32[256]{0:T(256)S(1)} %get-tuple-element.81) | copy-start | bytes 3076
  4.2 5.4 %copy-start.10 = (s32[256]{0:T(256)}, s32[256]{0:T(256)S(1)}, u32[]{:S(2)}) copy-start(s32[256]{0:T(256)S(1)} %get-tuple-element.82) | copy-start | bytes 3076
  4.2 5.4 %copy-start.12 = (pred[256]{0:T(512)(128)(4,1)}, pred[256]{0:T(512)(128)(4,1)S(1)}, u32[]{:S(2)}) copy-start(pred[256]{0:T(512)(128)(4,1)S(1)} %get-tuple-element.73) | copy-start | bytes 772
  4.2 5.4 %copy-start.13 = (pred[256]{0:T(512)(128)(4,1)}, pred[256]{0:T(512)(128)(4,1)S(1)}, u32[]{:S(2)}) copy-start(pred[256]{0:T(512)(128)(4,1)S(1)} %get-tuple-element.74) | copy-start | bytes 772
  4.2 5.4 %copy-start.3 = (bf16[2048,768]{1,0:T(8,128)(2,1)S(1)}, bf16[2048,768]{1,0:T(8,128)(2,1)}, u32[]{:S(2)}) copy-start(bf16[2048,768]{1,0:T(8,128)(2,1)} %param.5) | copy-start | bytes 9437188
  8.0 75.9 %collective-permute-start.1 = (bf16[1792,256]{1,0:T(8,128)(2,1)}, bf16[1792,256]{1,0:T(8,128)(2,1)}, u32[]{:S(2)}, u32[]{:S(2)}) collective-permute-start(bf16[1792,256]{1,0:T(8,128)(2,1)} %fusion.36), channel_id=1, source_target_pairs={{0,8},{8,16},{16,24},{24,0},{1,9},{9,17},{17,25},{25,1},{2,10},{10... | collective-permute-start | bytes 2752520 | tf_op jit(solution)/shard_map/ppermute | solution.py:17
  11.5 3.9 %copy-start.5 = (s32[4]{0:T(128)S(1)}, s32[4]{0:T(128)}, u32[]{:S(2)}) copy-start(s32[4]{0:T(128)} %param.7) | copy-start | bytes 52
  11.5 75.0 %collective-permute-start.6 = (bf16[1792,256]{1,0:T(8,128)(2,1)}, bf16[1792,256]{1,0:T(8,128)(2,1)}, u32[]{:S(2)}, u32[]{:S(2)}) collective-permute-start(bf16[1792,256]{1,0:T(8,128)(2,1)} %fusion.37), channel_id=1, source_target_pairs={{0,8},{8,16},{16,24},{24,0},{1,9},{9,17},{17,25},{25,1},{2,10},{10... | collective-permute-start | bytes 2752520 | tf_op jit(solution)/shard_map/ppermute | solution.py:17
  13.1 0.6 copy-start.16
  13.1 3.0 %copy-start.14 = (s32[128]{0:T(128)}, s32[128]{0:T(128)S(1)}, u32[]{:S(2)}) copy-start(s32[128]{0:T(128)S(1)} %get-tuple-element.75) | copy-start | bytes 1540
  13.1 2.3 %copy-start.18 = (s32[128]{0:T(128)}, s32[128]{0:T(128)S(1)}, u32[]{:S(2)}) copy-start(s32[128]{0:T(128)S(1)} %get-tuple-element.77) | copy-start | bytes 1540
  13.1 2.3 %copy-start.20 = (s32[128]{0:T(128)}, s32[128]{0:T(128)S(1)}, u32[]{:S(2)}) copy-start(s32[128]{0:T(128)S(1)} %get-tuple-element.78) | copy-start | bytes 1540
  13.1 2.3 %copy-start.22 = (pred[128]{0:T(512)(128)(4,1)}, pred[128]{0:T(512)(128)(4,1)S(1)}, u32[]{:S(2)}) copy-start(pred[128]{0:T(512)(128)(4,1)S(1)} %get-tuple-element.71) | copy-start | bytes 388
  13.1 2.3 %copy-start.24 = (pred[128]{0:T(512)(128)(4,1)}, pred[128]{0:T(512)(128)(4,1)S(1)}, u32[]{:S(2)}) copy-start(pred[128]{0:T(512)(128)(4,1)S(1)} %get-tuple-element.72) | copy-start | bytes 388
  15.4 50.0 %collective-permute-start.11 = (bf16[1792,128]{1,0:T(8,128)(2,1)}, bf16[1792,128]{1,0:T(8,128)(2,1)}, u32[]{:S(2)}, u32[]{:S(2)}) collective-permute-start(bf16[1792,128]{1,0:T(8,128)(2,1)} %fusion.38), channel_id=1, source_target_pairs={{0,8},{8,16},{16,24},{24,0},{1,9},{9,17},{17,25},{25,1},{2,10},{10... | collective-permute-start | bytes 1376264 | tf_op jit(solution)/shard_map/ppermute | solution.py:17
  17.8 6.6 %collective-permute-start.16 = (f32[768]{0:T(1024)S(1)}, f32[768]{0:T(1024)S(1)}, u32[]{:S(2)}, u32[]{:S(2)}) collective-permute-start(f32[768]{0:T(1024)S(1)} %multiply_reduce_fusion), channel_id=1, source_target_pairs={{0,1},{1,0},{2,3},{3,2},{4,5},{5,4},{6,7},{7,6},{8,9},{9,8},{10,11... | collective-permute-start | bytes 9224 | tf_op jit(solution)/shard_map/ppermute | solution.py:22
  22.0 4.1 %copy-start.4 = (bf16[2048,768]{1,0:T(8,128)(2,1)S(1)}, bf16[2048,768]{1,0:T(8,128)(2,1)}, u32[]{:S(2)}) copy-start(bf16[2048,768]{1,0:T(8,128)(2,1)} %param.5) | copy-start | bytes 9437188
  22.1 4.1 %copy-start.15 = (s32[128]{0:T(128)S(1)}, s32[128]{0:T(128)}, u32[]{:S(2)}) copy-start(s32[128]{0:T(128)} %copy-done.14) | copy-start | bytes 1540
  22.1 4.1 %copy-start.17 = (s32[128]{0:T(128)S(1)}, s32[128]{0:T(128)}, u32[]{:S(2)}) copy-start(s32[128]{0:T(128)} %copy-done.16) | copy-start | bytes 1540
  22.1 4.1 %copy-start.19 = (s32[128]{0:T(128)S(1)}, s32[128]{0:T(128)}, u32[]{:S(2)}) copy-start(s32[128]{0:T(128)} %copy-done.18) | copy-start | bytes 1540
  22.1 4.1 %copy-start.21 = (s32[128]{0:T(128)S(1)}, s32[128]{0:T(128)}, u32[]{:S(2)}) copy-start(s32[128]{0:T(128)} %copy-done.20) | copy-start | bytes 1540
  22.1 4.1 %copy-start.23 = (pred[128]{0:T(512)(128)(4,1)S(1)}, pred[128]{0:T(512)(128)(4,1)}, u32[]{:S(2)}) copy-start(pred[128]{0:T(512)(128)(4,1)} %copy-done.22) | copy-start | bytes 388
  22.1 4.1 %copy-start.25 = (pred[128]{0:T(512)(128)(4,1)S(1)}, pred[128]{0:T(512)(128)(4,1)}, u32[]{:S(2)}) copy-start(pred[128]{0:T(512)(128)(4,1)} %copy-done.24) | copy-start | bytes 388
  24.4 3.5 %copy-start.11 = (s32[1,2]{1,0:T(1,128)S(1)}, s32[1,2]{1,0:T(1,128)}, u32[]{:S(2)}) copy-start(s32[1,2]{1,0:T(1,128)} %param.6) | copy-start | bytes 28
  24.4 12.0 %copy-start.7 = (s32[256]{0:T(256)S(1)}, s32[256]{0:T(256)}, u32[]{:S(2)}) copy-start(s32[256]{0:T(256)} %copy-done.6) | copy-start | bytes 3076
  24.4 3.7 %collective-permute-start.17 = (f32[768]{0:T(1024)S(1)}, f32[768]{0:T(1024)S(1)}, u32[]{:S(2)}, u32[]{:S(2)}) collective-permute-start(f32[768]{0:T(1024)S(1)} %add.272), channel_id=1, source_target_pairs={{0,2},{1,3},{2,0},{3,1},{4,6},{5,7},{6,4},{7,5},{8,10},{9,11},{10,... | collective-permute-start | bytes 9224 | tf_op jit(solution)/shard_map/ppermute | solution.py:22
  28.1 3.6 %collective-permute-start.18 = (f32[768]{0:T(1024)S(1)}, f32[768]{0:T(1024)S(1)}, u32[]{:S(2)}, u32[]{:S(2)}) collective-permute-start(f32[768]{0:T(1024)S(1)} %add.273), channel_id=1, source_target_pairs={{0,4},{1,5},{2,6},{3,7},{4,0},{5,1},{6,2},{7,3},{8,12},{9,13},{10,... | collective-permute-start | bytes 9224 | tf_op jit(solution)/shard_map/ppermute | solution.py:22
  31.7 42.7 %collective-permute-start.20 = (bf16[1792,128]{1,0:T(8,128)(2,1)}, bf16[1792,128]{1,0:T(8,128)(2,1)S(1)}, u32[]{:S(2)}, u32[]{:S(2)}) collective-permute-start(bf16[1792,128]{1,0:T(8,128)(2,1)} %fusion.39), channel_id=1, source_target_pairs={{0,8},{8,16},{16,24},{24,0},{1,9},{9,17},{17,25},{25,1},{2,10},{10... | collective-permute-start | bytes 1376264 | tf_op jit(solution)/shard_map/ppermute | solution.py:17
  33.4 40.9 %collective-permute-start.19 = (f32[768]{0:T(1024)S(1)}, f32[768]{0:T(1024)S(1)}, u32[]{:S(2)}, u32[]{:S(2)}) collective-permute-start(f32[768]{0:T(1024)S(1)} %add.274), channel_id=1, source_target_pairs={{0,8},{8,16},{16,24},{24,0},{1,9},{9,17},{17,25},{25,1},{2,10},{10... | collective-permute-start | bytes 9224 | tf_op jit(solution)/shard_map/ppermute | solution.py:17
  68.2 8.5 %copy-start.2 = (f32[4,16,768]{2,1,0:T(8,128)}, f32[4,16,768]{2,1,0:T(8,128)S(1)}, u32[]{:S(2)}) copy-start(f32[4,16,768]{2,1,0:T(8,128)S(1)} %get-tuple-element.38) | copy-start | bytes 589828
  68.2 10.0 %collective-permute-start.12 = (f32[4,16,768]{2,1,0:T(8,128)}, f32[4,16,768]{2,1,0:T(8,128)}, u32[]{:S(2)}, u32[]{:S(2)}) collective-permute-start(f32[4,16,768]{2,1,0:T(8,128)} %get-tuple-element.39), channel_id=1, source_target_pairs={{0,1},{1,0},{2,3},{3,2},{4,5},{5,4},{6,7},{7,6},{8,9},{9,8},{10,11... | collective-permute-start | bytes 589832 | tf_op jit(solution)/shard_map/ppermute | solution.py:22
  76.7 0.7 copy-start.1
  77.4 4.9 %collective-permute-start.21 = (f32[4,16,768]{2,1,0:T(8,128)}, f32[4,16,768]{2,1,0:T(8,128)}, u32[]{:S(2)}, u32[]{:S(2)}) collective-permute-start(f32[4,16,768]{2,1,0:T(8,128)} %get-tuple-element.41), channel_id=1, source_target_pairs={{0,1},{1,0},{2,3},{3,2},{4,5},{5,4},{6,7},{7,6},{8,9},{9,8},{10,11... | collective-permute-start | bytes 589832 | tf_op jit(solution)/shard_map/ppermute | solution.py:22
  79.3 10.4 %collective-permute-start.15 = (f32[16,768]{1,0:T(8,128)S(1)}, f32[16,768]{1,0:T(8,128)S(1)}, u32[]{:S(2)}, u32[]{:S(2)}) collective-permute-start(f32[16,768]{1,0:T(8,128)S(1)} %get-tuple-element.65), channel_id=1, source_target_pairs={{0,6},{1,7},{2,4},{3,5},{4,2},{5,3},{6,0},{7,1},{8,14},{9,15},{10,... | collective-permute-start | bytes 147464 | tf_op jit(solution)/shard_map/ppermute | solution.py:22
  81.8 9.4 %collective-permute-start.14 = (f32[16,768]{1,0:T(8,128)S(1)}, f32[16,768]{1,0:T(8,128)S(1)}, u32[]{:S(2)}, u32[]{:S(2)}) collective-permute-start(f32[16,768]{1,0:T(8,128)S(1)} %get-tuple-element.66), channel_id=1, source_target_pairs={{0,4},{1,5},{2,6},{3,7},{4,0},{5,1},{6,2},{7,3},{8,12},{9,13},{10,... | collective-permute-start | bytes 147464 | tf_op jit(solution)/shard_map/ppermute | solution.py:22
  82.3 10.4 %collective-permute-start.13 = (f32[16,768]{1,0:T(8,128)S(1)}, f32[16,768]{1,0:T(8,128)S(1)}, u32[]{:S(2)}, u32[]{:S(2)}) collective-permute-start(f32[16,768]{1,0:T(8,128)S(1)} %get-tuple-element.64), channel_id=1, source_target_pairs={{0,2},{1,3},{2,0},{3,1},{4,6},{5,7},{6,4},{7,5},{8,10},{9,11},{10,... | collective-permute-start | bytes 147464 | tf_op jit(solution)/shard_map/ppermute | solution.py:22
  86.4 6.4 %collective-permute-start.2 = (f32[4,32,768]{2,1,0:T(8,128)S(1)}, f32[4,32,768]{2,1,0:T(8,128)S(1)}, u32[]{:S(2)}, u32[]{:S(2)}) collective-permute-start(f32[4,32,768]{2,1,0:T(8,128)S(1)} %get-tuple-element.35), channel_id=1, source_target_pairs={{0,1},{1,0},{2,3},{3,2},{4,5},{5,4},{6,7},{7,6},{8,9},{9,8},{10,11... | collective-permute-start | bytes 1179656 | tf_op jit(solution)/shard_map/ppermute | solution.py:22
  89.1 5.9 %collective-permute-start.7 = (f32[4,32,768]{2,1,0:T(8,128)S(1)}, f32[4,32,768]{2,1,0:T(8,128)S(1)}, u32[]{:S(2)}, u32[]{:S(2)}) collective-permute-start(f32[4,32,768]{2,1,0:T(8,128)S(1)} %get-tuple-element.37), channel_id=1, source_target_pairs={{0,1},{1,0},{2,3},{3,2},{4,5},{5,4},{6,7},{7,6},{8,9},{9,8},{10,11... | collective-permute-start | bytes 1179656 | tf_op jit(solution)/shard_map/ppermute | solution.py:22
  89.7 17.3 %collective-permute-start.22 = (f32[16,768]{1,0:T(8,128)S(1)}, f32[16,768]{1,0:T(8,128)S(1)}, u32[]{:S(2)}, u32[]{:S(2)}) collective-permute-start(f32[16,768]{1,0:T(8,128)S(1)} %get-tuple-element.62), channel_id=1, source_target_pairs={{0,2},{1,3},{2,0},{3,1},{4,6},{5,7},{6,4},{7,5},{8,10},{9,11},{10,... | collective-permute-start | bytes 147464 | tf_op jit(solution)/shard_map/ppermute | solution.py:22
  91.3 15.7 %collective-permute-start.23 = (f32[16,768]{1,0:T(8,128)S(1)}, f32[16,768]{1,0:T(8,128)S(1)}, u32[]{:S(2)}, u32[]{:S(2)}) collective-permute-start(f32[16,768]{1,0:T(8,128)S(1)} %get-tuple-element.61), channel_id=1, source_target_pairs={{0,4},{1,5},{2,6},{3,7},{4,0},{5,1},{6,2},{7,3},{8,12},{9,13},{10,... | collective-permute-start | bytes 147464 | tf_op jit(solution)/shard_map/ppermute | solution.py:22
  92.9 6.2 %collective-permute-start.5 = (f32[32,768]{1,0:T(8,128)S(1)}, f32[32,768]{1,0:T(8,128)S(1)}, u32[]{:S(2)}, u32[]{:S(2)}) collective-permute-start(f32[32,768]{1,0:T(8,128)S(1)} %get-tuple-element.58), channel_id=1, source_target_pairs={{0,6},{1,7},{2,4},{3,5},{4,2},{5,3},{6,0},{7,1},{8,14},{9,15},{10,... | collective-permute-start | bytes 294920 | tf_op jit(solution)/shard_map/ppermute | solution.py:22
  93.4 6.1 %collective-permute-start.4 = (f32[32,768]{1,0:T(8,128)S(1)}, f32[32,768]{1,0:T(8,128)S(1)}, u32[]{:S(2)}, u32[]{:S(2)}) collective-permute-start(f32[32,768]{1,0:T(8,128)S(1)} %get-tuple-element.59), channel_id=1, source_target_pairs={{0,4},{1,5},{2,6},{3,7},{4,0},{5,1},{6,2},{7,3},{8,12},{9,13},{10,... | collective-permute-start | bytes 294920 | tf_op jit(solution)/shard_map/ppermute | solution.py:22
  95.0 6.5 %collective-permute-start.3 = (f32[32,768]{1,0:T(8,128)S(1)}, f32[32,768]{1,0:T(8,128)S(1)}, u32[]{:S(2)}, u32[]{:S(2)}) collective-permute-start(f32[32,768]{1,0:T(8,128)S(1)} %get-tuple-element.57), channel_id=1, source_target_pairs={{0,2},{1,3},{2,0},{3,1},{4,6},{5,7},{6,4},{7,5},{8,10},{9,11},{10,... | collective-permute-start | bytes 294920 | tf_op jit(solution)/shard_map/ppermute | solution.py:22
  99.1 6.2 %collective-permute-start.10 = (f32[32,768]{1,0:T(8,128)S(1)}, f32[32,768]{1,0:T(8,128)S(1)}, u32[]{:S(2)}, u32[]{:S(2)}) collective-permute-start(f32[32,768]{1,0:T(8,128)S(1)} %get-tuple-element.55), channel_id=1, source_target_pairs={{0,6},{1,7},{2,4},{3,5},{4,2},{5,3},{6,0},{7,1},{8,14},{9,15},{10,... | collective-permute-start | bytes 294920 | tf_op jit(solution)/shard_map/ppermute | solution.py:22
  99.6 6.1 %collective-permute-start.9 = (f32[32,768]{1,0:T(8,128)S(1)}, f32[32,768]{1,0:T(8,128)S(1)}, u32[]{:S(2)}, u32[]{:S(2)}) collective-permute-start(f32[32,768]{1,0:T(8,128)S(1)} %get-tuple-element.56), channel_id=1, source_target_pairs={{0,4},{1,5},{2,6},{3,7},{4,0},{5,1},{6,2},{7,3},{8,12},{9,13},{10,... | collective-permute-start | bytes 294920 | tf_op jit(solution)/shard_map/ppermute | solution.py:22
  101.5 5.2 %collective-permute-start.8 = (f32[32,768]{1,0:T(8,128)S(1)}, f32[32,768]{1,0:T(8,128)S(1)}, u32[]{:S(2)}, u32[]{:S(2)}) collective-permute-start(f32[32,768]{1,0:T(8,128)S(1)} %get-tuple-element.54), channel_id=1, source_target_pairs={{0,2},{1,3},{2,0},{3,1},{4,6},{5,7},{6,4},{7,5},{8,10},{9,11},{10,... | collective-permute-start | bytes 294920 | tf_op jit(solution)/shard_map/ppermute | solution.py:22
  102.7 7.7 %copy-start = (f32[96,1]{1,0:T(8,128)S(1)}, f32[96,1]{1,0:T(8,128)}, u32[]{:S(2)}) copy-start(f32[96,1]{1,0:T(8,128)} %copy.26.scale_rows) | copy-start | bytes 1156
  105.3 5.0 %collective-permute-start.24 = (f32[16,768]{1,0:T(8,128)S(1)}, f32[16,768]{1,0:T(8,128)S(1)}, u32[]{:S(2)}, u32[]{:S(2)}) collective-permute-start(f32[16,768]{1,0:T(8,128)S(1)} %get-tuple-element.60), channel_id=1, source_target_pairs={{0,6},{1,7},{2,4},{3,5},{4,2},{5,3},{6,0},{7,1},{8,14},{9,15},{10,... | collective-permute-start | bytes 147464 | tf_op jit(solution)/shard_map/ppermute | solution.py:22
where the time goes:
time: 112 us
  waiting for transfers between devices  43.5 us (39%)
  starting transfers between devices  27 us (24%)
  matrix products  14.4 us (13%)
  Pallas kernels  11.7 us (10%)
  local copies, waits for them, and re-layouts  6.89 us (6%)
  other arithmetic  6.4 us (6%)
  between operations  1.81 us (2%)
    ppermute x6, waiting for transfers between devices, from_behind(): lax.ppermute(value, axis, [(i, (i + by) % length) for i in range(length)])  31.1 us
    ppermute x19, starting transfers between devices, swapped(): return lax.ppermute(value, axis, [(i, i ^ bits) for i in range(length)])  17.4 us
    dot_general x8, matrix products, picked(): jnp.dot(block, picker(block.shape[1], share, start, run).astype(jnp.bfloa...  14.4 us
    ppermute x19, waiting for transfers between devices, swapped(): return lax.ppermute(value, axis, [(i, i ^ bits) for i in range(length)])  12.4 us
    pallas_call x4, Pallas kernels, gram(): pl.pallas_call(functools.partial(gram_kernel, start * groups, share, run)...  10.3 us
    ppermute x6, starting transfers between devices, from_behind(): lax.ppermute(value, axis, [(i, (i + by) % length) for i in range(length)])  9.62 us
    unnamed x53, local copies, waits for them, and re-layouts  4.25 us
    transpose x1, other arithmetic, on_device(): jnp.where((row_ids >= arrival)[:, None], greens, jnp.zeros_like(greens))  2.25 us
  transfers between devices with their start and end apart: 25, of which 10 were waited for; matrix products, arithmetic and copies ran while one was open for 23% of the time, Pallas kernels for 9%

commit v1 on v0

--- a/solution.py
+++ b/solution.py
@@ -8,7 +8,7 @@
 from jax.sharding import PartitionSpec as P
 
 
-PARTS = (2, 2, 1, 1)
+PARTS = (2, 2, 2)
 HEAD = 8
 
 
@@ -73,15 +73,65 @@
     return (q // run) * share + start + q % run == source
 
 
-def picked(block, share, start, run):
-    return jnp.dot(
-        block,
-        picker(block.shape[1], share, start, run).astype(jnp.bfloat16),
-        preferred_element_type=jnp.float32,
-    ).astype(jnp.bfloat16)
-
-
-def gram_kernel(lane, share, run, flags, own, head, rest, keep, give, part):
+def picks_kernel(share, runs, skip, block, *outs):
+    width = block.shape[1]
+    source = block[skip:, :]
+    for (start, run), out in zip(runs, outs):
+        order = picker(width, share, start, run).astype(jnp.float32).astype(jnp.bfloat16)
+        out[...] = jnp.dot(source, order, preferred_element_type=jnp.float32).astype(jnp.bfloat16)
+
+
+def picks(block, share, runs, skip):
+    rows, width = block.shape
+    groups = width // share
+    return pl.pallas_call(
+        functools.partial(picks_kernel, share, runs, skip),
+        out_shape=[
+            jax.ShapeDtypeStruct((rows - skip, groups * run), jnp.bfloat16) for _, run in runs
+        ],
+        in_specs=[pl.BlockSpec(memory_space=pltpu.VMEM)],
+        out_specs=[pl.BlockSpec(memory_space=pltpu.VMEM) for _ in runs],
+        cost_estimate=pl.CostEstimate(
+            flops=2 * block.size * width, bytes_accessed=4 * block.size, transcendentals=0
+        ),
+        compiler_params=pltpu.CompilerParams(vmem_limit_bytes=24 << 20),
+        name="picks",
+    )(block)
+
+
+def turn_kernel(step, firsts, block, turned, squares):
+    rows, width = block.shape
+    total = jnp.zeros((1, width), jnp.float32)
+    for top in range(0, rows, step):
+        piece = block[top : top + step, :]
+        ids = lax.broadcasted_iota(jnp.int32, (step, width), 0) + top
+        wide = jnp.where(ids >= firsts[0], piece.astype(jnp.float32), 0.0)
+        total = total + jnp.sum(wide * wide, axis=0, keepdims=True)
+        shown = jnp.where(ids >= firsts[1], piece.astype(jnp.float32), 0.0)
+        turned[:, top : top + step] = shown.T.astype(jnp.bfloat16)
+    squares[...] = total
+
+
+def turn(firsts, block):
+    rows, width = block.shape
+    step = 128 if rows % 128 == 0 else rows
+    return pl.pallas_call(
+        functools.partial(turn_kernel, step),
+        out_shape=(
+            jax.ShapeDtypeStruct((width, rows), jnp.bfloat16),
+            jax.ShapeDtypeStruct((1, width), jnp.float32),
+        ),
+        in_specs=[pl.BlockSpec(memory_space=pltpu.SMEM), pl.BlockSpec(memory_space=pltpu.VMEM)],
+        out_specs=(pl.BlockSpec(memory_space=pltpu.VMEM),) * 2,
+        cost_estimate=pl.CostEstimate(
+            flops=4 * block.size, bytes_accessed=4 * block.size, transcendentals=0
+        ),
+        compiler_params=pltpu.CompilerParams(vmem_limit_bytes=16 << 20),
+        name="turn",
+    )(firsts, block)
+
+
+def gram_kernel(share, run, flags, own, head, rest, keep, give, part):
     cut = head.shape[0]
     columns = rest.shape[1]
     groups = keep.shape[0] * 2
@@ -89,7 +139,7 @@
     product = jnp.dot(
         own[:, cut:], rest[...], preferred_element_type=jnp.float32
     ) + jnp.dot(
-        own[:, :cut], head[:, lane : lane + columns], preferred_element_type=jnp.float32
+        own[:, :cut], head[...], preferred_element_type=jnp.float32
     )
 
     @pl.when(flags[0] == 1)
@@ -112,13 +162,13 @@
             give[pair] = jnp.where(bit == 0, uneven, even)
 
 
-def gram(flags, own, head, rest, share, start, run):
+def gram(flags, own, head, rest, share, run):
     width = own.shape[0]
     groups = width // share
-    half = jax.ShapeDtypeStruct((groups // 2, run, width), jnp.float32)
+    half = pltpu.VMEM((groups // 2, run, width), jnp.float32)
     columns = groups * run
     return pl.pallas_call(
-        functools.partial(gram_kernel, start * groups, share, run),
+        functools.partial(gram_kernel, share, run),
         out_shape=(half, half),
         in_specs=[pl.BlockSpec(memory_space=pltpu.SMEM)]
         + [pl.BlockSpec(memory_space=pltpu.VMEM)] * 3,
@@ -132,11 +182,11 @@
     )(flags, own, head, rest)
 
 
-def gram_plain(flags, own, head, rest, share, start, run):
+def gram_plain(flags, own, head, rest, share, run):
     width = own.shape[0]
     groups = width // share
     columns = groups * run
-    block = jnp.concatenate([head[:, start * groups : start * groups + columns], rest], axis=0)
+    block = jnp.concatenate([head, rest], axis=0)
     product = jnp.dot(own, block, preferred_element_type=jnp.float32)
     strips = jnp.where(
         flags[0] == 1,
@@ -166,13 +216,9 @@
     return total
 
 
-def finish_kernel(share, start, run, flags, base, scale_rows, scale_cols, *refs):
-    *terms, out = refs
-    width = base.shape[1]
+def placed(flags, share, start, run, part, total):
+    width = total.shape[1]
     columns = width // share * run
-    part = terms[0][...]
-    for term in terms[1:]:
-        part = part + term[...]
 
     @pl.when(flags[0] == 1)
     def _():
@@ -182,20 +228,49 @@
         q = lax.broadcasted_iota(jnp.int32, (columns, width), 0)
         source = lax.broadcasted_iota(jnp.int32, (columns, width), 1)
         order = (q // run) * share + start + q % run == source
-        placed = jnp.dot(
+        total[...] += jnp.dot(
             spread,
             order.astype(jnp.float32),
             precision=lax.Precision.HIGHEST,
             preferred_element_type=jnp.float32,
         )
-        out[0] = (base[...] + placed) * scale_rows[...] * scale_cols[...]
 
     @pl.when(flags[0] == 0)
     def _():
-        out[0] = base[...] * scale_rows[...] * scale_cols[...]
-        out[0, start : start + run, :] = (
-            part * scale_rows[start : start + run, :] * scale_cols[...]
-        )
+        total[start : start + run, :] = part
+
+
+def base_kernel(share, runs, flags, *refs):
+    *parts, total = refs
+    total[...] = jnp.zeros_like(total)
+    for (start, run), part in zip(runs, parts):
+        placed(flags, share, start, run, part[...], total)
+
+
+def finish_kernel(share, start, run, flags, base, scale_rows, scale_cols, *refs):
+    *terms, out, total = refs
+    total[...] = base[...]
+    part = terms[0][...]
+    for term in terms[1:]:
+        part = part + term[...]
+    placed(flags, share, start, run, part, total)
+    out[0] = total[...] * scale_rows[...] * scale_cols[...]
+
+
+def base_of(flags, parts, share, runs):
+    width = parts[0].shape[1]
+    return pl.pallas_call(
+        functools.partial(base_kernel, share, runs),
+        out_shape=pltpu.VMEM((share, width), jnp.float32),
+        in_specs=[pl.BlockSpec(memory_space=pltpu.SMEM)]
+        + [pl.BlockSpec(memory_space=pltpu.VMEM)] * len(parts),
+        out_specs=pl.BlockSpec(memory_space=pltpu.VMEM),
+        cost_estimate=pl.CostEstimate(
+            flops=2 * share * width * 512, bytes_accessed=8 * share * width, transcendentals=0
+        ),
+        compiler_params=pltpu.CompilerParams(vmem_limit_bytes=8 << 20),
+        name="base",
+    )(flags, *parts)
 
 
 def finish(flags, base, scale_rows, scale_cols, terms, share, start, run):
@@ -205,6 +280,7 @@
         in_specs=[pl.BlockSpec(memory_space=pltpu.SMEM)]
         + [pl.BlockSpec(memory_space=pltpu.VMEM)] * (3 + len(terms)),
         out_specs=pl.BlockSpec(memory_space=pltpu.VMEM),
+        scratch_shapes=[pltpu.VMEM(base.shape, jnp.float32)],
         cost_estimate=pl.CostEstimate(
             flops=2 * base.size * 256, bytes_accessed=8 * base.size, transcendentals=0
         ),
@@ -228,23 +304,23 @@
     owner_first = pairs[0, 0] == owner
     own_onset = onsets[owner]
     arrival = jnp.maximum(own_onset, onsets[(owner + blocks - 1) % blocks])
-    row_ids = row_start + jnp.arange(rows_dev, dtype=jnp.int32)
+    firsts = jnp.stack([own_onset, arrival]) - row_start
     flags = jnp.stack([owner_first.astype(jnp.int32), row_group % 2])
 
     head = from_behind(greens[:cut], "src", 1)
+    chosen = picks(greens, share, runs, cut)
     lower = []
-    for run in runs:
-        lower.append(from_behind(picked(greens[cut:], share, *run), "src", 1))
-    own_f = jnp.where((row_ids >= own_onset)[:, None], greens.astype(jnp.float32), 0.0)
-    norm_own = summed(jnp.sum(own_f * own_f, axis=0), "tm")
+    for block in chosen:
+        lower.append(from_behind(block, "src", 1))
+    own, squares = turn(firsts, greens)
+    norm_own = summed(squares[0], "tm")
     norm_low = from_behind(norm_own, "src", 1)
-    own = jnp.where((row_ids >= arrival)[:, None], greens, jnp.zeros_like(greens)).T
-    head = jnp.concatenate([picked(head, share, *run) for run in runs], axis=1)
+    heads = picks(head, share, runs, 0)
 
     done = []
-    for step, (run, block) in enumerate(zip(runs, lower)):
+    for step, (run, top, block) in enumerate(zip(runs, heads, lower)):
         form = gram if aligned else gram_plain
-        keep, give = form(flags, own, head, block, share, *run)
+        keep, give = form(flags, own, top, block, share, run[1])
         terms = strips_arrived(keep, give, "tm")
         if step == len(runs) - 1:
             done.append(terms)
@@ -257,20 +333,13 @@
         jnp.where(owner_first, scale_own, scale_low), row_group * share, share, 0
     )[:, None]
     scale_cols = jnp.where(owner_first, scale_low, scale_own)[None, :]
-    early, last = done[:-1], done[-1]
-    if not aligned:
-        early, last = early + [functools.reduce(jnp.add, last)], []
-    base = lax.cond(
-        owner_first,
-        lambda *parts: put_back(runs, share, parts),
-        lambda *parts: jnp.concatenate(
-            parts + (jnp.zeros((share - sum(p.shape[0] for p in parts), width), jnp.float32),),
-            axis=0,
-        ),
-        *early,
+    if aligned:
+        base = base_of(flags, done[:-1], share, runs[:-1])
+        return finish(flags, base, scale_rows, scale_cols, done[-1], share, *runs[-1])
+    parts = done[:-1] + [functools.reduce(jnp.add, done[-1])]
+    base = jnp.where(
+        owner_first, put_back(runs, share, parts), jnp.concatenate(parts, axis=0)
     )
-    if aligned:
-        return finish(flags, base, scale_rows, scale_cols, last, share, *runs[-1])
     return (base * scale_rows * scale_cols)[None]
 
 

time: 112 us -> 117 us (1.045)
  waiting for transfers between devices: 43.5 us -> 64 us
  matrix products: 14.4 us -> 0 us
  Pallas kernels: 11.7 us -> 19.2 us
  starting transfers between devices: 27 us -> 22.3 us
  other arithmetic: 6.4 us -> 3.22 us
    ppermute x6 -> x5, waiting for transfers between devices: 31.1 us -> 49.4 us  [from_behind(): lax.ppermute(value, axis, [(i, (i + by) % length) for i in range(length)])]
    dot_general x8 -> x0, matrix products: 14.4 us -> none  [picked(): jnp.dot(block, picker(block.shape[1], share, start, run).astype(jnp.bfloa...]
    pallas_call x4 -> x7, Pallas kernels: 10.3 us -> 17.8 us  [the longest x3 9.54 us: gram(): pl.pallas_call(functools.partial(gram_kernel, share, run), out_shape=(hal...]
    ppermute x19 -> x15, starting transfers between devices: 17.4 us -> 14.3 us  [swapped(): return lax.ppermute(value, axis, [(i, i ^ bits) for i in range(length)])]
    transpose x1 -> x0, other arithmetic: 2.25 us -> none  [on_device(): jnp.where((row_ids >= arrival)[:, None], greens, jnp.zeros_like(greens))]
    ppermute x19 -> x15, waiting for transfers between devices: 12.4 us -> 14.7 us  [swapped(): return lax.ppermute(value, axis, [(i, i ^ bits) for i in range(length)])]
    ppermute x6 -> x5, starting transfers between devices: 9.62 us -> 8 us  [from_behind(): lax.ppermute(value, axis, [(i, (i + by) % length) for i in range(length)])]
    unnamed x53 -> x12, local copies, waits for them, and re-layouts: 4.25 us -> 4.54 us
  transfers between devices with their start and end apart: 25 -> 20, of which waited for: 10 -> 8; matrix products, arithmetic and copies ran while one was open for 23% -> 4% of each run, Pallas kernels for 9% -> 12%
where the time goes in v1:
time: 117 us; the launch traced here: 116 us
  waiting for transfers between devices  64 us (55%)
  starting transfers between devices  22.3 us (19%)
  Pallas kernels  19.2 us (16%)
  local copies, waits for them, and re-layouts  6.21 us (5%)
  other arithmetic  3.22 us (3%)
  between operations  1.48 us (1%)
    ppermute x5, waiting for transfers between devices, from_behind(): lax.ppermute(value, axis, [(i, (i + by) % length) for i in range(length)])  49.4 us
    ppermute x15, waiting for transfers between devices, swapped(): return lax.ppermute(value, axis, [(i, i ^ bits) for i in range(length)])  14.7 us
    ppermute x15, starting transfers between devices, swapped(): return lax.ppermute(value, axis, [(i, i ^ bits) for i in range(length)])  14.3 us
    pallas_call x3, Pallas kernels, gram(): pl.pallas_call(functools.partial(gram_kernel, share, run), out_shape=(hal...  9.54 us
    ppermute x5, starting transfers between devices, from_behind(): lax.ppermute(value, axis, [(i, (i + by) % length) for i in range(length)])  8 us
    pallas_call x2, Pallas kernels, picks(): pl.pallas_call(functools.partial(picks_kernel, share, runs, skip), out_sh...  5.21 us
    unnamed x12, local copies, waits for them, and re-layouts  4.54 us
    pallas_call x1, Pallas kernels, turn(): pl.pallas_call(functools.partial(turn_kernel, step), out_shape=(jax.Shape...  2.42 us
  transfers between devices with their start and end apart: 20, of which 8 were waited for; matrix products, arithmetic and copies ran while one was open for 4% of the time, Pallas kernels for 12%

profile of v1, /device:TPU:0, one launch (start us, length us, event | category | flops | bytes accessed | tf_op | source)
XLA Modules:
  0.0 116.4 jit_solution(17073249340031949790)
XLA Ops:
  0.0 0.0 copy-start
  0.0 1.9 %copy-done = bf16[2048,768]{1,0:T(8,128)(2,1)S(1)} copy-done((bf16[2048,768]{1,0:T(8,128)(2,1)S(1)}, bf16[2048,768]{1,0:T(8,128)(2,1)}, u32[]{:S(2)}) %copy-start) | copy-done | bytes 3145752
  1.9 3.7 %picks.3 = (bf16[1792,256]{1,0:T(8,128)(2,1)}, bf16[1792,256]{1,0:T(8,128)(2,1)}, bf16[1792,256]{1,0:T(8,128)(2,1)}) custom-call(bf16[2048,768]{1,0:T(8,128)(2,1)S(1)} %copy-done), custom_call_target="tpu_custom_call" | custom-call | flops 2415919104 | bytes 6291456 | tf_op jit(solution)/shard_map/picks/pallas_call | solution.py:87
  5.6 3.1 %collective-permute-start.15 = (bf16[1792,256]{1,0:T(8,128)(2,1)}, bf16[1792,256]{1,0:T(8,128)(2,1)}, u32[]{:S(2)}, u32[]{:S(2)}) collective-permute-start(bf16[1792,256]{1,0:T(8,128)(2,1)} %get-tuple-element.30), channel_id=1, source_target_pairs={{0,8},{8,16},{16,24},{24,0},{1,9},{9,17},{17,25},{25,1},{2,10},{10... | collective-permute-start | bytes 2752520 | tf_op jit(solution)/shard_map/ppermute | solution.py:17
  8.7 1.6 %collective-permute-start.6 = (bf16[1792,256]{1,0:T(8,128)(2,1)}, bf16[1792,256]{1,0:T(8,128)(2,1)}, u32[]{:S(2)}, u32[]{:S(2)}) collective-permute-start(bf16[1792,256]{1,0:T(8,128)(2,1)} %get-tuple-element.25), channel_id=1, source_target_pairs={{0,8},{8,16},{16,24},{24,0},{1,9},{9,17},{17,25},{25,1},{2,10},{10... | collective-permute-start | bytes 2752520 | tf_op jit(solution)/shard_map/ppermute | solution.py:17
  10.2 1.6 %collective-permute-start.1 = (bf16[1792,256]{1,0:T(8,128)(2,1)}, bf16[1792,256]{1,0:T(8,128)(2,1)}, u32[]{:S(2)}, u32[]{:S(2)}) collective-permute-start(bf16[1792,256]{1,0:T(8,128)(2,1)} %get-tuple-element.21), channel_id=1, source_target_pairs={{0,8},{8,16},{16,24},{24,0},{1,9},{9,17},{17,25},{25,1},{2,10},{10... | collective-permute-start | bytes 2752520 | tf_op jit(solution)/shard_map/ppermute | solution.py:17
  11.8 0.8 slice.7
  12.6 0.0 collective-permute-start
  12.6 0.0 copy-done.4
  12.6 0.6 fusion.6
  14.5 0.7 add_subtract_fusion.firsts
  15.2 1.9 %copy-done.1 = bf16[2048,768]{1,0:T(8,128)(2,1)S(1)} copy-done((bf16[2048,768]{1,0:T(8,128)(2,1)S(1)}, bf16[2048,768]{1,0:T(8,128)(2,1)}, u32[]{:S(2)}) %copy-start.1) | copy-done | bytes 3145752
  17.1 2.4 %turn.1 = (bf16[768,2048]{1,0:T(8,128)(2,1)S(1)}, f32[1,768]{1,0:T(1,128)S(1)}) custom-call(s32[2]{0:T(128)S(1)} %add_subtract_fusion.firsts, bf16[2048,768]{1,0:T(8,128)(2,1)S(1)} %copy-done.1), custom_call_target="tpu_custom_call" | custom-call | flops 6291456 | bytes 6291456 | tf_op jit(solution)/shard_map/turn/pallas_call | solution.py:118
  19.5 0.1 collective-permute-start.11
  19.6 1.2 collective-permute-done.11
  20.8 1.7 %collective-permute-start.12 = (f32[768]{0:T(1024)S(1)}, f32[768]{0:T(1024)S(1)}, u32[]{:S(2)}, u32[]{:S(2)}) collective-permute-start(f32[768]{0:T(1024)S(1)} %add.100), channel_id=1, source_target_pairs={{0,2},{1,3},{2,0},{3,1},{4,6},{5,7},{6,4},{7,5},{8,10},{9,11},{10,... | collective-permute-start | bytes 9224 | tf_op jit(solution)/shard_map/ppermute | solution.py:22
  22.5 0.0 copy-done.5
  22.5 1.9 %collective-permute-done.12 = f32[768]{0:T(1024)S(1)} collective-permute-done((f32[768]{0:T(1024)S(1)}, f32[768]{0:T(1024)S(1)}, u32[]{:S(2)}, u32[]{:S(2)}) %collective-permute-start.12) | collective-permute-done | bytes 3104 | tf_op jit(solution)/shard_map/ppermute | solution.py:22
  24.4 1.7 %collective-permute-start.13 = (f32[768]{0:T(1024)S(1)}, f32[768]{0:T(1024)S(1)}, u32[]{:S(2)}, u32[]{:S(2)}) collective-permute-start(f32[768]{0:T(1024)S(1)} %add.101), channel_id=1, source_target_pairs={{0,4},{1,5},{2,6},{3,7},{4,0},{5,1},{6,2},{7,3},{8,12},{9,13},{10,... | collective-permute-start | bytes 9224 | tf_op jit(solution)/shard_map/ppermute | solution.py:22
  26.1 0.1 pad_add_fusion.flags
  26.2 1.8 %collective-permute-done.13 = f32[768]{0:T(1024)S(1)} collective-permute-done((f32[768]{0:T(1024)S(1)}, f32[768]{0:T(1024)S(1)}, u32[]{:S(2)}, u32[]{:S(2)}) %collective-permute-start.13) | collective-permute-done | bytes 3104 | tf_op jit(solution)/shard_map/ppermute | solution.py:22
  28.0 1.8 %collective-permute-start.14 = (f32[768]{0:T(1024)S(1)}, f32[768]{0:T(1024)S(1)}, u32[]{:S(2)}, u32[]{:S(2)}) collective-permute-start(f32[768]{0:T(1024)S(1)} %add.102), channel_id=1, source_target_pairs={{0,8},{8,16},{16,24},{24,0},{1,9},{9,17},{17,25},{25,1},{2,10},{10... | collective-permute-start | bytes 9224 | tf_op jit(solution)/shard_map/ppermute | solution.py:17
  29.8 49.4 %collective-permute-done.block = bf16[256,768]{1,0:T(8,128)(2,1)} collective-permute-done((bf16[256,768]{1,0:T(8,128)(2,1)}, bf16[256,768]{1,0:T(8,128)(2,1)}, u32[]{:S(2)}, u32[]{:S(2)}) %collective-permute-start) | collective-permute-done | bytes 393248 | tf_op jit(solution)/shard_map/ppermute | solution.py:17
  79.1 1.5 %picks.2 = (bf16[256,256]{1,0:T(8,128)(2,1)S(1)}, bf16[256,256]{1,0:T(8,128)(2,1)S(1)}, bf16[256,256]{1,0:T(8,128)(2,1)S(1)}) custom-call(bf16[256,768]{1,0:T(8,128)(2,1)} %collective-permute-done.block), custom_call_target="tpu_custom_call" | custom-call | flops 301989888 | bytes 786432 | tf_op jit(solution)/shard_map/picks/pallas_call | solution.py:87
  80.7 0.0 collective-permute-done.15.rest
  80.7 3.2 %gram.5 = (f32[4,32,768]{2,1,0:T(8,128)S(1)}, f32[4,32,768]{2,1,0:T(8,128)}) custom-call(s32[2]{0:T(128)S(1)} %pad_add_fusion.flags, bf16[768,2048]{1,0:T(8,128)(2,1)S(1)} %get-tuple-element.19.own, bf16[256,256]{1,0:T(8,128)(2,1)S(1)} %get-tuple-element.29.head, bf16[1792,256]{1,0:T(8,128)(2,1)} %collective-permute-done.15.rest), custom_call_target="tpu_custom_call" | custom-call | flops 805306368 | bytes 3145728 | tf_op jit(solution)/shard_map/gram/pallas_call | solution.py:170
  83.8 0.8 copy-done.3
  84.6 0.0 collective-permute-start.16
  84.6 0.0 collective-permute-done.6.rest
  84.6 3.2 %gram.4 = (f32[4,32,768]{2,1,0:T(8,128)S(1)}, f32[4,32,768]{2,1,0:T(8,128)}) custom-call(s32[2]{0:T(128)S(1)} %pad_add_fusion.flags, bf16[768,2048]{1,0:T(8,128)(2,1)S(1)} %get-tuple-element.19.own, bf16[256,256]{1,0:T(8,128)(2,1)S(1)} %get-tuple-element.24.head, bf16[1792,256]{1,0:T(8,128)(2,1)} %collective-permute-done.6.rest), custom_call_target="tpu_custom_call" | custom-call | flops 805306368 | bytes 3145728 | tf_op jit(solution)/shard_map/gram/pallas_call | solution.py:170
  87.8 0.5 collective-permute-start.7
  88.3 0.0 collective-permute-done.1.rest
  88.3 3.2 %gram.3 = (f32[4,32,768]{2,1,0:T(8,128)S(1)}, f32[4,32,768]{2,1,0:T(8,128)}) custom-call(s32[2]{0:T(128)S(1)} %pad_add_fusion.flags, bf16[768,2048]{1,0:T(8,128)(2,1)S(1)} %get-tuple-element.19.own, bf16[256,256]{1,0:T(8,128)(2,1)S(1)} %get-tuple-element.20.head, bf16[1792,256]{1,0:T(8,128)(2,1)} %collective-permute-done.1.rest), custom_call_target="tpu_custom_call" | custom-call | flops 805306368 | bytes 3145728 | tf_op jit(solution)/shard_map/gram/pallas_call | solution.py:170
  91.5 0.0 copy-done.2
  91.5 0.1 collective-permute-start.2
  91.6 0.0 collective-permute-done.14
  91.6 0.1 dynamic-slice_bitcast_fusion.10
  91.7 0.1 copy.4.scale_rows
  91.8 0.0 collective-permute-done.16
  91.8 1.2 add.106
  93.1 1.6 %collective-permute-start.17 = (f32[32,768]{1,0:T(8,128)S(1)}, f32[32,768]{1,0:T(8,128)S(1)}, u32[]{:S(2)}, u32[]{:S(2)}) collective-permute-start(f32[32,768]{1,0:T(8,128)S(1)} %get-tuple-element.35), channel_id=1, source_target_pairs={{0,2},{1,3},{2,0},{3,1},{4,6},{5,7},{6,4},{7,5},{8,10},{9,11},{10,... | collective-permute-start | bytes 294920 | tf_op jit(solution)/shard_map/ppermute | solution.py:22
  94.6 1.5 %collective-permute-start.18 = (f32[32,768]{1,0:T(8,128)S(1)}, f32[32,768]{1,0:T(8,128)S(1)}, u32[]{:S(2)}, u32[]{:S(2)}) collective-permute-start(f32[32,768]{1,0:T(8,128)S(1)} %get-tuple-element.34), channel_id=1, source_target_pairs={{0,4},{1,5},{2,6},{3,7},{4,0},{5,1},{6,2},{7,3},{8,12},{9,13},{10,... | collective-permute-start | bytes 294920 | tf_op jit(solution)/shard_map/ppermute | solution.py:22
  96.1 0.0 collective-permute-done.7
  96.1 1.2 add.96
  97.3 0.5 collective-permute-start.10
  97.9 1.5 %collective-permute-start.8 = (f32[32,768]{1,0:T(8,128)S(1)}, f32[32,768]{1,0:T(8,128)S(1)}, u32[]{:S(2)}, u32[]{:S(2)}) collective-permute-start(f32[32,768]{1,0:T(8,128)S(1)} %get-tuple-element.37), channel_id=1, source_target_pairs={{0,2},{1,3},{2,0},{3,1},{4,6},{5,7},{6,4},{7,5},{8,10},{9,11},{10,... | collective-permute-start | bytes 294920 | tf_op jit(solution)/shard_map/ppermute | solution.py:22
  99.4 0.0 collective-permute-done.2
  99.4 1.5 %collective-permute-start.9 = (f32[32,768]{1,0:T(8,128)S(1)}, f32[32,768]{1,0:T(8,128)S(1)}, u32[]{:S(2)}, u32[]{:S(2)}) collective-permute-start(f32[32,768]{1,0:T(8,128)S(1)} %get-tuple-element.39), channel_id=1, source_target_pairs={{0,4},{1,5},{2,6},{3,7},{4,0},{5,1},{6,2},{7,3},{8,12},{9,13},{10,... | collective-permute-start | bytes 294920 | tf_op jit(solution)/shard_map/ppermute | solution.py:22
  100.9 0.1 add.88
  101.0 2.9 %collective-permute-done.10 = f32[32,768]{1,0:T(8,128)S(1)} collective-permute-done((f32[32,768]{1,0:T(8,128)S(1)}, f32[32,768]{1,0:T(8,128)S(1)}, u32[]{:S(2)}, u32[]{:S(2)}) %collective-permute-start.10) | collective-permute-done | bytes 98336 | tf_op jit(solution)/shard_map/ppermute | solution.py:22
  103.9 0.6 collective-permute-start.3
  104.5 0.0 collective-permute-done.8
  104.5 1.8 %collective-permute-start.4 = (f32[32,768]{1,0:T(8,128)S(1)}, f32[32,768]{1,0:T(8,128)S(1)}, u32[]{:S(2)}, u32[]{:S(2)}) collective-permute-start(f32[32,768]{1,0:T(8,128)S(1)} %get-tuple-element.42), channel_id=1, source_target_pairs={{0,4},{1,5},{2,6},{3,7},{4,0},{5,1},{6,2},{7,3},{8,12},{9,13},{10,... | collective-permute-start | bytes 294920 | tf_op jit(solution)/shard_map/ppermute | solution.py:22
  106.3 0.0 collective-permute-done.9
  106.3 1.1 collective-permute-start.5
  107.4 2.1 %collective-permute-done.3 = f32[32,768]{1,0:T(8,128)S(1)} collective-permute-done((f32[32,768]{1,0:T(8,128)S(1)}, f32[32,768]{1,0:T(8,128)S(1)}, u32[]{:S(2)}, u32[]{:S(2)}) %collective-permute-start.3) | collective-permute-done | bytes 98336 | tf_op jit(solution)/shard_map/ppermute | solution.py:22
  109.5 0.1 collective-permute-start.19
  109.6 2.6 %collective-permute-done.4 = f32[32,768]{1,0:T(8,128)S(1)} collective-permute-done((f32[32,768]{1,0:T(8,128)S(1)}, f32[32,768]{1,0:T(8,128)S(1)}, u32[]{:S(2)}, u32[]{:S(2)}) %collective-permute-start.4) | collective-permute-done | bytes 98336 | tf_op jit(solution)/shard_map/ppermute | solution.py:22
  112.2 0.0 collective-permute-done.5
  112.2 0.6 base.1
  112.8 0.0 collective-permute-done.17.refs_1_
  112.8 0.0 collective-permute-done.18.refs_2_
  112.8 2.2 %collective-permute-done.19.refs_3_ = f32[32,768]{1,0:T(8,128)S(1)} collective-permute-done((f32[32,768]{1,0:T(8,128)S(1)}, f32[32,768]{1,0:T(8,128)S(1)}, u32[]{:S(2)}, u32[]{:S(2)}) %collective-permute-start.19) | collective-permute-done | bytes 98336 | tf_op jit(solution)/shard_map/ppermute | solution.py:22
  115.0 1.4 %finish.1 = f32[1,96,768]{2,1,0:T(8,128)} custom-call(s32[2]{0:T(128)S(1)} %pad_add_fusion.flags, f32[96,768]{1,0:T(8,128)S(1)} %base.1, f32[96,1]{1,0:T(8,128)S(1)} %copy.4.scale_rows, f32[1,768]{1,0:T(1,128)S(1)} %broadcast_in_dim.7.scale_cols, f32[32,768]{1,0:T(8,128)S(1)} %get-tuple-element.36.refs_0_, f32[32,768]{1,0:T(8,128)S(1)} %collective-permute-done.17.refs_1_, ...), custom_call_target="tpu_custom_call" | custom-call | flops 37748736 | bytes 589824 | tf_op jit(solution)/shard_map/finish/pallas_call | solution.py:277
  (16 shorter events, 0.2 us)
Async XLA Ops:
  0.0 1.9 %copy-start = (bf16[2048,768]{1,0:T(8,128)(2,1)S(1)}, bf16[2048,768]{1,0:T(8,128)(2,1)}, u32[]{:S(2)}) copy-start(bf16[2048,768]{1,0:T(8,128)(2,1)} %block.3) | copy-start | bytes 9437188
  1.9 10.7 %copy-start.4 = (s32[4]{0:T(128)S(1)}, s32[4]{0:T(128)}, u32[]{:S(2)}) copy-start(s32[4]{0:T(128)} %param.5) | copy-start | bytes 52
  5.6 16.9 %copy-start.5 = (s32[1,2]{1,0:T(1,128)S(1)}, s32[1,2]{1,0:T(1,128)}, u32[]{:S(2)}) copy-start(s32[1,2]{1,0:T(1,128)} %param.4) | copy-start | bytes 28
  5.6 75.0 %collective-permute-start.15 = (bf16[1792,256]{1,0:T(8,128)(2,1)}, bf16[1792,256]{1,0:T(8,128)(2,1)}, u32[]{:S(2)}, u32[]{:S(2)}) collective-permute-start(bf16[1792,256]{1,0:T(8,128)(2,1)} %get-tuple-element.30), channel_id=1, source_target_pairs={{0,8},{8,16},{16,24},{24,0},{1,9},{9,17},{17,25},{25,1},{2,10},{10... | collective-permute-start | bytes 2752520 | tf_op jit(solution)/shard_map/ppermute | solution.py:17
  8.7 75.9 %collective-permute-start.6 = (bf16[1792,256]{1,0:T(8,128)(2,1)}, bf16[1792,256]{1,0:T(8,128)(2,1)}, u32[]{:S(2)}, u32[]{:S(2)}) collective-permute-start(bf16[1792,256]{1,0:T(8,128)(2,1)} %get-tuple-element.25), channel_id=1, source_target_pairs={{0,8},{8,16},{16,24},{24,0},{1,9},{9,17},{17,25},{25,1},{2,10},{10... | collective-permute-start | bytes 2752520 | tf_op jit(solution)/shard_map/ppermute | solution.py:17
  10.2 78.1 %collective-permute-start.1 = (bf16[1792,256]{1,0:T(8,128)(2,1)}, bf16[1792,256]{1,0:T(8,128)(2,1)}, u32[]{:S(2)}, u32[]{:S(2)}) collective-permute-start(bf16[1792,256]{1,0:T(8,128)(2,1)} %get-tuple-element.21), channel_id=1, source_target_pairs={{0,8},{8,16},{16,24},{24,0},{1,9},{9,17},{17,25},{25,1},{2,10},{10... | collective-permute-start | bytes 2752520 | tf_op jit(solution)/shard_map/ppermute | solution.py:17
  12.6 66.6 %collective-permute-start = (bf16[256,768]{1,0:T(8,128)(2,1)}, bf16[256,768]{1,0:T(8,128)(2,1)}, u32[]{:S(2)}, u32[]{:S(2)}) collective-permute-start(bf16[256,768]{1,0:T(8,128)(2,1)} %slice.7), channel_id=1, source_target_pairs={{0,8},{8,16},{16,24},{24,0},{1,9},{9,17},{17,25},{25,1},{2,10},{10... | collective-permute-start | bytes 1179656 | tf_op jit(solution)/shard_map/ppermute | solution.py:17
  15.2 1.9 %copy-start.1 = (bf16[2048,768]{1,0:T(8,128)(2,1)S(1)}, bf16[2048,768]{1,0:T(8,128)(2,1)}, u32[]{:S(2)}) copy-start(bf16[2048,768]{1,0:T(8,128)(2,1)} %block.3) | copy-start | bytes 9437188
  19.5 1.2 %collective-permute-start.11 = (f32[768]{0:T(1024)S(1)}, f32[768]{0:T(1024)S(1)}, u32[]{:S(2)}, u32[]{:S(2)}) collective-permute-start(f32[768]{0:T(1024)S(1)} %reduce), channel_id=1, source_target_pairs={{0,1},{1,0},{2,3},{3,2},{4,5},{5,4},{6,7},{7,6},{8,9},{9,8},{10,11... | collective-permute-start | bytes 9224 | tf_op jit(solution)/shard_map/ppermute | solution.py:22
  20.8 3.6 %collective-permute-start.12 = (f32[768]{0:T(1024)S(1)}, f32[768]{0:T(1024)S(1)}, u32[]{:S(2)}, u32[]{:S(2)}) collective-permute-start(f32[768]{0:T(1024)S(1)} %add.100), channel_id=1, source_target_pairs={{0,2},{1,3},{2,0},{3,1},{4,6},{5,7},{6,4},{7,5},{8,10},{9,11},{10,... | collective-permute-start | bytes 9224 | tf_op jit(solution)/shard_map/ppermute | solution.py:22
  24.4 3.6 %collective-permute-start.13 = (f32[768]{0:T(1024)S(1)}, f32[768]{0:T(1024)S(1)}, u32[]{:S(2)}, u32[]{:S(2)}) collective-permute-start(f32[768]{0:T(1024)S(1)} %add.101), channel_id=1, source_target_pairs={{0,4},{1,5},{2,6},{3,7},{4,0},{5,1},{6,2},{7,3},{8,12},{9,13},{10,... | collective-permute-start | bytes 9224 | tf_op jit(solution)/shard_map/ppermute | solution.py:22
  28.0 63.6 %collective-permute-start.14 = (f32[768]{0:T(1024)S(1)}, f32[768]{0:T(1024)S(1)}, u32[]{:S(2)}, u32[]{:S(2)}) collective-permute-start(f32[768]{0:T(1024)S(1)} %add.102), channel_id=1, source_target_pairs={{0,8},{8,16},{16,24},{24,0},{1,9},{9,17},{17,25},{25,1},{2,10},{10... | collective-permute-start | bytes 9224 | tf_op jit(solution)/shard_map/ppermute | solution.py:17
  83.8 0.8 copy-start.3
  84.6 7.2 %collective-permute-start.16 = (f32[4,32,768]{2,1,0:T(8,128)}, f32[4,32,768]{2,1,0:T(8,128)}, u32[]{:S(2)}, u32[]{:S(2)}) collective-permute-start(f32[4,32,768]{2,1,0:T(8,128)} %get-tuple-element.32), channel_id=1, source_target_pairs={{0,1},{1,0},{2,3},{3,2},{4,5},{5,4},{6,7},{7,6},{8,9},{9,8},{10,11... | collective-permute-start | bytes 1179656 | tf_op jit(solution)/shard_map/ppermute | solution.py:22
  87.8 3.7 %copy-start.2 = (f32[4,32,768]{2,1,0:T(8,128)}, f32[4,32,768]{2,1,0:T(8,128)S(1)}, u32[]{:S(2)}) copy-start(f32[4,32,768]{2,1,0:T(8,128)S(1)} %get-tuple-element.26) | copy-start | bytes 1179652
  87.8 8.4 %collective-permute-start.7 = (f32[4,32,768]{2,1,0:T(8,128)}, f32[4,32,768]{2,1,0:T(8,128)}, u32[]{:S(2)}, u32[]{:S(2)}) collective-permute-start(f32[4,32,768]{2,1,0:T(8,128)} %get-tuple-element.27), channel_id=1, source_target_pairs={{0,1},{1,0},{2,3},{3,2},{4,5},{5,4},{6,7},{7,6},{8,9},{9,8},{10,11... | collective-permute-start | bytes 1179656 | tf_op jit(solution)/shard_map/ppermute | solution.py:22
  91.5 7.9 %collective-permute-start.2 = (f32[4,32,768]{2,1,0:T(8,128)}, f32[4,32,768]{2,1,0:T(8,128)S(1)}, u32[]{:S(2)}, u32[]{:S(2)}) collective-permute-start(f32[4,32,768]{2,1,0:T(8,128)} %get-tuple-element.23), channel_id=1, source_target_pairs={{0,1},{1,0},{2,3},{3,2},{4,5},{5,4},{6,7},{7,6},{8,9},{9,8},{10,11... | collective-permute-start | bytes 1179656 | tf_op jit(solution)/shard_map/ppermute | solution.py:22
  93.1 19.7 %collective-permute-start.17 = (f32[32,768]{1,0:T(8,128)S(1)}, f32[32,768]{1,0:T(8,128)S(1)}, u32[]{:S(2)}, u32[]{:S(2)}) collective-permute-start(f32[32,768]{1,0:T(8,128)S(1)} %get-tuple-element.35), channel_id=1, source_target_pairs={{0,2},{1,3},{2,0},{3,1},{4,6},{5,7},{6,4},{7,5},{8,10},{9,11},{10,... | collective-permute-start | bytes 294920 | tf_op jit(solution)/shard_map/ppermute | solution.py:22
  94.6 18.2 %collective-permute-start.18 = (f32[32,768]{1,0:T(8,128)S(1)}, f32[32,768]{1,0:T(8,128)S(1)}, u32[]{:S(2)}, u32[]{:S(2)}) collective-permute-start(f32[32,768]{1,0:T(8,128)S(1)} %get-tuple-element.34), channel_id=1, source_target_pairs={{0,4},{1,5},{2,6},{3,7},{4,0},{5,1},{6,2},{7,3},{8,12},{9,13},{10,... | collective-permute-start | bytes 294920 | tf_op jit(solution)/shard_map/ppermute | solution.py:22
  97.3 6.5 %collective-permute-start.10 = (f32[32,768]{1,0:T(8,128)S(1)}, f32[32,768]{1,0:T(8,128)S(1)}, u32[]{:S(2)}, u32[]{:S(2)}) collective-permute-start(f32[32,768]{1,0:T(8,128)S(1)} %get-tuple-element.38), channel_id=1, source_target_pairs={{0,6},{1,7},{2,4},{3,5},{4,2},{5,3},{6,0},{7,1},{8,14},{9,15},{10,... | collective-permute-start | bytes 294920 | tf_op jit(solution)/shard_map/ppermute | solution.py:22
  97.9 6.6 %collective-permute-start.8 = (f32[32,768]{1,0:T(8,128)S(1)}, f32[32,768]{1,0:T(8,128)S(1)}, u32[]{:S(2)}, u32[]{:S(2)}) collective-permute-start(f32[32,768]{1,0:T(8,128)S(1)} %get-tuple-element.37), channel_id=1, source_target_pairs={{0,2},{1,3},{2,0},{3,1},{4,6},{5,7},{6,4},{7,5},{8,10},{9,11},{10,... | collective-permute-start | bytes 294920 | tf_op jit(solution)/shard_map/ppermute | solution.py:22
  99.4 6.9 %collective-permute-start.9 = (f32[32,768]{1,0:T(8,128)S(1)}, f32[32,768]{1,0:T(8,128)S(1)}, u32[]{:S(2)}, u32[]{:S(2)}) collective-permute-start(f32[32,768]{1,0:T(8,128)S(1)} %get-tuple-element.39), channel_id=1, source_target_pairs={{0,4},{1,5},{2,6},{3,7},{4,0},{5,1},{6,2},{7,3},{8,12},{9,13},{10,... | collective-permute-start | bytes 294920 | tf_op jit(solution)/shard_map/ppermute | solution.py:22
  103.9 5.7 %collective-permute-start.3 = (f32[32,768]{1,0:T(8,128)S(1)}, f32[32,768]{1,0:T(8,128)S(1)}, u32[]{:S(2)}, u32[]{:S(2)}) collective-permute-start(f32[32,768]{1,0:T(8,128)S(1)} %get-tuple-element.40), channel_id=1, source_target_pairs={{0,2},{1,3},{2,0},{3,1},{4,6},{5,7},{6,4},{7,5},{8,10},{9,11},{10,... | collective-permute-start | bytes 294920 | tf_op jit(solution)/shard_map/ppermute | solution.py:22
  104.5 7.7 %collective-permute-start.4 = (f32[32,768]{1,0:T(8,128)S(1)}, f32[32,768]{1,0:T(8,128)S(1)}, u32[]{:S(2)}, u32[]{:S(2)}) collective-permute-start(f32[32,768]{1,0:T(8,128)S(1)} %get-tuple-element.42), channel_id=1, source_target_pairs={{0,4},{1,5},{2,6},{3,7},{4,0},{5,1},{6,2},{7,3},{8,12},{9,13},{10,... | collective-permute-start | bytes 294920 | tf_op jit(solution)/shard_map/ppermute | solution.py:22
  106.3 5.9 %collective-permute-start.5 = (f32[32,768]{1,0:T(8,128)S(1)}, f32[32,768]{1,0:T(8,128)S(1)}, u32[]{:S(2)}, u32[]{:S(2)}) collective-permute-start(f32[32,768]{1,0:T(8,128)S(1)} %get-tuple-element.41), channel_id=1, source_target_pairs={{0,6},{1,7},{2,4},{3,5},{4,2},{5,3},{6,0},{7,1},{8,14},{9,15},{10,... | collective-permute-start | bytes 294920 | tf_op jit(solution)/shard_map/ppermute | solution.py:22
  109.5 5.5 %collective-permute-start.19 = (f32[32,768]{1,0:T(8,128)S(1)}, f32[32,768]{1,0:T(8,128)S(1)}, u32[]{:S(2)}, u32[]{:S(2)}) collective-permute-start(f32[32,768]{1,0:T(8,128)S(1)} %get-tuple-element.33), channel_id=1, source_target_pairs={{0,6},{1,7},{2,4},{3,5},{4,2},{5,3},{6,0},{7,1},{8,14},{9,15},{10,... | collective-permute-start | bytes 294920 | tf_op jit(solution)/shard_map/ppermute | solution.py:22

commit v2 on v1

--- a/solution.py
+++ b/solution.py
@@ -25,7 +25,7 @@
 def summed(value, axis):
     bits = 1
     while bits < lax.axis_size(axis):
-        value = value + swapped(value, axis, bits)
+        value = plus(value, swapped(value, axis, bits))
         bits *= 2
     return value
 
@@ -87,7 +87,7 @@
     return pl.pallas_call(
         functools.partial(picks_kernel, share, runs, skip),
         out_shape=[
-            jax.ShapeDtypeStruct((rows - skip, groups * run), jnp.bfloat16) for _, run in runs
+            pltpu.VMEM((rows - skip, groups * run), jnp.bfloat16) for _, run in runs
         ],
         in_specs=[pl.BlockSpec(memory_space=pltpu.VMEM)],
         out_specs=[pl.BlockSpec(memory_space=pltpu.VMEM) for _ in runs],
@@ -99,27 +99,34 @@
     )(block)
 
 
-def turn_kernel(step, firsts, block, turned, squares):
+def turn_kernel(step, onsets, block, turned, squares):
     rows, width = block.shape
+    owner = lax.axis_index("src")
+    blocks = lax.axis_size("src")
+    top_row = lax.axis_index("tm") * rows
+    own_first = onsets[owner] - top_row
+    both_first = (
+        jnp.maximum(onsets[owner], onsets[lax.rem(owner + blocks - 1, blocks)]) - top_row
+    )
     total = jnp.zeros((1, width), jnp.float32)
     for top in range(0, rows, step):
         piece = block[top : top + step, :]
         ids = lax.broadcasted_iota(jnp.int32, (step, width), 0) + top
-        wide = jnp.where(ids >= firsts[0], piece.astype(jnp.float32), 0.0)
+        wide = jnp.where(ids >= own_first, piece.astype(jnp.float32), 0.0)
         total = total + jnp.sum(wide * wide, axis=0, keepdims=True)
-        shown = jnp.where(ids >= firsts[1], piece.astype(jnp.float32), 0.0)
+        shown = jnp.where(ids >= both_first, piece.astype(jnp.float32), 0.0)
         turned[:, top : top + step] = shown.T.astype(jnp.bfloat16)
     squares[...] = total
 
 
-def turn(firsts, block):
+def turn(onsets, block):
     rows, width = block.shape
     step = 128 if rows % 128 == 0 else rows
     return pl.pallas_call(
         functools.partial(turn_kernel, step),
         out_shape=(
-            jax.ShapeDtypeStruct((width, rows), jnp.bfloat16),
-            jax.ShapeDtypeStruct((1, width), jnp.float32),
+            pltpu.VMEM((width, rows), jnp.bfloat16),
+            pltpu.VMEM((1, width), jnp.float32),
         ),
         in_specs=[pl.BlockSpec(memory_space=pltpu.SMEM), pl.BlockSpec(memory_space=pltpu.VMEM)],
         out_specs=(pl.BlockSpec(memory_space=pltpu.VMEM),) * 2,
@@ -128,21 +135,22 @@
         ),
         compiler_params=pltpu.CompilerParams(vmem_limit_bytes=16 << 20),
         name="turn",
-    )(firsts, block)
-
-
-def gram_kernel(share, run, flags, own, head, rest, keep, give, part):
+    )(onsets, block)
+
+
+def gram_kernel(share, run, pairs, own, head, rest, keep, give, part):
     cut = head.shape[0]
     columns = rest.shape[1]
     groups = keep.shape[0] * 2
-    bit = flags[1]
+    bit = lax.rem(lax.axis_index("tm"), 2)
+    owner_first = pairs[0, 0] == lax.axis_index("src")
     product = jnp.dot(
         own[:, cut:], rest[...], preferred_element_type=jnp.float32
     ) + jnp.dot(
         own[:, :cut], head[...], preferred_element_type=jnp.float32
     )
 
-    @pl.when(flags[0] == 1)
+    @pl.when(owner_first)
     def _():
         part[...] = product
         for pair in range(groups // 2):
@@ -152,7 +160,7 @@
                     rows = pl.ds(pl.multiple_of(top + piece * run, 8), run)
                     target[pair, :, piece * columns : (piece + 1) * columns] = part[rows, :]
 
-    @pl.when(flags[0] == 0)
+    @pl.when(jnp.logical_not(owner_first))
     def _():
         turned = product.T
         for pair in range(groups // 2):
@@ -162,7 +170,7 @@
             give[pair] = jnp.where(bit == 0, uneven, even)
 
 
-def gram(flags, own, head, rest, share, run):
+def gram(pairs, own, head, rest, share, run):
     width = own.shape[0]
     groups = width // share
     half = pltpu.VMEM((groups // 2, run, width), jnp.float32)
@@ -179,7 +187,7 @@
         ),
         compiler_params=pltpu.CompilerParams(vmem_limit_bytes=16 << 20),
         name="gram",
-    )(flags, own, head, rest)
+    )(pairs, own, head, rest)
 
 
 def gram_plain(flags, own, head, rest, share, run):
@@ -216,11 +224,51 @@
     return total
 
 
-def placed(flags, share, start, run, part, total):
+def fold_kernel(keep, arrived, mine, *gives):
+    me = lax.axis_index("tm") // 2
+    mine[...] = keep[me] + arrived[me]
+    for m, give in enumerate(gives, 1):
+        give[...] = keep[me ^ m] + arrived[me ^ m]
+
+
+def fold(keep, arrived):
+    strip = pltpu.VMEM(keep.shape[1:], jnp.float32)
+    return pl.pallas_call(
+        fold_kernel,
+        out_shape=[strip] * keep.shape[0],
+        in_specs=[pl.BlockSpec(memory_space=pltpu.VMEM)] * 2,
+        out_specs=[pl.BlockSpec(memory_space=pltpu.VMEM)] * keep.shape[0],
+        cost_estimate=pl.CostEstimate(
+            flops=keep.size, bytes_accessed=12 * keep.size, transcendentals=0
+        ),
+        compiler_params=pltpu.CompilerParams(vmem_limit_bytes=8 << 20),
+        name="fold",
+    )(keep, arrived)
+
+
+def plus_kernel(a, b, out):
+    out[...] = a[...] + b[...]
+
+
+def plus(a, b):
+    return pl.pallas_call(
+        plus_kernel,
+        out_shape=pltpu.VMEM(a.shape, a.dtype),
+        in_specs=[pl.BlockSpec(memory_space=pltpu.VMEM)] * 2,
+        out_specs=pl.BlockSpec(memory_space=pltpu.VMEM),
+        compiler_params=pltpu.CompilerParams(vmem_limit_bytes=1 << 20),
+        name="plus",
+    )(a, b)
+
+
+def placed(owner_first, share, start, run, terms, total):
     width = total.shape[1]
     columns = width // share * run
-
-    @pl.when(flags[0] == 1)
+    part = terms[0][...]
+    for term in terms[1:]:
+        part = part + term[...]
+
+    @pl.when(owner_first)
     def _():
         spread = jnp.concatenate(
             [part[:, n * columns : (n + 1) * columns] for n in range(share // run)], axis=0
@@ -235,45 +283,53 @@
             preferred_element_type=jnp.float32,
         )
 
-    @pl.when(flags[0] == 0)
+    @pl.when(jnp.logical_not(owner_first))
     def _():
         total[start : start + run, :] = part
 
 
-def base_kernel(share, runs, flags, *refs):
-    *parts, total = refs
-    total[...] = jnp.zeros_like(total)
-    for (start, run), part in zip(runs, parts):
-        placed(flags, share, start, run, part[...], total)
-
-
-def finish_kernel(share, start, run, flags, base, scale_rows, scale_cols, *refs):
+def place_kernel(share, start, run, pairs, *refs):
+    *terms, total = refs
+    if len(terms) > 4:
+        total[...] = terms.pop()[...]
+    else:
+        total[...] = jnp.zeros_like(total)
+    placed(pairs[0, 0] == lax.axis_index("src"), share, start, run, terms, total)
+
+
+def finish_kernel(share, start, run, pairs, base, norm_own, norm_low, *refs):
     *terms, out, total = refs
+    width = total.shape[1]
+    owner_first = pairs[0, 0] == lax.axis_index("src")
     total[...] = base[...]
-    part = terms[0][...]
-    for term in terms[1:]:
-        part = part + term[...]
-    placed(flags, share, start, run, part, total)
-    out[0] = total[...] * scale_rows[...] * scale_cols[...]
-
-
-def base_of(flags, parts, share, runs):
-    width = parts[0].shape[1]
-    return pl.pallas_call(
-        functools.partial(base_kernel, share, runs),
+    placed(owner_first, share, start, run, terms, total)
+    scale_own = lax.rsqrt(norm_own[...] + 1e-06)
+    scale_low = lax.rsqrt(norm_low[...] + 1e-06)
+    scale_first = jnp.where(owner_first, scale_own, scale_low)
+    scale_second = jnp.where(owner_first, scale_low, scale_own)
+    row = lax.broadcasted_iota(jnp.int32, (share, width), 0) + lax.axis_index("tm") * share
+    column = lax.broadcasted_iota(jnp.int32, (share, width), 1)
+    scale_rows = jnp.sum(jnp.where(row == column, scale_first, 0.0), axis=1, keepdims=True)
+    out[0] = total[...] * scale_rows * scale_second
+
+
+def place(pairs, terms, base, share, width, start, run):
+    given = list(terms) + ([] if base is None else [base])
+    return pl.pallas_call(
+        functools.partial(place_kernel, share, start, run),
         out_shape=pltpu.VMEM((share, width), jnp.float32),
         in_specs=[pl.BlockSpec(memory_space=pltpu.SMEM)]
-        + [pl.BlockSpec(memory_space=pltpu.VMEM)] * len(parts),
+        + [pl.BlockSpec(memory_space=pltpu.VMEM)] * len(given),
         out_specs=pl.BlockSpec(memory_space=pltpu.VMEM),
         cost_estimate=pl.CostEstimate(
-            flops=2 * share * width * 512, bytes_accessed=8 * share * width, transcendentals=0
+            flops=2 * share * width * 256, bytes_accessed=8 * share * width, transcendentals=0
         ),
         compiler_params=pltpu.CompilerParams(vmem_limit_bytes=8 << 20),
-        name="base",
-    )(flags, *parts)
-
-
-def finish(flags, base, scale_rows, scale_cols, terms, share, start, run):
+        name="place",
+    )(pairs, *given)
+
+
+def finish(pairs, base, norm_own, norm_low, terms, share, start, run):
     return pl.pallas_call(
         functools.partial(finish_kernel, share, start, run),
         out_shape=jax.ShapeDtypeStruct((1,) + base.shape, jnp.float32),
@@ -286,57 +342,56 @@
         ),
         compiler_params=pltpu.CompilerParams(vmem_limit_bytes=8 << 20),
         name="finish",
-    )(flags, base, scale_rows, scale_cols, *terms)
+    )(pairs, base, norm_own, norm_low, *terms)
 
 
 def on_device(greens, pairs, onsets):
     rows_dev, width = greens.shape
     groups = lax.axis_size("tm")
     share = width // groups
-    row_group = lax.axis_index("tm")
-    row_start = row_group * rows_dev
-    owner = lax.axis_index("src")
-    blocks = lax.axis_size("src")
     runs = runs_of(share)
-    aligned = all(run % 8 == 0 and groups * run % 128 == 0 for _, run in runs)
+    aligned = groups == 8 and all(run % 8 == 0 and groups * run % 128 == 0 for _, run in runs)
     cut = rows_dev // HEAD
-
-    owner_first = pairs[0, 0] == owner
-    own_onset = onsets[owner]
-    arrival = jnp.maximum(own_onset, onsets[(owner + blocks - 1) % blocks])
-    firsts = jnp.stack([own_onset, arrival]) - row_start
-    flags = jnp.stack([owner_first.astype(jnp.int32), row_group % 2])
 
     head = from_behind(greens[:cut], "src", 1)
     chosen = picks(greens, share, runs, cut)
     lower = []
     for block in chosen:
         lower.append(from_behind(block, "src", 1))
-    own, squares = turn(firsts, greens)
-    norm_own = summed(squares[0], "tm")
+    own, squares = turn(onsets, greens)
+    norm_own = summed(squares, "tm")
     norm_low = from_behind(norm_own, "src", 1)
     heads = picks(head, share, runs, 0)
-
-    done = []
+    if not aligned:
+        return plain_tail(pairs, own, heads, lower, norm_own[0], norm_low[0], share, runs)
+
+    base = None
     for step, (run, top, block) in enumerate(zip(runs, heads, lower)):
-        form = gram if aligned else gram_plain
-        keep, give = form(flags, own, top, block, share, run[1])
-        terms = strips_arrived(keep, give, "tm")
-        if step == len(runs) - 1:
-            done.append(terms)
-        else:
-            done.append(functools.reduce(jnp.add, terms))
-
+        keep, give = gram(pairs, own, top, block, share, run[1])
+        arrived = swapped(give, "tm", 1)
+        mine, *gives = fold(keep, arrived)
+        terms = [mine]
+        for m, strip in enumerate(gives, 1):
+            terms.append(swapped(strip, "tm", 2 * m))
+        if step < len(runs) - 1:
+            base = place(pairs, terms, base, share, width, *run)
+    return finish(pairs, base, norm_own, norm_low, terms, share, *runs[-1])
+
+
+def plain_tail(pairs, own, heads, lower, norm_own, norm_low, share, runs):
+    row_group = lax.axis_index("tm")
+    owner_first = pairs[0, 0] == lax.axis_index("src")
+    flags = jnp.stack([owner_first.astype(jnp.int32), row_group % 2])
+    parts = []
+    for run, top, block in zip(runs, heads, lower):
+        keep, give = gram_plain(flags, own, top, block, share, run[1])
+        parts.append(functools.reduce(jnp.add, strips_arrived(keep, give, "tm")))
     scale_own = lax.rsqrt(norm_own + 1e-06)
     scale_low = lax.rsqrt(norm_low + 1e-06)
     scale_rows = lax.dynamic_slice_in_dim(
         jnp.where(owner_first, scale_own, scale_low), row_group * share, share, 0
     )[:, None]
     scale_cols = jnp.where(owner_first, scale_low, scale_own)[None, :]
-    if aligned:
-        base = base_of(flags, done[:-1], share, runs[:-1])
-        return finish(flags, base, scale_rows, scale_cols, done[-1], share, *runs[-1])
-    parts = done[:-1] + [functools.reduce(jnp.add, done[-1])]
     base = jnp.where(
         owner_first, put_back(runs, share, parts), jnp.concatenate(parts, axis=0)
     )

time: 117 us -> 110 us (0.940)
  waiting for transfers between devices: 64 us -> 72.4 us
  Pallas kernels: 19.2 us -> 13.4 us
  local copies, waits for them, and re-layouts: 6.21 us -> 1.93 us
  other arithmetic: 3.22 us -> 0 us
  between operations: 1.48 us -> 0.15 us
    ppermute x5, waiting for transfers between devices: 49.4 us -> 69.2 us  [from_behind(): lax.ppermute(value, axis, [(i, (i + by) % length) for i in range(length)])]
    ppermute x15, waiting for transfers between devices: 14.7 us -> 3.2 us  [swapped(): return lax.ppermute(value, axis, [(i, i ^ bits) for i in range(length)])]
    pallas_call x3, Pallas kernels: 9.54 us -> 5.37 us  [gram(): pl.pallas_call(functools.partial(gram_kernel, share, run), out_shape=(hal...]
    unnamed x12 -> x8, local copies, waits for them, and re-layouts: 4.54 us -> 1.9 us
    add x8 -> x0, other arithmetic: 2.43 us -> none  [the longest x3 2.37 us: strips_arrived(): strips = keep + swapped(give, axis, bits)]
    pallas_call x2, Pallas kernels: 5.21 us -> 2.83 us  [picks(): pl.pallas_call(functools.partial(picks_kernel, share, runs, skip), out_sh...]
    ppermute x5, starting transfers between devices: 8 us -> 6.38 us  [from_behind(): lax.ppermute(value, axis, [(i, (i + by) % length) for i in range(length)])]
    pallas_call x2 -> x9, Pallas kernels: 3.01 us -> 3.74 us  [the longest x1 2.44 us: turn(): pl.pallas_call(functools.partial(turn_kernel, step), out_shape=(pltpu.VME...]
  transfers between devices with their start and end apart: 20 -> 20, of which waited for: 8 -> 5; matrix products, arithmetic and copies ran while one was open for 4% -> 0% of each run, Pallas kernels for 12% -> 9%
where the time goes in v2:
time: 110 us
  waiting for transfers between devices  72.4 us (66%)
  starting transfers between devices  21.7 us (20%)
  Pallas kernels  13.4 us (12%)
  local copies, waits for them, and re-layouts  1.93 us (2%)
    ppermute x5, waiting for transfers between devices, from_behind(): lax.ppermute(value, axis, [(i, (i + by) % length) for i in range(length)])  69.2 us
    ppermute x15, starting transfers between devices, swapped(): return lax.ppermute(value, axis, [(i, i ^ bits) for i in range(length)])  15.3 us
    ppermute x5, starting transfers between devices, from_behind(): lax.ppermute(value, axis, [(i, (i + by) % length) for i in range(length)])  6.38 us
    pallas_call x3, Pallas kernels, gram(): pl.pallas_call(functools.partial(gram_kernel, share, run), out_shape=(hal...  5.37 us
    ppermute x15, waiting for transfers between devices, swapped(): return lax.ppermute(value, axis, [(i, i ^ bits) for i in range(length)])  3.2 us
    pallas_call x2, Pallas kernels, picks(): pl.pallas_call(functools.partial(picks_kernel, share, runs, skip), out_sh...  2.83 us
    pallas_call x1, Pallas kernels, turn(): pl.pallas_call(functools.partial(turn_kernel, step), out_shape=(pltpu.VME...  2.44 us
  transfers between devices with their start and end apart: 20, of which 5 were waited for; matrix products, arithmetic and copies ran while one was open for 0% of the time, Pallas kernels for 9%

profile of v2, /device:TPU:0, one launch (start us, length us, event | category | flops | bytes accessed | tf_op | source)
XLA Modules:
  0.0 109.5 jit_solution(3664627934393291750)
XLA Ops:
  0.0 0.0 copy-start
  0.0 1.9 %copy-done = bf16[2048,768]{1,0:T(8,128)(2,1)S(1)} copy-done((bf16[2048,768]{1,0:T(8,128)(2,1)S(1)}, bf16[2048,768]{1,0:T(8,128)(2,1)}, u32[]{:S(2)}) %copy-start) | copy-done | bytes 3145752
  1.9 0.0 copy-start.1
  1.9 0.0 copy-start.3
  1.9 2.3 %picks.3 = (bf16[1792,256]{1,0:T(8,128)(2,1)S(1)}, bf16[1792,256]{1,0:T(8,128)(2,1)S(1)}, bf16[1792,256]{1,0:T(8,128)(2,1)S(1)}) custom-call(bf16[2048,768]{1,0:T(8,128)(2,1)S(1)} %copy-done), custom_call_target="tpu_custom_call" | custom-call | flops 2415919104 | bytes 6291456 | tf_op jit(solution)/shard_map/picks/pallas_call | solution.py:87
  4.2 0.0 copy-start.2
  4.2 3.1 %collective-permute-start.6 = (bf16[1792,256]{1,0:T(8,128)(2,1)S(1)}, bf16[1792,256]{1,0:T(8,128)(2,1)S(1)}, u32[]{:S(2)}, u32[]{:S(2)}) collective-permute-start(bf16[1792,256]{1,0:T(8,128)(2,1)S(1)} %get-tuple-element.41), channel_id=1, source_target_pairs={{0,8},{8,16},{16,24},{24,0},{1,9},{9,17},{17,25},{25,1},{2,10},{10... | collective-permute-start | bytes 2752520 | tf_op jit(solution)/shard_map/ppermute | solution.py:17
  7.3 1.6 %collective-permute-start.1 = (bf16[1792,256]{1,0:T(8,128)(2,1)S(1)}, bf16[1792,256]{1,0:T(8,128)(2,1)S(1)}, u32[]{:S(2)}, u32[]{:S(2)}) collective-permute-start(bf16[1792,256]{1,0:T(8,128)(2,1)S(1)} %get-tuple-element.33), channel_id=1, source_target_pairs={{0,8},{8,16},{16,24},{24,0},{1,9},{9,17},{17,25},{25,1},{2,10},{10... | collective-permute-start | bytes 2752520 | tf_op jit(solution)/shard_map/ppermute | solution.py:17
  8.9 1.6 %collective-permute-start.15 = (bf16[1792,256]{1,0:T(8,128)(2,1)S(1)}, bf16[1792,256]{1,0:T(8,128)(2,1)S(1)}, u32[]{:S(2)}, u32[]{:S(2)}) collective-permute-start(bf16[1792,256]{1,0:T(8,128)(2,1)S(1)} %get-tuple-element.50), channel_id=1, source_target_pairs={{0,8},{8,16},{16,24},{24,0},{1,9},{9,17},{17,25},{25,1},{2,10},{10... | collective-permute-start | bytes 2752520 | tf_op jit(solution)/shard_map/ppermute | solution.py:17
  10.5 0.1 collective-permute-start
  10.6 0.0 copy-done.1
  10.7 0.0 copy-done.3
  10.7 2.4 %turn.1 = (bf16[768,2048]{1,0:T(8,128)(2,1)S(1)}, f32[1,768]{1,0:T(1,128)S(1)}) custom-call(s32[4]{0:T(128)S(1)} %copy-done.3, bf16[2048,768]{1,0:T(8,128)(2,1)S(1)} %copy-done.1), custom_call_target="tpu_custom_call" | custom-call | flops 6291456 | bytes 6291456 | tf_op jit(solution)/shard_map/turn/pallas_call | solution.py:125
  13.1 64.4 %collective-permute-done.block = bf16[256,768]{1,0:T(8,128)(2,1)S(1)} collective-permute-done((bf16[256,768]{1,0:T(8,128)(2,1)S(1)}, bf16[256,768]{1,0:T(8,128)(2,1)S(1)}, u32[]{:S(2)}, u32[]{:S(2)}) %collective-permute-start) | collective-permute-done | bytes 393248 | tf_op jit(solution)/shard_map/ppermute | solution.py:17
  77.5 0.5 picks.2
  78.0 0.0 collective-permute-done.6.rest
  78.0 0.0 copy-done.2
  78.0 1.8 %gram.4 = (f32[4,32,768]{2,1,0:T(8,128)S(1)}, f32[4,32,768]{2,1,0:T(8,128)S(1)}) custom-call(s32[1,2]{1,0:T(1,128)S(1)} %copy-done.2, bf16[768,2048]{1,0:T(8,128)(2,1)S(1)} %get-tuple-element.31.own, bf16[256,256]{1,0:T(8,128)(2,1)S(1)} %get-tuple-element.40.head, bf16[1792,256]{1,0:T(8,128)(2,1)S(1)} %collective-permute-done.6.rest), custom_call_target="tpu_custom_call" | custom-call | flops 805306368 | bytes 3145728 | tf_op jit(solution)/shard_map/gram/pallas_call | solution.py:178
  79.8 0.1 collective-permute-start.7
  79.9 0.0 collective-permute-done.1.rest
  79.9 1.8 %gram.3 = (f32[4,32,768]{2,1,0:T(8,128)S(1)}, f32[4,32,768]{2,1,0:T(8,128)S(1)}) custom-call(s32[1,2]{1,0:T(1,128)S(1)} %copy-done.2, bf16[768,2048]{1,0:T(8,128)(2,1)S(1)} %get-tuple-element.31.own, bf16[256,256]{1,0:T(8,128)(2,1)S(1)} %get-tuple-element.32.head, bf16[1792,256]{1,0:T(8,128)(2,1)S(1)} %collective-permute-done.1.rest), custom_call_target="tpu_custom_call" | custom-call | flops 805306368 | bytes 3145728 | tf_op jit(solution)/shard_map/gram/pallas_call | solution.py:178
  81.7 0.6 collective-permute-start.2
  82.2 0.0 collective-permute-done.15.rest
  82.2 1.8 %gram.5 = (f32[4,32,768]{2,1,0:T(8,128)S(1)}, f32[4,32,768]{2,1,0:T(8,128)S(1)}) custom-call(s32[1,2]{1,0:T(1,128)S(1)} %copy-done.2, bf16[768,2048]{1,0:T(8,128)(2,1)S(1)} %get-tuple-element.31.own, bf16[256,256]{1,0:T(8,128)(2,1)S(1)} %get-tuple-element.49.head, bf16[1792,256]{1,0:T(8,128)(2,1)S(1)} %collective-permute-done.15.rest), custom_call_target="tpu_custom_call" | custom-call | flops 805306368 | bytes 3145728 | tf_op jit(solution)/shard_map/gram/pallas_call | solution.py:178
  84.0 0.1 collective-permute-start.16
  84.1 0.5 collective-permute-start.11
  84.6 1.2 %collective-permute-done.11.b = f32[1,768]{1,0:T(1,128)S(1)} collective-permute-done((f32[1,768]{1,0:T(1,128)S(1)}, f32[1,768]{1,0:T(1,128)S(1)}, u32[]{:S(2)}, u32[]{:S(2)}) %collective-permute-start.11) | collective-permute-done | bytes 3104 | tf_op jit(solution)/shard_map/ppermute | solution.py:22
  85.8 1.5 %collective-permute-start.12 = (f32[1,768]{1,0:T(1,128)S(1)}, f32[1,768]{1,0:T(1,128)S(1)}, u32[]{:S(2)}, u32[]{:S(2)}) collective-permute-start(f32[1,768]{1,0:T(1,128)S(1)} %plus.3.a), channel_id=1, source_target_pairs={{0,2},{1,3},{2,0},{3,1},{4,6},{5,7},{6,4},{7,5},{8,10},{9,11},{10,... | collective-permute-start | bytes 9224 | tf_op jit(solution)/shard_map/ppermute | solution.py:22
  87.3 0.0 collective-permute-done.7.arrived
  87.4 0.6 collective-permute-start.8
  88.0 1.5 %collective-permute-done.12.b = f32[1,768]{1,0:T(1,128)S(1)} collective-permute-done((f32[1,768]{1,0:T(1,128)S(1)}, f32[1,768]{1,0:T(1,128)S(1)}, u32[]{:S(2)}, u32[]{:S(2)}) %collective-permute-start.12) | collective-permute-done | bytes 3104 | tf_op jit(solution)/shard_map/ppermute | solution.py:22
  89.4 1.5 %collective-permute-start.13 = (f32[1,768]{1,0:T(1,128)S(1)}, f32[1,768]{1,0:T(1,128)S(1)}, u32[]{:S(2)}, u32[]{:S(2)}) collective-permute-start(f32[1,768]{1,0:T(1,128)S(1)} %plus.4.a), channel_id=1, source_target_pairs={{0,4},{1,5},{2,6},{3,7},{4,0},{5,1},{6,2},{7,3},{8,12},{9,13},{10,... | collective-permute-start | bytes 9224 | tf_op jit(solution)/shard_map/ppermute | solution.py:22
  91.0 0.5 collective-permute-start.9
  91.5 0.0 collective-permute-done.2.arrived
  91.5 2.5 %collective-permute-start.10 = (f32[32,768]{1,0:T(8,128)S(1)}, f32[32,768]{1,0:T(8,128)S(1)}, u32[]{:S(2)}, u32[]{:S(2)}) collective-permute-start(f32[32,768]{1,0:T(8,128)S(1)} %get-tuple-element.47), channel_id=1, source_target_pairs={{0,6},{1,7},{2,4},{3,5},{4,2},{5,3},{6,0},{7,1},{8,14},{9,15},{10,... | collective-permute-start | bytes 294920 | tf_op jit(solution)/shard_map/ppermute | solution.py:22
  94.0 0.0 collective-permute-done.13.b
  94.0 0.6 collective-permute-start.3
  94.6 0.0 collective-permute-done.16.arrived
  94.6 1.5 %collective-permute-start.4 = (f32[32,768]{1,0:T(8,128)S(1)}, f32[32,768]{1,0:T(8,128)S(1)}, u32[]{:S(2)}, u32[]{:S(2)}) collective-permute-start(f32[32,768]{1,0:T(8,128)S(1)} %get-tuple-element.38), channel_id=1, source_target_pairs={{0,4},{1,5},{2,6},{3,7},{4,0},{5,1},{6,2},{7,3},{8,12},{9,13},{10,... | collective-permute-start | bytes 294920 | tf_op jit(solution)/shard_map/ppermute | solution.py:22
  96.1 0.0 collective-permute-done.8.refs_1_
  96.1 1.5 %collective-permute-start.5 = (f32[32,768]{1,0:T(8,128)S(1)}, f32[32,768]{1,0:T(8,128)S(1)}, u32[]{:S(2)}, u32[]{:S(2)}) collective-permute-start(f32[32,768]{1,0:T(8,128)S(1)} %get-tuple-element.39), channel_id=1, source_target_pairs={{0,6},{1,7},{2,4},{3,5},{4,2},{5,3},{6,0},{7,1},{8,14},{9,15},{10,... | collective-permute-start | bytes 294920 | tf_op jit(solution)/shard_map/ppermute | solution.py:22
  97.6 0.0 collective-permute-done.9.refs_2_
  97.6 2.1 %collective-permute-start.17 = (f32[32,768]{1,0:T(8,128)S(1)}, f32[32,768]{1,0:T(8,128)S(1)}, u32[]{:S(2)}, u32[]{:S(2)}) collective-permute-start(f32[32,768]{1,0:T(8,128)S(1)} %get-tuple-element.54), channel_id=1, source_target_pairs={{0,2},{1,3},{2,0},{3,1},{4,6},{5,7},{6,4},{7,5},{8,10},{9,11},{10,... | collective-permute-start | bytes 294920 | tf_op jit(solution)/shard_map/ppermute | solution.py:22
  99.7 0.0 collective-permute-done.10.refs_3_
  99.7 1.9 %collective-permute-start.18 = (f32[32,768]{1,0:T(8,128)S(1)}, f32[32,768]{1,0:T(8,128)S(1)}, u32[]{:S(2)}, u32[]{:S(2)}) collective-permute-start(f32[32,768]{1,0:T(8,128)S(1)} %get-tuple-element.55), channel_id=1, source_target_pairs={{0,4},{1,5},{2,6},{3,7},{4,0},{5,1},{6,2},{7,3},{8,12},{9,13},{10,... | collective-permute-start | bytes 294920 | tf_op jit(solution)/shard_map/ppermute | solution.py:22
  101.6 0.0 collective-permute-done.3.refs_1_
  101.6 0.0 collective-permute-start.19
  101.6 0.6 place.2.refs_4_
  102.2 0.5 collective-permute-done.4.refs_2_
  102.7 0.0 collective-permute-start.14
  102.7 0.0 collective-permute-done.5.refs_3_
  102.7 0.6 place.3.base
  103.3 4.8 %collective-permute-done.14.norm_low = f32[1,768]{1,0:T(1,128)S(1)} collective-permute-done((f32[1,768]{1,0:T(1,128)S(1)}, f32[1,768]{1,0:T(1,128)S(1)}, u32[]{:S(2)}, u32[]{:S(2)}) %collective-permute-start.14) | collective-permute-done | bytes 3104 | tf_op jit(solution)/shard_map/ppermute | solution.py:17
  108.1 0.0 collective-permute-done.17.refs_1_
  108.1 0.0 collective-permute-done.18.refs_2_
  108.1 0.0 collective-permute-done.19.refs_3_
  108.1 1.4 %finish.1 = f32[1,96,768]{2,1,0:T(8,128)} custom-call(s32[1,2]{1,0:T(1,128)S(1)} %copy-done.2, f32[96,768]{1,0:T(8,128)S(1)} %place.3.base, f32[1,768]{1,0:T(1,128)S(1)} %plus.5.norm_own, f32[1,768]{1,0:T(1,128)S(1)} %collective-permute-done.14.norm_low, f32[32,768]{1,0:T(8,128)S(1)} %get-tuple-element.53.refs_0_, ...), custom_call_target="tpu_custom_call" | custom-call | flops 37748736 | bytes 589824 | tf_op jit(solution)/shard_map/finish/pallas_call | solution.py:333
  (7 shorter events, 0.2 us)
Async XLA Ops:
  0.0 1.9 %copy-start = (bf16[2048,768]{1,0:T(8,128)(2,1)S(1)}, bf16[2048,768]{1,0:T(8,128)(2,1)}, u32[]{:S(2)}) copy-start(bf16[2048,768]{1,0:T(8,128)(2,1)} %block.3) | copy-start | bytes 9437188
  1.9 8.8 %copy-start.1 = (bf16[2048,768]{1,0:T(8,128)(2,1)S(1)}, bf16[2048,768]{1,0:T(8,128)(2,1)}, u32[]{:S(2)}) copy-start(bf16[2048,768]{1,0:T(8,128)(2,1)} %block.3) | copy-start | bytes 9437188
  1.9 8.8 %copy-start.3 = (s32[4]{0:T(128)S(1)}, s32[4]{0:T(128)}, u32[]{:S(2)}) copy-start(s32[4]{0:T(128)} %onsets.1) | copy-start | bytes 52
  4.2 73.8 %copy-start.2 = (s32[1,2]{1,0:T(1,128)S(1)}, s32[1,2]{1,0:T(1,128)}, u32[]{:S(2)}) copy-start(s32[1,2]{1,0:T(1,128)} %pairs.11) | copy-start | bytes 28
  4.2 73.7 %collective-permute-start.6 = (bf16[1792,256]{1,0:T(8,128)(2,1)S(1)}, bf16[1792,256]{1,0:T(8,128)(2,1)S(1)}, u32[]{:S(2)}, u32[]{:S(2)}) collective-permute-start(bf16[1792,256]{1,0:T(8,128)(2,1)S(1)} %get-tuple-element.41), channel_id=1, source_target_pairs={{0,8},{8,16},{16,24},{24,0},{1,9},{9,17},{17,25},{25,1},{2,10},{10... | collective-permute-start | bytes 2752520 | tf_op jit(solution)/shard_map/ppermute | solution.py:17
  7.3 72.5 %collective-permute-start.1 = (bf16[1792,256]{1,0:T(8,128)(2,1)S(1)}, bf16[1792,256]{1,0:T(8,128)(2,1)S(1)}, u32[]{:S(2)}, u32[]{:S(2)}) collective-permute-start(bf16[1792,256]{1,0:T(8,128)(2,1)S(1)} %get-tuple-element.33), channel_id=1, source_target_pairs={{0,8},{8,16},{16,24},{24,0},{1,9},{9,17},{17,25},{25,1},{2,10},{10... | collective-permute-start | bytes 2752520 | tf_op jit(solution)/shard_map/ppermute | solution.py:17
  8.9 73.3 %collective-permute-start.15 = (bf16[1792,256]{1,0:T(8,128)(2,1)S(1)}, bf16[1792,256]{1,0:T(8,128)(2,1)S(1)}, u32[]{:S(2)}, u32[]{:S(2)}) collective-permute-start(bf16[1792,256]{1,0:T(8,128)(2,1)S(1)} %get-tuple-element.50), channel_id=1, source_target_pairs={{0,8},{8,16},{16,24},{24,0},{1,9},{9,17},{17,25},{25,1},{2,10},{10... | collective-permute-start | bytes 2752520 | tf_op jit(solution)/shard_map/ppermute | solution.py:17
  10.5 66.9 %collective-permute-start = (bf16[256,768]{1,0:T(8,128)(2,1)S(1)}, bf16[256,768]{1,0:T(8,128)(2,1)S(1)}, u32[]{:S(2)}, u32[]{:S(2)}) collective-permute-start(bf16[256,768]{1,0:T(8,128)(2,1)S(1)} %slice.3), channel_id=1, source_target_pairs={{0,8},{8,16},{16,24},{24,0},{1,9},{9,17},{17,25},{25,1},{2,10},{10... | collective-permute-start | bytes 1179656 | tf_op jit(solution)/shard_map/ppermute | solution.py:17
  79.8 7.5 %collective-permute-start.7 = (f32[4,32,768]{2,1,0:T(8,128)S(1)}, f32[4,32,768]{2,1,0:T(8,128)S(1)}, u32[]{:S(2)}, u32[]{:S(2)}) collective-permute-start(f32[4,32,768]{2,1,0:T(8,128)S(1)} %get-tuple-element.43), channel_id=1, source_target_pairs={{0,1},{1,0},{2,3},{3,2},{4,5},{5,4},{6,7},{7,6},{8,9},{9,8},{10,11... | collective-permute-start | bytes 1179656 | tf_op jit(solution)/shard_map/ppermute | solution.py:22
  81.7 9.8 %collective-permute-start.2 = (f32[4,32,768]{2,1,0:T(8,128)S(1)}, f32[4,32,768]{2,1,0:T(8,128)S(1)}, u32[]{:S(2)}, u32[]{:S(2)}) collective-permute-start(f32[4,32,768]{2,1,0:T(8,128)S(1)} %get-tuple-element.35), channel_id=1, source_target_pairs={{0,1},{1,0},{2,3},{3,2},{4,5},{5,4},{6,7},{7,6},{8,9},{9,8},{10,11... | collective-permute-start | bytes 1179656 | tf_op jit(solution)/shard_map/ppermute | solution.py:22
  84.0 10.6 %collective-permute-start.16 = (f32[4,32,768]{2,1,0:T(8,128)S(1)}, f32[4,32,768]{2,1,0:T(8,128)S(1)}, u32[]{:S(2)}, u32[]{:S(2)}) collective-permute-start(f32[4,32,768]{2,1,0:T(8,128)S(1)} %get-tuple-element.52), channel_id=1, source_target_pairs={{0,1},{1,0},{2,3},{3,2},{4,5},{5,4},{6,7},{7,6},{8,9},{9,8},{10,11... | collective-permute-start | bytes 1179656 | tf_op jit(solution)/shard_map/ppermute | solution.py:22
  84.1 1.7 %collective-permute-start.11 = (f32[1,768]{1,0:T(1,128)S(1)}, f32[1,768]{1,0:T(1,128)S(1)}, u32[]{:S(2)}, u32[]{:S(2)}) collective-permute-start(f32[1,768]{1,0:T(1,128)S(1)} %get-tuple-element.48.a), channel_id=1, source_target_pairs={{0,1},{1,0},{2,3},{3,2},{4,5},{5,4},{6,7},{7,6},{8,9},{9,8},{10,11... | collective-permute-start | bytes 9224 | tf_op jit(solution)/shard_map/ppermute | solution.py:22
  85.8 3.6 %collective-permute-start.12 = (f32[1,768]{1,0:T(1,128)S(1)}, f32[1,768]{1,0:T(1,128)S(1)}, u32[]{:S(2)}, u32[]{:S(2)}) collective-permute-start(f32[1,768]{1,0:T(1,128)S(1)} %plus.3.a), channel_id=1, source_target_pairs={{0,2},{1,3},{2,0},{3,1},{4,6},{5,7},{6,4},{7,5},{8,10},{9,11},{10,... | collective-permute-start | bytes 9224 | tf_op jit(solution)/shard_map/ppermute | solution.py:22
  87.4 8.7 %collective-permute-start.8 = (f32[32,768]{1,0:T(8,128)S(1)}, f32[32,768]{1,0:T(8,128)S(1)}, u32[]{:S(2)}, u32[]{:S(2)}) collective-permute-start(f32[32,768]{1,0:T(8,128)S(1)} %get-tuple-element.45), channel_id=1, source_target_pairs={{0,2},{1,3},{2,0},{3,1},{4,6},{5,7},{6,4},{7,5},{8,10},{9,11},{10,... | collective-permute-start | bytes 294920 | tf_op jit(solution)/shard_map/ppermute | solution.py:22
  89.4 4.6 %collective-permute-start.13 = (f32[1,768]{1,0:T(1,128)S(1)}, f32[1,768]{1,0:T(1,128)S(1)}, u32[]{:S(2)}, u32[]{:S(2)}) collective-permute-start(f32[1,768]{1,0:T(1,128)S(1)} %plus.4.a), channel_id=1, source_target_pairs={{0,4},{1,5},{2,6},{3,7},{4,0},{5,1},{6,2},{7,3},{8,12},{9,13},{10,... | collective-permute-start | bytes 9224 | tf_op jit(solution)/shard_map/ppermute | solution.py:22
  91.0 6.7 %collective-permute-start.9 = (f32[32,768]{1,0:T(8,128)S(1)}, f32[32,768]{1,0:T(8,128)S(1)}, u32[]{:S(2)}, u32[]{:S(2)}) collective-permute-start(f32[32,768]{1,0:T(8,128)S(1)} %get-tuple-element.46), channel_id=1, source_target_pairs={{0,4},{1,5},{2,6},{3,7},{4,0},{5,1},{6,2},{7,3},{8,12},{9,13},{10,... | collective-permute-start | bytes 294920 | tf_op jit(solution)/shard_map/ppermute | solution.py:22
  91.5 8.3 %collective-permute-start.10 = (f32[32,768]{1,0:T(8,128)S(1)}, f32[32,768]{1,0:T(8,128)S(1)}, u32[]{:S(2)}, u32[]{:S(2)}) collective-permute-start(f32[32,768]{1,0:T(8,128)S(1)} %get-tuple-element.47), channel_id=1, source_target_pairs={{0,6},{1,7},{2,4},{3,5},{4,2},{5,3},{6,0},{7,1},{8,14},{9,15},{10,... | collective-permute-start | bytes 294920 | tf_op jit(solution)/shard_map/ppermute | solution.py:22
  94.0 7.6 %collective-permute-start.3 = (f32[32,768]{1,0:T(8,128)S(1)}, f32[32,768]{1,0:T(8,128)S(1)}, u32[]{:S(2)}, u32[]{:S(2)}) collective-permute-start(f32[32,768]{1,0:T(8,128)S(1)} %get-tuple-element.37), channel_id=1, source_target_pairs={{0,2},{1,3},{2,0},{3,1},{4,6},{5,7},{6,4},{7,5},{8,10},{9,11},{10,... | collective-permute-start | bytes 294920 | tf_op jit(solution)/shard_map/ppermute | solution.py:22
  94.6 8.1 %collective-permute-start.4 = (f32[32,768]{1,0:T(8,128)S(1)}, f32[32,768]{1,0:T(8,128)S(1)}, u32[]{:S(2)}, u32[]{:S(2)}) collective-permute-start(f32[32,768]{1,0:T(8,128)S(1)} %get-tuple-element.38), channel_id=1, source_target_pairs={{0,4},{1,5},{2,6},{3,7},{4,0},{5,1},{6,2},{7,3},{8,12},{9,13},{10,... | collective-permute-start | bytes 294920 | tf_op jit(solution)/shard_map/ppermute | solution.py:22
  96.1 6.6 %collective-permute-start.5 = (f32[32,768]{1,0:T(8,128)S(1)}, f32[32,768]{1,0:T(8,128)S(1)}, u32[]{:S(2)}, u32[]{:S(2)}) collective-permute-start(f32[32,768]{1,0:T(8,128)S(1)} %get-tuple-element.39), channel_id=1, source_target_pairs={{0,6},{1,7},{2,4},{3,5},{4,2},{5,3},{6,0},{7,1},{8,14},{9,15},{10,... | collective-permute-start | bytes 294920 | tf_op jit(solution)/shard_map/ppermute | solution.py:22
  97.6 10.4 %collective-permute-start.17 = (f32[32,768]{1,0:T(8,128)S(1)}, f32[32,768]{1,0:T(8,128)S(1)}, u32[]{:S(2)}, u32[]{:S(2)}) collective-permute-start(f32[32,768]{1,0:T(8,128)S(1)} %get-tuple-element.54), channel_id=1, source_target_pairs={{0,2},{1,3},{2,0},{3,1},{4,6},{5,7},{6,4},{7,5},{8,10},{9,11},{10,... | collective-permute-start | bytes 294920 | tf_op jit(solution)/shard_map/ppermute | solution.py:22
  99.7 8.4 %collective-permute-start.18 = (f32[32,768]{1,0:T(8,128)S(1)}, f32[32,768]{1,0:T(8,128)S(1)}, u32[]{:S(2)}, u32[]{:S(2)}) collective-permute-start(f32[32,768]{1,0:T(8,128)S(1)} %get-tuple-element.55), channel_id=1, source_target_pairs={{0,4},{1,5},{2,6},{3,7},{4,0},{5,1},{6,2},{7,3},{8,12},{9,13},{10,... | collective-permute-start | bytes 294920 | tf_op jit(solution)/shard_map/ppermute | solution.py:22
  101.6 6.5 %collective-permute-start.19 = (f32[32,768]{1,0:T(8,128)S(1)}, f32[32,768]{1,0:T(8,128)S(1)}, u32[]{:S(2)}, u32[]{:S(2)}) collective-permute-start(f32[32,768]{1,0:T(8,128)S(1)} %get-tuple-element.56), channel_id=1, source_target_pairs={{0,6},{1,7},{2,4},{3,5},{4,2},{5,3},{6,0},{7,1},{8,14},{9,15},{10,... | collective-permute-start | bytes 294920 | tf_op jit(solution)/shard_map/ppermute | solution.py:22
  102.7 5.4 %collective-permute-start.14 = (f32[1,768]{1,0:T(1,128)S(1)}, f32[1,768]{1,0:T(1,128)S(1)}, u32[]{:S(2)}, u32[]{:S(2)}) collective-permute-start(f32[1,768]{1,0:T(1,128)S(1)} %plus.5.norm_own), channel_id=1, source_target_pairs={{0,8},{8,16},{16,24},{24,0},{1,9},{9,17},{17,25},{25,1},{2,10},{10... | collective-permute-start | bytes 9224 | tf_op jit(solution)/shard_map/ppermute | solution.py:17

commit v3 on v2

--- a/solution.py
+++ b/solution.py
@@ -8,7 +8,7 @@
 from jax.sharding import PartitionSpec as P
 
 
-PARTS = (2, 2, 2)
+PARTS = (2, 2, 1, 1)
 HEAD = 8
 
 
@@ -261,7 +261,7 @@
     )(a, b)
 
 
-def placed(owner_first, share, start, run, terms, total):
+def placed(owner_first, share, start, run, terms, total, scales=None):
     width = total.shape[1]
     columns = width // share * run
     part = terms[0][...]
@@ -273,19 +273,30 @@
         spread = jnp.concatenate(
             [part[:, n * columns : (n + 1) * columns] for n in range(share // run)], axis=0
         )
+        left = spread * 0.0625
+        pieces = []
+        for _ in range(3):
+            pieces.append(left.astype(jnp.bfloat16))
+            left = left - pieces[-1].astype(jnp.float32)
         q = lax.broadcasted_iota(jnp.int32, (columns, width), 0)
         source = lax.broadcasted_iota(jnp.int32, (columns, width), 1)
         order = (q // run) * share + start + q % run == source
-        total[...] += jnp.dot(
-            spread,
-            order.astype(jnp.float32),
-            precision=lax.Precision.HIGHEST,
+        spots = jnp.dot(
+            jnp.concatenate(pieces, axis=0),
+            order.astype(jnp.float32).astype(jnp.bfloat16),
             preferred_element_type=jnp.float32,
         )
+        added = (spots[:share] + spots[share : 2 * share] + spots[2 * share :]) * 16.0
+        if scales is not None:
+            added = added * scales[0][:, :1] * scales[1][...]
+        total[...] += added
 
     @pl.when(jnp.logical_not(owner_first))
     def _():
-        total[start : start + run, :] = part
+        rows = part
+        if scales is not None:
+            rows = rows * scales[0][start : start + run, :1] * scales[1][...]
+        total[start : start + run, :] = rows
 
 
 def place_kernel(share, start, run, pairs, *refs):
@@ -297,52 +308,86 @@
     placed(pairs[0, 0] == lax.axis_index("src"), share, start, run, terms, total)
 
 
-def finish_kernel(share, start, run, pairs, base, norm_own, norm_low, *refs):
-    *terms, out, total = refs
-    width = total.shape[1]
+def scales_kernel(share, pairs, norm_own, norm_low, rows, columns):
+    width = columns.shape[1]
     owner_first = pairs[0, 0] == lax.axis_index("src")
-    total[...] = base[...]
-    placed(owner_first, share, start, run, terms, total)
     scale_own = lax.rsqrt(norm_own[...] + 1e-06)
     scale_low = lax.rsqrt(norm_low[...] + 1e-06)
     scale_first = jnp.where(owner_first, scale_own, scale_low)
-    scale_second = jnp.where(owner_first, scale_low, scale_own)
     row = lax.broadcasted_iota(jnp.int32, (share, width), 0) + lax.axis_index("tm") * share
     column = lax.broadcasted_iota(jnp.int32, (share, width), 1)
-    scale_rows = jnp.sum(jnp.where(row == column, scale_first, 0.0), axis=1, keepdims=True)
-    out[0] = total[...] * scale_rows * scale_second
-
-
-def place(pairs, terms, base, share, width, start, run):
-    given = list(terms) + ([] if base is None else [base])
-    return pl.pallas_call(
-        functools.partial(place_kernel, share, start, run),
-        out_shape=pltpu.VMEM((share, width), jnp.float32),
+    mine = jnp.sum(jnp.where(row == column, scale_first, 0.0), axis=1, keepdims=True)
+    rows[...] = jnp.broadcast_to(mine, rows.shape)
+    columns[...] = jnp.where(owner_first, scale_low, scale_own)
+
+
+def finish_kernel(share, start, run, pairs, base, rows, columns, *refs):
+    *terms, out = refs
+    owner_first = pairs[0, 0] == lax.axis_index("src")
+    out[0] = base[...] * rows[:, :1] * columns[...]
+    placed(owner_first, share, start, run, terms, out.at[0], (rows, columns))
+
+
+def small_call(kernel, out_shape, pairs, given, flops):
+    return pl.pallas_call(
+        kernel,
+        out_shape=out_shape,
         in_specs=[pl.BlockSpec(memory_space=pltpu.SMEM)]
         + [pl.BlockSpec(memory_space=pltpu.VMEM)] * len(given),
+        out_specs=jax.tree.map(lambda _: pl.BlockSpec(memory_space=pltpu.VMEM), out_shape),
+        cost_estimate=pl.CostEstimate(
+            flops=flops,
+            bytes_accessed=sum(4 * x.size for x in given),
+            transcendentals=0,
+        ),
+        compiler_params=pltpu.CompilerParams(vmem_limit_bytes=8 << 20),
+    )(pairs, *given)
+
+
+def place(pairs, terms, base, share, width, start, run):
+    return small_call(
+        functools.partial(place_kernel, share, start, run),
+        pltpu.VMEM((share, width), jnp.float32),
+        pairs,
+        list(terms) + ([] if base is None else [base]),
+        2 * share * width * 256,
+    )
+
+
+def scales_of(pairs, norm_own, norm_low, share):
+    width = norm_own.shape[1]
+    return small_call(
+        functools.partial(scales_kernel, share),
+        (pltpu.VMEM((share, 128), jnp.float32), pltpu.VMEM((1, width), jnp.float32)),
+        pairs,
+        [norm_own, norm_low],
+        share * width,
+    )
+
+
+def finish(pairs, base, scales, terms, share, start, run):
+    return small_call(
+        functools.partial(finish_kernel, share, start, run),
+        jax.ShapeDtypeStruct((1,) + base.shape, jnp.float32),
+        pairs,
+        [base, *scales, *terms],
+        2 * base.size * 256,
+    )
+
+
+def top_kernel(block, out):
+    pltpu.sync_copy(block.at[pl.ds(0, out.shape[0])], out)
+
+
+def top_of(block, rows):
+    return pl.pallas_call(
+        top_kernel,
+        out_shape=pltpu.VMEM((rows,) + block.shape[1:], block.dtype),
+        in_specs=[pl.BlockSpec(memory_space=pltpu.HBM)],
         out_specs=pl.BlockSpec(memory_space=pltpu.VMEM),
-        cost_estimate=pl.CostEstimate(
-            flops=2 * share * width * 256, bytes_accessed=8 * share * width, transcendentals=0
-        ),
-        compiler_params=pltpu.CompilerParams(vmem_limit_bytes=8 << 20),
-        name="place",
-    )(pairs, *given)
-
-
-def finish(pairs, base, norm_own, norm_low, terms, share, start, run):
-    return pl.pallas_call(
-        functools.partial(finish_kernel, share, start, run),
-        out_shape=jax.ShapeDtypeStruct((1,) + base.shape, jnp.float32),
-        in_specs=[pl.BlockSpec(memory_space=pltpu.SMEM)]
-        + [pl.BlockSpec(memory_space=pltpu.VMEM)] * (3 + len(terms)),
-        out_specs=pl.BlockSpec(memory_space=pltpu.VMEM),
-        scratch_shapes=[pltpu.VMEM(base.shape, jnp.float32)],
-        cost_estimate=pl.CostEstimate(
-            flops=2 * base.size * 256, bytes_accessed=8 * base.size, transcendentals=0
-        ),
-        compiler_params=pltpu.CompilerParams(vmem_limit_bytes=8 << 20),
-        name="finish",
-    )(pairs, base, norm_own, norm_low, *terms)
+        compiler_params=pltpu.CompilerParams(vmem_limit_bytes=60 << 20),
+        name="top",
+    )(block)
 
 
 def on_device(greens, pairs, onsets):
@@ -353,7 +398,7 @@
     aligned = groups == 8 and all(run % 8 == 0 and groups * run % 128 == 0 for _, run in runs)
     cut = rows_dev // HEAD
 
-    head = from_behind(greens[:cut], "src", 1)
+    head = from_behind(top_of(greens, cut), "src", 1)
     chosen = picks(greens, share, runs, cut)
     lower = []
     for block in chosen:
@@ -375,7 +420,8 @@
             terms.append(swapped(strip, "tm", 2 * m))
         if step < len(runs) - 1:
             base = place(pairs, terms, base, share, width, *run)
-    return finish(pairs, base, norm_own, norm_low, terms, share, *runs[-1])
+    scales = scales_of(pairs, norm_own, norm_low, share)
+    return finish(pairs, base, scales, terms, share, *runs[-1])
 
 
 def plain_tail(pairs, own, heads, lower, norm_own, norm_low, share, runs):

time: 110 us -> 117 us (1.064)
  starting transfers between devices: 21.7 us -> 28.6 us
  Pallas kernels: 13.4 us -> 19.3 us
  waiting for transfers between devices: 72.4 us -> 67.1 us
    ppermute x5 -> x6, waiting for transfers between devices: 69.2 us -> 59.4 us  [from_behind(): lax.ppermute(value, axis, [(i, (i + by) % length) for i in range(length)])]
    ppermute x15 -> x19, starting transfers between devices: 15.3 us -> 20.5 us  [swapped(): return lax.ppermute(value, axis, [(i, i ^ bits) for i in range(length)])]
    ppermute x15 -> x19, waiting for transfers between devices: 3.2 us -> 7.73 us  [swapped(): return lax.ppermute(value, axis, [(i, i ^ bits) for i in range(length)])]
    pallas_call x3 -> x4, Pallas kernels: 5.37 us -> 8.24 us  [gram(): pl.pallas_call(functools.partial(gram_kernel, share, run), out_shape=(hal...]
    pallas_call x3 -> x6, Pallas kernels: 2.59 us -> 4.81 us  [the longest x5 3.82 us: small_call(): pl.pallas_call(kernel, out_shape=out_shape, in_specs=[pl.BlockSpec(memory...]
    ppermute x5 -> x6, starting transfers between devices: 6.38 us -> 8.06 us  [from_behind(): lax.ppermute(value, axis, [(i, (i + by) % length) for i in range(length)])]
  transfers between devices with their start and end apart: 20 -> 25, of which waited for: 5 -> 9; matrix products, arithmetic and copies ran while one was open for 0% -> 0% of each run, Pallas kernels for 9% -> 13%
where the time goes in v3:
time: 117 us
  waiting for transfers between devices  67.1 us (57%)
  starting transfers between devices  28.6 us (24%)
  Pallas kernels  19.3 us (16%)
  local copies, waits for them, and re-layouts  1.91 us (2%)
    ppermute x6, waiting for transfers between devices, from_behind(): lax.ppermute(value, axis, [(i, (i + by) % length) for i in range(length)])  59.4 us
    ppermute x19, starting transfers between devices, swapped(): return lax.ppermute(value, axis, [(i, i ^ bits) for i in range(length)])  20.5 us
    pallas_call x4, Pallas kernels, gram(): pl.pallas_call(functools.partial(gram_kernel, share, run), out_shape=(hal...  8.24 us
    ppermute x6, starting transfers between devices, from_behind(): lax.ppermute(value, axis, [(i, (i + by) % length) for i in range(length)])  8.06 us
    ppermute x19, waiting for transfers between devices, swapped(): return lax.ppermute(value, axis, [(i, i ^ bits) for i in range(length)])  7.73 us
    pallas_call x5, Pallas kernels, small_call(): pl.pallas_call(kernel, out_shape=out_shape, in_specs=[pl.BlockSpec(memory...  3.82 us
    pallas_call x2, Pallas kernels, picks(): pl.pallas_call(functools.partial(picks_kernel, share, runs, skip), out_sh...  3.61 us
    pallas_call x1, Pallas kernels, turn(): pl.pallas_call(functools.partial(turn_kernel, step), out_shape=(pltpu.VME...  2.44 us
  transfers between devices with their start and end apart: 25, of which 9 were waited for; matrix products, arithmetic and copies ran while one was open for 0% of the time, Pallas kernels for 13%

profile of v3, /device:TPU:0, one launch (start us, length us, event | category | flops | bytes accessed | tf_op | source)
XLA Modules:
  0.0 117.1 jit_solution(7014559777022353755)
XLA Ops:
  0.0 1.9 %copy-done = bf16[2048,768]{1,0:T(8,128)(2,1)S(1)} copy-done((bf16[2048,768]{1,0:T(8,128)(2,1)S(1)}, bf16[2048,768]{1,0:T(8,128)(2,1)}, u32[]{:S(2)}) %copy-start) | copy-done | bytes 3145752
  1.9 3.0 %picks.3 = (bf16[1792,256]{1,0:T(8,128)(2,1)}, bf16[1792,256]{1,0:T(8,128)(2,1)}, bf16[1792,128]{1,0:T(8,128)(2,1)S(1)}, bf16[1792,128]{1,0:T(8,128)(2,1)S(1)}) custom-call(bf16[2048,768]{1,0:T(8,128)(2,1)S(1)} %copy-done), custom_call_target="tpu_custom_call" | custom-call | flops 2415919104 | bytes 6291456 | tf_op jit(solution)/shard_map/picks/pallas_call | solution.py:87
  4.9 0.0 copy-start.1
  4.9 0.0 copy-start.3
  5.0 3.1 %collective-permute-start.6 = (bf16[1792,256]{1,0:T(8,128)(2,1)}, bf16[1792,256]{1,0:T(8,128)(2,1)}, u32[]{:S(2)}, u32[]{:S(2)}) collective-permute-start(bf16[1792,256]{1,0:T(8,128)(2,1)} %get-tuple-element.51), channel_id=1, source_target_pairs={{0,8},{8,16},{16,24},{24,0},{1,9},{9,17},{17,25},{25,1},{2,10},{10... | collective-permute-start | bytes 2752520 | tf_op jit(solution)/shard_map/ppermute | solution.py:17
  8.1 1.6 %collective-permute-start.11 = (bf16[1792,256]{1,0:T(8,128)(2,1)}, bf16[1792,256]{1,0:T(8,128)(2,1)}, u32[]{:S(2)}, u32[]{:S(2)}) collective-permute-start(bf16[1792,256]{1,0:T(8,128)(2,1)} %get-tuple-element.59), channel_id=1, source_target_pairs={{0,8},{8,16},{16,24},{24,0},{1,9},{9,17},{17,25},{25,1},{2,10},{10... | collective-permute-start | bytes 2752520 | tf_op jit(solution)/shard_map/ppermute | solution.py:17
  9.6 1.0 top.1
  10.6 1.6 %collective-permute-start = (bf16[256,768]{1,0:T(8,128)(2,1)S(1)}, bf16[256,768]{1,0:T(8,128)(2,1)S(1)}, u32[]{:S(2)}, u32[]{:S(2)}) collective-permute-start(bf16[256,768]{1,0:T(8,128)(2,1)S(1)} %top.1), channel_id=1, source_target_pairs={{0,8},{8,16},{16,24},{24,0},{1,9},{9,17},{17,25},{25,1},{2,10},{10... | collective-permute-start | bytes 1179656 | tf_op jit(solution)/shard_map/ppermute | solution.py:17
  12.2 0.7 collective-permute-start.1
  12.9 1.1 collective-permute-start.20
  14.0 2.4 %turn.1 = (bf16[768,2048]{1,0:T(8,128)(2,1)S(1)}, f32[1,768]{1,0:T(1,128)S(1)}) custom-call(s32[4]{0:T(128)S(1)} %copy-done.3, bf16[2048,768]{1,0:T(8,128)(2,1)S(1)} %copy-done.1), custom_call_target="tpu_custom_call" | custom-call | flops 6291456 | bytes 6291456 | tf_op jit(solution)/shard_map/turn/pallas_call | solution.py:125
  16.5 43.1 %collective-permute-done.block = bf16[256,768]{1,0:T(8,128)(2,1)S(1)} collective-permute-done((bf16[256,768]{1,0:T(8,128)(2,1)S(1)}, bf16[256,768]{1,0:T(8,128)(2,1)S(1)}, u32[]{:S(2)}, u32[]{:S(2)}) %collective-permute-start) | collective-permute-done | bytes 393248 | tf_op jit(solution)/shard_map/ppermute | solution.py:17
  59.6 0.6 picks.2
  60.2 0.0 collective-permute-done.6.rest
  60.2 2.4 %gram.5 = (f32[4,32,768]{2,1,0:T(8,128)S(1)}, f32[4,32,768]{2,1,0:T(8,128)S(1)}) custom-call(s32[1,2]{1,0:T(1,128)S(1)} %copy-done.2, bf16[768,2048]{1,0:T(8,128)(2,1)S(1)} %get-tuple-element.41.own, bf16[256,256]{1,0:T(8,128)(2,1)S(1)} %get-tuple-element.50.head, bf16[1792,256]{1,0:T(8,128)(2,1)} %collective-permute-done.6.rest), custom_call_target="tpu_custom_call" | custom-call | flops 805306368 | bytes 3145728 | tf_op jit(solution)/shard_map/gram/pallas_call | solution.py:178
  62.7 0.1 collective-permute-start.7
  62.7 0.0 collective-permute-done.11.rest
  62.7 2.4 %gram.6 = (f32[4,32,768]{2,1,0:T(8,128)S(1)}, f32[4,32,768]{2,1,0:T(8,128)S(1)}) custom-call(s32[1,2]{1,0:T(1,128)S(1)} %copy-done.2, bf16[768,2048]{1,0:T(8,128)(2,1)S(1)} %get-tuple-element.41.own, bf16[256,256]{1,0:T(8,128)(2,1)S(1)} %get-tuple-element.58.head, bf16[1792,256]{1,0:T(8,128)(2,1)} %collective-permute-done.11.rest), custom_call_target="tpu_custom_call" | custom-call | flops 805306368 | bytes 3145728 | tf_op jit(solution)/shard_map/gram/pallas_call | solution.py:178
  65.2 0.5 collective-permute-start.12
  65.7 3.7 %collective-permute-done.1.rest = bf16[1792,128]{1,0:T(8,128)(2,1)S(1)} collective-permute-done((bf16[1792,128]{1,0:T(8,128)(2,1)}, bf16[1792,128]{1,0:T(8,128)(2,1)S(1)}, u32[]{:S(2)}, u32[]{:S(2)}) %collective-permute-start.1) | collective-permute-done | bytes 458784 | tf_op jit(solution)/shard_map/ppermute | solution.py:17
  69.4 1.7 %gram.4 = (f32[4,16,768]{2,1,0:T(8,128)S(1)}, f32[4,16,768]{2,1,0:T(8,128)S(1)}) custom-call(s32[1,2]{1,0:T(1,128)S(1)} %copy-done.2, bf16[768,2048]{1,0:T(8,128)(2,1)S(1)} %get-tuple-element.41.own, bf16[256,128]{1,0:T(8,128)(2,1)S(1)} %get-tuple-element.42.head, bf16[1792,128]{1,0:T(8,128)(2,1)S(1)} %collective-permute-done.1.rest), custom_call_target="tpu_custom_call" | custom-call | flops 402653184 | bytes 3145728 | tf_op jit(solution)/shard_map/gram/pallas_call | solution.py:178
  71.1 0.1 collective-permute-start.2
  71.2 7.2 %collective-permute-done.20.rest = bf16[1792,128]{1,0:T(8,128)(2,1)S(1)} collective-permute-done((bf16[1792,128]{1,0:T(8,128)(2,1)S(1)}, bf16[1792,128]{1,0:T(8,128)(2,1)S(1)}, u32[]{:S(2)}, u32[]{:S(2)}) %collective-permute-start.20) | collective-permute-done | bytes 458784 | tf_op jit(solution)/shard_map/ppermute | solution.py:17
  78.4 1.7 %gram.7 = (f32[4,16,768]{2,1,0:T(8,128)S(1)}, f32[4,16,768]{2,1,0:T(8,128)S(1)}) custom-call(s32[1,2]{1,0:T(1,128)S(1)} %copy-done.2, bf16[768,2048]{1,0:T(8,128)(2,1)S(1)} %get-tuple-element.41.own, bf16[256,128]{1,0:T(8,128)(2,1)S(1)} %get-tuple-element.69.head, bf16[1792,128]{1,0:T(8,128)(2,1)S(1)} %collective-permute-done.20.rest), custom_call_target="tpu_custom_call" | custom-call | flops 402653184 | bytes 3145728 | tf_op jit(solution)/shard_map/gram/pallas_call | solution.py:178
  80.1 0.1 collective-permute-start.21
  80.2 0.0 collective-permute-done.7.arrived
  80.2 0.1 fold.5
  80.2 1.6 %collective-permute-start.8 = (f32[32,768]{1,0:T(8,128)S(1)}, f32[32,768]{1,0:T(8,128)S(1)}, u32[]{:S(2)}, u32[]{:S(2)}) collective-permute-start(f32[32,768]{1,0:T(8,128)S(1)} %get-tuple-element.55), channel_id=1, source_target_pairs={{0,2},{1,3},{2,0},{3,1},{4,6},{5,7},{6,4},{7,5},{8,10},{9,11},{10,... | collective-permute-start | bytes 294920 | tf_op jit(solution)/shard_map/ppermute | solution.py:22
  81.8 0.0 collective-permute-done.2.arrived
  81.8 0.6 collective-permute-start.3
  82.4 0.0 collective-permute-start.16
  82.4 1.2 collective-permute-done.16.b
  83.6 1.5 %collective-permute-start.17 = (f32[1,768]{1,0:T(1,128)S(1)}, f32[1,768]{1,0:T(1,128)S(1)}, u32[]{:S(2)}, u32[]{:S(2)}) collective-permute-start(f32[1,768]{1,0:T(1,128)S(1)} %plus.3.a), channel_id=1, source_target_pairs={{0,2},{1,3},{2,0},{3,1},{4,6},{5,7},{6,4},{7,5},{8,10},{9,11},{10,... | collective-permute-start | bytes 9224 | tf_op jit(solution)/shard_map/ppermute | solution.py:22
  85.1 2.1 %collective-permute-done.17.b = f32[1,768]{1,0:T(1,128)S(1)} collective-permute-done((f32[1,768]{1,0:T(1,128)S(1)}, f32[1,768]{1,0:T(1,128)S(1)}, u32[]{:S(2)}, u32[]{:S(2)}) %collective-permute-start.17) | collective-permute-done | bytes 3104 | tf_op jit(solution)/shard_map/ppermute | solution.py:22
  87.2 1.5 %collective-permute-start.18 = (f32[1,768]{1,0:T(1,128)S(1)}, f32[1,768]{1,0:T(1,128)S(1)}, u32[]{:S(2)}, u32[]{:S(2)}) collective-permute-start(f32[1,768]{1,0:T(1,128)S(1)} %plus.4.a), channel_id=1, source_target_pairs={{0,4},{1,5},{2,6},{3,7},{4,0},{5,1},{6,2},{7,3},{8,12},{9,13},{10,... | collective-permute-start | bytes 9224 | tf_op jit(solution)/shard_map/ppermute | solution.py:22
  88.7 2.1 %collective-permute-done.18.b = f32[1,768]{1,0:T(1,128)S(1)} collective-permute-done((f32[1,768]{1,0:T(1,128)S(1)}, f32[1,768]{1,0:T(1,128)S(1)}, u32[]{:S(2)}, u32[]{:S(2)}) %collective-permute-start.18) | collective-permute-done | bytes 3104 | tf_op jit(solution)/shard_map/ppermute | solution.py:22
  90.8 0.0 collective-permute-start.19
  90.8 5.4 %collective-permute-done.19.norm_low = f32[1,768]{1,0:T(1,128)S(1)} collective-permute-done((f32[1,768]{1,0:T(1,128)S(1)}, f32[1,768]{1,0:T(1,128)S(1)}, u32[]{:S(2)}, u32[]{:S(2)}) %collective-permute-start.19) | collective-permute-done | bytes 3104 | tf_op jit(solution)/shard_map/ppermute | solution.py:17
  96.2 1.5 %collective-permute-start.9 = (f32[32,768]{1,0:T(8,128)S(1)}, f32[32,768]{1,0:T(8,128)S(1)}, u32[]{:S(2)}, u32[]{:S(2)}) collective-permute-start(f32[32,768]{1,0:T(8,128)S(1)} %get-tuple-element.56), channel_id=1, source_target_pairs={{0,4},{1,5},{2,6},{3,7},{4,0},{5,1},{6,2},{7,3},{8,12},{9,13},{10,... | collective-permute-start | bytes 294920 | tf_op jit(solution)/shard_map/ppermute | solution.py:22
  97.7 0.0 collective-permute-done.12.arrived
  97.7 1.4 %collective-permute-start.10 = (f32[32,768]{1,0:T(8,128)S(1)}, f32[32,768]{1,0:T(8,128)S(1)}, u32[]{:S(2)}, u32[]{:S(2)}) collective-permute-start(f32[32,768]{1,0:T(8,128)S(1)} %get-tuple-element.57), channel_id=1, source_target_pairs={{0,6},{1,7},{2,4},{3,5},{4,2},{5,3},{6,0},{7,1},{8,14},{9,15},{10,... | collective-permute-start | bytes 294920 | tf_op jit(solution)/shard_map/ppermute | solution.py:22
  99.2 0.0 collective-permute-done.21.arrived
  99.2 0.6 collective-permute-start.13
  99.8 0.0 collective-permute-done.3.refs_1_
  99.8 1.5 %collective-permute-start.14 = (f32[32,768]{1,0:T(8,128)S(1)}, f32[32,768]{1,0:T(8,128)S(1)}, u32[]{:S(2)}, u32[]{:S(2)}) collective-permute-start(f32[32,768]{1,0:T(8,128)S(1)} %get-tuple-element.64), channel_id=1, source_target_pairs={{0,4},{1,5},{2,6},{3,7},{4,0},{5,1},{6,2},{7,3},{8,12},{9,13},{10,... | collective-permute-start | bytes 294920 | tf_op jit(solution)/shard_map/ppermute | solution.py:22
  101.3 0.0 collective-permute-done.8.refs_1_
  101.3 1.4 %collective-permute-start.15 = (f32[32,768]{1,0:T(8,128)S(1)}, f32[32,768]{1,0:T(8,128)S(1)}, u32[]{:S(2)}, u32[]{:S(2)}) collective-permute-start(f32[32,768]{1,0:T(8,128)S(1)} %get-tuple-element.65), channel_id=1, source_target_pairs={{0,6},{1,7},{2,4},{3,5},{4,2},{5,3},{6,0},{7,1},{8,14},{9,15},{10,... | collective-permute-start | bytes 294920 | tf_op jit(solution)/shard_map/ppermute | solution.py:22
  102.8 1.3 %collective-permute-done.9.refs_2_ = f32[32,768]{1,0:T(8,128)S(1)} collective-permute-done((f32[32,768]{1,0:T(8,128)S(1)}, f32[32,768]{1,0:T(8,128)S(1)}, u32[]{:S(2)}, u32[]{:S(2)}) %collective-permute-start.9) | collective-permute-done | bytes 98336 | tf_op jit(solution)/shard_map/ppermute | solution.py:22
  104.1 1.6 %collective-permute-start.4 = (f32[16,768]{1,0:T(8,128)S(1)}, f32[16,768]{1,0:T(8,128)S(1)}, u32[]{:S(2)}, u32[]{:S(2)}) collective-permute-start(f32[16,768]{1,0:T(8,128)S(1)} %get-tuple-element.48), channel_id=1, source_target_pairs={{0,4},{1,5},{2,6},{3,7},{4,0},{5,1},{6,2},{7,3},{8,12},{9,13},{10,... | collective-permute-start | bytes 147464 | tf_op jit(solution)/shard_map/ppermute | solution.py:22
  105.6 0.0 collective-permute-done.10.refs_3_
  105.7 2.8 %collective-permute-start.5 = (f32[16,768]{1,0:T(8,128)S(1)}, f32[16,768]{1,0:T(8,128)S(1)}, u32[]{:S(2)}, u32[]{:S(2)}) collective-permute-start(f32[16,768]{1,0:T(8,128)S(1)} %get-tuple-element.49), channel_id=1, source_target_pairs={{0,6},{1,7},{2,4},{3,5},{4,2},{5,3},{6,0},{7,1},{8,14},{9,15},{10,... | collective-permute-start | bytes 147464 | tf_op jit(solution)/shard_map/ppermute | solution.py:22
  108.5 0.6 collective-permute-start.22
  109.2 1.5 %collective-permute-start.23 = (f32[16,768]{1,0:T(8,128)S(1)}, f32[16,768]{1,0:T(8,128)S(1)}, u32[]{:S(2)}, u32[]{:S(2)}) collective-permute-start(f32[16,768]{1,0:T(8,128)S(1)} %get-tuple-element.75), channel_id=1, source_target_pairs={{0,4},{1,5},{2,6},{3,7},{4,0},{5,1},{6,2},{7,3},{8,12},{9,13},{10,... | collective-permute-start | bytes 147464 | tf_op jit(solution)/shard_map/ppermute | solution.py:22
  110.7 0.0 collective-permute-done.15.refs_3_
  110.7 1.4 %collective-permute-start.24 = (f32[16,768]{1,0:T(8,128)S(1)}, f32[16,768]{1,0:T(8,128)S(1)}, u32[]{:S(2)}, u32[]{:S(2)}) collective-permute-start(f32[16,768]{1,0:T(8,128)S(1)} %get-tuple-element.76), channel_id=1, source_target_pairs={{0,6},{1,7},{2,4},{3,5},{4,2},{5,3},{6,0},{7,1},{8,14},{9,15},{10,... | collective-permute-start | bytes 147464 | tf_op jit(solution)/shard_map/ppermute | solution.py:22
  112.1 0.7 shard_map.40
  112.8 0.6 shard_map.37.refs_4_
  113.4 0.6 shard_map.38.refs_4_
  114.0 0.0 collective-permute-done.4.refs_2_
  114.0 0.6 shard_map.39.base
  114.6 0.0 collective-permute-done.22.refs_1_
  114.6 0.0 collective-permute-done.23.refs_2_
  114.6 1.1 collective-permute-done.24.refs_3_
  115.7 1.4 %shard_map.41 = f32[1,96,768]{2,1,0:T(8,128)} custom-call(s32[1,2]{1,0:T(1,128)S(1)} %copy-done.2, f32[96,768]{1,0:T(8,128)S(1)} %shard_map.39.base, f32[96,128]{1,0:T(8,128)S(1)} %get-tuple-element.67.rows, f32[1,768]{1,0:T(1,128)S(1)} %get-tuple-element.68.columns, f32[16,768]{1,0:T(8,128)S(1)} %get-tuple-element.73.refs_0_, ...), custom_call_target="tpu_custom_call" | custom-call | flops 37748736 | bytes 543744 | tf_op jit(solution)/shard_map/pallas_call | solution.py:332
  (16 shorter events, 0.1 us)
Async XLA Ops:
  0.0 1.9 %copy-start = (bf16[2048,768]{1,0:T(8,128)(2,1)S(1)}, bf16[2048,768]{1,0:T(8,128)(2,1)}, u32[]{:S(2)}) copy-start(bf16[2048,768]{1,0:T(8,128)(2,1)} %block.5) | copy-start | bytes 9437188
  4.9 3.1 %copy-start.4 = (bf16[1792,128]{1,0:T(8,128)(2,1)}, bf16[1792,128]{1,0:T(8,128)(2,1)S(1)}, u32[]{:S(2)}) copy-start(bf16[1792,128]{1,0:T(8,128)(2,1)S(1)} %get-tuple-element.43) | copy-start | bytes 1376260
  4.9 9.1 %copy-start.1 = (bf16[2048,768]{1,0:T(8,128)(2,1)S(1)}, bf16[2048,768]{1,0:T(8,128)(2,1)}, u32[]{:S(2)}) copy-start(bf16[2048,768]{1,0:T(8,128)(2,1)} %block.5) | copy-start | bytes 9437188
  4.9 9.1 %copy-start.3 = (s32[4]{0:T(128)S(1)}, s32[4]{0:T(128)}, u32[]{:S(2)}) copy-start(s32[4]{0:T(128)} %onsets.1) | copy-start | bytes 52
  5.0 55.2 %collective-permute-start.6 = (bf16[1792,256]{1,0:T(8,128)(2,1)}, bf16[1792,256]{1,0:T(8,128)(2,1)}, u32[]{:S(2)}, u32[]{:S(2)}) collective-permute-start(bf16[1792,256]{1,0:T(8,128)(2,1)} %get-tuple-element.51), channel_id=1, source_target_pairs={{0,8},{8,16},{16,24},{24,0},{1,9},{9,17},{17,25},{25,1},{2,10},{10... | collective-permute-start | bytes 2752520 | tf_op jit(solution)/shard_map/ppermute | solution.py:17
  8.1 52.1 %copy-start.2 = (s32[1,2]{1,0:T(1,128)S(1)}, s32[1,2]{1,0:T(1,128)}, u32[]{:S(2)}) copy-start(s32[1,2]{1,0:T(1,128)} %pairs.17) | copy-start | bytes 28
  8.1 54.7 %collective-permute-start.11 = (bf16[1792,256]{1,0:T(8,128)(2,1)}, bf16[1792,256]{1,0:T(8,128)(2,1)}, u32[]{:S(2)}, u32[]{:S(2)}) collective-permute-start(bf16[1792,256]{1,0:T(8,128)(2,1)} %get-tuple-element.59), channel_id=1, source_target_pairs={{0,8},{8,16},{16,24},{24,0},{1,9},{9,17},{17,25},{25,1},{2,10},{10... | collective-permute-start | bytes 2752520 | tf_op jit(solution)/shard_map/ppermute | solution.py:17
  10.6 49.0 %collective-permute-start = (bf16[256,768]{1,0:T(8,128)(2,1)S(1)}, bf16[256,768]{1,0:T(8,128)(2,1)S(1)}, u32[]{:S(2)}, u32[]{:S(2)}) collective-permute-start(bf16[256,768]{1,0:T(8,128)(2,1)S(1)} %top.1), channel_id=1, source_target_pairs={{0,8},{8,16},{16,24},{24,0},{1,9},{9,17},{17,25},{25,1},{2,10},{10... | collective-permute-start | bytes 1179656 | tf_op jit(solution)/shard_map/ppermute | solution.py:17
  12.2 57.2 %collective-permute-start.1 = (bf16[1792,128]{1,0:T(8,128)(2,1)}, bf16[1792,128]{1,0:T(8,128)(2,1)S(1)}, u32[]{:S(2)}, u32[]{:S(2)}) collective-permute-start(bf16[1792,128]{1,0:T(8,128)(2,1)} %copy-done.4), channel_id=1, source_target_pairs={{0,8},{8,16},{16,24},{24,0},{1,9},{9,17},{17,25},{25,1},{2,10},{10... | collective-permute-start | bytes 1376264 | tf_op jit(solution)/shard_map/ppermute | solution.py:17
  12.9 65.5 %collective-permute-start.20 = (bf16[1792,128]{1,0:T(8,128)(2,1)S(1)}, bf16[1792,128]{1,0:T(8,128)(2,1)S(1)}, u32[]{:S(2)}, u32[]{:S(2)}) collective-permute-start(bf16[1792,128]{1,0:T(8,128)(2,1)S(1)} %get-tuple-element.70), channel_id=1, source_target_pairs={{0,8},{8,16},{16,24},{24,0},{1,9},{9,17},{17,25},{25,1},{2,10},{10... | collective-permute-start | bytes 1376264 | tf_op jit(solution)/shard_map/ppermute | solution.py:17
  62.7 17.5 %collective-permute-start.7 = (f32[4,32,768]{2,1,0:T(8,128)S(1)}, f32[4,32,768]{2,1,0:T(8,128)S(1)}, u32[]{:S(2)}, u32[]{:S(2)}) collective-permute-start(f32[4,32,768]{2,1,0:T(8,128)S(1)} %get-tuple-element.53), channel_id=1, source_target_pairs={{0,1},{1,0},{2,3},{3,2},{4,5},{5,4},{6,7},{7,6},{8,9},{9,8},{10,11... | collective-permute-start | bytes 1179656 | tf_op jit(solution)/shard_map/ppermute | solution.py:22
  65.2 32.5 %collective-permute-start.12 = (f32[4,32,768]{2,1,0:T(8,128)S(1)}, f32[4,32,768]{2,1,0:T(8,128)S(1)}, u32[]{:S(2)}, u32[]{:S(2)}) collective-permute-start(f32[4,32,768]{2,1,0:T(8,128)S(1)} %get-tuple-element.61), channel_id=1, source_target_pairs={{0,1},{1,0},{2,3},{3,2},{4,5},{5,4},{6,7},{7,6},{8,9},{9,8},{10,11... | collective-permute-start | bytes 1179656 | tf_op jit(solution)/shard_map/ppermute | solution.py:22
  71.1 10.7 %collective-permute-start.2 = (f32[4,16,768]{2,1,0:T(8,128)S(1)}, f32[4,16,768]{2,1,0:T(8,128)S(1)}, u32[]{:S(2)}, u32[]{:S(2)}) collective-permute-start(f32[4,16,768]{2,1,0:T(8,128)S(1)} %get-tuple-element.45), channel_id=1, source_target_pairs={{0,1},{1,0},{2,3},{3,2},{4,5},{5,4},{6,7},{7,6},{8,9},{9,8},{10,11... | collective-permute-start | bytes 589832 | tf_op jit(solution)/shard_map/ppermute | solution.py:22
  80.1 19.1 %collective-permute-start.21 = (f32[4,16,768]{2,1,0:T(8,128)S(1)}, f32[4,16,768]{2,1,0:T(8,128)S(1)}, u32[]{:S(2)}, u32[]{:S(2)}) collective-permute-start(f32[4,16,768]{2,1,0:T(8,128)S(1)} %get-tuple-element.72), channel_id=1, source_target_pairs={{0,1},{1,0},{2,3},{3,2},{4,5},{5,4},{6,7},{7,6},{8,9},{9,8},{10,11... | collective-permute-start | bytes 589832 | tf_op jit(solution)/shard_map/ppermute | solution.py:22
  80.2 21.1 %collective-permute-start.8 = (f32[32,768]{1,0:T(8,128)S(1)}, f32[32,768]{1,0:T(8,128)S(1)}, u32[]{:S(2)}, u32[]{:S(2)}) collective-permute-start(f32[32,768]{1,0:T(8,128)S(1)} %get-tuple-element.55), channel_id=1, source_target_pairs={{0,2},{1,3},{2,0},{3,1},{4,6},{5,7},{6,4},{7,5},{8,10},{9,11},{10,... | collective-permute-start | bytes 294920 | tf_op jit(solution)/shard_map/ppermute | solution.py:22
  81.8 18.0 %collective-permute-start.3 = (f32[16,768]{1,0:T(8,128)S(1)}, f32[16,768]{1,0:T(8,128)S(1)}, u32[]{:S(2)}, u32[]{:S(2)}) collective-permute-start(f32[16,768]{1,0:T(8,128)S(1)} %get-tuple-element.47), channel_id=1, source_target_pairs={{0,2},{1,3},{2,0},{3,1},{4,6},{5,7},{6,4},{7,5},{8,10},{9,11},{10,... | collective-permute-start | bytes 147464 | tf_op jit(solution)/shard_map/ppermute | solution.py:22
  82.4 1.2 collective-permute-start.16
  83.6 3.6 %collective-permute-start.17 = (f32[1,768]{1,0:T(1,128)S(1)}, f32[1,768]{1,0:T(1,128)S(1)}, u32[]{:S(2)}, u32[]{:S(2)}) collective-permute-start(f32[1,768]{1,0:T(1,128)S(1)} %plus.3.a), channel_id=1, source_target_pairs={{0,2},{1,3},{2,0},{3,1},{4,6},{5,7},{6,4},{7,5},{8,10},{9,11},{10,... | collective-permute-start | bytes 9224 | tf_op jit(solution)/shard_map/ppermute | solution.py:22
  87.2 3.6 %collective-permute-start.18 = (f32[1,768]{1,0:T(1,128)S(1)}, f32[1,768]{1,0:T(1,128)S(1)}, u32[]{:S(2)}, u32[]{:S(2)}) collective-permute-start(f32[1,768]{1,0:T(1,128)S(1)} %plus.4.a), channel_id=1, source_target_pairs={{0,4},{1,5},{2,6},{3,7},{4,0},{5,1},{6,2},{7,3},{8,12},{9,13},{10,... | collective-permute-start | bytes 9224 | tf_op jit(solution)/shard_map/ppermute | solution.py:22
  90.8 5.4 %collective-permute-start.19 = (f32[1,768]{1,0:T(1,128)S(1)}, f32[1,768]{1,0:T(1,128)S(1)}, u32[]{:S(2)}, u32[]{:S(2)}) collective-permute-start(f32[1,768]{1,0:T(1,128)S(1)} %plus.5.norm_own), channel_id=1, source_target_pairs={{0,8},{8,16},{16,24},{24,0},{1,9},{9,17},{17,25},{25,1},{2,10},{10... | collective-permute-start | bytes 9224 | tf_op jit(solution)/shard_map/ppermute | solution.py:17
  96.2 7.9 %collective-permute-start.9 = (f32[32,768]{1,0:T(8,128)S(1)}, f32[32,768]{1,0:T(8,128)S(1)}, u32[]{:S(2)}, u32[]{:S(2)}) collective-permute-start(f32[32,768]{1,0:T(8,128)S(1)} %get-tuple-element.56), channel_id=1, source_target_pairs={{0,4},{1,5},{2,6},{3,7},{4,0},{5,1},{6,2},{7,3},{8,12},{9,13},{10,... | collective-permute-start | bytes 294920 | tf_op jit(solution)/shard_map/ppermute | solution.py:22
  97.7 7.9 %collective-permute-start.10 = (f32[32,768]{1,0:T(8,128)S(1)}, f32[32,768]{1,0:T(8,128)S(1)}, u32[]{:S(2)}, u32[]{:S(2)}) collective-permute-start(f32[32,768]{1,0:T(8,128)S(1)} %get-tuple-element.57), channel_id=1, source_target_pairs={{0,6},{1,7},{2,4},{3,5},{4,2},{5,3},{6,0},{7,1},{8,14},{9,15},{10,... | collective-permute-start | bytes 294920 | tf_op jit(solution)/shard_map/ppermute | solution.py:22
  99.2 9.3 %collective-permute-start.13 = (f32[32,768]{1,0:T(8,128)S(1)}, f32[32,768]{1,0:T(8,128)S(1)}, u32[]{:S(2)}, u32[]{:S(2)}) collective-permute-start(f32[32,768]{1,0:T(8,128)S(1)} %get-tuple-element.63), channel_id=1, source_target_pairs={{0,2},{1,3},{2,0},{3,1},{4,6},{5,7},{6,4},{7,5},{8,10},{9,11},{10,... | collective-permute-start | bytes 294920 | tf_op jit(solution)/shard_map/ppermute | solution.py:22
  99.8 9.3 %collective-permute-start.14 = (f32[32,768]{1,0:T(8,128)S(1)}, f32[32,768]{1,0:T(8,128)S(1)}, u32[]{:S(2)}, u32[]{:S(2)}) collective-permute-start(f32[32,768]{1,0:T(8,128)S(1)} %get-tuple-element.64), channel_id=1, source_target_pairs={{0,4},{1,5},{2,6},{3,7},{4,0},{5,1},{6,2},{7,3},{8,12},{9,13},{10,... | collective-permute-start | bytes 294920 | tf_op jit(solution)/shard_map/ppermute | solution.py:22
  101.3 9.4 %collective-permute-start.15 = (f32[32,768]{1,0:T(8,128)S(1)}, f32[32,768]{1,0:T(8,128)S(1)}, u32[]{:S(2)}, u32[]{:S(2)}) collective-permute-start(f32[32,768]{1,0:T(8,128)S(1)} %get-tuple-element.65), channel_id=1, source_target_pairs={{0,6},{1,7},{2,4},{3,5},{4,2},{5,3},{6,0},{7,1},{8,14},{9,15},{10,... | collective-permute-start | bytes 294920 | tf_op jit(solution)/shard_map/ppermute | solution.py:22
  104.1 9.9 %collective-permute-start.4 = (f32[16,768]{1,0:T(8,128)S(1)}, f32[16,768]{1,0:T(8,128)S(1)}, u32[]{:S(2)}, u32[]{:S(2)}) collective-permute-start(f32[16,768]{1,0:T(8,128)S(1)} %get-tuple-element.48), channel_id=1, source_target_pairs={{0,4},{1,5},{2,6},{3,7},{4,0},{5,1},{6,2},{7,3},{8,12},{9,13},{10,... | collective-permute-start | bytes 147464 | tf_op jit(solution)/shard_map/ppermute | solution.py:22
  105.7 8.3 %collective-permute-start.5 = (f32[16,768]{1,0:T(8,128)S(1)}, f32[16,768]{1,0:T(8,128)S(1)}, u32[]{:S(2)}, u32[]{:S(2)}) collective-permute-start(f32[16,768]{1,0:T(8,128)S(1)} %get-tuple-element.49), channel_id=1, source_target_pairs={{0,6},{1,7},{2,4},{3,5},{4,2},{5,3},{6,0},{7,1},{8,14},{9,15},{10,... | collective-permute-start | bytes 147464 | tf_op jit(solution)/shard_map/ppermute | solution.py:22
  108.5 6.1 %collective-permute-start.22 = (f32[16,768]{1,0:T(8,128)S(1)}, f32[16,768]{1,0:T(8,128)S(1)}, u32[]{:S(2)}, u32[]{:S(2)}) collective-permute-start(f32[16,768]{1,0:T(8,128)S(1)} %get-tuple-element.74), channel_id=1, source_target_pairs={{0,2},{1,3},{2,0},{3,1},{4,6},{5,7},{6,4},{7,5},{8,10},{9,11},{10,... | collective-permute-start | bytes 147464 | tf_op jit(solution)/shard_map/ppermute | solution.py:22
  109.2 5.4 %collective-permute-start.23 = (f32[16,768]{1,0:T(8,128)S(1)}, f32[16,768]{1,0:T(8,128)S(1)}, u32[]{:S(2)}, u32[]{:S(2)}) collective-permute-start(f32[16,768]{1,0:T(8,128)S(1)} %get-tuple-element.75), channel_id=1, source_target_pairs={{0,4},{1,5},{2,6},{3,7},{4,0},{5,1},{6,2},{7,3},{8,12},{9,13},{10,... | collective-permute-start | bytes 147464 | tf_op jit(solution)/shard_map/ppermute | solution.py:22
  110.7 5.0 %collective-permute-start.24 = (f32[16,768]{1,0:T(8,128)S(1)}, f32[16,768]{1,0:T(8,128)S(1)}, u32[]{:S(2)}, u32[]{:S(2)}) collective-permute-start(f32[16,768]{1,0:T(8,128)S(1)} %get-tuple-element.76), channel_id=1, source_target_pairs={{0,6},{1,7},{2,4},{3,5},{4,2},{5,3},{6,0},{7,1},{8,14},{9,15},{10,... | collective-permute-start | bytes 147464 | tf_op jit(solution)/shard_map/ppermute | solution.py:22

commit v4 on v3

--- a/solution.py
+++ b/solution.py
@@ -10,6 +10,7 @@
 
 PARTS = (2, 2, 1, 1)
 HEAD = 8
+LATE = 4
 
 
 def from_behind(value, axis, by):
@@ -73,24 +74,25 @@
     return (q // run) * share + start + q % run == source
 
 
-def picks_kernel(share, runs, skip, block, *outs):
+def picks_kernel(share, pieces, block, *outs):
     width = block.shape[1]
-    source = block[skip:, :]
-    for (start, run), out in zip(runs, outs):
+    for (low, high, start, run), out in zip(pieces, outs):
         order = picker(width, share, start, run).astype(jnp.float32).astype(jnp.bfloat16)
-        out[...] = jnp.dot(source, order, preferred_element_type=jnp.float32).astype(jnp.bfloat16)
-
-
-def picks(block, share, runs, skip):
-    rows, width = block.shape
+        out[...] = jnp.dot(
+            block[low:high, :], order, preferred_element_type=jnp.float32
+        ).astype(jnp.bfloat16)
+
+
+def picks(block, share, pieces):
+    width = block.shape[1]
     groups = width // share
     return pl.pallas_call(
-        functools.partial(picks_kernel, share, runs, skip),
+        functools.partial(picks_kernel, share, pieces),
         out_shape=[
-            pltpu.VMEM((rows - skip, groups * run), jnp.bfloat16) for _, run in runs
+            pltpu.VMEM((high - low, groups * run), jnp.bfloat16) for low, high, _, run in pieces
         ],
         in_specs=[pl.BlockSpec(memory_space=pltpu.VMEM)],
-        out_specs=[pl.BlockSpec(memory_space=pltpu.VMEM) for _ in runs],
+        out_specs=[pl.BlockSpec(memory_space=pltpu.VMEM) for _ in pieces],
         cost_estimate=pl.CostEstimate(
             flops=2 * block.size * width, bytes_accessed=4 * block.size, transcendentals=0
         ),
@@ -138,17 +140,45 @@
     )(onsets, block)
 
 
-def gram_kernel(share, run, pairs, own, head, rest, keep, give, part):
-    cut = head.shape[0]
-    columns = rest.shape[1]
+def product_of(own, ranges, refs):
+    return functools.reduce(
+        jnp.add,
+        (
+            jnp.dot(own[:, low:high], ref[...], preferred_element_type=jnp.float32)
+            for (low, high), ref in zip(ranges, refs)
+        ),
+    )
+
+
+def early_kernel(ranges, own, *refs):
+    *rows, out = refs
+    out[...] = product_of(own, ranges, rows)
+
+
+def early(own, ranges, blocks):
+    columns = blocks[0].shape[1]
+    return pl.pallas_call(
+        functools.partial(early_kernel, ranges),
+        out_shape=pltpu.VMEM((own.shape[0], columns), jnp.float32),
+        in_specs=[pl.BlockSpec(memory_space=pltpu.VMEM)] * (1 + len(blocks)),
+        out_specs=pl.BlockSpec(memory_space=pltpu.VMEM),
+        cost_estimate=pl.CostEstimate(
+            flops=2 * own.size * columns, bytes_accessed=2 * own.size, transcendentals=0
+        ),
+        compiler_params=pltpu.CompilerParams(vmem_limit_bytes=16 << 20),
+        name="early",
+    )(own, *blocks)
+
+
+def gram_kernel(share, run, ranges, pairs, own, *refs):
+    *rows, keep, give, part = refs
+    columns = rows[0].shape[1]
     groups = keep.shape[0] * 2
     bit = lax.rem(lax.axis_index("tm"), 2)
     owner_first = pairs[0, 0] == lax.axis_index("src")
-    product = jnp.dot(
-        own[:, cut:], rest[...], preferred_element_type=jnp.float32
-    ) + jnp.dot(
-        own[:, :cut], head[...], preferred_element_type=jnp.float32
-    )
+    product = product_of(own, ranges, rows)
+    if len(rows) > len(ranges):
+        product = product + rows[-1][...]
 
     @pl.when(owner_first)
     def _():
@@ -170,16 +200,16 @@
             give[pair] = jnp.where(bit == 0, uneven, even)
 
 
-def gram(pairs, own, head, rest, share, run):
+def gram(pairs, own, ranges, blocks, share, run):
     width = own.shape[0]
     groups = width // share
     half = pltpu.VMEM((groups // 2, run, width), jnp.float32)
     columns = groups * run
     return pl.pallas_call(
-        functools.partial(gram_kernel, share, run),
+        functools.partial(gram_kernel, share, run, ranges),
         out_shape=(half, half),
         in_specs=[pl.BlockSpec(memory_space=pltpu.SMEM)]
-        + [pl.BlockSpec(memory_space=pltpu.VMEM)] * 3,
+        + [pl.BlockSpec(memory_space=pltpu.VMEM)] * (1 + len(blocks)),
         out_specs=(pl.BlockSpec(memory_space=pltpu.VMEM),) * 2,
         scratch_shapes=[pltpu.VMEM((width, columns), jnp.float32)],
         cost_estimate=pl.CostEstimate(
@@ -187,14 +217,14 @@
         ),
         compiler_params=pltpu.CompilerParams(vmem_limit_bytes=16 << 20),
         name="gram",
-    )(pairs, own, head, rest)
-
-
-def gram_plain(flags, own, head, rest, share, run):
+    )(pairs, own, *blocks)
+
+
+def gram_plain(flags, own, blocks, share, run):
     width = own.shape[0]
     groups = width // share
     columns = groups * run
-    block = jnp.concatenate([head, rest], axis=0)
+    block = jnp.concatenate(blocks, axis=0)
     product = jnp.dot(own, block, preferred_element_type=jnp.float32)
     strips = jnp.where(
         flags[0] == 1,
@@ -399,20 +429,28 @@
     cut = rows_dev // HEAD
 
     head = from_behind(top_of(greens, cut), "src", 1)
-    chosen = picks(greens, share, runs, cut)
+    late = rows_dev - rows_dev // LATE
+    pieces = [(cut, rows_dev, *run) for run in runs[:-1]]
+    pieces += [(cut, late, *runs[-1]), (late, rows_dev, *runs[-1])]
+    chosen = picks(greens, share, pieces)
     lower = []
     for block in chosen:
         lower.append(from_behind(block, "src", 1))
     own, squares = turn(onsets, greens)
     norm_own = summed(squares, "tm")
     norm_low = from_behind(norm_own, "src", 1)
-    heads = picks(head, share, runs, 0)
+    heads = picks(head, share, [(0, cut, *run) for run in runs])
     if not aligned:
         return plain_tail(pairs, own, heads, lower, norm_own[0], norm_low[0], share, runs)
 
     base = None
-    for step, (run, top, block) in enumerate(zip(runs, heads, lower)):
-        keep, give = gram(pairs, own, top, block, share, run[1])
+    for step, (run, top) in enumerate(zip(runs, heads)):
+        if step < len(runs) - 1:
+            ranges, blocks = [(0, cut), (cut, rows_dev)], [top, lower[step]]
+        else:
+            so_far = early(own, [(0, cut), (cut, late)], [top, lower[-2]])
+            ranges, blocks = [(late, rows_dev)], [lower[-1], so_far]
+        keep, give = gram(pairs, own, ranges, blocks, share, run[1])
         arrived = swapped(give, "tm", 1)
         mine, *gives = fold(keep, arrived)
         terms = [mine]
@@ -429,8 +467,9 @@
     owner_first = pairs[0, 0] == lax.axis_index("src")
     flags = jnp.stack([owner_first.astype(jnp.int32), row_group % 2])
     parts = []
-    for run, top, block in zip(runs, heads, lower):
-        keep, give = gram_plain(flags, own, top, block, share, run[1])
+    rests = [[block] for block in lower[:-2]] + [lower[-2:]]
+    for run, top, rest in zip(runs, heads, rests):
+        keep, give = gram_plain(flags, own, [top, *rest], share, run[1])
         parts.append(functools.reduce(jnp.add, strips_arrived(keep, give, "tm")))
     scale_own = lax.rsqrt(norm_own + 1e-06)
     scale_low = lax.rsqrt(norm_low + 1e-06)

time: 117 us -> 118 us (level)
  local copies, waits for them, and re-layouts: 1.91 us -> 3.28 us
    unnamed x10 -> x14, local copies, waits for them, and re-layouts: 1.91 us -> 3.28 us
    ppermute x6 -> x7, waiting for transfers between devices: 59.4 us -> 58.6 us  [from_behind(): lax.ppermute(value, axis, [(i, (i + by) % length) for i in range(length)])]
    pallas_call x6 -> x7, Pallas kernels: 11.9 us -> 12 us  [the longest x4 7.64 us: gram(): pl.pallas_call(functools.partial(gram_kernel, share, run, ranges), out_sh...]
    ppermute x6 -> x7, starting transfers between devices: 8.06 us -> 8.01 us  [from_behind(): lax.ppermute(value, axis, [(i, (i + by) % length) for i in range(length)])]
  transfers between devices with their start and end apart: 25 -> 26, of which waited for: 9 -> 10; matrix products, arithmetic and copies ran while one was open for 0% -> 0% of each run, Pallas kernels for 13% -> 13%
where the time goes in v4:
time: 118 us
  waiting for transfers between devices  66.4 us (56%)
  starting transfers between devices  28.5 us (24%)
  Pallas kernels  19.4 us (16%)
  local copies, waits for them, and re-layouts  3.28 us (3%)
    ppermute x7, waiting for transfers between devices, from_behind(): lax.ppermute(value, axis, [(i, (i + by) % length) for i in range(length)])  58.6 us
    ppermute x19, starting transfers between devices, swapped(): return lax.ppermute(value, axis, [(i, i ^ bits) for i in range(length)])  20.5 us
    ppermute x7, starting transfers between devices, from_behind(): lax.ppermute(value, axis, [(i, (i + by) % length) for i in range(length)])  8.01 us
    ppermute x19, waiting for transfers between devices, swapped(): return lax.ppermute(value, axis, [(i, i ^ bits) for i in range(length)])  7.76 us
    pallas_call x4, Pallas kernels, gram(): pl.pallas_call(functools.partial(gram_kernel, share, run, ranges), out_sh...  7.64 us
    pallas_call x5, Pallas kernels, small_call(): pl.pallas_call(kernel, out_shape=out_shape, in_specs=[pl.BlockSpec(memory...  3.82 us
    pallas_call x2, Pallas kernels, picks(): pl.pallas_call(functools.partial(picks_kernel, share, pieces), out_shape=...  3.64 us
    unnamed x14, local copies, waits for them, and re-layouts  3.28 us
  transfers between devices with their start and end apart: 26, of which 10 were waited for; matrix products, arithmetic and copies ran while one was open for 0% of the time, Pallas kernels for 13%

profile of v4, /device:TPU:0, one launch (start us, length us, event | category | flops | bytes accessed | tf_op | source)
XLA Modules:
  0.0 117.8 jit_solution(4143294375830411548)
XLA Ops:
  0.0 1.9 %copy-done = bf16[2048,768]{1,0:T(8,128)(2,1)S(1)} copy-done((bf16[2048,768]{1,0:T(8,128)(2,1)S(1)}, bf16[2048,768]{1,0:T(8,128)(2,1)}, u32[]{:S(2)}) %copy-start) | copy-done | bytes 3145752
  1.9 3.1 %picks.3 = (bf16[1792,256]{1,0:T(8,128)(2,1)}, bf16[1792,256]{1,0:T(8,128)(2,1)}, bf16[1792,128]{1,0:T(8,128)(2,1)S(1)}, bf16[1280,128]{1,0:T(8,128)(2,1)S(1)}, bf16[512,128]{1,0:T(8,128)(2,1)S(1)}) custom-call(bf16[2048,768]{1,0:T(8,128)(2,1)S(1)} %copy-done), custom_call_target="tpu_custom_call" | custom-call | flops 2415919104 | bytes 6291456 | tf_op jit(solution)/shard_map/picks/pallas_call | solution.py:89
  5.0 0.7 copy-done.4
  5.7 0.7 copy-done.5
  6.3 3.1 %collective-permute-start.6 = (bf16[1792,256]{1,0:T(8,128)(2,1)}, bf16[1792,256]{1,0:T(8,128)(2,1)}, u32[]{:S(2)}, u32[]{:S(2)}) collective-permute-start(bf16[1792,256]{1,0:T(8,128)(2,1)} %get-tuple-element.52), channel_id=1, source_target_pairs={{0,8},{8,16},{16,24},{24,0},{1,9},{9,17},{17,25},{25,1},{2,10},{10... | collective-permute-start | bytes 2752520 | tf_op jit(solution)/shard_map/ppermute | solution.py:18
  9.4 1.6 %collective-permute-start.11 = (bf16[1792,256]{1,0:T(8,128)(2,1)}, bf16[1792,256]{1,0:T(8,128)(2,1)}, u32[]{:S(2)}, u32[]{:S(2)}) collective-permute-start(bf16[1792,256]{1,0:T(8,128)(2,1)} %get-tuple-element.60), channel_id=1, source_target_pairs={{0,8},{8,16},{16,24},{24,0},{1,9},{9,17},{17,25},{25,1},{2,10},{10... | collective-permute-start | bytes 2752520 | tf_op jit(solution)/shard_map/ppermute | solution.py:18
  11.0 1.0 top.1
  12.0 1.6 %collective-permute-start = (bf16[256,768]{1,0:T(8,128)(2,1)S(1)}, bf16[256,768]{1,0:T(8,128)(2,1)S(1)}, u32[]{:S(2)}, u32[]{:S(2)}) collective-permute-start(bf16[256,768]{1,0:T(8,128)(2,1)S(1)} %top.1), channel_id=1, source_target_pairs={{0,8},{8,16},{16,24},{24,0},{1,9},{9,17},{17,25},{25,1},{2,10},{10... | collective-permute-start | bytes 1179656 | tf_op jit(solution)/shard_map/ppermute | solution.py:18
  13.5 0.1 collective-permute-start.1
  13.6 1.7 %collective-permute-start.21 = (bf16[1280,128]{1,0:T(8,128)(2,1)}, bf16[1280,128]{1,0:T(8,128)(2,1)S(1)}, u32[]{:S(2)}, u32[]{:S(2)}) collective-permute-start(bf16[1280,128]{1,0:T(8,128)(2,1)} %copy-done.4), channel_id=1, source_target_pairs={{0,8},{8,16},{16,24},{24,0},{1,9},{9,17},{17,25},{25,1},{2,10},{10... | collective-permute-start | bytes 983048 | tf_op jit(solution)/shard_map/ppermute | solution.py:18
  15.4 2.4 %turn.1 = (bf16[768,2048]{1,0:T(8,128)(2,1)S(1)}, f32[1,768]{1,0:T(1,128)S(1)}) custom-call(s32[4]{0:T(128)S(1)} %copy-done.3, bf16[2048,768]{1,0:T(8,128)(2,1)S(1)} %copy-done.1), custom_call_target="tpu_custom_call" | custom-call | flops 6291456 | bytes 6291456 | tf_op jit(solution)/shard_map/turn/pallas_call | solution.py:127
  17.8 43.1 %collective-permute-done.block = bf16[256,768]{1,0:T(8,128)(2,1)S(1)} collective-permute-done((bf16[256,768]{1,0:T(8,128)(2,1)S(1)}, bf16[256,768]{1,0:T(8,128)(2,1)S(1)}, u32[]{:S(2)}, u32[]{:S(2)}) %collective-permute-start) | collective-permute-done | bytes 393248 | tf_op jit(solution)/shard_map/ppermute | solution.py:18
  60.9 0.6 picks.2
  61.5 0.0 collective-permute-done.6.refs_1_
  61.5 2.4 %gram.5 = (f32[4,32,768]{2,1,0:T(8,128)S(1)}, f32[4,32,768]{2,1,0:T(8,128)S(1)}) custom-call(s32[1,2]{1,0:T(1,128)S(1)} %copy-done.2, bf16[768,2048]{1,0:T(8,128)(2,1)S(1)} %get-tuple-element.42.own, bf16[256,256]{1,0:T(8,128)(2,1)S(1)} %get-tuple-element.51.refs_0_, bf16[1792,256]{1,0:T(8,128)(2,1)} %collective-permute-done.6.refs_1_), custom_call_target="tpu_custom_call" | custom-call | flops 805306368 | bytes 3145728 | tf_op jit(solution)/shard_map/gram/pallas_call | solution.py:208
  64.0 0.0 copy-start.6
  64.0 0.1 collective-permute-start.7
  64.1 0.0 collective-permute-done.11.refs_1_
  64.1 2.4 %gram.6 = (f32[4,32,768]{2,1,0:T(8,128)S(1)}, f32[4,32,768]{2,1,0:T(8,128)S(1)}) custom-call(s32[1,2]{1,0:T(1,128)S(1)} %copy-done.2, bf16[768,2048]{1,0:T(8,128)(2,1)S(1)} %get-tuple-element.42.own, bf16[256,256]{1,0:T(8,128)(2,1)S(1)} %get-tuple-element.59.refs_0_, bf16[1792,256]{1,0:T(8,128)(2,1)} %collective-permute-done.11.refs_1_), custom_call_target="tpu_custom_call" | custom-call | flops 805306368 | bytes 3145728 | tf_op jit(solution)/shard_map/gram/pallas_call | solution.py:208
  66.5 0.5 collective-permute-start.12
  67.1 3.7 %collective-permute-done.1.refs_1_ = bf16[1792,128]{1,0:T(8,128)(2,1)S(1)} collective-permute-done((bf16[1792,128]{1,0:T(8,128)(2,1)S(1)}, bf16[1792,128]{1,0:T(8,128)(2,1)S(1)}, u32[]{:S(2)}, u32[]{:S(2)}) %collective-permute-start.1) | collective-permute-done | bytes 458784 | tf_op jit(solution)/shard_map/ppermute | solution.py:18
  70.8 1.7 %gram.4 = (f32[4,16,768]{2,1,0:T(8,128)S(1)}, f32[4,16,768]{2,1,0:T(8,128)S(1)}) custom-call(s32[1,2]{1,0:T(1,128)S(1)} %copy-done.2, bf16[768,2048]{1,0:T(8,128)(2,1)S(1)} %get-tuple-element.42.own, bf16[256,128]{1,0:T(8,128)(2,1)S(1)} %get-tuple-element.43.refs_0_, bf16[1792,128]{1,0:T(8,128)(2,1)S(1)} %collective-permute-done.1.refs_1_), custom_call_target="tpu_custom_call" | custom-call | flops 402653184 | bytes 3145728 | tf_op jit(solution)/shard_map/gram/pallas_call | solution.py:208
  72.4 0.1 collective-permute-start.2
  72.5 5.3 %collective-permute-done.21.refs_1_ = bf16[1280,128]{1,0:T(8,128)(2,1)S(1)} collective-permute-done((bf16[1280,128]{1,0:T(8,128)(2,1)}, bf16[1280,128]{1,0:T(8,128)(2,1)S(1)}, u32[]{:S(2)}, u32[]{:S(2)}) %collective-permute-start.21) | collective-permute-done | bytes 327712 | tf_op jit(solution)/shard_map/ppermute | solution.py:18
  77.8 0.8 early.1.refs_1_
  78.6 1.2 %collective-permute-done.20.refs_0_ = bf16[512,128]{1,0:T(8,128)(2,1)S(1)} collective-permute-done((bf16[512,128]{1,0:T(8,128)(2,1)S(1)}, bf16[512,128]{1,0:T(8,128)(2,1)S(1)}, u32[]{:S(2)}, u32[]{:S(2)}) %collective-permute-start.20) | collective-permute-done | bytes 131104 | tf_op jit(solution)/shard_map/ppermute | solution.py:18
  79.7 1.1 gram.7
  80.8 0.1 collective-permute-start.22
  80.9 0.1 fold.5
  81.0 1.5 %collective-permute-start.8 = (f32[32,768]{1,0:T(8,128)S(1)}, f32[32,768]{1,0:T(8,128)S(1)}, u32[]{:S(2)}, u32[]{:S(2)}) collective-permute-start(f32[32,768]{1,0:T(8,128)S(1)} %get-tuple-element.56), channel_id=1, source_target_pairs={{0,2},{1,3},{2,0},{3,1},{4,6},{5,7},{6,4},{7,5},{8,10},{9,11},{10,... | collective-permute-start | bytes 294920 | tf_op jit(solution)/shard_map/ppermute | solution.py:23
  82.5 0.0 collective-permute-done.2.arrived
  82.5 0.6 collective-permute-start.3
  83.2 0.0 collective-permute-start.16
  83.2 1.2 collective-permute-done.16.b
  84.3 1.5 %collective-permute-start.17 = (f32[1,768]{1,0:T(1,128)S(1)}, f32[1,768]{1,0:T(1,128)S(1)}, u32[]{:S(2)}, u32[]{:S(2)}) collective-permute-start(f32[1,768]{1,0:T(1,128)S(1)} %plus.3.a), channel_id=1, source_target_pairs={{0,2},{1,3},{2,0},{3,1},{4,6},{5,7},{6,4},{7,5},{8,10},{9,11},{10,... | collective-permute-start | bytes 9224 | tf_op jit(solution)/shard_map/ppermute | solution.py:23
  85.8 2.1 %collective-permute-done.17.b = f32[1,768]{1,0:T(1,128)S(1)} collective-permute-done((f32[1,768]{1,0:T(1,128)S(1)}, f32[1,768]{1,0:T(1,128)S(1)}, u32[]{:S(2)}, u32[]{:S(2)}) %collective-permute-start.17) | collective-permute-done | bytes 3104 | tf_op jit(solution)/shard_map/ppermute | solution.py:23
  87.9 1.5 %collective-permute-start.18 = (f32[1,768]{1,0:T(1,128)S(1)}, f32[1,768]{1,0:T(1,128)S(1)}, u32[]{:S(2)}, u32[]{:S(2)}) collective-permute-start(f32[1,768]{1,0:T(1,128)S(1)} %plus.4.a), channel_id=1, source_target_pairs={{0,4},{1,5},{2,6},{3,7},{4,0},{5,1},{6,2},{7,3},{8,12},{9,13},{10,... | collective-permute-start | bytes 9224 | tf_op jit(solution)/shard_map/ppermute | solution.py:23
  89.4 2.1 %collective-permute-done.18.b = f32[1,768]{1,0:T(1,128)S(1)} collective-permute-done((f32[1,768]{1,0:T(1,128)S(1)}, f32[1,768]{1,0:T(1,128)S(1)}, u32[]{:S(2)}, u32[]{:S(2)}) %collective-permute-start.18) | collective-permute-done | bytes 3104 | tf_op jit(solution)/shard_map/ppermute | solution.py:23
  91.5 5.4 %collective-permute-done.19.norm_low = f32[1,768]{1,0:T(1,128)S(1)} collective-permute-done((f32[1,768]{1,0:T(1,128)S(1)}, f32[1,768]{1,0:T(1,128)S(1)}, u32[]{:S(2)}, u32[]{:S(2)}) %collective-permute-start.19) | collective-permute-done | bytes 3104 | tf_op jit(solution)/shard_map/ppermute | solution.py:18
  96.9 1.5 %collective-permute-start.9 = (f32[32,768]{1,0:T(8,128)S(1)}, f32[32,768]{1,0:T(8,128)S(1)}, u32[]{:S(2)}, u32[]{:S(2)}) collective-permute-start(f32[32,768]{1,0:T(8,128)S(1)} %get-tuple-element.57), channel_id=1, source_target_pairs={{0,4},{1,5},{2,6},{3,7},{4,0},{5,1},{6,2},{7,3},{8,12},{9,13},{10,... | collective-permute-start | bytes 294920 | tf_op jit(solution)/shard_map/ppermute | solution.py:23
  98.4 1.4 %collective-permute-start.10 = (f32[32,768]{1,0:T(8,128)S(1)}, f32[32,768]{1,0:T(8,128)S(1)}, u32[]{:S(2)}, u32[]{:S(2)}) collective-permute-start(f32[32,768]{1,0:T(8,128)S(1)} %get-tuple-element.58), channel_id=1, source_target_pairs={{0,6},{1,7},{2,4},{3,5},{4,2},{5,3},{6,0},{7,1},{8,14},{9,15},{10,... | collective-permute-start | bytes 294920 | tf_op jit(solution)/shard_map/ppermute | solution.py:23
  99.9 0.0 collective-permute-done.22.arrived
  99.9 0.6 collective-permute-start.13
  100.5 1.5 %collective-permute-start.14 = (f32[32,768]{1,0:T(8,128)S(1)}, f32[32,768]{1,0:T(8,128)S(1)}, u32[]{:S(2)}, u32[]{:S(2)}) collective-permute-start(f32[32,768]{1,0:T(8,128)S(1)} %get-tuple-element.65), channel_id=1, source_target_pairs={{0,4},{1,5},{2,6},{3,7},{4,0},{5,1},{6,2},{7,3},{8,12},{9,13},{10,... | collective-permute-start | bytes 294920 | tf_op jit(solution)/shard_map/ppermute | solution.py:23
  102.1 0.0 collective-permute-done.8.refs_1_
  102.1 1.4 %collective-permute-start.15 = (f32[32,768]{1,0:T(8,128)S(1)}, f32[32,768]{1,0:T(8,128)S(1)}, u32[]{:S(2)}, u32[]{:S(2)}) collective-permute-start(f32[32,768]{1,0:T(8,128)S(1)} %get-tuple-element.66), channel_id=1, source_target_pairs={{0,6},{1,7},{2,4},{3,5},{4,2},{5,3},{6,0},{7,1},{8,14},{9,15},{10,... | collective-permute-start | bytes 294920 | tf_op jit(solution)/shard_map/ppermute | solution.py:23
  103.5 1.3 %collective-permute-done.9.refs_2_ = f32[32,768]{1,0:T(8,128)S(1)} collective-permute-done((f32[32,768]{1,0:T(8,128)S(1)}, f32[32,768]{1,0:T(8,128)S(1)}, u32[]{:S(2)}, u32[]{:S(2)}) %collective-permute-start.9) | collective-permute-done | bytes 98336 | tf_op jit(solution)/shard_map/ppermute | solution.py:23
  104.8 1.6 %collective-permute-start.4 = (f32[16,768]{1,0:T(8,128)S(1)}, f32[16,768]{1,0:T(8,128)S(1)}, u32[]{:S(2)}, u32[]{:S(2)}) collective-permute-start(f32[16,768]{1,0:T(8,128)S(1)} %get-tuple-element.49), channel_id=1, source_target_pairs={{0,4},{1,5},{2,6},{3,7},{4,0},{5,1},{6,2},{7,3},{8,12},{9,13},{10,... | collective-permute-start | bytes 147464 | tf_op jit(solution)/shard_map/ppermute | solution.py:23
  106.4 0.0 collective-permute-done.10.refs_3_
  106.4 2.8 %collective-permute-start.5 = (f32[16,768]{1,0:T(8,128)S(1)}, f32[16,768]{1,0:T(8,128)S(1)}, u32[]{:S(2)}, u32[]{:S(2)}) collective-permute-start(f32[16,768]{1,0:T(8,128)S(1)} %get-tuple-element.50), channel_id=1, source_target_pairs={{0,6},{1,7},{2,4},{3,5},{4,2},{5,3},{6,0},{7,1},{8,14},{9,15},{10,... | collective-permute-start | bytes 147464 | tf_op jit(solution)/shard_map/ppermute | solution.py:23
  109.2 0.0 collective-permute-done.13.refs_1_
  109.2 0.6 collective-permute-start.23
  109.9 0.0 collective-permute-done.14.refs_2_
  109.9 1.5 %collective-permute-start.24 = (f32[16,768]{1,0:T(8,128)S(1)}, f32[16,768]{1,0:T(8,128)S(1)}, u32[]{:S(2)}, u32[]{:S(2)}) collective-permute-start(f32[16,768]{1,0:T(8,128)S(1)} %get-tuple-element.77), channel_id=1, source_target_pairs={{0,4},{1,5},{2,6},{3,7},{4,0},{5,1},{6,2},{7,3},{8,12},{9,13},{10,... | collective-permute-start | bytes 147464 | tf_op jit(solution)/shard_map/ppermute | solution.py:23
  111.4 0.0 collective-permute-done.15.refs_3_
  111.4 1.4 %collective-permute-start.25 = (f32[16,768]{1,0:T(8,128)S(1)}, f32[16,768]{1,0:T(8,128)S(1)}, u32[]{:S(2)}, u32[]{:S(2)}) collective-permute-start(f32[16,768]{1,0:T(8,128)S(1)} %get-tuple-element.78), channel_id=1, source_target_pairs={{0,6},{1,7},{2,4},{3,5},{4,2},{5,3},{6,0},{7,1},{8,14},{9,15},{10,... | collective-permute-start | bytes 147464 | tf_op jit(solution)/shard_map/ppermute | solution.py:23
  112.9 0.7 shard_map.40
  113.5 0.6 shard_map.37.refs_4_
  114.1 0.6 shard_map.38.refs_4_
  114.7 0.0 collective-permute-done.4.refs_2_
  114.7 0.6 shard_map.39.base
  115.3 0.0 collective-permute-done.24.refs_2_
  115.3 1.1 collective-permute-done.25.refs_3_
  116.4 1.4 %shard_map.41 = f32[1,96,768]{2,1,0:T(8,128)} custom-call(s32[1,2]{1,0:T(1,128)S(1)} %copy-done.2, f32[96,768]{1,0:T(8,128)S(1)} %shard_map.39.base, f32[96,128]{1,0:T(8,128)S(1)} %get-tuple-element.68.rows, f32[1,768]{1,0:T(1,128)S(1)} %get-tuple-element.69.columns, f32[16,768]{1,0:T(8,128)S(1)} %get-tuple-element.75.refs_0_, ...), custom_call_target="tpu_custom_call" | custom-call | flops 37748736 | bytes 543744 | tf_op jit(solution)/shard_map/pallas_call | solution.py:362
  (23 shorter events, 0.1 us)
Async XLA Ops:
  0.0 1.9 %copy-start = (bf16[2048,768]{1,0:T(8,128)(2,1)S(1)}, bf16[2048,768]{1,0:T(8,128)(2,1)}, u32[]{:S(2)}) copy-start(bf16[2048,768]{1,0:T(8,128)(2,1)} %block.5) | copy-start | bytes 9437188
  5.0 0.7 copy-start.4
  5.7 0.7 copy-start.5
  6.3 9.0 %copy-start.1 = (bf16[2048,768]{1,0:T(8,128)(2,1)S(1)}, bf16[2048,768]{1,0:T(8,128)(2,1)}, u32[]{:S(2)}) copy-start(bf16[2048,768]{1,0:T(8,128)(2,1)} %block.5) | copy-start | bytes 9437188
  6.3 9.0 %copy-start.3 = (s32[4]{0:T(128)S(1)}, s32[4]{0:T(128)}, u32[]{:S(2)}) copy-start(s32[4]{0:T(128)} %onsets.1) | copy-start | bytes 52
  6.3 55.2 %collective-permute-start.6 = (bf16[1792,256]{1,0:T(8,128)(2,1)}, bf16[1792,256]{1,0:T(8,128)(2,1)}, u32[]{:S(2)}, u32[]{:S(2)}) collective-permute-start(bf16[1792,256]{1,0:T(8,128)(2,1)} %get-tuple-element.52), channel_id=1, source_target_pairs={{0,8},{8,16},{16,24},{24,0},{1,9},{9,17},{17,25},{25,1},{2,10},{10... | collective-permute-start | bytes 2752520 | tf_op jit(solution)/shard_map/ppermute | solution.py:18
  9.4 52.1 %copy-start.2 = (s32[1,2]{1,0:T(1,128)S(1)}, s32[1,2]{1,0:T(1,128)}, u32[]{:S(2)}) copy-start(s32[1,2]{1,0:T(1,128)} %pairs.17) | copy-start | bytes 28
  9.4 54.7 %collective-permute-start.11 = (bf16[1792,256]{1,0:T(8,128)(2,1)}, bf16[1792,256]{1,0:T(8,128)(2,1)}, u32[]{:S(2)}, u32[]{:S(2)}) collective-permute-start(bf16[1792,256]{1,0:T(8,128)(2,1)} %get-tuple-element.60), channel_id=1, source_target_pairs={{0,8},{8,16},{16,24},{24,0},{1,9},{9,17},{17,25},{25,1},{2,10},{10... | collective-permute-start | bytes 2752520 | tf_op jit(solution)/shard_map/ppermute | solution.py:18
  12.0 48.9 %collective-permute-start = (bf16[256,768]{1,0:T(8,128)(2,1)S(1)}, bf16[256,768]{1,0:T(8,128)(2,1)S(1)}, u32[]{:S(2)}, u32[]{:S(2)}) collective-permute-start(bf16[256,768]{1,0:T(8,128)(2,1)S(1)} %top.1), channel_id=1, source_target_pairs={{0,8},{8,16},{16,24},{24,0},{1,9},{9,17},{17,25},{25,1},{2,10},{10... | collective-permute-start | bytes 1179656 | tf_op jit(solution)/shard_map/ppermute | solution.py:18
  13.5 57.2 %collective-permute-start.1 = (bf16[1792,128]{1,0:T(8,128)(2,1)S(1)}, bf16[1792,128]{1,0:T(8,128)(2,1)S(1)}, u32[]{:S(2)}, u32[]{:S(2)}) collective-permute-start(bf16[1792,128]{1,0:T(8,128)(2,1)S(1)} %get-tuple-element.44), channel_id=1, source_target_pairs={{0,8},{8,16},{16,24},{24,0},{1,9},{9,17},{17,25},{25,1},{2,10},{10... | collective-permute-start | bytes 1376264 | tf_op jit(solution)/shard_map/ppermute | solution.py:18
  13.6 64.2 %collective-permute-start.21 = (bf16[1280,128]{1,0:T(8,128)(2,1)}, bf16[1280,128]{1,0:T(8,128)(2,1)S(1)}, u32[]{:S(2)}, u32[]{:S(2)}) collective-permute-start(bf16[1280,128]{1,0:T(8,128)(2,1)} %copy-done.4), channel_id=1, source_target_pairs={{0,8},{8,16},{16,24},{24,0},{1,9},{9,17},{17,25},{25,1},{2,10},{10... | collective-permute-start | bytes 983048 | tf_op jit(solution)/shard_map/ppermute | solution.py:18
  64.0 3.1 %copy-start.6 = (bf16[512,128]{1,0:T(8,128)(2,1)S(1)}, bf16[512,128]{1,0:T(8,128)(2,1)}, u32[]{:S(2)}) copy-start(bf16[512,128]{1,0:T(8,128)(2,1)} %copy-done.5) | copy-start | bytes 393220
  64.0 16.9 %collective-permute-start.7 = (f32[4,32,768]{2,1,0:T(8,128)S(1)}, f32[4,32,768]{2,1,0:T(8,128)S(1)}, u32[]{:S(2)}, u32[]{:S(2)}) collective-permute-start(f32[4,32,768]{2,1,0:T(8,128)S(1)} %get-tuple-element.54), channel_id=1, source_target_pairs={{0,1},{1,0},{2,3},{3,2},{4,5},{5,4},{6,7},{7,6},{8,9},{9,8},{10,11... | collective-permute-start | bytes 1179656 | tf_op jit(solution)/shard_map/ppermute | solution.py:23
  66.5 31.9 %collective-permute-start.12 = (f32[4,32,768]{2,1,0:T(8,128)S(1)}, f32[4,32,768]{2,1,0:T(8,128)S(1)}, u32[]{:S(2)}, u32[]{:S(2)}) collective-permute-start(f32[4,32,768]{2,1,0:T(8,128)S(1)} %get-tuple-element.62), channel_id=1, source_target_pairs={{0,1},{1,0},{2,3},{3,2},{4,5},{5,4},{6,7},{7,6},{8,9},{9,8},{10,11... | collective-permute-start | bytes 1179656 | tf_op jit(solution)/shard_map/ppermute | solution.py:23
  67.1 12.6 %collective-permute-start.20 = (bf16[512,128]{1,0:T(8,128)(2,1)S(1)}, bf16[512,128]{1,0:T(8,128)(2,1)S(1)}, u32[]{:S(2)}, u32[]{:S(2)}) collective-permute-start(bf16[512,128]{1,0:T(8,128)(2,1)S(1)} %copy-done.6), channel_id=1, source_target_pairs={{0,8},{8,16},{16,24},{24,0},{1,9},{9,17},{17,25},{25,1},{2,10},{10... | collective-permute-start | bytes 393224 | tf_op jit(solution)/shard_map/ppermute | solution.py:18
  72.4 10.1 %collective-permute-start.2 = (f32[4,16,768]{2,1,0:T(8,128)S(1)}, f32[4,16,768]{2,1,0:T(8,128)S(1)}, u32[]{:S(2)}, u32[]{:S(2)}) collective-permute-start(f32[4,16,768]{2,1,0:T(8,128)S(1)} %get-tuple-element.46), channel_id=1, source_target_pairs={{0,1},{1,0},{2,3},{3,2},{4,5},{5,4},{6,7},{7,6},{8,9},{9,8},{10,11... | collective-permute-start | bytes 589832 | tf_op jit(solution)/shard_map/ppermute | solution.py:23
  80.8 19.1 %collective-permute-start.22 = (f32[4,16,768]{2,1,0:T(8,128)S(1)}, f32[4,16,768]{2,1,0:T(8,128)S(1)}, u32[]{:S(2)}, u32[]{:S(2)}) collective-permute-start(f32[4,16,768]{2,1,0:T(8,128)S(1)} %get-tuple-element.74), channel_id=1, source_target_pairs={{0,1},{1,0},{2,3},{3,2},{4,5},{5,4},{6,7},{7,6},{8,9},{9,8},{10,11... | collective-permute-start | bytes 589832 | tf_op jit(solution)/shard_map/ppermute | solution.py:23
  81.0 21.1 %collective-permute-start.8 = (f32[32,768]{1,0:T(8,128)S(1)}, f32[32,768]{1,0:T(8,128)S(1)}, u32[]{:S(2)}, u32[]{:S(2)}) collective-permute-start(f32[32,768]{1,0:T(8,128)S(1)} %get-tuple-element.56), channel_id=1, source_target_pairs={{0,2},{1,3},{2,0},{3,1},{4,6},{5,7},{6,4},{7,5},{8,10},{9,11},{10,... | collective-permute-start | bytes 294920 | tf_op jit(solution)/shard_map/ppermute | solution.py:23
  82.5 18.0 %collective-permute-start.3 = (f32[16,768]{1,0:T(8,128)S(1)}, f32[16,768]{1,0:T(8,128)S(1)}, u32[]{:S(2)}, u32[]{:S(2)}) collective-permute-start(f32[16,768]{1,0:T(8,128)S(1)} %get-tuple-element.48), channel_id=1, source_target_pairs={{0,2},{1,3},{2,0},{3,1},{4,6},{5,7},{6,4},{7,5},{8,10},{9,11},{10,... | collective-permute-start | bytes 147464 | tf_op jit(solution)/shard_map/ppermute | solution.py:23
  83.2 1.2 collective-permute-start.16
  84.3 3.6 %collective-permute-start.17 = (f32[1,768]{1,0:T(1,128)S(1)}, f32[1,768]{1,0:T(1,128)S(1)}, u32[]{:S(2)}, u32[]{:S(2)}) collective-permute-start(f32[1,768]{1,0:T(1,128)S(1)} %plus.3.a), channel_id=1, source_target_pairs={{0,2},{1,3},{2,0},{3,1},{4,6},{5,7},{6,4},{7,5},{8,10},{9,11},{10,... | collective-permute-start | bytes 9224 | tf_op jit(solution)/shard_map/ppermute | solution.py:23
  87.9 3.6 %collective-permute-start.18 = (f32[1,768]{1,0:T(1,128)S(1)}, f32[1,768]{1,0:T(1,128)S(1)}, u32[]{:S(2)}, u32[]{:S(2)}) collective-permute-start(f32[1,768]{1,0:T(1,128)S(1)} %plus.4.a), channel_id=1, source_target_pairs={{0,4},{1,5},{2,6},{3,7},{4,0},{5,1},{6,2},{7,3},{8,12},{9,13},{10,... | collective-permute-start | bytes 9224 | tf_op jit(solution)/shard_map/ppermute | solution.py:23
  91.5 5.4 %collective-permute-start.19 = (f32[1,768]{1,0:T(1,128)S(1)}, f32[1,768]{1,0:T(1,128)S(1)}, u32[]{:S(2)}, u32[]{:S(2)}) collective-permute-start(f32[1,768]{1,0:T(1,128)S(1)} %plus.5.norm_own), channel_id=1, source_target_pairs={{0,8},{8,16},{16,24},{24,0},{1,9},{9,17},{17,25},{25,1},{2,10},{10... | collective-permute-start | bytes 9224 | tf_op jit(solution)/shard_map/ppermute | solution.py:18
  96.9 7.8 %collective-permute-start.9 = (f32[32,768]{1,0:T(8,128)S(1)}, f32[32,768]{1,0:T(8,128)S(1)}, u32[]{:S(2)}, u32[]{:S(2)}) collective-permute-start(f32[32,768]{1,0:T(8,128)S(1)} %get-tuple-element.57), channel_id=1, source_target_pairs={{0,4},{1,5},{2,6},{3,7},{4,0},{5,1},{6,2},{7,3},{8,12},{9,13},{10,... | collective-permute-start | bytes 294920 | tf_op jit(solution)/shard_map/ppermute | solution.py:23
  98.4 7.9 %collective-permute-start.10 = (f32[32,768]{1,0:T(8,128)S(1)}, f32[32,768]{1,0:T(8,128)S(1)}, u32[]{:S(2)}, u32[]{:S(2)}) collective-permute-start(f32[32,768]{1,0:T(8,128)S(1)} %get-tuple-element.58), channel_id=1, source_target_pairs={{0,6},{1,7},{2,4},{3,5},{4,2},{5,3},{6,0},{7,1},{8,14},{9,15},{10,... | collective-permute-start | bytes 294920 | tf_op jit(solution)/shard_map/ppermute | solution.py:23
  99.9 9.3 %collective-permute-start.13 = (f32[32,768]{1,0:T(8,128)S(1)}, f32[32,768]{1,0:T(8,128)S(1)}, u32[]{:S(2)}, u32[]{:S(2)}) collective-permute-start(f32[32,768]{1,0:T(8,128)S(1)} %get-tuple-element.64), channel_id=1, source_target_pairs={{0,2},{1,3},{2,0},{3,1},{4,6},{5,7},{6,4},{7,5},{8,10},{9,11},{10,... | collective-permute-start | bytes 294920 | tf_op jit(solution)/shard_map/ppermute | solution.py:23
  100.5 9.3 %collective-permute-start.14 = (f32[32,768]{1,0:T(8,128)S(1)}, f32[32,768]{1,0:T(8,128)S(1)}, u32[]{:S(2)}, u32[]{:S(2)}) collective-permute-start(f32[32,768]{1,0:T(8,128)S(1)} %get-tuple-element.65), channel_id=1, source_target_pairs={{0,4},{1,5},{2,6},{3,7},{4,0},{5,1},{6,2},{7,3},{8,12},{9,13},{10,... | collective-permute-start | bytes 294920 | tf_op jit(solution)/shard_map/ppermute | solution.py:23
  102.1 9.4 %collective-permute-start.15 = (f32[32,768]{1,0:T(8,128)S(1)}, f32[32,768]{1,0:T(8,128)S(1)}, u32[]{:S(2)}, u32[]{:S(2)}) collective-permute-start(f32[32,768]{1,0:T(8,128)S(1)} %get-tuple-element.66), channel_id=1, source_target_pairs={{0,6},{1,7},{2,4},{3,5},{4,2},{5,3},{6,0},{7,1},{8,14},{9,15},{10,... | collective-permute-start | bytes 294920 | tf_op jit(solution)/shard_map/ppermute | solution.py:23
  104.8 9.9 %collective-permute-start.4 = (f32[16,768]{1,0:T(8,128)S(1)}, f32[16,768]{1,0:T(8,128)S(1)}, u32[]{:S(2)}, u32[]{:S(2)}) collective-permute-start(f32[16,768]{1,0:T(8,128)S(1)} %get-tuple-element.49), channel_id=1, source_target_pairs={{0,4},{1,5},{2,6},{3,7},{4,0},{5,1},{6,2},{7,3},{8,12},{9,13},{10,... | collective-permute-start | bytes 147464 | tf_op jit(solution)/shard_map/ppermute | solution.py:23
  106.4 8.3 %collective-permute-start.5 = (f32[16,768]{1,0:T(8,128)S(1)}, f32[16,768]{1,0:T(8,128)S(1)}, u32[]{:S(2)}, u32[]{:S(2)}) collective-permute-start(f32[16,768]{1,0:T(8,128)S(1)} %get-tuple-element.50), channel_id=1, source_target_pairs={{0,6},{1,7},{2,4},{3,5},{4,2},{5,3},{6,0},{7,1},{8,14},{9,15},{10,... | collective-permute-start | bytes 147464 | tf_op jit(solution)/shard_map/ppermute | solution.py:23
  109.2 6.1 %collective-permute-start.23 = (f32[16,768]{1,0:T(8,128)S(1)}, f32[16,768]{1,0:T(8,128)S(1)}, u32[]{:S(2)}, u32[]{:S(2)}) collective-permute-start(f32[16,768]{1,0:T(8,128)S(1)} %get-tuple-element.76), channel_id=1, source_target_pairs={{0,2},{1,3},{2,0},{3,1},{4,6},{5,7},{6,4},{7,5},{8,10},{9,11},{10,... | collective-permute-start | bytes 147464 | tf_op jit(solution)/shard_map/ppermute | solution.py:23
  109.9 5.4 %collective-permute-start.24 = (f32[16,768]{1,0:T(8,128)S(1)}, f32[16,768]{1,0:T(8,128)S(1)}, u32[]{:S(2)}, u32[]{:S(2)}) collective-permute-start(f32[16,768]{1,0:T(8,128)S(1)} %get-tuple-element.77), channel_id=1, source_target_pairs={{0,4},{1,5},{2,6},{3,7},{4,0},{5,1},{6,2},{7,3},{8,12},{9,13},{10,... | collective-permute-start | bytes 147464 | tf_op jit(solution)/shard_map/ppermute | solution.py:23
  111.4 5.0 %collective-permute-start.25 = (f32[16,768]{1,0:T(8,128)S(1)}, f32[16,768]{1,0:T(8,128)S(1)}, u32[]{:S(2)}, u32[]{:S(2)}) collective-permute-start(f32[16,768]{1,0:T(8,128)S(1)} %get-tuple-element.78), channel_id=1, source_target_pairs={{0,6},{1,7},{2,4},{3,5},{4,2},{5,3},{6,0},{7,1},{8,14},{9,15},{10,... | collective-permute-start | bytes 147464 | tf_op jit(solution)/shard_map/ppermute | solution.py:23

commit v5 on v4

--- a/solution.py
+++ b/solution.py
@@ -10,7 +10,7 @@
 
 PARTS = (2, 2, 1, 1)
 HEAD = 8
-LATE = 4
+LATE = 8
 
 
 def from_behind(value, axis, by):
@@ -96,7 +96,7 @@
         cost_estimate=pl.CostEstimate(
             flops=2 * block.size * width, bytes_accessed=4 * block.size, transcendentals=0
         ),
-        compiler_params=pltpu.CompilerParams(vmem_limit_bytes=24 << 20),
+        compiler_params=pltpu.CompilerParams(vmem_limit_bytes=55 << 20),
         name="picks",
     )(block)
 
@@ -135,7 +135,7 @@
         cost_estimate=pl.CostEstimate(
             flops=4 * block.size, bytes_accessed=4 * block.size, transcendentals=0
         ),
-        compiler_params=pltpu.CompilerParams(vmem_limit_bytes=16 << 20),
+        compiler_params=pltpu.CompilerParams(vmem_limit_bytes=53 << 20),
         name="turn",
     )(onsets, block)
 

time: 118 us -> 117 us (level)
  Pallas kernels: 19.4 us -> 22.3 us
  local copies, waits for them, and re-layouts: 3.28 us -> 1.38 us
  waiting for transfers between devices: 66.4 us -> 64.7 us
    pallas_call x2, Pallas kernels: 3.64 us -> 6.49 us  [picks(): pl.pallas_call(functools.partial(picks_kernel, share, pieces), out_shape=...]
    unnamed x14 -> x8, local copies, waits for them, and re-layouts: 3.28 us -> 1.38 us
    ppermute x7, waiting for transfers between devices: 58.6 us -> 56.9 us  [from_behind(): lax.ppermute(value, axis, [(i, (i + by) % length) for i in range(length)])]
    pallas_call x4, Pallas kernels: 7.64 us -> 6.21 us  [gram(): pl.pallas_call(functools.partial(gram_kernel, share, run, ranges), out_sh...]
    pallas_call x1, Pallas kernels: 2.44 us -> 3.79 us  [turn(): pl.pallas_call(functools.partial(turn_kernel, step), out_shape=(pltpu.VME...]
  transfers between devices with their start and end apart: 26 -> 26, of which waited for: 10 -> 9; matrix products, arithmetic and copies ran while one was open for 0% -> 0% of each run, Pallas kernels for 13% -> 14%
where the time goes in v5:
time: 117 us
  waiting for transfers between devices  64.7 us (55%)
  starting transfers between devices  28.5 us (24%)
  Pallas kernels  22.3 us (19%)
  local copies, waits for them, and re-layouts  1.38 us (1%)
    ppermute x7, waiting for transfers between devices, from_behind(): lax.ppermute(value, axis, [(i, (i + by) % length) for i in range(length)])  56.9 us
    ppermute x19, starting transfers between devices, swapped(): return lax.ppermute(value, axis, [(i, i ^ bits) for i in range(length)])  20.5 us
    ppermute x7, starting transfers between devices, from_behind(): lax.ppermute(value, axis, [(i, (i + by) % length) for i in range(length)])  8.01 us
    ppermute x19, waiting for transfers between devices, swapped(): return lax.ppermute(value, axis, [(i, i ^ bits) for i in range(length)])  7.74 us
    pallas_call x2, Pallas kernels, picks(): pl.pallas_call(functools.partial(picks_kernel, share, pieces), out_shape=...  6.49 us
    pallas_call x4, Pallas kernels, gram(): pl.pallas_call(functools.partial(gram_kernel, share, run, ranges), out_sh...  6.21 us
    pallas_call x5, Pallas kernels, small_call(): pl.pallas_call(kernel, out_shape=out_shape, in_specs=[pl.BlockSpec(memory...  3.82 us
    pallas_call x1, Pallas kernels, turn(): pl.pallas_call(functools.partial(turn_kernel, step), out_shape=(pltpu.VME...  3.79 us
  transfers between devices with their start and end apart: 26, of which 9 were waited for; matrix products, arithmetic and copies ran while one was open for 0% of the time, Pallas kernels for 14%

profile of v5, /device:TPU:0, one launch (start us, length us, event | category | flops | bytes accessed | tf_op | source)
XLA Modules:
  0.0 117.1 jit_solution(13779643721247207359)
XLA Ops:
  0.0 4.9 %picks.3 = (bf16[1792,256]{1,0:T(8,128)(2,1)S(1)}, bf16[1792,256]{1,0:T(8,128)(2,1)}, bf16[1792,128]{1,0:T(8,128)(2,1)S(1)}, bf16[1536,128]{1,0:T(8,128)(2,1)S(1)}, bf16[256,128]{1,0:T(8,128)(2,1)S(1)}) custom-call(bf16[2048,768]{1,0:T(8,128)(2,1)} %block.5), custom_call_target="tpu_custom_call" | custom-call | flops 2415919104 | bytes 6291456 | tf_op jit(solution)/shard_map/picks/pallas_call | solution.py:89
  4.9 0.0 copy-start.1
  4.9 0.6 copy-done.1
  5.6 3.1 %collective-permute-start.6 = (bf16[1792,256]{1,0:T(8,128)(2,1)}, bf16[1792,256]{1,0:T(8,128)(2,1)S(1)}, u32[]{:S(2)}, u32[]{:S(2)}) collective-permute-start(bf16[1792,256]{1,0:T(8,128)(2,1)} %get-tuple-element.52), channel_id=1, source_target_pairs={{0,8},{8,16},{16,24},{24,0},{1,9},{9,17},{17,25},{25,1},{2,10},{10... | collective-permute-start | bytes 2752520 | tf_op jit(solution)/shard_map/ppermute | solution.py:18
  8.6 1.6 %collective-permute-start.11 = (bf16[1792,256]{1,0:T(8,128)(2,1)S(1)}, bf16[1792,256]{1,0:T(8,128)(2,1)S(1)}, u32[]{:S(2)}, u32[]{:S(2)}) collective-permute-start(bf16[1792,256]{1,0:T(8,128)(2,1)S(1)} %get-tuple-element.60), channel_id=1, source_target_pairs={{0,8},{8,16},{16,24},{24,0},{1,9},{9,17},{17,25},{25,1},{2,10},{10... | collective-permute-start | bytes 2752520 | tf_op jit(solution)/shard_map/ppermute | solution.py:18
  10.2 1.0 top.1
  11.2 1.6 %collective-permute-start = (bf16[256,768]{1,0:T(8,128)(2,1)S(1)}, bf16[256,768]{1,0:T(8,128)(2,1)S(1)}, u32[]{:S(2)}, u32[]{:S(2)}) collective-permute-start(bf16[256,768]{1,0:T(8,128)(2,1)S(1)} %top.1), channel_id=1, source_target_pairs={{0,8},{8,16},{16,24},{24,0},{1,9},{9,17},{17,25},{25,1},{2,10},{10... | collective-permute-start | bytes 1179656 | tf_op jit(solution)/shard_map/ppermute | solution.py:18
  12.8 0.0 collective-permute-start.1
  12.8 1.8 %collective-permute-start.21 = (bf16[1536,128]{1,0:T(8,128)(2,1)S(1)}, bf16[1536,128]{1,0:T(8,128)(2,1)S(1)}, u32[]{:S(2)}, u32[]{:S(2)}) collective-permute-start(bf16[1536,128]{1,0:T(8,128)(2,1)S(1)} %get-tuple-element.72), channel_id=1, source_target_pairs={{0,8},{8,16},{16,24},{24,0},{1,9},{9,17},{17,25},{25,1},{2,10},{10... | collective-permute-start | bytes 1179656 | tf_op jit(solution)/shard_map/ppermute | solution.py:18
  14.6 3.8 %turn.1 = (bf16[768,2048]{1,0:T(8,128)(2,1)S(1)}, f32[1,768]{1,0:T(1,128)S(1)}) custom-call(s32[4]{0:T(128)} %onsets.1, bf16[2048,768]{1,0:T(8,128)(2,1)} %block.5), custom_call_target="tpu_custom_call" | custom-call | flops 6291456 | bytes 6291456 | tf_op jit(solution)/shard_map/turn/pallas_call | solution.py:127
  18.4 41.8 %collective-permute-done.block = bf16[256,768]{1,0:T(8,128)(2,1)S(1)} collective-permute-done((bf16[256,768]{1,0:T(8,128)(2,1)S(1)}, bf16[256,768]{1,0:T(8,128)(2,1)S(1)}, u32[]{:S(2)}, u32[]{:S(2)}) %collective-permute-start) | collective-permute-done | bytes 393248 | tf_op jit(solution)/shard_map/ppermute | solution.py:18
  60.1 0.7 copy-done.3
  60.9 1.6 %picks.2 = (bf16[256,256]{1,0:T(8,128)(2,1)S(1)}, bf16[256,256]{1,0:T(8,128)(2,1)S(1)}, bf16[256,128]{1,0:T(8,128)(2,1)S(1)}, bf16[256,128]{1,0:T(8,128)(2,1)S(1)}) custom-call(bf16[256,768]{1,0:T(8,128)(2,1)} %copy-done.3), custom_call_target="tpu_custom_call" | custom-call | flops 301989888 | bytes 786432 | tf_op jit(solution)/shard_map/picks/pallas_call | solution.py:89
  62.5 0.0 collective-permute-done.6.refs_1_
  62.5 1.8 %gram.5 = (f32[4,32,768]{2,1,0:T(8,128)S(1)}, f32[4,32,768]{2,1,0:T(8,128)S(1)}) custom-call(s32[1,2]{1,0:T(1,128)S(1)} %copy-done, bf16[768,2048]{1,0:T(8,128)(2,1)S(1)} %get-tuple-element.42.own, bf16[256,256]{1,0:T(8,128)(2,1)S(1)} %get-tuple-element.51.refs_0_, bf16[1792,256]{1,0:T(8,128)(2,1)S(1)} %collective-permute-done.6.refs_1_), custom_call_target="tpu_custom_call" | custom-call | flops 805306368 | bytes 3145728 | tf_op jit(solution)/shard_map/gram/pallas_call | solution.py:208
  64.3 0.0 copy-start.2
  64.3 0.1 collective-permute-start.7
  64.4 0.0 collective-permute-done.11.refs_1_
  64.4 1.8 %gram.6 = (f32[4,32,768]{2,1,0:T(8,128)S(1)}, f32[4,32,768]{2,1,0:T(8,128)S(1)}) custom-call(s32[1,2]{1,0:T(1,128)S(1)} %copy-done, bf16[768,2048]{1,0:T(8,128)(2,1)S(1)} %get-tuple-element.42.own, bf16[256,256]{1,0:T(8,128)(2,1)S(1)} %get-tuple-element.59.refs_0_, bf16[1792,256]{1,0:T(8,128)(2,1)S(1)} %collective-permute-done.11.refs_1_), custom_call_target="tpu_custom_call" | custom-call | flops 805306368 | bytes 3145728 | tf_op jit(solution)/shard_map/gram/pallas_call | solution.py:208
  66.2 0.6 collective-permute-start.12
  66.7 0.0 collective-permute-start.20
  66.7 3.2 %collective-permute-done.1.refs_1_ = bf16[1792,128]{1,0:T(8,128)(2,1)S(1)} collective-permute-done((bf16[1792,128]{1,0:T(8,128)(2,1)S(1)}, bf16[1792,128]{1,0:T(8,128)(2,1)S(1)}, u32[]{:S(2)}, u32[]{:S(2)}) %collective-permute-start.1) | collective-permute-done | bytes 458784 | tf_op jit(solution)/shard_map/ppermute | solution.py:18
  70.0 1.7 %gram.4 = (f32[4,16,768]{2,1,0:T(8,128)S(1)}, f32[4,16,768]{2,1,0:T(8,128)S(1)}) custom-call(s32[1,2]{1,0:T(1,128)S(1)} %copy-done, bf16[768,2048]{1,0:T(8,128)(2,1)S(1)} %get-tuple-element.42.own, bf16[256,128]{1,0:T(8,128)(2,1)S(1)} %get-tuple-element.43.refs_0_, bf16[1792,128]{1,0:T(8,128)(2,1)S(1)} %collective-permute-done.1.refs_1_), custom_call_target="tpu_custom_call" | custom-call | flops 402653184 | bytes 3145728 | tf_op jit(solution)/shard_map/gram/pallas_call | solution.py:208
  71.6 0.1 collective-permute-start.2
  71.7 6.5 %collective-permute-done.21.refs_1_ = bf16[1536,128]{1,0:T(8,128)(2,1)S(1)} collective-permute-done((bf16[1536,128]{1,0:T(8,128)(2,1)S(1)}, bf16[1536,128]{1,0:T(8,128)(2,1)S(1)}, u32[]{:S(2)}, u32[]{:S(2)}) %collective-permute-start.21) | collective-permute-done | bytes 393248 | tf_op jit(solution)/shard_map/ppermute | solution.py:18
  78.2 0.9 early.1.refs_1_
  79.1 0.0 collective-permute-done.20.refs_0_
  79.1 1.0 gram.7
  80.1 0.1 collective-permute-start.22
  80.2 0.0 collective-permute-done.7.arrived
  80.2 0.1 fold.5
  80.3 1.6 %collective-permute-start.8 = (f32[32,768]{1,0:T(8,128)S(1)}, f32[32,768]{1,0:T(8,128)S(1)}, u32[]{:S(2)}, u32[]{:S(2)}) collective-permute-start(f32[32,768]{1,0:T(8,128)S(1)} %get-tuple-element.56), channel_id=1, source_target_pairs={{0,2},{1,3},{2,0},{3,1},{4,6},{5,7},{6,4},{7,5},{8,10},{9,11},{10,... | collective-permute-start | bytes 294920 | tf_op jit(solution)/shard_map/ppermute | solution.py:23
  81.8 0.0 collective-permute-done.2.arrived
  81.8 0.6 collective-permute-start.3
  82.4 0.0 collective-permute-start.16
  82.4 1.2 collective-permute-done.16.b
  83.6 1.5 %collective-permute-start.17 = (f32[1,768]{1,0:T(1,128)S(1)}, f32[1,768]{1,0:T(1,128)S(1)}, u32[]{:S(2)}, u32[]{:S(2)}) collective-permute-start(f32[1,768]{1,0:T(1,128)S(1)} %plus.3.a), channel_id=1, source_target_pairs={{0,2},{1,3},{2,0},{3,1},{4,6},{5,7},{6,4},{7,5},{8,10},{9,11},{10,... | collective-permute-start | bytes 9224 | tf_op jit(solution)/shard_map/ppermute | solution.py:23
  85.1 2.1 %collective-permute-done.17.b = f32[1,768]{1,0:T(1,128)S(1)} collective-permute-done((f32[1,768]{1,0:T(1,128)S(1)}, f32[1,768]{1,0:T(1,128)S(1)}, u32[]{:S(2)}, u32[]{:S(2)}) %collective-permute-start.17) | collective-permute-done | bytes 3104 | tf_op jit(solution)/shard_map/ppermute | solution.py:23
  87.2 1.5 %collective-permute-start.18 = (f32[1,768]{1,0:T(1,128)S(1)}, f32[1,768]{1,0:T(1,128)S(1)}, u32[]{:S(2)}, u32[]{:S(2)}) collective-permute-start(f32[1,768]{1,0:T(1,128)S(1)} %plus.4.a), channel_id=1, source_target_pairs={{0,4},{1,5},{2,6},{3,7},{4,0},{5,1},{6,2},{7,3},{8,12},{9,13},{10,... | collective-permute-start | bytes 9224 | tf_op jit(solution)/shard_map/ppermute | solution.py:23
  88.7 2.1 %collective-permute-done.18.b = f32[1,768]{1,0:T(1,128)S(1)} collective-permute-done((f32[1,768]{1,0:T(1,128)S(1)}, f32[1,768]{1,0:T(1,128)S(1)}, u32[]{:S(2)}, u32[]{:S(2)}) %collective-permute-start.18) | collective-permute-done | bytes 3104 | tf_op jit(solution)/shard_map/ppermute | solution.py:23
  90.8 5.4 %collective-permute-done.19.norm_low = f32[1,768]{1,0:T(1,128)S(1)} collective-permute-done((f32[1,768]{1,0:T(1,128)S(1)}, f32[1,768]{1,0:T(1,128)S(1)}, u32[]{:S(2)}, u32[]{:S(2)}) %collective-permute-start.19) | collective-permute-done | bytes 3104 | tf_op jit(solution)/shard_map/ppermute | solution.py:18
  96.2 1.5 %collective-permute-start.9 = (f32[32,768]{1,0:T(8,128)S(1)}, f32[32,768]{1,0:T(8,128)S(1)}, u32[]{:S(2)}, u32[]{:S(2)}) collective-permute-start(f32[32,768]{1,0:T(8,128)S(1)} %get-tuple-element.57), channel_id=1, source_target_pairs={{0,4},{1,5},{2,6},{3,7},{4,0},{5,1},{6,2},{7,3},{8,12},{9,13},{10,... | collective-permute-start | bytes 294920 | tf_op jit(solution)/shard_map/ppermute | solution.py:23
  97.7 0.0 collective-permute-done.12.arrived
  97.7 1.4 %collective-permute-start.10 = (f32[32,768]{1,0:T(8,128)S(1)}, f32[32,768]{1,0:T(8,128)S(1)}, u32[]{:S(2)}, u32[]{:S(2)}) collective-permute-start(f32[32,768]{1,0:T(8,128)S(1)} %get-tuple-element.58), channel_id=1, source_target_pairs={{0,6},{1,7},{2,4},{3,5},{4,2},{5,3},{6,0},{7,1},{8,14},{9,15},{10,... | collective-permute-start | bytes 294920 | tf_op jit(solution)/shard_map/ppermute | solution.py:23
  99.2 0.0 collective-permute-done.22.arrived
  99.2 0.6 collective-permute-start.13
  99.8 1.5 %collective-permute-start.14 = (f32[32,768]{1,0:T(8,128)S(1)}, f32[32,768]{1,0:T(8,128)S(1)}, u32[]{:S(2)}, u32[]{:S(2)}) collective-permute-start(f32[32,768]{1,0:T(8,128)S(1)} %get-tuple-element.65), channel_id=1, source_target_pairs={{0,4},{1,5},{2,6},{3,7},{4,0},{5,1},{6,2},{7,3},{8,12},{9,13},{10,... | collective-permute-start | bytes 294920 | tf_op jit(solution)/shard_map/ppermute | solution.py:23
  101.3 1.4 %collective-permute-start.15 = (f32[32,768]{1,0:T(8,128)S(1)}, f32[32,768]{1,0:T(8,128)S(1)}, u32[]{:S(2)}, u32[]{:S(2)}) collective-permute-start(f32[32,768]{1,0:T(8,128)S(1)} %get-tuple-element.66), channel_id=1, source_target_pairs={{0,6},{1,7},{2,4},{3,5},{4,2},{5,3},{6,0},{7,1},{8,14},{9,15},{10,... | collective-permute-start | bytes 294920 | tf_op jit(solution)/shard_map/ppermute | solution.py:23
  102.8 1.3 %collective-permute-done.9.refs_2_ = f32[32,768]{1,0:T(8,128)S(1)} collective-permute-done((f32[32,768]{1,0:T(8,128)S(1)}, f32[32,768]{1,0:T(8,128)S(1)}, u32[]{:S(2)}, u32[]{:S(2)}) %collective-permute-start.9) | collective-permute-done | bytes 98336 | tf_op jit(solution)/shard_map/ppermute | solution.py:23
  104.1 1.6 %collective-permute-start.4 = (f32[16,768]{1,0:T(8,128)S(1)}, f32[16,768]{1,0:T(8,128)S(1)}, u32[]{:S(2)}, u32[]{:S(2)}) collective-permute-start(f32[16,768]{1,0:T(8,128)S(1)} %get-tuple-element.49), channel_id=1, source_target_pairs={{0,4},{1,5},{2,6},{3,7},{4,0},{5,1},{6,2},{7,3},{8,12},{9,13},{10,... | collective-permute-start | bytes 147464 | tf_op jit(solution)/shard_map/ppermute | solution.py:23
  105.7 2.8 %collective-permute-start.5 = (f32[16,768]{1,0:T(8,128)S(1)}, f32[16,768]{1,0:T(8,128)S(1)}, u32[]{:S(2)}, u32[]{:S(2)}) collective-permute-start(f32[16,768]{1,0:T(8,128)S(1)} %get-tuple-element.50), channel_id=1, source_target_pairs={{0,6},{1,7},{2,4},{3,5},{4,2},{5,3},{6,0},{7,1},{8,14},{9,15},{10,... | collective-permute-start | bytes 147464 | tf_op jit(solution)/shard_map/ppermute | solution.py:23
  108.5 0.0 collective-permute-done.13.refs_1_
  108.5 0.6 collective-permute-start.23
  109.2 0.0 collective-permute-done.14.refs_2_
  109.2 1.5 %collective-permute-start.24 = (f32[16,768]{1,0:T(8,128)S(1)}, f32[16,768]{1,0:T(8,128)S(1)}, u32[]{:S(2)}, u32[]{:S(2)}) collective-permute-start(f32[16,768]{1,0:T(8,128)S(1)} %get-tuple-element.77), channel_id=1, source_target_pairs={{0,4},{1,5},{2,6},{3,7},{4,0},{5,1},{6,2},{7,3},{8,12},{9,13},{10,... | collective-permute-start | bytes 147464 | tf_op jit(solution)/shard_map/ppermute | solution.py:23
  110.7 1.4 %collective-permute-start.25 = (f32[16,768]{1,0:T(8,128)S(1)}, f32[16,768]{1,0:T(8,128)S(1)}, u32[]{:S(2)}, u32[]{:S(2)}) collective-permute-start(f32[16,768]{1,0:T(8,128)S(1)} %get-tuple-element.78), channel_id=1, source_target_pairs={{0,6},{1,7},{2,4},{3,5},{4,2},{5,3},{6,0},{7,1},{8,14},{9,15},{10,... | collective-permute-start | bytes 147464 | tf_op jit(solution)/shard_map/ppermute | solution.py:23
  112.2 0.7 shard_map.40
  112.8 0.6 shard_map.37.refs_4_
  113.4 0.6 shard_map.38.refs_4_
  114.0 0.0 collective-permute-done.5.refs_3_
  114.0 0.6 shard_map.39.base
  114.6 0.0 collective-permute-done.23.refs_1_
  114.6 1.1 collective-permute-done.25.refs_3_
  115.7 1.4 %shard_map.41 = f32[1,96,768]{2,1,0:T(8,128)} custom-call(s32[1,2]{1,0:T(1,128)S(1)} %copy-done, f32[96,768]{1,0:T(8,128)S(1)} %shard_map.39.base, f32[96,128]{1,0:T(8,128)S(1)} %get-tuple-element.68.rows, f32[1,768]{1,0:T(1,128)S(1)} %get-tuple-element.69.columns, f32[16,768]{1,0:T(8,128)S(1)} %get-tuple-element.75.refs_0_, ...), custom_call_target="tpu_custom_call" | custom-call | flops 37748736 | bytes 543744 | tf_op jit(solution)/shard_map/pallas_call | solution.py:362
  (17 shorter events, 0.1 us)
Async XLA Ops:
  4.9 0.6 copy-start.1
  5.6 56.9 %collective-permute-start.6 = (bf16[1792,256]{1,0:T(8,128)(2,1)}, bf16[1792,256]{1,0:T(8,128)(2,1)S(1)}, u32[]{:S(2)}, u32[]{:S(2)}) collective-permute-start(bf16[1792,256]{1,0:T(8,128)(2,1)} %get-tuple-element.52), channel_id=1, source_target_pairs={{0,8},{8,16},{16,24},{24,0},{1,9},{9,17},{17,25},{25,1},{2,10},{10... | collective-permute-start | bytes 2752520 | tf_op jit(solution)/shard_map/ppermute | solution.py:18
  8.6 53.9 %copy-start = (s32[1,2]{1,0:T(1,128)S(1)}, s32[1,2]{1,0:T(1,128)}, u32[]{:S(2)}) copy-start(s32[1,2]{1,0:T(1,128)} %pairs.17) | copy-start | bytes 28
  8.6 55.8 %collective-permute-start.11 = (bf16[1792,256]{1,0:T(8,128)(2,1)S(1)}, bf16[1792,256]{1,0:T(8,128)(2,1)S(1)}, u32[]{:S(2)}, u32[]{:S(2)}) collective-permute-start(bf16[1792,256]{1,0:T(8,128)(2,1)S(1)} %get-tuple-element.60), channel_id=1, source_target_pairs={{0,8},{8,16},{16,24},{24,0},{1,9},{9,17},{17,25},{25,1},{2,10},{10... | collective-permute-start | bytes 2752520 | tf_op jit(solution)/shard_map/ppermute | solution.py:18
  11.2 48.9 %collective-permute-start = (bf16[256,768]{1,0:T(8,128)(2,1)S(1)}, bf16[256,768]{1,0:T(8,128)(2,1)S(1)}, u32[]{:S(2)}, u32[]{:S(2)}) collective-permute-start(bf16[256,768]{1,0:T(8,128)(2,1)S(1)} %top.1), channel_id=1, source_target_pairs={{0,8},{8,16},{16,24},{24,0},{1,9},{9,17},{17,25},{25,1},{2,10},{10... | collective-permute-start | bytes 1179656 | tf_op jit(solution)/shard_map/ppermute | solution.py:18
  12.8 57.2 %collective-permute-start.1 = (bf16[1792,128]{1,0:T(8,128)(2,1)S(1)}, bf16[1792,128]{1,0:T(8,128)(2,1)S(1)}, u32[]{:S(2)}, u32[]{:S(2)}) collective-permute-start(bf16[1792,128]{1,0:T(8,128)(2,1)S(1)} %get-tuple-element.44), channel_id=1, source_target_pairs={{0,8},{8,16},{16,24},{24,0},{1,9},{9,17},{17,25},{25,1},{2,10},{10... | collective-permute-start | bytes 1376264 | tf_op jit(solution)/shard_map/ppermute | solution.py:18
  12.8 65.5 %collective-permute-start.21 = (bf16[1536,128]{1,0:T(8,128)(2,1)S(1)}, bf16[1536,128]{1,0:T(8,128)(2,1)S(1)}, u32[]{:S(2)}, u32[]{:S(2)}) collective-permute-start(bf16[1536,128]{1,0:T(8,128)(2,1)S(1)} %get-tuple-element.72), channel_id=1, source_target_pairs={{0,8},{8,16},{16,24},{24,0},{1,9},{9,17},{17,25},{25,1},{2,10},{10... | collective-permute-start | bytes 1179656 | tf_op jit(solution)/shard_map/ppermute | solution.py:18
  60.1 0.7 copy-start.3
  64.3 2.5 %copy-start.2 = (bf16[256,128]{1,0:T(8,128)(2,1)S(1)}, bf16[256,128]{1,0:T(8,128)(2,1)}, u32[]{:S(2)}) copy-start(bf16[256,128]{1,0:T(8,128)(2,1)} %copy-done.1) | copy-start | bytes 196612
  64.3 15.9 %collective-permute-start.7 = (f32[4,32,768]{2,1,0:T(8,128)S(1)}, f32[4,32,768]{2,1,0:T(8,128)S(1)}, u32[]{:S(2)}, u32[]{:S(2)}) collective-permute-start(f32[4,32,768]{2,1,0:T(8,128)S(1)} %get-tuple-element.54), channel_id=1, source_target_pairs={{0,1},{1,0},{2,3},{3,2},{4,5},{5,4},{6,7},{7,6},{8,9},{9,8},{10,11... | collective-permute-start | bytes 1179656 | tf_op jit(solution)/shard_map/ppermute | solution.py:23
  66.2 31.6 %collective-permute-start.12 = (f32[4,32,768]{2,1,0:T(8,128)S(1)}, f32[4,32,768]{2,1,0:T(8,128)S(1)}, u32[]{:S(2)}, u32[]{:S(2)}) collective-permute-start(f32[4,32,768]{2,1,0:T(8,128)S(1)} %get-tuple-element.62), channel_id=1, source_target_pairs={{0,1},{1,0},{2,3},{3,2},{4,5},{5,4},{6,7},{7,6},{8,9},{9,8},{10,11... | collective-permute-start | bytes 1179656 | tf_op jit(solution)/shard_map/ppermute | solution.py:23
  66.7 12.4 %collective-permute-start.20 = (bf16[256,128]{1,0:T(8,128)(2,1)S(1)}, bf16[256,128]{1,0:T(8,128)(2,1)S(1)}, u32[]{:S(2)}, u32[]{:S(2)}) collective-permute-start(bf16[256,128]{1,0:T(8,128)(2,1)S(1)} %copy-done.2), channel_id=1, source_target_pairs={{0,8},{8,16},{16,24},{24,0},{1,9},{9,17},{17,25},{25,1},{2,10},{10... | collective-permute-start | bytes 196616 | tf_op jit(solution)/shard_map/ppermute | solution.py:18
  71.6 10.2 %collective-permute-start.2 = (f32[4,16,768]{2,1,0:T(8,128)S(1)}, f32[4,16,768]{2,1,0:T(8,128)S(1)}, u32[]{:S(2)}, u32[]{:S(2)}) collective-permute-start(f32[4,16,768]{2,1,0:T(8,128)S(1)} %get-tuple-element.46), channel_id=1, source_target_pairs={{0,1},{1,0},{2,3},{3,2},{4,5},{5,4},{6,7},{7,6},{8,9},{9,8},{10,11... | collective-permute-start | bytes 589832 | tf_op jit(solution)/shard_map/ppermute | solution.py:23
  80.1 19.1 %collective-permute-start.22 = (f32[4,16,768]{2,1,0:T(8,128)S(1)}, f32[4,16,768]{2,1,0:T(8,128)S(1)}, u32[]{:S(2)}, u32[]{:S(2)}) collective-permute-start(f32[4,16,768]{2,1,0:T(8,128)S(1)} %get-tuple-element.74), channel_id=1, source_target_pairs={{0,1},{1,0},{2,3},{3,2},{4,5},{5,4},{6,7},{7,6},{8,9},{9,8},{10,11... | collective-permute-start | bytes 589832 | tf_op jit(solution)/shard_map/ppermute | solution.py:23
  80.3 21.1 %collective-permute-start.8 = (f32[32,768]{1,0:T(8,128)S(1)}, f32[32,768]{1,0:T(8,128)S(1)}, u32[]{:S(2)}, u32[]{:S(2)}) collective-permute-start(f32[32,768]{1,0:T(8,128)S(1)} %get-tuple-element.56), channel_id=1, source_target_pairs={{0,2},{1,3},{2,0},{3,1},{4,6},{5,7},{6,4},{7,5},{8,10},{9,11},{10,... | collective-permute-start | bytes 294920 | tf_op jit(solution)/shard_map/ppermute | solution.py:23
  81.8 18.0 %collective-permute-start.3 = (f32[16,768]{1,0:T(8,128)S(1)}, f32[16,768]{1,0:T(8,128)S(1)}, u32[]{:S(2)}, u32[]{:S(2)}) collective-permute-start(f32[16,768]{1,0:T(8,128)S(1)} %get-tuple-element.48), channel_id=1, source_target_pairs={{0,2},{1,3},{2,0},{3,1},{4,6},{5,7},{6,4},{7,5},{8,10},{9,11},{10,... | collective-permute-start | bytes 147464 | tf_op jit(solution)/shard_map/ppermute | solution.py:23
  82.4 1.2 collective-permute-start.16
  83.6 3.6 %collective-permute-start.17 = (f32[1,768]{1,0:T(1,128)S(1)}, f32[1,768]{1,0:T(1,128)S(1)}, u32[]{:S(2)}, u32[]{:S(2)}) collective-permute-start(f32[1,768]{1,0:T(1,128)S(1)} %plus.3.a), channel_id=1, source_target_pairs={{0,2},{1,3},{2,0},{3,1},{4,6},{5,7},{6,4},{7,5},{8,10},{9,11},{10,... | collective-permute-start | bytes 9224 | tf_op jit(solution)/shard_map/ppermute | solution.py:23
  87.2 3.6 %collective-permute-start.18 = (f32[1,768]{1,0:T(1,128)S(1)}, f32[1,768]{1,0:T(1,128)S(1)}, u32[]{:S(2)}, u32[]{:S(2)}) collective-permute-start(f32[1,768]{1,0:T(1,128)S(1)} %plus.4.a), channel_id=1, source_target_pairs={{0,4},{1,5},{2,6},{3,7},{4,0},{5,1},{6,2},{7,3},{8,12},{9,13},{10,... | collective-permute-start | bytes 9224 | tf_op jit(solution)/shard_map/ppermute | solution.py:23
  90.8 5.4 %collective-permute-start.19 = (f32[1,768]{1,0:T(1,128)S(1)}, f32[1,768]{1,0:T(1,128)S(1)}, u32[]{:S(2)}, u32[]{:S(2)}) collective-permute-start(f32[1,768]{1,0:T(1,128)S(1)} %plus.5.norm_own), channel_id=1, source_target_pairs={{0,8},{8,16},{16,24},{24,0},{1,9},{9,17},{17,25},{25,1},{2,10},{10... | collective-permute-start | bytes 9224 | tf_op jit(solution)/shard_map/ppermute | solution.py:18
  96.2 7.9 %collective-permute-start.9 = (f32[32,768]{1,0:T(8,128)S(1)}, f32[32,768]{1,0:T(8,128)S(1)}, u32[]{:S(2)}, u32[]{:S(2)}) collective-permute-start(f32[32,768]{1,0:T(8,128)S(1)} %get-tuple-element.57), channel_id=1, source_target_pairs={{0,4},{1,5},{2,6},{3,7},{4,0},{5,1},{6,2},{7,3},{8,12},{9,13},{10,... | collective-permute-start | bytes 294920 | tf_op jit(solution)/shard_map/ppermute | solution.py:23
  97.7 7.9 %collective-permute-start.10 = (f32[32,768]{1,0:T(8,128)S(1)}, f32[32,768]{1,0:T(8,128)S(1)}, u32[]{:S(2)}, u32[]{:S(2)}) collective-permute-start(f32[32,768]{1,0:T(8,128)S(1)} %get-tuple-element.58), channel_id=1, source_target_pairs={{0,6},{1,7},{2,4},{3,5},{4,2},{5,3},{6,0},{7,1},{8,14},{9,15},{10,... | collective-permute-start | bytes 294920 | tf_op jit(solution)/shard_map/ppermute | solution.py:23
  99.2 9.3 %collective-permute-start.13 = (f32[32,768]{1,0:T(8,128)S(1)}, f32[32,768]{1,0:T(8,128)S(1)}, u32[]{:S(2)}, u32[]{:S(2)}) collective-permute-start(f32[32,768]{1,0:T(8,128)S(1)} %get-tuple-element.64), channel_id=1, source_target_pairs={{0,2},{1,3},{2,0},{3,1},{4,6},{5,7},{6,4},{7,5},{8,10},{9,11},{10,... | collective-permute-start | bytes 294920 | tf_op jit(solution)/shard_map/ppermute | solution.py:23
  99.8 9.3 %collective-permute-start.14 = (f32[32,768]{1,0:T(8,128)S(1)}, f32[32,768]{1,0:T(8,128)S(1)}, u32[]{:S(2)}, u32[]{:S(2)}) collective-permute-start(f32[32,768]{1,0:T(8,128)S(1)} %get-tuple-element.65), channel_id=1, source_target_pairs={{0,4},{1,5},{2,6},{3,7},{4,0},{5,1},{6,2},{7,3},{8,12},{9,13},{10,... | collective-permute-start | bytes 294920 | tf_op jit(solution)/shard_map/ppermute | solution.py:23
  101.3 9.4 %collective-permute-start.15 = (f32[32,768]{1,0:T(8,128)S(1)}, f32[32,768]{1,0:T(8,128)S(1)}, u32[]{:S(2)}, u32[]{:S(2)}) collective-permute-start(f32[32,768]{1,0:T(8,128)S(1)} %get-tuple-element.66), channel_id=1, source_target_pairs={{0,6},{1,7},{2,4},{3,5},{4,2},{5,3},{6,0},{7,1},{8,14},{9,15},{10,... | collective-permute-start | bytes 294920 | tf_op jit(solution)/shard_map/ppermute | solution.py:23
  104.1 9.9 %collective-permute-start.4 = (f32[16,768]{1,0:T(8,128)S(1)}, f32[16,768]{1,0:T(8,128)S(1)}, u32[]{:S(2)}, u32[]{:S(2)}) collective-permute-start(f32[16,768]{1,0:T(8,128)S(1)} %get-tuple-element.49), channel_id=1, source_target_pairs={{0,4},{1,5},{2,6},{3,7},{4,0},{5,1},{6,2},{7,3},{8,12},{9,13},{10,... | collective-permute-start | bytes 147464 | tf_op jit(solution)/shard_map/ppermute | solution.py:23
  105.7 8.3 %collective-permute-start.5 = (f32[16,768]{1,0:T(8,128)S(1)}, f32[16,768]{1,0:T(8,128)S(1)}, u32[]{:S(2)}, u32[]{:S(2)}) collective-permute-start(f32[16,768]{1,0:T(8,128)S(1)} %get-tuple-element.50), channel_id=1, source_target_pairs={{0,6},{1,7},{2,4},{3,5},{4,2},{5,3},{6,0},{7,1},{8,14},{9,15},{10,... | collective-permute-start | bytes 147464 | tf_op jit(solution)/shard_map/ppermute | solution.py:23
  108.5 6.1 %collective-permute-start.23 = (f32[16,768]{1,0:T(8,128)S(1)}, f32[16,768]{1,0:T(8,128)S(1)}, u32[]{:S(2)}, u32[]{:S(2)}) collective-permute-start(f32[16,768]{1,0:T(8,128)S(1)} %get-tuple-element.76), channel_id=1, source_target_pairs={{0,2},{1,3},{2,0},{3,1},{4,6},{5,7},{6,4},{7,5},{8,10},{9,11},{10,... | collective-permute-start | bytes 147464 | tf_op jit(solution)/shard_map/ppermute | solution.py:23
  109.2 5.4 %collective-permute-start.24 = (f32[16,768]{1,0:T(8,128)S(1)}, f32[16,768]{1,0:T(8,128)S(1)}, u32[]{:S(2)}, u32[]{:S(2)}) collective-permute-start(f32[16,768]{1,0:T(8,128)S(1)} %get-tuple-element.77), channel_id=1, source_target_pairs={{0,4},{1,5},{2,6},{3,7},{4,0},{5,1},{6,2},{7,3},{8,12},{9,13},{10,... | collective-permute-start | bytes 147464 | tf_op jit(solution)/shard_map/ppermute | solution.py:23
  110.7 5.0 %collective-permute-start.25 = (f32[16,768]{1,0:T(8,128)S(1)}, f32[16,768]{1,0:T(8,128)S(1)}, u32[]{:S(2)}, u32[]{:S(2)}) collective-permute-start(f32[16,768]{1,0:T(8,128)S(1)} %get-tuple-element.78), channel_id=1, source_target_pairs={{0,6},{1,7},{2,4},{3,5},{4,2},{5,3},{6,0},{7,1},{8,14},{9,15},{10,... | collective-permute-start | bytes 147464 | tf_op jit(solution)/shard_map/ppermute | solution.py:23

commit v6 on v5

--- a/solution.py
+++ b/solution.py
@@ -10,7 +10,7 @@
 
 PARTS = (2, 2, 1, 1)
 HEAD = 8
-LATE = 8
+LATE = 16
 
 
 def from_behind(value, axis, by):
@@ -291,6 +291,14 @@
     )(a, b)
 
 
+def spots_of(share, start, run, width):
+    columns = width // share * run
+    q = lax.broadcasted_iota(jnp.int32, (columns, width), 0)
+    source = lax.broadcasted_iota(jnp.int32, (columns, width), 1)
+    order = (q // run) * share + start + q % run == source
+    return order.astype(jnp.float32).astype(jnp.bfloat16)
+
+
 def placed(owner_first, share, start, run, terms, total, scales=None):
     width = total.shape[1]
     columns = width // share * run
@@ -308,12 +316,9 @@
         for _ in range(3):
             pieces.append(left.astype(jnp.bfloat16))
             left = left - pieces[-1].astype(jnp.float32)
-        q = lax.broadcasted_iota(jnp.int32, (columns, width), 0)
-        source = lax.broadcasted_iota(jnp.int32, (columns, width), 1)
-        order = (q // run) * share + start + q % run == source
         spots = jnp.dot(
             jnp.concatenate(pieces, axis=0),
-            order.astype(jnp.float32).astype(jnp.bfloat16),
+            spots_of(share, start, run, width) if scales is None else scales[2][...],
             preferred_element_type=jnp.float32,
         )
         added = (spots[:share] + spots[share : 2 * share] + spots[2 * share :]) * 16.0
@@ -329,16 +334,16 @@
         total[start : start + run, :] = rows
 
 
-def place_kernel(share, start, run, pairs, *refs):
-    *terms, total = refs
-    if len(terms) > 4:
-        total[...] = terms.pop()[...]
-    else:
-        total[...] = jnp.zeros_like(total)
-    placed(pairs[0, 0] == lax.axis_index("src"), share, start, run, terms, total)
-
-
-def scales_kernel(share, pairs, norm_own, norm_low, rows, columns):
+def place_kernel(share, start, run, given, pairs, *refs):
+    *refs, total = refs
+    owner_first = pairs[0, 0] == lax.axis_index("src")
+    total[...] = refs[4][...] if given else jnp.zeros_like(total)
+    placed(owner_first, share, start, run, refs[:4], total)
+    if given > 1:
+        total[...] = total[...] * refs[5][:, :1] * refs[6][...]
+
+
+def scales_kernel(share, start, run, pairs, norm_own, norm_low, rows, columns, spots):
     width = columns.shape[1]
     owner_first = pairs[0, 0] == lax.axis_index("src")
     scale_own = lax.rsqrt(norm_own[...] + 1e-06)
@@ -349,13 +354,14 @@
     mine = jnp.sum(jnp.where(row == column, scale_first, 0.0), axis=1, keepdims=True)
     rows[...] = jnp.broadcast_to(mine, rows.shape)
     columns[...] = jnp.where(owner_first, scale_low, scale_own)
-
-
-def finish_kernel(share, start, run, pairs, base, rows, columns, *refs):
+    spots[...] = spots_of(share, start, run, width)
+
+
+def finish_kernel(share, start, run, pairs, base, rows, columns, spots, *refs):
     *terms, out = refs
     owner_first = pairs[0, 0] == lax.axis_index("src")
-    out[0] = base[...] * rows[:, :1] * columns[...]
-    placed(owner_first, share, start, run, terms, out.at[0], (rows, columns))
+    out[0] = base[...]
+    placed(owner_first, share, start, run, terms, out.at[0], (rows, columns, spots))
 
 
 def small_call(kernel, out_shape, pairs, given, flops):
@@ -374,21 +380,27 @@
     )(pairs, *given)
 
 
-def place(pairs, terms, base, share, width, start, run):
+def place(pairs, terms, base, scales, share, width, start, run):
+    given = [] if base is None else [base]
+    given += list(scales[:2])
     return small_call(
-        functools.partial(place_kernel, share, start, run),
+        functools.partial(place_kernel, share, start, run, len(given)),
         pltpu.VMEM((share, width), jnp.float32),
         pairs,
-        list(terms) + ([] if base is None else [base]),
+        list(terms) + given,
         2 * share * width * 256,
     )
 
 
-def scales_of(pairs, norm_own, norm_low, share):
+def scales_of(pairs, norm_own, norm_low, share, start, run):
     width = norm_own.shape[1]
     return small_call(
-        functools.partial(scales_kernel, share),
-        (pltpu.VMEM((share, 128), jnp.float32), pltpu.VMEM((1, width), jnp.float32)),
+        functools.partial(scales_kernel, share, start, run),
+        (
+            pltpu.VMEM((share, 128), jnp.float32),
+            pltpu.VMEM((1, width), jnp.float32),
+            pltpu.VMEM((width // share * run, width), jnp.bfloat16),
+        ),
         pairs,
         [norm_own, norm_low],
         share * width,
@@ -443,6 +455,7 @@
     if not aligned:
         return plain_tail(pairs, own, heads, lower, norm_own[0], norm_low[0], share, runs)
 
+    scales = scales_of(pairs, norm_own, norm_low, share, *runs[-1])
     base = None
     for step, (run, top) in enumerate(zip(runs, heads)):
         if step < len(runs) - 1:
@@ -457,8 +470,8 @@
         for m, strip in enumerate(gives, 1):
             terms.append(swapped(strip, "tm", 2 * m))
         if step < len(runs) - 1:
-            base = place(pairs, terms, base, share, width, *run)
-    scales = scales_of(pairs, norm_own, norm_low, share)
+            used = scales if step == len(runs) - 2 else ()
+            base = place(pairs, terms, base, used, share, width, *run)
     return finish(pairs, base, scales, terms, share, *runs[-1])
 
 

time: 117 us -> 117 us (level)
  no operation moved by 1% of the time
where the time goes in v6:
time: 117 us
  waiting for transfers between devices  64.7 us (55%)
  starting transfers between devices  28.5 us (24%)
  Pallas kernels  22.4 us (19%)
    ppermute x7, waiting for transfers between devices, from_behind(): lax.ppermute(value, axis, [(i, (i + by) % length) for i in range(length)])  57.1 us
    ppermute x19, starting transfers between devices, swapped(): return lax.ppermute(value, axis, [(i, i ^ bits) for i in range(length)])  20.5 us
    ppermute x7, starting transfers between devices, from_behind(): lax.ppermute(value, axis, [(i, (i + by) % length) for i in range(length)])  8.06 us
    ppermute x19, waiting for transfers between devices, swapped(): return lax.ppermute(value, axis, [(i, i ^ bits) for i in range(length)])  7.6 us
    pallas_call x2, Pallas kernels, picks(): pl.pallas_call(functools.partial(picks_kernel, share, pieces), out_shape=...  6.49 us
    pallas_call x4, Pallas kernels, gram(): pl.pallas_call(functools.partial(gram_kernel, share, run, ranges), out_sh...  6.17 us
    pallas_call x5, Pallas kernels, small_call(): pl.pallas_call(kernel, out_shape=out_shape, in_specs=[pl.BlockSpec(memory...  3.9 us
    pallas_call x1, Pallas kernels, turn(): pl.pallas_call(functools.partial(turn_kernel, step), out_shape=(pltpu.VME...  3.79 us
  transfers between devices with their start and end apart: 26, of which 9 were waited for; matrix products, arithmetic and copies ran while one was open for 0% of the time, Pallas kernels for 14%

profile of v6, /device:TPU:0, one launch (start us, length us, event | category | flops | bytes accessed | tf_op | source)
XLA Modules:
  0.0 116.6 jit_solution(3516764628375705461)
XLA Ops:
  0.0 4.9 %picks.3 = (bf16[1792,256]{1,0:T(8,128)(2,1)S(1)}, bf16[1792,256]{1,0:T(8,128)(2,1)S(1)}, bf16[1792,128]{1,0:T(8,128)(2,1)S(1)}, bf16[1664,128]{1,0:T(8,128)(2,1)S(1)}, bf16[128,128]{1,0:T(8,128)(2,1)S(1)}) custom-call(bf16[2048,768]{1,0:T(8,128)(2,1)} %block.5), custom_call_target="tpu_custom_call" | custom-call | flops 2415919104 | bytes 6291456 | tf_op jit(solution)/shard_map/picks/pallas_call | solution.py:89
  4.9 3.1 %collective-permute-start.6 = (bf16[1792,256]{1,0:T(8,128)(2,1)S(1)}, bf16[1792,256]{1,0:T(8,128)(2,1)S(1)}, u32[]{:S(2)}, u32[]{:S(2)}) collective-permute-start(bf16[1792,256]{1,0:T(8,128)(2,1)S(1)} %get-tuple-element.53), channel_id=1, source_target_pairs={{0,8},{8,16},{16,24},{24,0},{1,9},{9,17},{17,25},{25,1},{2,10},{10... | collective-permute-start | bytes 2752520 | tf_op jit(solution)/shard_map/ppermute | solution.py:18
  8.1 1.6 %collective-permute-start.11 = (bf16[1792,256]{1,0:T(8,128)(2,1)S(1)}, bf16[1792,256]{1,0:T(8,128)(2,1)S(1)}, u32[]{:S(2)}, u32[]{:S(2)}) collective-permute-start(bf16[1792,256]{1,0:T(8,128)(2,1)S(1)} %get-tuple-element.61), channel_id=1, source_target_pairs={{0,8},{8,16},{16,24},{24,0},{1,9},{9,17},{17,25},{25,1},{2,10},{10... | collective-permute-start | bytes 2752520 | tf_op jit(solution)/shard_map/ppermute | solution.py:18
  9.6 1.0 top.1
  10.6 1.6 %collective-permute-start = (bf16[256,768]{1,0:T(8,128)(2,1)S(1)}, bf16[256,768]{1,0:T(8,128)(2,1)S(1)}, u32[]{:S(2)}, u32[]{:S(2)}) collective-permute-start(bf16[256,768]{1,0:T(8,128)(2,1)S(1)} %top.1), channel_id=1, source_target_pairs={{0,8},{8,16},{16,24},{24,0},{1,9},{9,17},{17,25},{25,1},{2,10},{10... | collective-permute-start | bytes 1179656 | tf_op jit(solution)/shard_map/ppermute | solution.py:18
  12.2 0.9 collective-permute-start.1
  13.1 0.9 collective-permute-start.21
  14.0 3.8 %turn.1 = (bf16[768,2048]{1,0:T(8,128)(2,1)S(1)}, f32[1,768]{1,0:T(1,128)S(1)}) custom-call(s32[4]{0:T(128)} %onsets.1, bf16[2048,768]{1,0:T(8,128)(2,1)} %block.5), custom_call_target="tpu_custom_call" | custom-call | flops 6291456 | bytes 6291456 | tf_op jit(solution)/shard_map/turn/pallas_call | solution.py:127
  17.8 41.6 %collective-permute-done.block = bf16[256,768]{1,0:T(8,128)(2,1)S(1)} collective-permute-done((bf16[256,768]{1,0:T(8,128)(2,1)S(1)}, bf16[256,768]{1,0:T(8,128)(2,1)S(1)}, u32[]{:S(2)}, u32[]{:S(2)}) %collective-permute-start) | collective-permute-done | bytes 393248 | tf_op jit(solution)/shard_map/ppermute | solution.py:18
  59.4 0.7 copy-done.3
  60.1 1.6 %picks.2 = (bf16[256,256]{1,0:T(8,128)(2,1)S(1)}, bf16[256,256]{1,0:T(8,128)(2,1)S(1)}, bf16[256,128]{1,0:T(8,128)(2,1)S(1)}, bf16[256,128]{1,0:T(8,128)(2,1)S(1)}) custom-call(bf16[256,768]{1,0:T(8,128)(2,1)} %copy-done.3), custom_call_target="tpu_custom_call" | custom-call | flops 301989888 | bytes 786432 | tf_op jit(solution)/shard_map/picks/pallas_call | solution.py:89
  61.7 0.0 collective-permute-done.6.refs_1_
  61.7 1.8 %gram.5 = (f32[4,32,768]{2,1,0:T(8,128)S(1)}, f32[4,32,768]{2,1,0:T(8,128)S(1)}) custom-call(s32[1,2]{1,0:T(1,128)S(1)} %copy-done, bf16[768,2048]{1,0:T(8,128)(2,1)S(1)} %get-tuple-element.43.own, bf16[256,256]{1,0:T(8,128)(2,1)S(1)} %get-tuple-element.52.refs_0_, bf16[1792,256]{1,0:T(8,128)(2,1)S(1)} %collective-permute-done.6.refs_1_), custom_call_target="tpu_custom_call" | custom-call | flops 805306368 | bytes 3145728 | tf_op jit(solution)/shard_map/gram/pallas_call | solution.py:208
  63.5 0.1 collective-permute-start.7
  63.6 0.0 collective-permute-done.11.refs_1_
  63.6 1.8 %gram.6 = (f32[4,32,768]{2,1,0:T(8,128)S(1)}, f32[4,32,768]{2,1,0:T(8,128)S(1)}) custom-call(s32[1,2]{1,0:T(1,128)S(1)} %copy-done, bf16[768,2048]{1,0:T(8,128)(2,1)S(1)} %get-tuple-element.43.own, bf16[256,256]{1,0:T(8,128)(2,1)S(1)} %get-tuple-element.60.refs_0_, bf16[1792,256]{1,0:T(8,128)(2,1)S(1)} %collective-permute-done.11.refs_1_), custom_call_target="tpu_custom_call" | custom-call | flops 805306368 | bytes 3145728 | tf_op jit(solution)/shard_map/gram/pallas_call | solution.py:208
  65.4 0.5 collective-permute-start.12
  65.9 0.0 collective-permute-start.20
  65.9 3.2 %collective-permute-done.1.refs_1_ = bf16[1792,128]{1,0:T(8,128)(2,1)S(1)} collective-permute-done((bf16[1792,128]{1,0:T(8,128)(2,1)}, bf16[1792,128]{1,0:T(8,128)(2,1)S(1)}, u32[]{:S(2)}, u32[]{:S(2)}) %collective-permute-start.1) | collective-permute-done | bytes 458784 | tf_op jit(solution)/shard_map/ppermute | solution.py:18
  69.2 1.7 %gram.4 = (f32[4,16,768]{2,1,0:T(8,128)S(1)}, f32[4,16,768]{2,1,0:T(8,128)S(1)}) custom-call(s32[1,2]{1,0:T(1,128)S(1)} %copy-done, bf16[768,2048]{1,0:T(8,128)(2,1)S(1)} %get-tuple-element.43.own, bf16[256,128]{1,0:T(8,128)(2,1)S(1)} %get-tuple-element.44.refs_0_, bf16[1792,128]{1,0:T(8,128)(2,1)S(1)} %collective-permute-done.1.refs_1_), custom_call_target="tpu_custom_call" | custom-call | flops 402653184 | bytes 3145728 | tf_op jit(solution)/shard_map/gram/pallas_call | solution.py:208
  70.9 0.1 collective-permute-start.2
  71.0 6.9 %collective-permute-done.21.refs_1_ = bf16[1664,128]{1,0:T(8,128)(2,1)S(1)} collective-permute-done((bf16[1664,128]{1,0:T(8,128)(2,1)}, bf16[1664,128]{1,0:T(8,128)(2,1)S(1)}, u32[]{:S(2)}, u32[]{:S(2)}) %collective-permute-start.21) | collective-permute-done | bytes 426016 | tf_op jit(solution)/shard_map/ppermute | solution.py:18
  77.8 0.9 early.1.refs_1_
  78.8 0.0 collective-permute-done.20.refs_0_
  78.8 0.9 gram.7
  79.7 0.1 collective-permute-start.22
  79.8 0.0 collective-permute-done.7.arrived
  79.8 0.1 fold.5
  79.8 1.6 %collective-permute-start.8 = (f32[32,768]{1,0:T(8,128)S(1)}, f32[32,768]{1,0:T(8,128)S(1)}, u32[]{:S(2)}, u32[]{:S(2)}) collective-permute-start(f32[32,768]{1,0:T(8,128)S(1)} %get-tuple-element.57), channel_id=1, source_target_pairs={{0,2},{1,3},{2,0},{3,1},{4,6},{5,7},{6,4},{7,5},{8,10},{9,11},{10,... | collective-permute-start | bytes 294920 | tf_op jit(solution)/shard_map/ppermute | solution.py:23
  81.4 0.0 collective-permute-done.2.arrived
  81.4 0.6 collective-permute-start.3
  82.0 0.0 collective-permute-start.16
  82.0 1.2 collective-permute-done.16.b
  83.2 1.5 %collective-permute-start.17 = (f32[1,768]{1,0:T(1,128)S(1)}, f32[1,768]{1,0:T(1,128)S(1)}, u32[]{:S(2)}, u32[]{:S(2)}) collective-permute-start(f32[1,768]{1,0:T(1,128)S(1)} %plus.3.a), channel_id=1, source_target_pairs={{0,2},{1,3},{2,0},{3,1},{4,6},{5,7},{6,4},{7,5},{8,10},{9,11},{10,... | collective-permute-start | bytes 9224 | tf_op jit(solution)/shard_map/ppermute | solution.py:23
  84.7 2.1 %collective-permute-done.17.b = f32[1,768]{1,0:T(1,128)S(1)} collective-permute-done((f32[1,768]{1,0:T(1,128)S(1)}, f32[1,768]{1,0:T(1,128)S(1)}, u32[]{:S(2)}, u32[]{:S(2)}) %collective-permute-start.17) | collective-permute-done | bytes 3104 | tf_op jit(solution)/shard_map/ppermute | solution.py:23
  86.8 1.5 %collective-permute-start.18 = (f32[1,768]{1,0:T(1,128)S(1)}, f32[1,768]{1,0:T(1,128)S(1)}, u32[]{:S(2)}, u32[]{:S(2)}) collective-permute-start(f32[1,768]{1,0:T(1,128)S(1)} %plus.4.a), channel_id=1, source_target_pairs={{0,4},{1,5},{2,6},{3,7},{4,0},{5,1},{6,2},{7,3},{8,12},{9,13},{10,... | collective-permute-start | bytes 9224 | tf_op jit(solution)/shard_map/ppermute | solution.py:23
  88.3 2.1 %collective-permute-done.18.b = f32[1,768]{1,0:T(1,128)S(1)} collective-permute-done((f32[1,768]{1,0:T(1,128)S(1)}, f32[1,768]{1,0:T(1,128)S(1)}, u32[]{:S(2)}, u32[]{:S(2)}) %collective-permute-start.18) | collective-permute-done | bytes 3104 | tf_op jit(solution)/shard_map/ppermute | solution.py:23
  90.4 0.0 collective-permute-start.19
  90.4 5.4 %collective-permute-done.19.norm_low = f32[1,768]{1,0:T(1,128)S(1)} collective-permute-done((f32[1,768]{1,0:T(1,128)S(1)}, f32[1,768]{1,0:T(1,128)S(1)}, u32[]{:S(2)}, u32[]{:S(2)}) %collective-permute-start.19) | collective-permute-done | bytes 3104 | tf_op jit(solution)/shard_map/ppermute | solution.py:18
  95.8 1.5 %collective-permute-start.9 = (f32[32,768]{1,0:T(8,128)S(1)}, f32[32,768]{1,0:T(8,128)S(1)}, u32[]{:S(2)}, u32[]{:S(2)}) collective-permute-start(f32[32,768]{1,0:T(8,128)S(1)} %get-tuple-element.58), channel_id=1, source_target_pairs={{0,4},{1,5},{2,6},{3,7},{4,0},{5,1},{6,2},{7,3},{8,12},{9,13},{10,... | collective-permute-start | bytes 294920 | tf_op jit(solution)/shard_map/ppermute | solution.py:23
  97.3 1.4 %collective-permute-start.10 = (f32[32,768]{1,0:T(8,128)S(1)}, f32[32,768]{1,0:T(8,128)S(1)}, u32[]{:S(2)}, u32[]{:S(2)}) collective-permute-start(f32[32,768]{1,0:T(8,128)S(1)} %get-tuple-element.59), channel_id=1, source_target_pairs={{0,6},{1,7},{2,4},{3,5},{4,2},{5,3},{6,0},{7,1},{8,14},{9,15},{10,... | collective-permute-start | bytes 294920 | tf_op jit(solution)/shard_map/ppermute | solution.py:23
  98.8 0.0 collective-permute-done.22.arrived
  98.8 0.6 collective-permute-start.13
  99.4 0.0 collective-permute-done.3.refs_1_
  99.4 1.5 %collective-permute-start.14 = (f32[32,768]{1,0:T(8,128)S(1)}, f32[32,768]{1,0:T(8,128)S(1)}, u32[]{:S(2)}, u32[]{:S(2)}) collective-permute-start(f32[32,768]{1,0:T(8,128)S(1)} %get-tuple-element.66), channel_id=1, source_target_pairs={{0,4},{1,5},{2,6},{3,7},{4,0},{5,1},{6,2},{7,3},{8,12},{9,13},{10,... | collective-permute-start | bytes 294920 | tf_op jit(solution)/shard_map/ppermute | solution.py:23
  100.9 0.0 collective-permute-done.8.refs_1_
  100.9 1.4 %collective-permute-start.15 = (f32[32,768]{1,0:T(8,128)S(1)}, f32[32,768]{1,0:T(8,128)S(1)}, u32[]{:S(2)}, u32[]{:S(2)}) collective-permute-start(f32[32,768]{1,0:T(8,128)S(1)} %get-tuple-element.67), channel_id=1, source_target_pairs={{0,6},{1,7},{2,4},{3,5},{4,2},{5,3},{6,0},{7,1},{8,14},{9,15},{10,... | collective-permute-start | bytes 294920 | tf_op jit(solution)/shard_map/ppermute | solution.py:23
  102.4 1.3 %collective-permute-done.9.refs_2_ = f32[32,768]{1,0:T(8,128)S(1)} collective-permute-done((f32[32,768]{1,0:T(8,128)S(1)}, f32[32,768]{1,0:T(8,128)S(1)}, u32[]{:S(2)}, u32[]{:S(2)}) %collective-permute-start.9) | collective-permute-done | bytes 98336 | tf_op jit(solution)/shard_map/ppermute | solution.py:23
  103.6 1.6 %collective-permute-start.4 = (f32[16,768]{1,0:T(8,128)S(1)}, f32[16,768]{1,0:T(8,128)S(1)}, u32[]{:S(2)}, u32[]{:S(2)}) collective-permute-start(f32[16,768]{1,0:T(8,128)S(1)} %get-tuple-element.50), channel_id=1, source_target_pairs={{0,4},{1,5},{2,6},{3,7},{4,0},{5,1},{6,2},{7,3},{8,12},{9,13},{10,... | collective-permute-start | bytes 147464 | tf_op jit(solution)/shard_map/ppermute | solution.py:23
  105.3 2.8 %collective-permute-start.5 = (f32[16,768]{1,0:T(8,128)S(1)}, f32[16,768]{1,0:T(8,128)S(1)}, u32[]{:S(2)}, u32[]{:S(2)}) collective-permute-start(f32[16,768]{1,0:T(8,128)S(1)} %get-tuple-element.51), channel_id=1, source_target_pairs={{0,6},{1,7},{2,4},{3,5},{4,2},{5,3},{6,0},{7,1},{8,14},{9,15},{10,... | collective-permute-start | bytes 147464 | tf_op jit(solution)/shard_map/ppermute | solution.py:23
  108.1 0.0 collective-permute-done.13.refs_1_
  108.1 0.6 collective-permute-start.23
  108.7 0.0 collective-permute-done.14.refs_2_
  108.7 1.5 %collective-permute-start.24 = (f32[16,768]{1,0:T(8,128)S(1)}, f32[16,768]{1,0:T(8,128)S(1)}, u32[]{:S(2)}, u32[]{:S(2)}) collective-permute-start(f32[16,768]{1,0:T(8,128)S(1)} %get-tuple-element.79), channel_id=1, source_target_pairs={{0,4},{1,5},{2,6},{3,7},{4,0},{5,1},{6,2},{7,3},{8,12},{9,13},{10,... | collective-permute-start | bytes 147464 | tf_op jit(solution)/shard_map/ppermute | solution.py:23
  110.3 1.4 %collective-permute-start.25 = (f32[16,768]{1,0:T(8,128)S(1)}, f32[16,768]{1,0:T(8,128)S(1)}, u32[]{:S(2)}, u32[]{:S(2)}) collective-permute-start(f32[16,768]{1,0:T(8,128)S(1)} %get-tuple-element.80), channel_id=1, source_target_pairs={{0,6},{1,7},{2,4},{3,5},{4,2},{5,3},{6,0},{7,1},{8,14},{9,15},{10,... | collective-permute-start | bytes 147464 | tf_op jit(solution)/shard_map/ppermute | solution.py:23
  111.7 0.7 shard_map.39
  112.5 0.6 shard_map.37.refs_4_
  113.0 0.6 shard_map.38.refs_4_
  113.6 0.0 collective-permute-done.4.refs_2_
  113.6 0.0 collective-permute-done.5.refs_3_
  113.7 0.7 shard_map.40.base
  114.3 0.0 collective-permute-done.23.refs_1_
  114.3 0.9 collective-permute-done.25.refs_3_
  115.3 1.4 %shard_map.41 = f32[1,96,768]{2,1,0:T(8,128)} custom-call(s32[1,2]{1,0:T(1,128)S(1)} %copy-done, f32[96,768]{1,0:T(8,128)S(1)} %shard_map.40.base, f32[96,128]{1,0:T(8,128)S(1)} %get-tuple-element.69.refs_5_.rows, f32[1,768]{1,0:T(1,128)S(1)} %get-tuple-element.70.refs_6_.columns, bf16[128,768]{1,0:T(8,128)(2,1)S(1)} %get-tuple-element.71.spots, ...), custom_call_target="tpu_custom_call" | custom-call | flops 37748736 | bytes 936960 | tf_op jit(solution)/shard_map/pallas_call | solution.py:368
  (17 shorter events, 0.1 us)
Async XLA Ops:
  4.9 3.1 %copy-start.1 = (bf16[1792,128]{1,0:T(8,128)(2,1)}, bf16[1792,128]{1,0:T(8,128)(2,1)S(1)}, u32[]{:S(2)}) copy-start(bf16[1792,128]{1,0:T(8,128)(2,1)S(1)} %get-tuple-element.45) | copy-start | bytes 1376260
  4.9 3.1 %copy-start.2 = (bf16[1664,128]{1,0:T(8,128)(2,1)}, bf16[1664,128]{1,0:T(8,128)(2,1)S(1)}, u32[]{:S(2)}) copy-start(bf16[1664,128]{1,0:T(8,128)(2,1)S(1)} %get-tuple-element.74) | copy-start | bytes 1277956
  4.9 56.7 %collective-permute-start.6 = (bf16[1792,256]{1,0:T(8,128)(2,1)S(1)}, bf16[1792,256]{1,0:T(8,128)(2,1)S(1)}, u32[]{:S(2)}, u32[]{:S(2)}) collective-permute-start(bf16[1792,256]{1,0:T(8,128)(2,1)S(1)} %get-tuple-element.53), channel_id=1, source_target_pairs={{0,8},{8,16},{16,24},{24,0},{1,9},{9,17},{17,25},{25,1},{2,10},{10... | collective-permute-start | bytes 2752520 | tf_op jit(solution)/shard_map/ppermute | solution.py:18
  8.1 53.6 %copy-start = (s32[1,2]{1,0:T(1,128)S(1)}, s32[1,2]{1,0:T(1,128)}, u32[]{:S(2)}) copy-start(s32[1,2]{1,0:T(1,128)} %pairs.17) | copy-start | bytes 28
  8.1 55.5 %collective-permute-start.11 = (bf16[1792,256]{1,0:T(8,128)(2,1)S(1)}, bf16[1792,256]{1,0:T(8,128)(2,1)S(1)}, u32[]{:S(2)}, u32[]{:S(2)}) collective-permute-start(bf16[1792,256]{1,0:T(8,128)(2,1)S(1)} %get-tuple-element.61), channel_id=1, source_target_pairs={{0,8},{8,16},{16,24},{24,0},{1,9},{9,17},{17,25},{25,1},{2,10},{10... | collective-permute-start | bytes 2752520 | tf_op jit(solution)/shard_map/ppermute | solution.py:18
  10.6 48.7 %collective-permute-start = (bf16[256,768]{1,0:T(8,128)(2,1)S(1)}, bf16[256,768]{1,0:T(8,128)(2,1)S(1)}, u32[]{:S(2)}, u32[]{:S(2)}) collective-permute-start(bf16[256,768]{1,0:T(8,128)(2,1)S(1)} %top.1), channel_id=1, source_target_pairs={{0,8},{8,16},{16,24},{24,0},{1,9},{9,17},{17,25},{25,1},{2,10},{10... | collective-permute-start | bytes 1179656 | tf_op jit(solution)/shard_map/ppermute | solution.py:18
  12.2 57.0 %collective-permute-start.1 = (bf16[1792,128]{1,0:T(8,128)(2,1)}, bf16[1792,128]{1,0:T(8,128)(2,1)S(1)}, u32[]{:S(2)}, u32[]{:S(2)}) collective-permute-start(bf16[1792,128]{1,0:T(8,128)(2,1)} %copy-done.1), channel_id=1, source_target_pairs={{0,8},{8,16},{16,24},{24,0},{1,9},{9,17},{17,25},{25,1},{2,10},{10... | collective-permute-start | bytes 1376264 | tf_op jit(solution)/shard_map/ppermute | solution.py:18
  13.1 64.8 %collective-permute-start.21 = (bf16[1664,128]{1,0:T(8,128)(2,1)}, bf16[1664,128]{1,0:T(8,128)(2,1)S(1)}, u32[]{:S(2)}, u32[]{:S(2)}) collective-permute-start(bf16[1664,128]{1,0:T(8,128)(2,1)} %copy-done.2), channel_id=1, source_target_pairs={{0,8},{8,16},{16,24},{24,0},{1,9},{9,17},{17,25},{25,1},{2,10},{10... | collective-permute-start | bytes 1277960 | tf_op jit(solution)/shard_map/ppermute | solution.py:18
  59.4 0.7 copy-start.3
  63.5 16.3 %collective-permute-start.7 = (f32[4,32,768]{2,1,0:T(8,128)S(1)}, f32[4,32,768]{2,1,0:T(8,128)S(1)}, u32[]{:S(2)}, u32[]{:S(2)}) collective-permute-start(f32[4,32,768]{2,1,0:T(8,128)S(1)} %get-tuple-element.55), channel_id=1, source_target_pairs={{0,1},{1,0},{2,3},{3,2},{4,5},{5,4},{6,7},{7,6},{8,9},{9,8},{10,11... | collective-permute-start | bytes 1179656 | tf_op jit(solution)/shard_map/ppermute | solution.py:23
  65.4 31.9 %collective-permute-start.12 = (f32[4,32,768]{2,1,0:T(8,128)S(1)}, f32[4,32,768]{2,1,0:T(8,128)S(1)}, u32[]{:S(2)}, u32[]{:S(2)}) collective-permute-start(f32[4,32,768]{2,1,0:T(8,128)S(1)} %get-tuple-element.63), channel_id=1, source_target_pairs={{0,1},{1,0},{2,3},{3,2},{4,5},{5,4},{6,7},{7,6},{8,9},{9,8},{10,11... | collective-permute-start | bytes 1179656 | tf_op jit(solution)/shard_map/ppermute | solution.py:23
  65.9 12.8 %collective-permute-start.20 = (bf16[128,128]{1,0:T(8,128)(2,1)S(1)}, bf16[128,128]{1,0:T(8,128)(2,1)S(1)}, u32[]{:S(2)}, u32[]{:S(2)}) collective-permute-start(bf16[128,128]{1,0:T(8,128)(2,1)S(1)} %get-tuple-element.72), channel_id=1, source_target_pairs={{0,8},{8,16},{16,24},{24,0},{1,9},{9,17},{17,25},{25,1},{2,10},{10... | collective-permute-start | bytes 98312 | tf_op jit(solution)/shard_map/ppermute | solution.py:18
  70.9 10.5 %collective-permute-start.2 = (f32[4,16,768]{2,1,0:T(8,128)S(1)}, f32[4,16,768]{2,1,0:T(8,128)S(1)}, u32[]{:S(2)}, u32[]{:S(2)}) collective-permute-start(f32[4,16,768]{2,1,0:T(8,128)S(1)} %get-tuple-element.47), channel_id=1, source_target_pairs={{0,1},{1,0},{2,3},{3,2},{4,5},{5,4},{6,7},{7,6},{8,9},{9,8},{10,11... | collective-permute-start | bytes 589832 | tf_op jit(solution)/shard_map/ppermute | solution.py:23
  79.7 19.1 %collective-permute-start.22 = (f32[4,16,768]{2,1,0:T(8,128)S(1)}, f32[4,16,768]{2,1,0:T(8,128)S(1)}, u32[]{:S(2)}, u32[]{:S(2)}) collective-permute-start(f32[4,16,768]{2,1,0:T(8,128)S(1)} %get-tuple-element.76), channel_id=1, source_target_pairs={{0,1},{1,0},{2,3},{3,2},{4,5},{5,4},{6,7},{7,6},{8,9},{9,8},{10,11... | collective-permute-start | bytes 589832 | tf_op jit(solution)/shard_map/ppermute | solution.py:23
  79.8 21.1 %collective-permute-start.8 = (f32[32,768]{1,0:T(8,128)S(1)}, f32[32,768]{1,0:T(8,128)S(1)}, u32[]{:S(2)}, u32[]{:S(2)}) collective-permute-start(f32[32,768]{1,0:T(8,128)S(1)} %get-tuple-element.57), channel_id=1, source_target_pairs={{0,2},{1,3},{2,0},{3,1},{4,6},{5,7},{6,4},{7,5},{8,10},{9,11},{10,... | collective-permute-start | bytes 294920 | tf_op jit(solution)/shard_map/ppermute | solution.py:23
  81.4 18.0 %collective-permute-start.3 = (f32[16,768]{1,0:T(8,128)S(1)}, f32[16,768]{1,0:T(8,128)S(1)}, u32[]{:S(2)}, u32[]{:S(2)}) collective-permute-start(f32[16,768]{1,0:T(8,128)S(1)} %get-tuple-element.49), channel_id=1, source_target_pairs={{0,2},{1,3},{2,0},{3,1},{4,6},{5,7},{6,4},{7,5},{8,10},{9,11},{10,... | collective-permute-start | bytes 147464 | tf_op jit(solution)/shard_map/ppermute | solution.py:23
  82.0 1.2 collective-permute-start.16
  83.2 3.6 %collective-permute-start.17 = (f32[1,768]{1,0:T(1,128)S(1)}, f32[1,768]{1,0:T(1,128)S(1)}, u32[]{:S(2)}, u32[]{:S(2)}) collective-permute-start(f32[1,768]{1,0:T(1,128)S(1)} %plus.3.a), channel_id=1, source_target_pairs={{0,2},{1,3},{2,0},{3,1},{4,6},{5,7},{6,4},{7,5},{8,10},{9,11},{10,... | collective-permute-start | bytes 9224 | tf_op jit(solution)/shard_map/ppermute | solution.py:23
  86.8 3.6 %collective-permute-start.18 = (f32[1,768]{1,0:T(1,128)S(1)}, f32[1,768]{1,0:T(1,128)S(1)}, u32[]{:S(2)}, u32[]{:S(2)}) collective-permute-start(f32[1,768]{1,0:T(1,128)S(1)} %plus.4.a), channel_id=1, source_target_pairs={{0,4},{1,5},{2,6},{3,7},{4,0},{5,1},{6,2},{7,3},{8,12},{9,13},{10,... | collective-permute-start | bytes 9224 | tf_op jit(solution)/shard_map/ppermute | solution.py:23
  90.4 5.4 %collective-permute-start.19 = (f32[1,768]{1,0:T(1,128)S(1)}, f32[1,768]{1,0:T(1,128)S(1)}, u32[]{:S(2)}, u32[]{:S(2)}) collective-permute-start(f32[1,768]{1,0:T(1,128)S(1)} %plus.5.norm_own), channel_id=1, source_target_pairs={{0,8},{8,16},{16,24},{24,0},{1,9},{9,17},{17,25},{25,1},{2,10},{10... | collective-permute-start | bytes 9224 | tf_op jit(solution)/shard_map/ppermute | solution.py:18
  95.8 7.9 %collective-permute-start.9 = (f32[32,768]{1,0:T(8,128)S(1)}, f32[32,768]{1,0:T(8,128)S(1)}, u32[]{:S(2)}, u32[]{:S(2)}) collective-permute-start(f32[32,768]{1,0:T(8,128)S(1)} %get-tuple-element.58), channel_id=1, source_target_pairs={{0,4},{1,5},{2,6},{3,7},{4,0},{5,1},{6,2},{7,3},{8,12},{9,13},{10,... | collective-permute-start | bytes 294920 | tf_op jit(solution)/shard_map/ppermute | solution.py:23
  97.3 7.9 %collective-permute-start.10 = (f32[32,768]{1,0:T(8,128)S(1)}, f32[32,768]{1,0:T(8,128)S(1)}, u32[]{:S(2)}, u32[]{:S(2)}) collective-permute-start(f32[32,768]{1,0:T(8,128)S(1)} %get-tuple-element.59), channel_id=1, source_target_pairs={{0,6},{1,7},{2,4},{3,5},{4,2},{5,3},{6,0},{7,1},{8,14},{9,15},{10,... | collective-permute-start | bytes 294920 | tf_op jit(solution)/shard_map/ppermute | solution.py:23
  98.8 9.3 %collective-permute-start.13 = (f32[32,768]{1,0:T(8,128)S(1)}, f32[32,768]{1,0:T(8,128)S(1)}, u32[]{:S(2)}, u32[]{:S(2)}) collective-permute-start(f32[32,768]{1,0:T(8,128)S(1)} %get-tuple-element.65), channel_id=1, source_target_pairs={{0,2},{1,3},{2,0},{3,1},{4,6},{5,7},{6,4},{7,5},{8,10},{9,11},{10,... | collective-permute-start | bytes 294920 | tf_op jit(solution)/shard_map/ppermute | solution.py:23
  99.4 9.3 %collective-permute-start.14 = (f32[32,768]{1,0:T(8,128)S(1)}, f32[32,768]{1,0:T(8,128)S(1)}, u32[]{:S(2)}, u32[]{:S(2)}) collective-permute-start(f32[32,768]{1,0:T(8,128)S(1)} %get-tuple-element.66), channel_id=1, source_target_pairs={{0,4},{1,5},{2,6},{3,7},{4,0},{5,1},{6,2},{7,3},{8,12},{9,13},{10,... | collective-permute-start | bytes 294920 | tf_op jit(solution)/shard_map/ppermute | solution.py:23
  100.9 9.4 %collective-permute-start.15 = (f32[32,768]{1,0:T(8,128)S(1)}, f32[32,768]{1,0:T(8,128)S(1)}, u32[]{:S(2)}, u32[]{:S(2)}) collective-permute-start(f32[32,768]{1,0:T(8,128)S(1)} %get-tuple-element.67), channel_id=1, source_target_pairs={{0,6},{1,7},{2,4},{3,5},{4,2},{5,3},{6,0},{7,1},{8,14},{9,15},{10,... | collective-permute-start | bytes 294920 | tf_op jit(solution)/shard_map/ppermute | solution.py:23
  103.6 10.0 %collective-permute-start.4 = (f32[16,768]{1,0:T(8,128)S(1)}, f32[16,768]{1,0:T(8,128)S(1)}, u32[]{:S(2)}, u32[]{:S(2)}) collective-permute-start(f32[16,768]{1,0:T(8,128)S(1)} %get-tuple-element.50), channel_id=1, source_target_pairs={{0,4},{1,5},{2,6},{3,7},{4,0},{5,1},{6,2},{7,3},{8,12},{9,13},{10,... | collective-permute-start | bytes 147464 | tf_op jit(solution)/shard_map/ppermute | solution.py:23
  105.3 8.4 %collective-permute-start.5 = (f32[16,768]{1,0:T(8,128)S(1)}, f32[16,768]{1,0:T(8,128)S(1)}, u32[]{:S(2)}, u32[]{:S(2)}) collective-permute-start(f32[16,768]{1,0:T(8,128)S(1)} %get-tuple-element.51), channel_id=1, source_target_pairs={{0,6},{1,7},{2,4},{3,5},{4,2},{5,3},{6,0},{7,1},{8,14},{9,15},{10,... | collective-permute-start | bytes 147464 | tf_op jit(solution)/shard_map/ppermute | solution.py:23
  108.1 6.2 %collective-permute-start.23 = (f32[16,768]{1,0:T(8,128)S(1)}, f32[16,768]{1,0:T(8,128)S(1)}, u32[]{:S(2)}, u32[]{:S(2)}) collective-permute-start(f32[16,768]{1,0:T(8,128)S(1)} %get-tuple-element.78), channel_id=1, source_target_pairs={{0,2},{1,3},{2,0},{3,1},{4,6},{5,7},{6,4},{7,5},{8,10},{9,11},{10,... | collective-permute-start | bytes 147464 | tf_op jit(solution)/shard_map/ppermute | solution.py:23
  108.7 5.6 %collective-permute-start.24 = (f32[16,768]{1,0:T(8,128)S(1)}, f32[16,768]{1,0:T(8,128)S(1)}, u32[]{:S(2)}, u32[]{:S(2)}) collective-permute-start(f32[16,768]{1,0:T(8,128)S(1)} %get-tuple-element.79), channel_id=1, source_target_pairs={{0,4},{1,5},{2,6},{3,7},{4,0},{5,1},{6,2},{7,3},{8,12},{9,13},{10,... | collective-permute-start | bytes 147464 | tf_op jit(solution)/shard_map/ppermute | solution.py:23
  110.3 5.0 %collective-permute-start.25 = (f32[16,768]{1,0:T(8,128)S(1)}, f32[16,768]{1,0:T(8,128)S(1)}, u32[]{:S(2)}, u32[]{:S(2)}) collective-permute-start(f32[16,768]{1,0:T(8,128)S(1)} %get-tuple-element.80), channel_id=1, source_target_pairs={{0,6},{1,7},{2,4},{3,5},{4,2},{5,3},{6,0},{7,1},{8,14},{9,15},{10,... | collective-permute-start | bytes 147464 | tf_op jit(solution)/shard_map/ppermute | solution.py:23

commit v7 on v6

--- a/solution.py
+++ b/solution.py
@@ -10,7 +10,9 @@
 
 PARTS = (2, 2, 1, 1)
 HEAD = 8
-LATE = 16
+LATE = 8
+LANES = 128
+TOPS = 4
 
 
 def from_behind(value, axis, by):
@@ -291,14 +293,6 @@
     )(a, b)
 
 
-def spots_of(share, start, run, width):
-    columns = width // share * run
-    q = lax.broadcasted_iota(jnp.int32, (columns, width), 0)
-    source = lax.broadcasted_iota(jnp.int32, (columns, width), 1)
-    order = (q // run) * share + start + q % run == source
-    return order.astype(jnp.float32).astype(jnp.bfloat16)
-
-
 def placed(owner_first, share, start, run, terms, total, scales=None):
     width = total.shape[1]
     columns = width // share * run
@@ -311,20 +305,19 @@
         spread = jnp.concatenate(
             [part[:, n * columns : (n + 1) * columns] for n in range(share // run)], axis=0
         )
-        left = spread * 0.0625
-        pieces = []
-        for _ in range(3):
-            pieces.append(left.astype(jnp.bfloat16))
-            left = left - pieces[-1].astype(jnp.float32)
-        spots = jnp.dot(
-            jnp.concatenate(pieces, axis=0),
-            spots_of(share, start, run, width) if scales is None else scales[2][...],
-            preferred_element_type=jnp.float32,
-        )
-        added = (spots[:share] + spots[share : 2 * share] + spots[2 * share :]) * 16.0
-        if scales is not None:
-            added = added * scales[0][:, :1] * scales[1][...]
-        total[...] += added
+        lane = lax.broadcasted_iota(jnp.int32, (share, LANES), 1)
+        for strip in range(width // share):
+            source, target = strip * run, strip * share + start
+            piece = spread[:, source // LANES * LANES : (source // LANES + 1) * LANES]
+            shift = (target - source) % LANES
+            if shift:
+                piece = pltpu.roll(piece, shift, 1)
+            tile = slice(target // LANES * LANES, (target // LANES + 1) * LANES)
+            if scales is not None:
+                piece = piece * scales[0][:, :1] * scales[1][:, tile]
+            first = target % LANES
+            inside = (lane >= first) & (lane < first + run)
+            total[:, tile] = jnp.where(inside, piece, total[:, tile])
 
     @pl.when(jnp.logical_not(owner_first))
     def _():
@@ -343,7 +336,7 @@
         total[...] = total[...] * refs[5][:, :1] * refs[6][...]
 
 
-def scales_kernel(share, start, run, pairs, norm_own, norm_low, rows, columns, spots):
+def scales_kernel(share, pairs, norm_own, norm_low, rows, columns):
     width = columns.shape[1]
     owner_first = pairs[0, 0] == lax.axis_index("src")
     scale_own = lax.rsqrt(norm_own[...] + 1e-06)
@@ -354,14 +347,13 @@
     mine = jnp.sum(jnp.where(row == column, scale_first, 0.0), axis=1, keepdims=True)
     rows[...] = jnp.broadcast_to(mine, rows.shape)
     columns[...] = jnp.where(owner_first, scale_low, scale_own)
-    spots[...] = spots_of(share, start, run, width)
-
-
-def finish_kernel(share, start, run, pairs, base, rows, columns, spots, *refs):
+
+
+def finish_kernel(share, start, run, pairs, base, rows, columns, *refs):
     *terms, out = refs
     owner_first = pairs[0, 0] == lax.axis_index("src")
     out[0] = base[...]
-    placed(owner_first, share, start, run, terms, out.at[0], (rows, columns, spots))
+    placed(owner_first, share, start, run, terms, out.at[0], (rows, columns))
 
 
 def small_call(kernel, out_shape, pairs, given, flops):
@@ -382,7 +374,7 @@
 
 def place(pairs, terms, base, scales, share, width, start, run):
     given = [] if base is None else [base]
-    given += list(scales[:2])
+    given += list(scales)
     return small_call(
         functools.partial(place_kernel, share, start, run, len(given)),
         pltpu.VMEM((share, width), jnp.float32),
@@ -392,14 +384,13 @@
     )
 
 
-def scales_of(pairs, norm_own, norm_low, share, start, run):
+def scales_of(pairs, norm_own, norm_low, share):
     width = norm_own.shape[1]
     return small_call(
-        functools.partial(scales_kernel, share, start, run),
+        functools.partial(scales_kernel, share),
         (
-            pltpu.VMEM((share, 128), jnp.float32),
+            pltpu.VMEM((share, LANES), jnp.float32),
             pltpu.VMEM((1, width), jnp.float32),
-            pltpu.VMEM((width // share * run, width), jnp.bfloat16),
         ),
         pairs,
         [norm_own, norm_low],
@@ -417,8 +408,18 @@
     )
 
 
-def top_kernel(block, out):
-    pltpu.sync_copy(block.at[pl.ds(0, out.shape[0])], out)
+def top_kernel(block, out, sems):
+    step = out.shape[0] // TOPS
+    copies = [
+        pltpu.make_async_copy(
+            block.at[pl.ds(n * step, step)], out.at[pl.ds(n * step, step)], sems.at[n]
+        )
+        for n in range(TOPS)
+    ]
+    for copy in copies:
+        copy.start()
+    for copy in copies:
+        copy.wait()
 
 
 def top_of(block, rows):
@@ -427,6 +428,7 @@
         out_shape=pltpu.VMEM((rows,) + block.shape[1:], block.dtype),
         in_specs=[pl.BlockSpec(memory_space=pltpu.HBM)],
         out_specs=pl.BlockSpec(memory_space=pltpu.VMEM),
+        scratch_shapes=[pltpu.SemaphoreType.DMA((TOPS,))],
         compiler_params=pltpu.CompilerParams(vmem_limit_bytes=60 << 20),
         name="top",
     )(block)
@@ -437,7 +439,12 @@
     groups = lax.axis_size("tm")
     share = width // groups
     runs = runs_of(share)
-    aligned = groups == 8 and all(run % 8 == 0 and groups * run % 128 == 0 for _, run in runs)
+    aligned = groups == 8 and all(
+        run % 8 == 0
+        and groups * run % LANES == 0
+        and LANES % run == share % run == start % run == 0
+        for start, run in runs
+    )
     cut = rows_dev // HEAD
 
     head = from_behind(top_of(greens, cut), "src", 1)
@@ -455,7 +462,7 @@
     if not aligned:
         return plain_tail(pairs, own, heads, lower, norm_own[0], norm_low[0], share, runs)
 
-    scales = scales_of(pairs, norm_own, norm_low, share, *runs[-1])
+    scales = scales_of(pairs, norm_own, norm_low, share)
     base = None
     for step, (run, top) in enumerate(zip(runs, heads)):
         if step < len(runs) - 1:

time: 117 us -> 117 us (level)
  no operation moved by 1% of the time
where the time goes in v7:
time: 117 us
  waiting for transfers between devices  64.4 us (55%)
  starting transfers between devices  28.6 us (24%)
  Pallas kernels  22.4 us (19%)
  local copies, waits for them, and re-layouts  1.52 us (1%)
    ppermute x7, waiting for transfers between devices, from_behind(): lax.ppermute(value, axis, [(i, (i + by) % length) for i in range(length)])  56.8 us
    ppermute x19, starting transfers between devices, swapped(): return lax.ppermute(value, axis, [(i, i ^ bits) for i in range(length)])  20.5 us
    ppermute x7, starting transfers between devices, from_behind(): lax.ppermute(value, axis, [(i, (i + by) % length) for i in range(length)])  8.06 us
    ppermute x19, waiting for transfers between devices, swapped(): return lax.ppermute(value, axis, [(i, i ^ bits) for i in range(length)])  7.65 us
    pallas_call x2, Pallas kernels, picks(): pl.pallas_call(functools.partial(picks_kernel, share, pieces), out_shape=...  6.49 us
    pallas_call x4, Pallas kernels, gram(): pl.pallas_call(functools.partial(gram_kernel, share, run, ranges), out_sh...  6.21 us
    pallas_call x5, Pallas kernels, small_call(): pl.pallas_call(kernel, out_shape=out_shape, in_specs=[pl.BlockSpec(memory...  3.84 us
    pallas_call x1, Pallas kernels, turn(): pl.pallas_call(functools.partial(turn_kernel, step), out_shape=(pltpu.VME...  3.79 us
  transfers between devices with their start and end apart: 26, of which 9 were waited for; matrix products, arithmetic and copies ran while one was open for 0% of the time, Pallas kernels for 14%

profile of v7, /device:TPU:0, one launch (start us, length us, event | category | flops | bytes accessed | tf_op | source)
XLA Modules:
  0.0 117.2 jit_solution(1148486966969342999)
XLA Ops:
  0.0 4.9 %picks.3 = (bf16[1792,256]{1,0:T(8,128)(2,1)S(1)}, bf16[1792,256]{1,0:T(8,128)(2,1)}, bf16[1792,128]{1,0:T(8,128)(2,1)S(1)}, bf16[1536,128]{1,0:T(8,128)(2,1)S(1)}, bf16[256,128]{1,0:T(8,128)(2,1)S(1)}) custom-call(bf16[2048,768]{1,0:T(8,128)(2,1)} %block.5), custom_call_target="tpu_custom_call" | custom-call | flops 2415919104 | bytes 6291456 | tf_op jit(solution)/shard_map/picks/pallas_call | solution.py:91
  4.9 0.7 copy-done.1
  5.7 3.1 %collective-permute-start.6 = (bf16[1792,256]{1,0:T(8,128)(2,1)}, bf16[1792,256]{1,0:T(8,128)(2,1)S(1)}, u32[]{:S(2)}, u32[]{:S(2)}) collective-permute-start(bf16[1792,256]{1,0:T(8,128)(2,1)} %get-tuple-element.52), channel_id=1, source_target_pairs={{0,8},{8,16},{16,24},{24,0},{1,9},{9,17},{17,25},{25,1},{2,10},{10... | collective-permute-start | bytes 2752520 | tf_op jit(solution)/shard_map/ppermute | solution.py:20
  8.7 1.6 %collective-permute-start.11 = (bf16[1792,256]{1,0:T(8,128)(2,1)S(1)}, bf16[1792,256]{1,0:T(8,128)(2,1)S(1)}, u32[]{:S(2)}, u32[]{:S(2)}) collective-permute-start(bf16[1792,256]{1,0:T(8,128)(2,1)S(1)} %get-tuple-element.60), channel_id=1, source_target_pairs={{0,8},{8,16},{16,24},{24,0},{1,9},{9,17},{17,25},{25,1},{2,10},{10... | collective-permute-start | bytes 2752520 | tf_op jit(solution)/shard_map/ppermute | solution.py:20
  10.3 1.1 top.1
  11.4 1.6 %collective-permute-start = (bf16[256,768]{1,0:T(8,128)(2,1)S(1)}, bf16[256,768]{1,0:T(8,128)(2,1)S(1)}, u32[]{:S(2)}, u32[]{:S(2)}) collective-permute-start(bf16[256,768]{1,0:T(8,128)(2,1)S(1)} %top.1), channel_id=1, source_target_pairs={{0,8},{8,16},{16,24},{24,0},{1,9},{9,17},{17,25},{25,1},{2,10},{10... | collective-permute-start | bytes 1179656 | tf_op jit(solution)/shard_map/ppermute | solution.py:20
  13.0 0.1 collective-permute-start.1
  13.1 1.7 %collective-permute-start.21 = (bf16[1536,128]{1,0:T(8,128)(2,1)}, bf16[1536,128]{1,0:T(8,128)(2,1)S(1)}, u32[]{:S(2)}, u32[]{:S(2)}) collective-permute-start(bf16[1536,128]{1,0:T(8,128)(2,1)} %copy-done.1), channel_id=1, source_target_pairs={{0,8},{8,16},{16,24},{24,0},{1,9},{9,17},{17,25},{25,1},{2,10},{10... | collective-permute-start | bytes 1179656 | tf_op jit(solution)/shard_map/ppermute | solution.py:20
  14.8 3.8 %turn.1 = (bf16[768,2048]{1,0:T(8,128)(2,1)S(1)}, f32[1,768]{1,0:T(1,128)S(1)}) custom-call(s32[4]{0:T(128)} %onsets.1, bf16[2048,768]{1,0:T(8,128)(2,1)} %block.5), custom_call_target="tpu_custom_call" | custom-call | flops 6291456 | bytes 6291456 | tf_op jit(solution)/shard_map/turn/pallas_call | solution.py:129
  18.6 41.6 %collective-permute-done.block = bf16[256,768]{1,0:T(8,128)(2,1)S(1)} collective-permute-done((bf16[256,768]{1,0:T(8,128)(2,1)S(1)}, bf16[256,768]{1,0:T(8,128)(2,1)S(1)}, u32[]{:S(2)}, u32[]{:S(2)}) %collective-permute-start) | collective-permute-done | bytes 393248 | tf_op jit(solution)/shard_map/ppermute | solution.py:20
  60.2 0.8 copy-done.2
  61.0 1.6 %picks.2 = (bf16[256,256]{1,0:T(8,128)(2,1)S(1)}, bf16[256,256]{1,0:T(8,128)(2,1)S(1)}, bf16[256,128]{1,0:T(8,128)(2,1)S(1)}, bf16[256,128]{1,0:T(8,128)(2,1)S(1)}) custom-call(bf16[256,768]{1,0:T(8,128)(2,1)} %copy-done.2), custom_call_target="tpu_custom_call" | custom-call | flops 301989888 | bytes 786432 | tf_op jit(solution)/shard_map/picks/pallas_call | solution.py:91
  62.6 0.0 collective-permute-done.6.refs_1_
  62.6 1.8 %gram.5 = (f32[4,32,768]{2,1,0:T(8,128)S(1)}, f32[4,32,768]{2,1,0:T(8,128)S(1)}) custom-call(s32[1,2]{1,0:T(1,128)S(1)} %copy-done, bf16[768,2048]{1,0:T(8,128)(2,1)S(1)} %get-tuple-element.42.own, bf16[256,256]{1,0:T(8,128)(2,1)S(1)} %get-tuple-element.51.refs_0_, bf16[1792,256]{1,0:T(8,128)(2,1)S(1)} %collective-permute-done.6.refs_1_), custom_call_target="tpu_custom_call" | custom-call | flops 805306368 | bytes 3145728 | tf_op jit(solution)/shard_map/gram/pallas_call | solution.py:210
  64.4 0.1 collective-permute-start.7
  64.5 0.0 collective-permute-done.11.refs_1_
  64.5 1.8 %gram.6 = (f32[4,32,768]{2,1,0:T(8,128)S(1)}, f32[4,32,768]{2,1,0:T(8,128)S(1)}) custom-call(s32[1,2]{1,0:T(1,128)S(1)} %copy-done, bf16[768,2048]{1,0:T(8,128)(2,1)S(1)} %get-tuple-element.42.own, bf16[256,256]{1,0:T(8,128)(2,1)S(1)} %get-tuple-element.59.refs_0_, bf16[1792,256]{1,0:T(8,128)(2,1)S(1)} %collective-permute-done.11.refs_1_), custom_call_target="tpu_custom_call" | custom-call | flops 805306368 | bytes 3145728 | tf_op jit(solution)/shard_map/gram/pallas_call | solution.py:210
  66.3 0.6 collective-permute-start.12
  66.9 0.0 collective-permute-start.20
  66.9 3.2 %collective-permute-done.1.refs_1_ = bf16[1792,128]{1,0:T(8,128)(2,1)S(1)} collective-permute-done((bf16[1792,128]{1,0:T(8,128)(2,1)S(1)}, bf16[1792,128]{1,0:T(8,128)(2,1)S(1)}, u32[]{:S(2)}, u32[]{:S(2)}) %collective-permute-start.1) | collective-permute-done | bytes 458784 | tf_op jit(solution)/shard_map/ppermute | solution.py:20
  70.1 1.7 %gram.4 = (f32[4,16,768]{2,1,0:T(8,128)S(1)}, f32[4,16,768]{2,1,0:T(8,128)S(1)}) custom-call(s32[1,2]{1,0:T(1,128)S(1)} %copy-done, bf16[768,2048]{1,0:T(8,128)(2,1)S(1)} %get-tuple-element.42.own, bf16[256,128]{1,0:T(8,128)(2,1)S(1)} %get-tuple-element.43.refs_0_, bf16[1792,128]{1,0:T(8,128)(2,1)S(1)} %collective-permute-done.1.refs_1_), custom_call_target="tpu_custom_call" | custom-call | flops 402653184 | bytes 3145728 | tf_op jit(solution)/shard_map/gram/pallas_call | solution.py:210
  71.8 0.1 collective-permute-start.2
  71.8 6.5 %collective-permute-done.21.refs_1_ = bf16[1536,128]{1,0:T(8,128)(2,1)S(1)} collective-permute-done((bf16[1536,128]{1,0:T(8,128)(2,1)}, bf16[1536,128]{1,0:T(8,128)(2,1)S(1)}, u32[]{:S(2)}, u32[]{:S(2)}) %collective-permute-start.21) | collective-permute-done | bytes 393248 | tf_op jit(solution)/shard_map/ppermute | solution.py:20
  78.3 0.9 early.1.refs_1_
  79.2 0.0 collective-permute-done.20.refs_0_
  79.2 1.0 gram.7
  80.2 0.1 collective-permute-start.22
  80.3 0.0 collective-permute-done.7.arrived
  80.3 0.1 fold.5
  80.4 1.6 %collective-permute-start.8 = (f32[32,768]{1,0:T(8,128)S(1)}, f32[32,768]{1,0:T(8,128)S(1)}, u32[]{:S(2)}, u32[]{:S(2)}) collective-permute-start(f32[32,768]{1,0:T(8,128)S(1)} %get-tuple-element.56), channel_id=1, source_target_pairs={{0,2},{1,3},{2,0},{3,1},{4,6},{5,7},{6,4},{7,5},{8,10},{9,11},{10,... | collective-permute-start | bytes 294920 | tf_op jit(solution)/shard_map/ppermute | solution.py:25
  81.9 0.0 collective-permute-done.2.arrived
  81.9 0.6 collective-permute-start.3
  82.6 1.2 collective-permute-done.16.b
  83.7 1.5 %collective-permute-start.17 = (f32[1,768]{1,0:T(1,128)S(1)}, f32[1,768]{1,0:T(1,128)S(1)}, u32[]{:S(2)}, u32[]{:S(2)}) collective-permute-start(f32[1,768]{1,0:T(1,128)S(1)} %plus.3.a), channel_id=1, source_target_pairs={{0,2},{1,3},{2,0},{3,1},{4,6},{5,7},{6,4},{7,5},{8,10},{9,11},{10,... | collective-permute-start | bytes 9224 | tf_op jit(solution)/shard_map/ppermute | solution.py:25
  85.2 2.1 %collective-permute-done.17.b = f32[1,768]{1,0:T(1,128)S(1)} collective-permute-done((f32[1,768]{1,0:T(1,128)S(1)}, f32[1,768]{1,0:T(1,128)S(1)}, u32[]{:S(2)}, u32[]{:S(2)}) %collective-permute-start.17) | collective-permute-done | bytes 3104 | tf_op jit(solution)/shard_map/ppermute | solution.py:25
  87.3 1.5 %collective-permute-start.18 = (f32[1,768]{1,0:T(1,128)S(1)}, f32[1,768]{1,0:T(1,128)S(1)}, u32[]{:S(2)}, u32[]{:S(2)}) collective-permute-start(f32[1,768]{1,0:T(1,128)S(1)} %plus.4.a), channel_id=1, source_target_pairs={{0,4},{1,5},{2,6},{3,7},{4,0},{5,1},{6,2},{7,3},{8,12},{9,13},{10,... | collective-permute-start | bytes 9224 | tf_op jit(solution)/shard_map/ppermute | solution.py:25
  88.8 2.1 %collective-permute-done.18.b = f32[1,768]{1,0:T(1,128)S(1)} collective-permute-done((f32[1,768]{1,0:T(1,128)S(1)}, f32[1,768]{1,0:T(1,128)S(1)}, u32[]{:S(2)}, u32[]{:S(2)}) %collective-permute-start.18) | collective-permute-done | bytes 3104 | tf_op jit(solution)/shard_map/ppermute | solution.py:25
  90.9 0.0 collective-permute-start.19
  90.9 5.4 %collective-permute-done.19.norm_low = f32[1,768]{1,0:T(1,128)S(1)} collective-permute-done((f32[1,768]{1,0:T(1,128)S(1)}, f32[1,768]{1,0:T(1,128)S(1)}, u32[]{:S(2)}, u32[]{:S(2)}) %collective-permute-start.19) | collective-permute-done | bytes 3104 | tf_op jit(solution)/shard_map/ppermute | solution.py:20
  96.3 1.5 %collective-permute-start.9 = (f32[32,768]{1,0:T(8,128)S(1)}, f32[32,768]{1,0:T(8,128)S(1)}, u32[]{:S(2)}, u32[]{:S(2)}) collective-permute-start(f32[32,768]{1,0:T(8,128)S(1)} %get-tuple-element.57), channel_id=1, source_target_pairs={{0,4},{1,5},{2,6},{3,7},{4,0},{5,1},{6,2},{7,3},{8,12},{9,13},{10,... | collective-permute-start | bytes 294920 | tf_op jit(solution)/shard_map/ppermute | solution.py:25
  97.8 1.4 %collective-permute-start.10 = (f32[32,768]{1,0:T(8,128)S(1)}, f32[32,768]{1,0:T(8,128)S(1)}, u32[]{:S(2)}, u32[]{:S(2)}) collective-permute-start(f32[32,768]{1,0:T(8,128)S(1)} %get-tuple-element.58), channel_id=1, source_target_pairs={{0,6},{1,7},{2,4},{3,5},{4,2},{5,3},{6,0},{7,1},{8,14},{9,15},{10,... | collective-permute-start | bytes 294920 | tf_op jit(solution)/shard_map/ppermute | solution.py:25
  99.3 0.0 collective-permute-done.22.arrived
  99.3 0.6 collective-permute-start.13
  99.9 0.0 collective-permute-done.3.refs_1_
  99.9 1.5 %collective-permute-start.14 = (f32[32,768]{1,0:T(8,128)S(1)}, f32[32,768]{1,0:T(8,128)S(1)}, u32[]{:S(2)}, u32[]{:S(2)}) collective-permute-start(f32[32,768]{1,0:T(8,128)S(1)} %get-tuple-element.65), channel_id=1, source_target_pairs={{0,4},{1,5},{2,6},{3,7},{4,0},{5,1},{6,2},{7,3},{8,12},{9,13},{10,... | collective-permute-start | bytes 294920 | tf_op jit(solution)/shard_map/ppermute | solution.py:25
  101.5 0.0 collective-permute-done.8.refs_1_
  101.5 1.4 %collective-permute-start.15 = (f32[32,768]{1,0:T(8,128)S(1)}, f32[32,768]{1,0:T(8,128)S(1)}, u32[]{:S(2)}, u32[]{:S(2)}) collective-permute-start(f32[32,768]{1,0:T(8,128)S(1)} %get-tuple-element.66), channel_id=1, source_target_pairs={{0,6},{1,7},{2,4},{3,5},{4,2},{5,3},{6,0},{7,1},{8,14},{9,15},{10,... | collective-permute-start | bytes 294920 | tf_op jit(solution)/shard_map/ppermute | solution.py:25
  102.9 1.3 %collective-permute-done.9.refs_2_ = f32[32,768]{1,0:T(8,128)S(1)} collective-permute-done((f32[32,768]{1,0:T(8,128)S(1)}, f32[32,768]{1,0:T(8,128)S(1)}, u32[]{:S(2)}, u32[]{:S(2)}) %collective-permute-start.9) | collective-permute-done | bytes 98336 | tf_op jit(solution)/shard_map/ppermute | solution.py:25
  104.2 1.6 %collective-permute-start.4 = (f32[16,768]{1,0:T(8,128)S(1)}, f32[16,768]{1,0:T(8,128)S(1)}, u32[]{:S(2)}, u32[]{:S(2)}) collective-permute-start(f32[16,768]{1,0:T(8,128)S(1)} %get-tuple-element.49), channel_id=1, source_target_pairs={{0,4},{1,5},{2,6},{3,7},{4,0},{5,1},{6,2},{7,3},{8,12},{9,13},{10,... | collective-permute-start | bytes 147464 | tf_op jit(solution)/shard_map/ppermute | solution.py:25
  105.8 2.8 %collective-permute-start.5 = (f32[16,768]{1,0:T(8,128)S(1)}, f32[16,768]{1,0:T(8,128)S(1)}, u32[]{:S(2)}, u32[]{:S(2)}) collective-permute-start(f32[16,768]{1,0:T(8,128)S(1)} %get-tuple-element.50), channel_id=1, source_target_pairs={{0,6},{1,7},{2,4},{3,5},{4,2},{5,3},{6,0},{7,1},{8,14},{9,15},{10,... | collective-permute-start | bytes 147464 | tf_op jit(solution)/shard_map/ppermute | solution.py:25
  108.6 0.0 collective-permute-done.13.refs_1_
  108.6 0.6 collective-permute-start.23
  109.3 0.0 collective-permute-done.14.refs_2_
  109.3 1.5 %collective-permute-start.24 = (f32[16,768]{1,0:T(8,128)S(1)}, f32[16,768]{1,0:T(8,128)S(1)}, u32[]{:S(2)}, u32[]{:S(2)}) collective-permute-start(f32[16,768]{1,0:T(8,128)S(1)} %get-tuple-element.77), channel_id=1, source_target_pairs={{0,4},{1,5},{2,6},{3,7},{4,0},{5,1},{6,2},{7,3},{8,12},{9,13},{10,... | collective-permute-start | bytes 147464 | tf_op jit(solution)/shard_map/ppermute | solution.py:25
  110.8 1.4 %collective-permute-start.25 = (f32[16,768]{1,0:T(8,128)S(1)}, f32[16,768]{1,0:T(8,128)S(1)}, u32[]{:S(2)}, u32[]{:S(2)}) collective-permute-start(f32[16,768]{1,0:T(8,128)S(1)} %get-tuple-element.78), channel_id=1, source_target_pairs={{0,6},{1,7},{2,4},{3,5},{4,2},{5,3},{6,0},{7,1},{8,14},{9,15},{10,... | collective-permute-start | bytes 147464 | tf_op jit(solution)/shard_map/ppermute | solution.py:25
  112.3 0.7 shard_map.39
  112.9 0.6 shard_map.37.refs_4_
  113.5 0.6 shard_map.38.refs_4_
  114.1 0.0 collective-permute-done.4.refs_2_
  114.1 0.7 shard_map.40.base
  114.8 0.0 collective-permute-done.23.refs_1_
  114.8 0.0 collective-permute-done.24.refs_2_
  114.8 1.0 collective-permute-done.25.refs_3_
  115.8 1.4 %shard_map.41 = f32[1,96,768]{2,1,0:T(8,128)} custom-call(s32[1,2]{1,0:T(1,128)S(1)} %copy-done, f32[96,768]{1,0:T(8,128)S(1)} %shard_map.40.base, f32[96,128]{1,0:T(8,128)S(1)} %get-tuple-element.68.refs_5_.rows, f32[1,768]{1,0:T(1,128)S(1)} %get-tuple-element.69.refs_6_.columns, f32[16,768]{1,0:T(8,128)S(1)} %get-tuple-element.75.refs_0_, ...), custom_call_target="tpu_custom_call" | custom-call | flops 37748736 | bytes 543744 | tf_op jit(solution)/shard_map/pallas_call | solution.py:360
  (15 shorter events, 0.1 us)
Async XLA Ops:
  4.9 0.7 copy-start.1
  5.7 56.9 %collective-permute-start.6 = (bf16[1792,256]{1,0:T(8,128)(2,1)}, bf16[1792,256]{1,0:T(8,128)(2,1)S(1)}, u32[]{:S(2)}, u32[]{:S(2)}) collective-permute-start(bf16[1792,256]{1,0:T(8,128)(2,1)} %get-tuple-element.52), channel_id=1, source_target_pairs={{0,8},{8,16},{16,24},{24,0},{1,9},{9,17},{17,25},{25,1},{2,10},{10... | collective-permute-start | bytes 2752520 | tf_op jit(solution)/shard_map/ppermute | solution.py:20
  8.7 53.9 %copy-start = (s32[1,2]{1,0:T(1,128)S(1)}, s32[1,2]{1,0:T(1,128)}, u32[]{:S(2)}) copy-start(s32[1,2]{1,0:T(1,128)} %pairs.17) | copy-start | bytes 28
  8.7 55.8 %collective-permute-start.11 = (bf16[1792,256]{1,0:T(8,128)(2,1)S(1)}, bf16[1792,256]{1,0:T(8,128)(2,1)S(1)}, u32[]{:S(2)}, u32[]{:S(2)}) collective-permute-start(bf16[1792,256]{1,0:T(8,128)(2,1)S(1)} %get-tuple-element.60), channel_id=1, source_target_pairs={{0,8},{8,16},{16,24},{24,0},{1,9},{9,17},{17,25},{25,1},{2,10},{10... | collective-permute-start | bytes 2752520 | tf_op jit(solution)/shard_map/ppermute | solution.py:20
  11.4 48.9 %collective-permute-start = (bf16[256,768]{1,0:T(8,128)(2,1)S(1)}, bf16[256,768]{1,0:T(8,128)(2,1)S(1)}, u32[]{:S(2)}, u32[]{:S(2)}) collective-permute-start(bf16[256,768]{1,0:T(8,128)(2,1)S(1)} %top.1), channel_id=1, source_target_pairs={{0,8},{8,16},{16,24},{24,0},{1,9},{9,17},{17,25},{25,1},{2,10},{10... | collective-permute-start | bytes 1179656 | tf_op jit(solution)/shard_map/ppermute | solution.py:20
  13.0 57.1 %collective-permute-start.1 = (bf16[1792,128]{1,0:T(8,128)(2,1)S(1)}, bf16[1792,128]{1,0:T(8,128)(2,1)S(1)}, u32[]{:S(2)}, u32[]{:S(2)}) collective-permute-start(bf16[1792,128]{1,0:T(8,128)(2,1)S(1)} %get-tuple-element.44), channel_id=1, source_target_pairs={{0,8},{8,16},{16,24},{24,0},{1,9},{9,17},{17,25},{25,1},{2,10},{10... | collective-permute-start | bytes 1376264 | tf_op jit(solution)/shard_map/ppermute | solution.py:20
  13.1 65.3 %collective-permute-start.21 = (bf16[1536,128]{1,0:T(8,128)(2,1)}, bf16[1536,128]{1,0:T(8,128)(2,1)S(1)}, u32[]{:S(2)}, u32[]{:S(2)}) collective-permute-start(bf16[1536,128]{1,0:T(8,128)(2,1)} %copy-done.1), channel_id=1, source_target_pairs={{0,8},{8,16},{16,24},{24,0},{1,9},{9,17},{17,25},{25,1},{2,10},{10... | collective-permute-start | bytes 1179656 | tf_op jit(solution)/shard_map/ppermute | solution.py:20
  60.2 0.8 copy-start.2
  64.4 15.9 %collective-permute-start.7 = (f32[4,32,768]{2,1,0:T(8,128)S(1)}, f32[4,32,768]{2,1,0:T(8,128)S(1)}, u32[]{:S(2)}, u32[]{:S(2)}) collective-permute-start(f32[4,32,768]{2,1,0:T(8,128)S(1)} %get-tuple-element.54), channel_id=1, source_target_pairs={{0,1},{1,0},{2,3},{3,2},{4,5},{5,4},{6,7},{7,6},{8,9},{9,8},{10,11... | collective-permute-start | bytes 1179656 | tf_op jit(solution)/shard_map/ppermute | solution.py:25
  66.3 31.5 %collective-permute-start.12 = (f32[4,32,768]{2,1,0:T(8,128)S(1)}, f32[4,32,768]{2,1,0:T(8,128)S(1)}, u32[]{:S(2)}, u32[]{:S(2)}) collective-permute-start(f32[4,32,768]{2,1,0:T(8,128)S(1)} %get-tuple-element.62), channel_id=1, source_target_pairs={{0,1},{1,0},{2,3},{3,2},{4,5},{5,4},{6,7},{7,6},{8,9},{9,8},{10,11... | collective-permute-start | bytes 1179656 | tf_op jit(solution)/shard_map/ppermute | solution.py:25
  66.9 12.4 %collective-permute-start.20 = (bf16[256,128]{1,0:T(8,128)(2,1)S(1)}, bf16[256,128]{1,0:T(8,128)(2,1)S(1)}, u32[]{:S(2)}, u32[]{:S(2)}) collective-permute-start(bf16[256,128]{1,0:T(8,128)(2,1)S(1)} %get-tuple-element.70), channel_id=1, source_target_pairs={{0,8},{8,16},{16,24},{24,0},{1,9},{9,17},{17,25},{25,1},{2,10},{10... | collective-permute-start | bytes 196616 | tf_op jit(solution)/shard_map/ppermute | solution.py:20
  71.8 10.2 %collective-permute-start.2 = (f32[4,16,768]{2,1,0:T(8,128)S(1)}, f32[4,16,768]{2,1,0:T(8,128)S(1)}, u32[]{:S(2)}, u32[]{:S(2)}) collective-permute-start(f32[4,16,768]{2,1,0:T(8,128)S(1)} %get-tuple-element.46), channel_id=1, source_target_pairs={{0,1},{1,0},{2,3},{3,2},{4,5},{5,4},{6,7},{7,6},{8,9},{9,8},{10,11... | collective-permute-start | bytes 589832 | tf_op jit(solution)/shard_map/ppermute | solution.py:25
  80.2 19.1 %collective-permute-start.22 = (f32[4,16,768]{2,1,0:T(8,128)S(1)}, f32[4,16,768]{2,1,0:T(8,128)S(1)}, u32[]{:S(2)}, u32[]{:S(2)}) collective-permute-start(f32[4,16,768]{2,1,0:T(8,128)S(1)} %get-tuple-element.74), channel_id=1, source_target_pairs={{0,1},{1,0},{2,3},{3,2},{4,5},{5,4},{6,7},{7,6},{8,9},{9,8},{10,11... | collective-permute-start | bytes 589832 | tf_op jit(solution)/shard_map/ppermute | solution.py:25
  80.4 21.1 %collective-permute-start.8 = (f32[32,768]{1,0:T(8,128)S(1)}, f32[32,768]{1,0:T(8,128)S(1)}, u32[]{:S(2)}, u32[]{:S(2)}) collective-permute-start(f32[32,768]{1,0:T(8,128)S(1)} %get-tuple-element.56), channel_id=1, source_target_pairs={{0,2},{1,3},{2,0},{3,1},{4,6},{5,7},{6,4},{7,5},{8,10},{9,11},{10,... | collective-permute-start | bytes 294920 | tf_op jit(solution)/shard_map/ppermute | solution.py:25
  81.9 18.0 %collective-permute-start.3 = (f32[16,768]{1,0:T(8,128)S(1)}, f32[16,768]{1,0:T(8,128)S(1)}, u32[]{:S(2)}, u32[]{:S(2)}) collective-permute-start(f32[16,768]{1,0:T(8,128)S(1)} %get-tuple-element.48), channel_id=1, source_target_pairs={{0,2},{1,3},{2,0},{3,1},{4,6},{5,7},{6,4},{7,5},{8,10},{9,11},{10,... | collective-permute-start | bytes 147464 | tf_op jit(solution)/shard_map/ppermute | solution.py:25
  82.6 1.2 collective-permute-start.16
  83.7 3.6 %collective-permute-start.17 = (f32[1,768]{1,0:T(1,128)S(1)}, f32[1,768]{1,0:T(1,128)S(1)}, u32[]{:S(2)}, u32[]{:S(2)}) collective-permute-start(f32[1,768]{1,0:T(1,128)S(1)} %plus.3.a), channel_id=1, source_target_pairs={{0,2},{1,3},{2,0},{3,1},{4,6},{5,7},{6,4},{7,5},{8,10},{9,11},{10,... | collective-permute-start | bytes 9224 | tf_op jit(solution)/shard_map/ppermute | solution.py:25
  87.3 3.6 %collective-permute-start.18 = (f32[1,768]{1,0:T(1,128)S(1)}, f32[1,768]{1,0:T(1,128)S(1)}, u32[]{:S(2)}, u32[]{:S(2)}) collective-permute-start(f32[1,768]{1,0:T(1,128)S(1)} %plus.4.a), channel_id=1, source_target_pairs={{0,4},{1,5},{2,6},{3,7},{4,0},{5,1},{6,2},{7,3},{8,12},{9,13},{10,... | collective-permute-start | bytes 9224 | tf_op jit(solution)/shard_map/ppermute | solution.py:25
  90.9 5.4 %collective-permute-start.19 = (f32[1,768]{1,0:T(1,128)S(1)}, f32[1,768]{1,0:T(1,128)S(1)}, u32[]{:S(2)}, u32[]{:S(2)}) collective-permute-start(f32[1,768]{1,0:T(1,128)S(1)} %plus.5.norm_own), channel_id=1, source_target_pairs={{0,8},{8,16},{16,24},{24,0},{1,9},{9,17},{17,25},{25,1},{2,10},{10... | collective-permute-start | bytes 9224 | tf_op jit(solution)/shard_map/ppermute | solution.py:20
  96.3 7.9 %collective-permute-start.9 = (f32[32,768]{1,0:T(8,128)S(1)}, f32[32,768]{1,0:T(8,128)S(1)}, u32[]{:S(2)}, u32[]{:S(2)}) collective-permute-start(f32[32,768]{1,0:T(8,128)S(1)} %get-tuple-element.57), channel_id=1, source_target_pairs={{0,4},{1,5},{2,6},{3,7},{4,0},{5,1},{6,2},{7,3},{8,12},{9,13},{10,... | collective-permute-start | bytes 294920 | tf_op jit(solution)/shard_map/ppermute | solution.py:25
  97.8 7.9 %collective-permute-start.10 = (f32[32,768]{1,0:T(8,128)S(1)}, f32[32,768]{1,0:T(8,128)S(1)}, u32[]{:S(2)}, u32[]{:S(2)}) collective-permute-start(f32[32,768]{1,0:T(8,128)S(1)} %get-tuple-element.58), channel_id=1, source_target_pairs={{0,6},{1,7},{2,4},{3,5},{4,2},{5,3},{6,0},{7,1},{8,14},{9,15},{10,... | collective-permute-start | bytes 294920 | tf_op jit(solution)/shard_map/ppermute | solution.py:25
  99.3 9.3 %collective-permute-start.13 = (f32[32,768]{1,0:T(8,128)S(1)}, f32[32,768]{1,0:T(8,128)S(1)}, u32[]{:S(2)}, u32[]{:S(2)}) collective-permute-start(f32[32,768]{1,0:T(8,128)S(1)} %get-tuple-element.64), channel_id=1, source_target_pairs={{0,2},{1,3},{2,0},{3,1},{4,6},{5,7},{6,4},{7,5},{8,10},{9,11},{10,... | collective-permute-start | bytes 294920 | tf_op jit(solution)/shard_map/ppermute | solution.py:25
  99.9 9.3 %collective-permute-start.14 = (f32[32,768]{1,0:T(8,128)S(1)}, f32[32,768]{1,0:T(8,128)S(1)}, u32[]{:S(2)}, u32[]{:S(2)}) collective-permute-start(f32[32,768]{1,0:T(8,128)S(1)} %get-tuple-element.65), channel_id=1, source_target_pairs={{0,4},{1,5},{2,6},{3,7},{4,0},{5,1},{6,2},{7,3},{8,12},{9,13},{10,... | collective-permute-start | bytes 294920 | tf_op jit(solution)/shard_map/ppermute | solution.py:25
  101.5 9.4 %collective-permute-start.15 = (f32[32,768]{1,0:T(8,128)S(1)}, f32[32,768]{1,0:T(8,128)S(1)}, u32[]{:S(2)}, u32[]{:S(2)}) collective-permute-start(f32[32,768]{1,0:T(8,128)S(1)} %get-tuple-element.66), channel_id=1, source_target_pairs={{0,6},{1,7},{2,4},{3,5},{4,2},{5,3},{6,0},{7,1},{8,14},{9,15},{10,... | collective-permute-start | bytes 294920 | tf_op jit(solution)/shard_map/ppermute | solution.py:25
  104.2 9.9 %collective-permute-start.4 = (f32[16,768]{1,0:T(8,128)S(1)}, f32[16,768]{1,0:T(8,128)S(1)}, u32[]{:S(2)}, u32[]{:S(2)}) collective-permute-start(f32[16,768]{1,0:T(8,128)S(1)} %get-tuple-element.49), channel_id=1, source_target_pairs={{0,4},{1,5},{2,6},{3,7},{4,0},{5,1},{6,2},{7,3},{8,12},{9,13},{10,... | collective-permute-start | bytes 147464 | tf_op jit(solution)/shard_map/ppermute | solution.py:25
  105.8 8.3 %collective-permute-start.5 = (f32[16,768]{1,0:T(8,128)S(1)}, f32[16,768]{1,0:T(8,128)S(1)}, u32[]{:S(2)}, u32[]{:S(2)}) collective-permute-start(f32[16,768]{1,0:T(8,128)S(1)} %get-tuple-element.50), channel_id=1, source_target_pairs={{0,6},{1,7},{2,4},{3,5},{4,2},{5,3},{6,0},{7,1},{8,14},{9,15},{10,... | collective-permute-start | bytes 147464 | tf_op jit(solution)/shard_map/ppermute | solution.py:25
  108.6 6.2 %collective-permute-start.23 = (f32[16,768]{1,0:T(8,128)S(1)}, f32[16,768]{1,0:T(8,128)S(1)}, u32[]{:S(2)}, u32[]{:S(2)}) collective-permute-start(f32[16,768]{1,0:T(8,128)S(1)} %get-tuple-element.76), channel_id=1, source_target_pairs={{0,2},{1,3},{2,0},{3,1},{4,6},{5,7},{6,4},{7,5},{8,10},{9,11},{10,... | collective-permute-start | bytes 147464 | tf_op jit(solution)/shard_map/ppermute | solution.py:25
  109.3 5.5 %collective-permute-start.24 = (f32[16,768]{1,0:T(8,128)S(1)}, f32[16,768]{1,0:T(8,128)S(1)}, u32[]{:S(2)}, u32[]{:S(2)}) collective-permute-start(f32[16,768]{1,0:T(8,128)S(1)} %get-tuple-element.77), channel_id=1, source_target_pairs={{0,4},{1,5},{2,6},{3,7},{4,0},{5,1},{6,2},{7,3},{8,12},{9,13},{10,... | collective-permute-start | bytes 147464 | tf_op jit(solution)/shard_map/ppermute | solution.py:25
  110.8 5.0 %collective-permute-start.25 = (f32[16,768]{1,0:T(8,128)S(1)}, f32[16,768]{1,0:T(8,128)S(1)}, u32[]{:S(2)}, u32[]{:S(2)}) collective-permute-start(f32[16,768]{1,0:T(8,128)S(1)} %get-tuple-element.78), channel_id=1, source_target_pairs={{0,6},{1,7},{2,4},{3,5},{4,2},{5,3},{6,0},{7,1},{8,14},{9,15},{10,... | collective-permute-start | bytes 147464 | tf_op jit(solution)/shard_map/ppermute | solution.py:25

commit v8 on v7

--- a/solution.py
+++ b/solution.py
@@ -172,12 +172,12 @@
     )(own, *blocks)
 
 
-def gram_kernel(share, run, ranges, pairs, own, *refs):
+def gram_kernel(share, run, ranges, flag, own, *refs):
     *rows, keep, give, part = refs
     columns = rows[0].shape[1]
     groups = keep.shape[0] * 2
     bit = lax.rem(lax.axis_index("tm"), 2)
-    owner_first = pairs[0, 0] == lax.axis_index("src")
+    owner_first = flag[0] == 1
     product = product_of(own, ranges, rows)
     if len(rows) > len(ranges):
         product = product + rows[-1][...]
@@ -275,6 +275,49 @@
         ),
         compiler_params=pltpu.CompilerParams(vmem_limit_bytes=8 << 20),
         name="fold",
+    )(keep, arrived)
+
+
+def flag_kernel(pairs, out):
+    out[0] = jnp.where(pairs[0, 0] == lax.axis_index("src"), 1, 0)
+
+
+def flag_of(pairs):
+    return pl.pallas_call(
+        flag_kernel,
+        out_shape=pltpu.SMEM((1,), jnp.int32),
+        in_specs=[pl.BlockSpec(memory_space=pltpu.SMEM)],
+        out_specs=pl.BlockSpec(memory_space=pltpu.SMEM),
+        compiler_params=pltpu.CompilerParams(vmem_limit_bytes=1 << 20),
+        name="flag",
+    )(pairs)
+
+
+def across_kernel(keep, arrived, kept, given):
+    bit = lax.axis_index("tm") // 2 % 2
+    for n in range(kept.shape[0]):
+        kept[n] = keep[2 * n + bit] + arrived[2 * n + bit]
+        given[n] = keep[2 * n + 1 - bit] + arrived[2 * n + 1 - bit]
+
+
+def last_kernel(keep, arrived, kept, given):
+    bit = lax.axis_index("tm") // 4
+    kept[...] = keep[bit] + arrived[bit]
+    given[...] = keep[1 - bit] + arrived[1 - bit]
+
+
+def halved(kernel, keep, arrived, shape):
+    half = pltpu.VMEM(shape, jnp.float32)
+    return pl.pallas_call(
+        kernel,
+        out_shape=[half, half],
+        in_specs=[pl.BlockSpec(memory_space=pltpu.VMEM)] * 2,
+        out_specs=[pl.BlockSpec(memory_space=pltpu.VMEM)] * 2,
+        cost_estimate=pl.CostEstimate(
+            flops=keep.size, bytes_accessed=12 * keep.size, transcendentals=0
+        ),
+        compiler_params=pltpu.CompilerParams(vmem_limit_bytes=8 << 20),
+        name="halved",
     )(keep, arrived)
 
 
@@ -327,18 +370,18 @@
         total[start : start + run, :] = rows
 
 
-def place_kernel(share, start, run, given, pairs, *refs):
+def place_kernel(share, start, run, given, flag, *refs):
     *refs, total = refs
-    owner_first = pairs[0, 0] == lax.axis_index("src")
+    owner_first = flag[0] == 1
     total[...] = refs[4][...] if given else jnp.zeros_like(total)
     placed(owner_first, share, start, run, refs[:4], total)
     if given > 1:
         total[...] = total[...] * refs[5][:, :1] * refs[6][...]
 
 
-def scales_kernel(share, pairs, norm_own, norm_low, rows, columns):
+def scales_kernel(share, flag, norm_own, norm_low, rows, columns):
     width = columns.shape[1]
-    owner_first = pairs[0, 0] == lax.axis_index("src")
+    owner_first = flag[0] == 1
     scale_own = lax.rsqrt(norm_own[...] + 1e-06)
     scale_low = lax.rsqrt(norm_low[...] + 1e-06)
     scale_first = jnp.where(owner_first, scale_own, scale_low)
@@ -349,9 +392,9 @@
     columns[...] = jnp.where(owner_first, scale_low, scale_own)
 
 
-def finish_kernel(share, start, run, pairs, base, rows, columns, *refs):
+def finish_kernel(share, start, run, flag, base, rows, columns, *refs):
     *terms, out = refs
-    owner_first = pairs[0, 0] == lax.axis_index("src")
+    owner_first = flag[0] == 1
     out[0] = base[...]
     placed(owner_first, share, start, run, terms, out.at[0], (rows, columns))
 
@@ -462,7 +505,8 @@
     if not aligned:
         return plain_tail(pairs, own, heads, lower, norm_own[0], norm_low[0], share, runs)
 
-    scales = scales_of(pairs, norm_own, norm_low, share)
+    flag = flag_of(pairs)
+    scales = scales_of(flag, norm_own, norm_low, share)
     base = None
     for step, (run, top) in enumerate(zip(runs, heads)):
         if step < len(runs) - 1:
@@ -470,16 +514,22 @@
         else:
             so_far = early(own, [(0, cut), (cut, late)], [top, lower[-2]])
             ranges, blocks = [(late, rows_dev)], [lower[-1], so_far]
-        keep, give = gram(pairs, own, ranges, blocks, share, run[1])
+        keep, give = gram(flag, own, ranges, blocks, share, run[1])
         arrived = swapped(give, "tm", 1)
+        if step == len(runs) - 1:
+            strip = keep.shape[1:]
+            kept, given = halved(across_kernel, keep, arrived, (2, *strip))
+            arrived = swapped(given, "tm", 2)
+            kept, given = halved(last_kernel, kept, arrived, strip)
+            terms = [kept, swapped(given, "tm", 4)]
+            break
         mine, *gives = fold(keep, arrived)
         terms = [mine]
         for m, strip in enumerate(gives, 1):
             terms.append(swapped(strip, "tm", 2 * m))
-        if step < len(runs) - 1:
-            used = scales if step == len(runs) - 2 else ()
-            base = place(pairs, terms, base, used, share, width, *run)
-    return finish(pairs, base, scales, terms, share, *runs[-1])
+        used = scales if step == len(runs) - 2 else ()
+        base = place(flag, terms, base, used, share, width, *run)
+    return finish(flag, base, scales, terms, share, *runs[-1])
 
 
 def plain_tail(pairs, own, heads, lower, norm_own, norm_low, share, runs):

time: 117 us -> 112 us (0.957)
  Pallas kernels: 22.4 us -> 18.1 us
  starting transfers between devices: 28.6 us -> 25.6 us
  waiting for transfers between devices: 64.4 us -> 66.9 us
    ppermute x19 -> x18, starting transfers between devices: 20.5 us -> 17.5 us  [swapped(): return lax.ppermute(value, axis, [(i, i ^ bits) for i in range(length)])]
    pallas_call x5, Pallas kernels: 3.84 us -> 1.13 us  [small_call(): pl.pallas_call(kernel, out_shape=out_shape, in_specs=[pl.BlockSpec(memory...]
    pallas_call x4, Pallas kernels: 6.21 us -> 4.05 us  [gram(): pl.pallas_call(functools.partial(gram_kernel, share, run, ranges), out_sh...]
    ppermute x19 -> x18, waiting for transfers between devices: 7.65 us -> 9.58 us  [swapped(): return lax.ppermute(value, axis, [(i, i ^ bits) for i in range(length)])]
  transfers between devices with their start and end apart: 26 -> 25, of which waited for: 9 -> 10; matrix products, arithmetic and copies ran while one was open for 0% -> 0% of each run, Pallas kernels for 14% -> 11%
where the time goes in v8:
time: 112 us
  waiting for transfers between devices  66.9 us (60%)
  starting transfers between devices  25.6 us (23%)
  Pallas kernels  18.1 us (16%)
    ppermute x7, waiting for transfers between devices, from_behind(): lax.ppermute(value, axis, [(i, (i + by) % length) for i in range(length)])  57.3 us
    ppermute x18, starting transfers between devices, swapped(): return lax.ppermute(value, axis, [(i, i ^ bits) for i in range(length)])  17.5 us
    ppermute x18, waiting for transfers between devices, swapped(): return lax.ppermute(value, axis, [(i, i ^ bits) for i in range(length)])  9.58 us
    ppermute x7, starting transfers between devices, from_behind(): lax.ppermute(value, axis, [(i, (i + by) % length) for i in range(length)])  8.11 us
    pallas_call x2, Pallas kernels, picks(): pl.pallas_call(functools.partial(picks_kernel, share, pieces), out_shape=...  6.49 us
    pallas_call x4, Pallas kernels, gram(): pl.pallas_call(functools.partial(gram_kernel, share, run, ranges), out_sh...  4.05 us
    pallas_call x1, Pallas kernels, turn(): pl.pallas_call(functools.partial(turn_kernel, step), out_shape=(pltpu.VME...  3.8 us
  transfers between devices with their start and end apart: 25, of which 10 were waited for; matrix products, arithmetic and copies ran while one was open for 0% of the time, Pallas kernels for 11%

profile of v8, /device:TPU:0, one launch (start us, length us, event | category | flops | bytes accessed | tf_op | source)
XLA Modules:
  0.0 111.5 jit_solution(10606446523838821605)
XLA Ops:
  0.0 4.9 %picks.3 = (bf16[1792,256]{1,0:T(8,128)(2,1)}, bf16[1792,256]{1,0:T(8,128)(2,1)S(1)}, bf16[1792,128]{1,0:T(8,128)(2,1)S(1)}, bf16[1536,128]{1,0:T(8,128)(2,1)S(1)}, bf16[256,128]{1,0:T(8,128)(2,1)S(1)}) custom-call(bf16[2048,768]{1,0:T(8,128)(2,1)} %block.5), custom_call_target="tpu_custom_call" | custom-call | flops 2415919104 | bytes 6291456 | tf_op jit(solution)/shard_map/picks/pallas_call | solution.py:91
  4.9 0.0 copy-start
  4.9 3.1 %collective-permute-start.11 = (bf16[1792,256]{1,0:T(8,128)(2,1)}, bf16[1792,256]{1,0:T(8,128)(2,1)S(1)}, u32[]{:S(2)}, u32[]{:S(2)}) collective-permute-start(bf16[1792,256]{1,0:T(8,128)(2,1)} %get-tuple-element.60), channel_id=1, source_target_pairs={{0,8},{8,16},{16,24},{24,0},{1,9},{9,17},{17,25},{25,1},{2,10},{10... | collective-permute-start | bytes 2752520 | tf_op jit(solution)/shard_map/ppermute | solution.py:20
  8.0 1.6 %collective-permute-start.6 = (bf16[1792,256]{1,0:T(8,128)(2,1)S(1)}, bf16[1792,256]{1,0:T(8,128)(2,1)S(1)}, u32[]{:S(2)}, u32[]{:S(2)}) collective-permute-start(bf16[1792,256]{1,0:T(8,128)(2,1)S(1)} %get-tuple-element.52), channel_id=1, source_target_pairs={{0,8},{8,16},{16,24},{24,0},{1,9},{9,17},{17,25},{25,1},{2,10},{10... | collective-permute-start | bytes 2752520 | tf_op jit(solution)/shard_map/ppermute | solution.py:20
  9.6 1.1 top.1
  10.7 1.6 %collective-permute-start = (bf16[256,768]{1,0:T(8,128)(2,1)S(1)}, bf16[256,768]{1,0:T(8,128)(2,1)S(1)}, u32[]{:S(2)}, u32[]{:S(2)}) collective-permute-start(bf16[256,768]{1,0:T(8,128)(2,1)S(1)} %top.1), channel_id=1, source_target_pairs={{0,8},{8,16},{16,24},{24,0},{1,9},{9,17},{17,25},{25,1},{2,10},{10... | collective-permute-start | bytes 1179656 | tf_op jit(solution)/shard_map/ppermute | solution.py:20
  12.3 0.1 collective-permute-start.21
  12.4 1.7 %collective-permute-start.1 = (bf16[1792,128]{1,0:T(8,128)(2,1)S(1)}, bf16[1792,128]{1,0:T(8,128)(2,1)S(1)}, u32[]{:S(2)}, u32[]{:S(2)}) collective-permute-start(bf16[1792,128]{1,0:T(8,128)(2,1)S(1)} %get-tuple-element.44), channel_id=1, source_target_pairs={{0,8},{8,16},{16,24},{24,0},{1,9},{9,17},{17,25},{25,1},{2,10},{10... | collective-permute-start | bytes 1376264 | tf_op jit(solution)/shard_map/ppermute | solution.py:20
  14.1 0.6 flag.1
  14.7 3.8 %turn.1 = (bf16[768,2048]{1,0:T(8,128)(2,1)S(1)}, f32[1,768]{1,0:T(1,128)S(1)}) custom-call(s32[4]{0:T(128)} %onsets.1, bf16[2048,768]{1,0:T(8,128)(2,1)} %block.5), custom_call_target="tpu_custom_call" | custom-call | flops 6291456 | bytes 6291456 | tf_op jit(solution)/shard_map/turn/pallas_call | solution.py:129
  18.5 41.1 %collective-permute-done.block = bf16[256,768]{1,0:T(8,128)(2,1)S(1)} collective-permute-done((bf16[256,768]{1,0:T(8,128)(2,1)S(1)}, bf16[256,768]{1,0:T(8,128)(2,1)S(1)}, u32[]{:S(2)}, u32[]{:S(2)}) %collective-permute-start) | collective-permute-done | bytes 393248 | tf_op jit(solution)/shard_map/ppermute | solution.py:20
  59.6 0.0 collective-permute-start.20
  59.6 0.7 copy-done.1
  60.3 1.6 %picks.2 = (bf16[256,256]{1,0:T(8,128)(2,1)S(1)}, bf16[256,256]{1,0:T(8,128)(2,1)S(1)}, bf16[256,128]{1,0:T(8,128)(2,1)S(1)}, bf16[256,128]{1,0:T(8,128)(2,1)S(1)}) custom-call(bf16[256,768]{1,0:T(8,128)(2,1)} %copy-done.1), custom_call_target="tpu_custom_call" | custom-call | flops 301989888 | bytes 786432 | tf_op jit(solution)/shard_map/picks/pallas_call | solution.py:91
  61.9 0.0 collective-permute-done.11.refs_1_
  61.9 1.2 %gram.6 = (f32[4,32,768]{2,1,0:T(8,128)S(1)}, f32[4,32,768]{2,1,0:T(8,128)S(1)}) custom-call(s32[1]{0:T(128)S(4)} %flag.1, bf16[768,2048]{1,0:T(8,128)(2,1)S(1)} %get-tuple-element.42.own, bf16[256,256]{1,0:T(8,128)(2,1)S(1)} %get-tuple-element.59.refs_0_, bf16[1792,256]{1,0:T(8,128)(2,1)S(1)} %collective-permute-done.11.refs_1_), custom_call_target="tpu_custom_call" | custom-call | flops 805306368 | bytes 3145728 | tf_op jit(solution)/shard_map/gram/pallas_call | solution.py:210
  63.1 0.1 collective-permute-start.12
  63.2 0.0 collective-permute-done.6.refs_1_
  63.2 1.2 %gram.5 = (f32[4,32,768]{2,1,0:T(8,128)S(1)}, f32[4,32,768]{2,1,0:T(8,128)S(1)}) custom-call(s32[1]{0:T(128)S(4)} %flag.1, bf16[768,2048]{1,0:T(8,128)(2,1)S(1)} %get-tuple-element.42.own, bf16[256,256]{1,0:T(8,128)(2,1)S(1)} %get-tuple-element.51.refs_0_, bf16[1792,256]{1,0:T(8,128)(2,1)S(1)} %collective-permute-done.6.refs_1_), custom_call_target="tpu_custom_call" | custom-call | flops 805306368 | bytes 3145728 | tf_op jit(solution)/shard_map/gram/pallas_call | solution.py:210
  64.5 0.6 collective-permute-start.7
  65.0 2.9 %collective-permute-done.21.refs_1_ = bf16[1536,128]{1,0:T(8,128)(2,1)S(1)} collective-permute-done((bf16[1536,128]{1,0:T(8,128)(2,1)S(1)}, bf16[1536,128]{1,0:T(8,128)(2,1)S(1)}, u32[]{:S(2)}, u32[]{:S(2)}) %collective-permute-start.21) | collective-permute-done | bytes 393248 | tf_op jit(solution)/shard_map/ppermute | solution.py:20
  68.0 0.9 early.1.refs_1_
  68.9 9.5 %collective-permute-done.20.refs_0_ = bf16[256,128]{1,0:T(8,128)(2,1)S(1)} collective-permute-done((bf16[256,128]{1,0:T(8,128)(2,1)S(1)}, bf16[256,128]{1,0:T(8,128)(2,1)S(1)}, u32[]{:S(2)}, u32[]{:S(2)}) %collective-permute-start.20) | collective-permute-done | bytes 65568 | tf_op jit(solution)/shard_map/ppermute | solution.py:20
  78.4 0.4 gram.7
  78.8 0.1 collective-permute-start.22
  78.9 0.0 collective-permute-done.1.refs_1_
  78.9 1.1 %gram.4 = (f32[4,16,768]{2,1,0:T(8,128)S(1)}, f32[4,16,768]{2,1,0:T(8,128)S(1)}) custom-call(s32[1]{0:T(128)S(4)} %flag.1, bf16[768,2048]{1,0:T(8,128)(2,1)S(1)} %get-tuple-element.42.own, bf16[256,128]{1,0:T(8,128)(2,1)S(1)} %get-tuple-element.43.refs_0_, bf16[1792,128]{1,0:T(8,128)(2,1)S(1)} %collective-permute-done.1.refs_1_), custom_call_target="tpu_custom_call" | custom-call | flops 402653184 | bytes 3145728 | tf_op jit(solution)/shard_map/gram/pallas_call | solution.py:210
  80.0 0.6 collective-permute-start.2
  80.6 0.0 collective-permute-done.22.arrived
  80.6 1.6 %collective-permute-start.23 = (f32[2,16,768]{2,1,0:T(8,128)S(1)}, f32[2,16,768]{2,1,0:T(8,128)S(1)}, u32[]{:S(2)}, u32[]{:S(2)}) collective-permute-start(f32[2,16,768]{2,1,0:T(8,128)S(1)} %get-tuple-element.76), channel_id=1, source_target_pairs={{0,2},{1,3},{2,0},{3,1},{4,6},{5,7},{6,4},{7,5},{8,10},{9,11},{10,... | collective-permute-start | bytes 294920 | tf_op jit(solution)/shard_map/ppermute | solution.py:25
  82.2 0.0 collective-permute-done.12.arrived
  82.2 0.6 collective-permute-start.13
  82.8 0.0 collective-permute-start.16
  82.8 1.2 %collective-permute-done.16.b = f32[1,768]{1,0:T(1,128)S(1)} collective-permute-done((f32[1,768]{1,0:T(1,128)S(1)}, f32[1,768]{1,0:T(1,128)S(1)}, u32[]{:S(2)}, u32[]{:S(2)}) %collective-permute-start.16) | collective-permute-done | bytes 3104 | tf_op jit(solution)/shard_map/ppermute | solution.py:25
  84.0 1.5 %collective-permute-start.17 = (f32[1,768]{1,0:T(1,128)S(1)}, f32[1,768]{1,0:T(1,128)S(1)}, u32[]{:S(2)}, u32[]{:S(2)}) collective-permute-start(f32[1,768]{1,0:T(1,128)S(1)} %plus.3.a), channel_id=1, source_target_pairs={{0,2},{1,3},{2,0},{3,1},{4,6},{5,7},{6,4},{7,5},{8,10},{9,11},{10,... | collective-permute-start | bytes 9224 | tf_op jit(solution)/shard_map/ppermute | solution.py:25
  85.5 2.1 %collective-permute-done.17.b = f32[1,768]{1,0:T(1,128)S(1)} collective-permute-done((f32[1,768]{1,0:T(1,128)S(1)}, f32[1,768]{1,0:T(1,128)S(1)}, u32[]{:S(2)}, u32[]{:S(2)}) %collective-permute-start.17) | collective-permute-done | bytes 3104 | tf_op jit(solution)/shard_map/ppermute | solution.py:25
  87.6 1.5 %collective-permute-start.18 = (f32[1,768]{1,0:T(1,128)S(1)}, f32[1,768]{1,0:T(1,128)S(1)}, u32[]{:S(2)}, u32[]{:S(2)}) collective-permute-start(f32[1,768]{1,0:T(1,128)S(1)} %plus.4.a), channel_id=1, source_target_pairs={{0,4},{1,5},{2,6},{3,7},{4,0},{5,1},{6,2},{7,3},{8,12},{9,13},{10,... | collective-permute-start | bytes 9224 | tf_op jit(solution)/shard_map/ppermute | solution.py:25
  89.1 2.1 %collective-permute-done.18.b = f32[1,768]{1,0:T(1,128)S(1)} collective-permute-done((f32[1,768]{1,0:T(1,128)S(1)}, f32[1,768]{1,0:T(1,128)S(1)}, u32[]{:S(2)}, u32[]{:S(2)}) %collective-permute-start.18) | collective-permute-done | bytes 3104 | tf_op jit(solution)/shard_map/ppermute | solution.py:25
  91.2 0.0 collective-permute-start.19
  91.2 0.0 collective-permute-done.7.arrived
  91.2 1.6 %collective-permute-start.14 = (f32[32,768]{1,0:T(8,128)S(1)}, f32[32,768]{1,0:T(8,128)S(1)}, u32[]{:S(2)}, u32[]{:S(2)}) collective-permute-start(f32[32,768]{1,0:T(8,128)S(1)} %get-tuple-element.65), channel_id=1, source_target_pairs={{0,4},{1,5},{2,6},{3,7},{4,0},{5,1},{6,2},{7,3},{8,12},{9,13},{10,... | collective-permute-start | bytes 294920 | tf_op jit(solution)/shard_map/ppermute | solution.py:25
  92.9 3.8 %collective-permute-done.19.norm_low = f32[1,768]{1,0:T(1,128)S(1)} collective-permute-done((f32[1,768]{1,0:T(1,128)S(1)}, f32[1,768]{1,0:T(1,128)S(1)}, u32[]{:S(2)}, u32[]{:S(2)}) %collective-permute-start.19) | collective-permute-done | bytes 3104 | tf_op jit(solution)/shard_map/ppermute | solution.py:20
  96.6 2.5 %collective-permute-start.15 = (f32[32,768]{1,0:T(8,128)S(1)}, f32[32,768]{1,0:T(8,128)S(1)}, u32[]{:S(2)}, u32[]{:S(2)}) collective-permute-start(f32[32,768]{1,0:T(8,128)S(1)} %get-tuple-element.66), channel_id=1, source_target_pairs={{0,6},{1,7},{2,4},{3,5},{4,2},{5,3},{6,0},{7,1},{8,14},{9,15},{10,... | collective-permute-start | bytes 294920 | tf_op jit(solution)/shard_map/ppermute | solution.py:25
  99.1 0.0 collective-permute-done.2.arrived
  99.1 0.5 collective-permute-start.10
  99.5 0.0 collective-permute-done.23.arrived
  99.5 1.5 %collective-permute-start.8 = (f32[32,768]{1,0:T(8,128)S(1)}, f32[32,768]{1,0:T(8,128)S(1)}, u32[]{:S(2)}, u32[]{:S(2)}) collective-permute-start(f32[32,768]{1,0:T(8,128)S(1)} %get-tuple-element.56), channel_id=1, source_target_pairs={{0,2},{1,3},{2,0},{3,1},{4,6},{5,7},{6,4},{7,5},{8,10},{9,11},{10,... | collective-permute-start | bytes 294920 | tf_op jit(solution)/shard_map/ppermute | solution.py:25
  101.0 0.0 collective-permute-done.13.refs_1_
  101.0 1.5 %collective-permute-start.9 = (f32[32,768]{1,0:T(8,128)S(1)}, f32[32,768]{1,0:T(8,128)S(1)}, u32[]{:S(2)}, u32[]{:S(2)}) collective-permute-start(f32[32,768]{1,0:T(8,128)S(1)} %get-tuple-element.57), channel_id=1, source_target_pairs={{0,4},{1,5},{2,6},{3,7},{4,0},{5,1},{6,2},{7,3},{8,12},{9,13},{10,... | collective-permute-start | bytes 294920 | tf_op jit(solution)/shard_map/ppermute | solution.py:25
  102.6 0.0 collective-permute-done.14.refs_2_
  102.6 0.6 collective-permute-start.3
  103.2 0.0 collective-permute-done.15.refs_3_
  103.2 1.0 collective-permute-start.4
  104.2 1.0 collective-permute-done.10.refs_3_
  105.2 1.1 collective-permute-start.5
  106.3 0.0 collective-permute-done.8.refs_1_
  106.3 0.9 collective-permute-start.24
  107.2 0.1 shard_map.39
  107.3 0.0 collective-permute-done.9.refs_2_
  107.4 0.0 collective-permute-done.4.refs_2_
  107.4 2.8 %collective-permute-done.5.refs_3_ = f32[16,768]{1,0:T(8,128)S(1)} collective-permute-done((f32[16,768]{1,0:T(8,128)S(1)}, f32[16,768]{1,0:T(8,128)S(1)}, u32[]{:S(2)}, u32[]{:S(2)}) %collective-permute-start.5) | collective-permute-done | bytes 49184 | tf_op jit(solution)/shard_map/ppermute | solution.py:25
  110.2 0.1 shard_map.40.base
  110.4 0.4 collective-permute-done.24.refs_1_
  110.7 0.8 shard_map.41
  (13 shorter events, 0.2 us)
Async XLA Ops:
  4.9 9.2 %copy-start = (s32[1,2]{1,0:T(1,128)S(1)}, s32[1,2]{1,0:T(1,128)}, u32[]{:S(2)}) copy-start(s32[1,2]{1,0:T(1,128)} %pairs.1) | copy-start | bytes 28
  4.9 57.0 %collective-permute-start.11 = (bf16[1792,256]{1,0:T(8,128)(2,1)}, bf16[1792,256]{1,0:T(8,128)(2,1)S(1)}, u32[]{:S(2)}, u32[]{:S(2)}) collective-permute-start(bf16[1792,256]{1,0:T(8,128)(2,1)} %get-tuple-element.60), channel_id=1, source_target_pairs={{0,8},{8,16},{16,24},{24,0},{1,9},{9,17},{17,25},{25,1},{2,10},{10... | collective-permute-start | bytes 2752520 | tf_op jit(solution)/shard_map/ppermute | solution.py:20
  8.0 55.2 %collective-permute-start.6 = (bf16[1792,256]{1,0:T(8,128)(2,1)S(1)}, bf16[1792,256]{1,0:T(8,128)(2,1)S(1)}, u32[]{:S(2)}, u32[]{:S(2)}) collective-permute-start(bf16[1792,256]{1,0:T(8,128)(2,1)S(1)} %get-tuple-element.52), channel_id=1, source_target_pairs={{0,8},{8,16},{16,24},{24,0},{1,9},{9,17},{17,25},{25,1},{2,10},{10... | collective-permute-start | bytes 2752520 | tf_op jit(solution)/shard_map/ppermute | solution.py:20
  10.7 48.9 %collective-permute-start = (bf16[256,768]{1,0:T(8,128)(2,1)S(1)}, bf16[256,768]{1,0:T(8,128)(2,1)S(1)}, u32[]{:S(2)}, u32[]{:S(2)}) collective-permute-start(bf16[256,768]{1,0:T(8,128)(2,1)S(1)} %top.1), channel_id=1, source_target_pairs={{0,8},{8,16},{16,24},{24,0},{1,9},{9,17},{17,25},{25,1},{2,10},{10... | collective-permute-start | bytes 1179656 | tf_op jit(solution)/shard_map/ppermute | solution.py:20
  12.3 55.7 %collective-permute-start.21 = (bf16[1536,128]{1,0:T(8,128)(2,1)S(1)}, bf16[1536,128]{1,0:T(8,128)(2,1)S(1)}, u32[]{:S(2)}, u32[]{:S(2)}) collective-permute-start(bf16[1536,128]{1,0:T(8,128)(2,1)S(1)} %get-tuple-element.72), channel_id=1, source_target_pairs={{0,8},{8,16},{16,24},{24,0},{1,9},{9,17},{17,25},{25,1},{2,10},{10... | collective-permute-start | bytes 1179656 | tf_op jit(solution)/shard_map/ppermute | solution.py:20
  12.4 66.5 %collective-permute-start.1 = (bf16[1792,128]{1,0:T(8,128)(2,1)S(1)}, bf16[1792,128]{1,0:T(8,128)(2,1)S(1)}, u32[]{:S(2)}, u32[]{:S(2)}) collective-permute-start(bf16[1792,128]{1,0:T(8,128)(2,1)S(1)} %get-tuple-element.44), channel_id=1, source_target_pairs={{0,8},{8,16},{16,24},{24,0},{1,9},{9,17},{17,25},{25,1},{2,10},{10... | collective-permute-start | bytes 1376264 | tf_op jit(solution)/shard_map/ppermute | solution.py:20
  59.6 0.7 copy-start.1
  59.6 18.8 %collective-permute-start.20 = (bf16[256,128]{1,0:T(8,128)(2,1)S(1)}, bf16[256,128]{1,0:T(8,128)(2,1)S(1)}, u32[]{:S(2)}, u32[]{:S(2)}) collective-permute-start(bf16[256,128]{1,0:T(8,128)(2,1)S(1)} %get-tuple-element.70), channel_id=1, source_target_pairs={{0,8},{8,16},{16,24},{24,0},{1,9},{9,17},{17,25},{25,1},{2,10},{10... | collective-permute-start | bytes 196616 | tf_op jit(solution)/shard_map/ppermute | solution.py:20
  63.1 19.0 %collective-permute-start.12 = (f32[4,32,768]{2,1,0:T(8,128)S(1)}, f32[4,32,768]{2,1,0:T(8,128)S(1)}, u32[]{:S(2)}, u32[]{:S(2)}) collective-permute-start(f32[4,32,768]{2,1,0:T(8,128)S(1)} %get-tuple-element.62), channel_id=1, source_target_pairs={{0,1},{1,0},{2,3},{3,2},{4,5},{5,4},{6,7},{7,6},{8,9},{9,8},{10,11... | collective-permute-start | bytes 1179656 | tf_op jit(solution)/shard_map/ppermute | solution.py:25
  64.5 26.7 %collective-permute-start.7 = (f32[4,32,768]{2,1,0:T(8,128)S(1)}, f32[4,32,768]{2,1,0:T(8,128)S(1)}, u32[]{:S(2)}, u32[]{:S(2)}) collective-permute-start(f32[4,32,768]{2,1,0:T(8,128)S(1)} %get-tuple-element.54), channel_id=1, source_target_pairs={{0,1},{1,0},{2,3},{3,2},{4,5},{5,4},{6,7},{7,6},{8,9},{9,8},{10,11... | collective-permute-start | bytes 1179656 | tf_op jit(solution)/shard_map/ppermute | solution.py:25
  78.8 1.8 %collective-permute-start.22 = (f32[4,16,768]{2,1,0:T(8,128)S(1)}, f32[4,16,768]{2,1,0:T(8,128)S(1)}, u32[]{:S(2)}, u32[]{:S(2)}) collective-permute-start(f32[4,16,768]{2,1,0:T(8,128)S(1)} %get-tuple-element.74), channel_id=1, source_target_pairs={{0,1},{1,0},{2,3},{3,2},{4,5},{5,4},{6,7},{7,6},{8,9},{9,8},{10,11... | collective-permute-start | bytes 589832 | tf_op jit(solution)/shard_map/ppermute | solution.py:25
  80.0 19.0 %collective-permute-start.2 = (f32[4,16,768]{2,1,0:T(8,128)S(1)}, f32[4,16,768]{2,1,0:T(8,128)S(1)}, u32[]{:S(2)}, u32[]{:S(2)}) collective-permute-start(f32[4,16,768]{2,1,0:T(8,128)S(1)} %get-tuple-element.46), channel_id=1, source_target_pairs={{0,1},{1,0},{2,3},{3,2},{4,5},{5,4},{6,7},{7,6},{8,9},{9,8},{10,11... | collective-permute-start | bytes 589832 | tf_op jit(solution)/shard_map/ppermute | solution.py:25
  80.6 18.9 %collective-permute-start.23 = (f32[2,16,768]{2,1,0:T(8,128)S(1)}, f32[2,16,768]{2,1,0:T(8,128)S(1)}, u32[]{:S(2)}, u32[]{:S(2)}) collective-permute-start(f32[2,16,768]{2,1,0:T(8,128)S(1)} %get-tuple-element.76), channel_id=1, source_target_pairs={{0,2},{1,3},{2,0},{3,1},{4,6},{5,7},{6,4},{7,5},{8,10},{9,11},{10,... | collective-permute-start | bytes 294920 | tf_op jit(solution)/shard_map/ppermute | solution.py:25
  82.2 18.8 %collective-permute-start.13 = (f32[32,768]{1,0:T(8,128)S(1)}, f32[32,768]{1,0:T(8,128)S(1)}, u32[]{:S(2)}, u32[]{:S(2)}) collective-permute-start(f32[32,768]{1,0:T(8,128)S(1)} %get-tuple-element.64), channel_id=1, source_target_pairs={{0,2},{1,3},{2,0},{3,1},{4,6},{5,7},{6,4},{7,5},{8,10},{9,11},{10,... | collective-permute-start | bytes 294920 | tf_op jit(solution)/shard_map/ppermute | solution.py:25
  82.8 1.2 %collective-permute-start.16 = (f32[1,768]{1,0:T(1,128)S(1)}, f32[1,768]{1,0:T(1,128)S(1)}, u32[]{:S(2)}, u32[]{:S(2)}) collective-permute-start(f32[1,768]{1,0:T(1,128)S(1)} %get-tuple-element.67.a), channel_id=1, source_target_pairs={{0,1},{1,0},{2,3},{3,2},{4,5},{5,4},{6,7},{7,6},{8,9},{9,8},{10,11... | collective-permute-start | bytes 9224 | tf_op jit(solution)/shard_map/ppermute | solution.py:25
  84.0 3.6 %collective-permute-start.17 = (f32[1,768]{1,0:T(1,128)S(1)}, f32[1,768]{1,0:T(1,128)S(1)}, u32[]{:S(2)}, u32[]{:S(2)}) collective-permute-start(f32[1,768]{1,0:T(1,128)S(1)} %plus.3.a), channel_id=1, source_target_pairs={{0,2},{1,3},{2,0},{3,1},{4,6},{5,7},{6,4},{7,5},{8,10},{9,11},{10,... | collective-permute-start | bytes 9224 | tf_op jit(solution)/shard_map/ppermute | solution.py:25
  87.6 3.6 %collective-permute-start.18 = (f32[1,768]{1,0:T(1,128)S(1)}, f32[1,768]{1,0:T(1,128)S(1)}, u32[]{:S(2)}, u32[]{:S(2)}) collective-permute-start(f32[1,768]{1,0:T(1,128)S(1)} %plus.4.a), channel_id=1, source_target_pairs={{0,4},{1,5},{2,6},{3,7},{4,0},{5,1},{6,2},{7,3},{8,12},{9,13},{10,... | collective-permute-start | bytes 9224 | tf_op jit(solution)/shard_map/ppermute | solution.py:25
  91.2 5.4 %collective-permute-start.19 = (f32[1,768]{1,0:T(1,128)S(1)}, f32[1,768]{1,0:T(1,128)S(1)}, u32[]{:S(2)}, u32[]{:S(2)}) collective-permute-start(f32[1,768]{1,0:T(1,128)S(1)} %plus.5.norm_own), channel_id=1, source_target_pairs={{0,8},{8,16},{16,24},{24,0},{1,9},{9,17},{17,25},{25,1},{2,10},{10... | collective-permute-start | bytes 9224 | tf_op jit(solution)/shard_map/ppermute | solution.py:20
  91.2 11.4 %collective-permute-start.14 = (f32[32,768]{1,0:T(8,128)S(1)}, f32[32,768]{1,0:T(8,128)S(1)}, u32[]{:S(2)}, u32[]{:S(2)}) collective-permute-start(f32[32,768]{1,0:T(8,128)S(1)} %get-tuple-element.65), channel_id=1, source_target_pairs={{0,4},{1,5},{2,6},{3,7},{4,0},{5,1},{6,2},{7,3},{8,12},{9,13},{10,... | collective-permute-start | bytes 294920 | tf_op jit(solution)/shard_map/ppermute | solution.py:25
  96.6 6.6 %collective-permute-start.15 = (f32[32,768]{1,0:T(8,128)S(1)}, f32[32,768]{1,0:T(8,128)S(1)}, u32[]{:S(2)}, u32[]{:S(2)}) collective-permute-start(f32[32,768]{1,0:T(8,128)S(1)} %get-tuple-element.66), channel_id=1, source_target_pairs={{0,6},{1,7},{2,4},{3,5},{4,2},{5,3},{6,0},{7,1},{8,14},{9,15},{10,... | collective-permute-start | bytes 294920 | tf_op jit(solution)/shard_map/ppermute | solution.py:25
  99.1 6.1 %collective-permute-start.10 = (f32[32,768]{1,0:T(8,128)S(1)}, f32[32,768]{1,0:T(8,128)S(1)}, u32[]{:S(2)}, u32[]{:S(2)}) collective-permute-start(f32[32,768]{1,0:T(8,128)S(1)} %get-tuple-element.58), channel_id=1, source_target_pairs={{0,6},{1,7},{2,4},{3,5},{4,2},{5,3},{6,0},{7,1},{8,14},{9,15},{10,... | collective-permute-start | bytes 294920 | tf_op jit(solution)/shard_map/ppermute | solution.py:25
  99.5 6.7 %collective-permute-start.8 = (f32[32,768]{1,0:T(8,128)S(1)}, f32[32,768]{1,0:T(8,128)S(1)}, u32[]{:S(2)}, u32[]{:S(2)}) collective-permute-start(f32[32,768]{1,0:T(8,128)S(1)} %get-tuple-element.56), channel_id=1, source_target_pairs={{0,2},{1,3},{2,0},{3,1},{4,6},{5,7},{6,4},{7,5},{8,10},{9,11},{10,... | collective-permute-start | bytes 294920 | tf_op jit(solution)/shard_map/ppermute | solution.py:25
  101.0 6.3 %collective-permute-start.9 = (f32[32,768]{1,0:T(8,128)S(1)}, f32[32,768]{1,0:T(8,128)S(1)}, u32[]{:S(2)}, u32[]{:S(2)}) collective-permute-start(f32[32,768]{1,0:T(8,128)S(1)} %get-tuple-element.57), channel_id=1, source_target_pairs={{0,4},{1,5},{2,6},{3,7},{4,0},{5,1},{6,2},{7,3},{8,12},{9,13},{10,... | collective-permute-start | bytes 294920 | tf_op jit(solution)/shard_map/ppermute | solution.py:25
  102.6 4.8 %collective-permute-start.3 = (f32[16,768]{1,0:T(8,128)S(1)}, f32[16,768]{1,0:T(8,128)S(1)}, u32[]{:S(2)}, u32[]{:S(2)}) collective-permute-start(f32[16,768]{1,0:T(8,128)S(1)} %get-tuple-element.48), channel_id=1, source_target_pairs={{0,2},{1,3},{2,0},{3,1},{4,6},{5,7},{6,4},{7,5},{8,10},{9,11},{10,... | collective-permute-start | bytes 147464 | tf_op jit(solution)/shard_map/ppermute | solution.py:25
  103.2 4.2 %collective-permute-start.4 = (f32[16,768]{1,0:T(8,128)S(1)}, f32[16,768]{1,0:T(8,128)S(1)}, u32[]{:S(2)}, u32[]{:S(2)}) collective-permute-start(f32[16,768]{1,0:T(8,128)S(1)} %get-tuple-element.49), channel_id=1, source_target_pairs={{0,4},{1,5},{2,6},{3,7},{4,0},{5,1},{6,2},{7,3},{8,12},{9,13},{10,... | collective-permute-start | bytes 147464 | tf_op jit(solution)/shard_map/ppermute | solution.py:25
  105.2 5.0 %collective-permute-start.5 = (f32[16,768]{1,0:T(8,128)S(1)}, f32[16,768]{1,0:T(8,128)S(1)}, u32[]{:S(2)}, u32[]{:S(2)}) collective-permute-start(f32[16,768]{1,0:T(8,128)S(1)} %get-tuple-element.50), channel_id=1, source_target_pairs={{0,6},{1,7},{2,4},{3,5},{4,2},{5,3},{6,0},{7,1},{8,14},{9,15},{10,... | collective-permute-start | bytes 147464 | tf_op jit(solution)/shard_map/ppermute | solution.py:25
  106.3 4.4 %collective-permute-start.24 = (f32[16,768]{1,0:T(8,128)S(1)}, f32[16,768]{1,0:T(8,128)S(1)}, u32[]{:S(2)}, u32[]{:S(2)}) collective-permute-start(f32[16,768]{1,0:T(8,128)S(1)} %get-tuple-element.78), channel_id=1, source_target_pairs={{0,4},{1,5},{2,6},{3,7},{4,0},{5,1},{6,2},{7,3},{8,12},{9,13},{10,... | collective-permute-start | bytes 147464 | tf_op jit(solution)/shard_map/ppermute | solution.py:25

commit v9 on v8

--- a/solution.py
+++ b/solution.py
@@ -10,9 +10,9 @@
 
 PARTS = (2, 2, 1, 1)
 HEAD = 8
-LATE = 8
+LATE = 2
 LANES = 128
-TOPS = 4
+TOPS = 1
 
 
 def from_behind(value, axis, by):
@@ -291,34 +291,6 @@
         compiler_params=pltpu.CompilerParams(vmem_limit_bytes=1 << 20),
         name="flag",
     )(pairs)
-
-
-def across_kernel(keep, arrived, kept, given):
-    bit = lax.axis_index("tm") // 2 % 2
-    for n in range(kept.shape[0]):
-        kept[n] = keep[2 * n + bit] + arrived[2 * n + bit]
-        given[n] = keep[2 * n + 1 - bit] + arrived[2 * n + 1 - bit]
-
-
-def last_kernel(keep, arrived, kept, given):
-    bit = lax.axis_index("tm") // 4
-    kept[...] = keep[bit] + arrived[bit]
-    given[...] = keep[1 - bit] + arrived[1 - bit]
-
-
-def halved(kernel, keep, arrived, shape):
-    half = pltpu.VMEM(shape, jnp.float32)
-    return pl.pallas_call(
-        kernel,
-        out_shape=[half, half],
-        in_specs=[pl.BlockSpec(memory_space=pltpu.VMEM)] * 2,
-        out_specs=[pl.BlockSpec(memory_space=pltpu.VMEM)] * 2,
-        cost_estimate=pl.CostEstimate(
-            flops=keep.size, bytes_accessed=12 * keep.size, transcendentals=0
-        ),
-        compiler_params=pltpu.CompilerParams(vmem_limit_bytes=8 << 20),
-        name="halved",
-    )(keep, arrived)
 
 
 def plus_kernel(a, b, out):
@@ -516,19 +488,13 @@
             ranges, blocks = [(late, rows_dev)], [lower[-1], so_far]
         keep, give = gram(flag, own, ranges, blocks, share, run[1])
         arrived = swapped(give, "tm", 1)
-        if step == len(runs) - 1:
-            strip = keep.shape[1:]
-            kept, given = halved(across_kernel, keep, arrived, (2, *strip))
-            arrived = swapped(given, "tm", 2)
-            kept, given = halved(last_kernel, kept, arrived, strip)
-            terms = [kept, swapped(given, "tm", 4)]
-            break
         mine, *gives = fold(keep, arrived)
         terms = [mine]
         for m, strip in enumerate(gives, 1):
             terms.append(swapped(strip, "tm", 2 * m))
-        used = scales if step == len(runs) - 2 else ()
-        base = place(flag, terms, base, used, share, width, *run)
+        if step < len(runs) - 1:
+            used = scales if step == len(runs) - 2 else ()
+            base = place(flag, terms, base, used, share, width, *run)
     return finish(flag, base, scales, terms, share, *runs[-1])
 
 

time: 112 us -> 117 us (1.045)
  starting transfers between devices: 25.6 us -> 28.5 us
  local copies, waits for them, and re-layouts: 0.74 us -> 2.08 us
    ppermute x18 -> x19, starting transfers between devices: 17.5 us -> 20.4 us  [swapped(): return lax.ppermute(value, axis, [(i, i ^ bits) for i in range(length)])]
    unnamed x4 -> x8, local copies, waits for them, and re-layouts: 0.74 us -> 2.08 us
    ppermute x18 -> x19, waiting for transfers between devices: 9.58 us -> 9.83 us  [swapped(): return lax.ppermute(value, axis, [(i, i ^ bits) for i in range(length)])]
  transfers between devices with their start and end apart: 25 -> 26, of which waited for: 10 -> 11; matrix products, arithmetic and copies ran while one was open for 0% -> 0% of each run, Pallas kernels for 11% -> 11%
where the time goes in v9:
time: 117 us
  waiting for transfers between devices  67.8 us (58%)
  starting transfers between devices  28.5 us (24%)
  Pallas kernels  18.1 us (15%)
  local copies, waits for them, and re-layouts  2.08 us (2%)
    ppermute x7, waiting for transfers between devices, from_behind(): lax.ppermute(value, axis, [(i, (i + by) % length) for i in range(length)])  58 us
    ppermute x19, starting transfers between devices, swapped(): return lax.ppermute(value, axis, [(i, i ^ bits) for i in range(length)])  20.4 us
    ppermute x19, waiting for transfers between devices, swapped(): return lax.ppermute(value, axis, [(i, i ^ bits) for i in range(length)])  9.83 us
    ppermute x7, starting transfers between devices, from_behind(): lax.ppermute(value, axis, [(i, (i + by) % length) for i in range(length)])  8.12 us
    pallas_call x2, Pallas kernels, picks(): pl.pallas_call(functools.partial(picks_kernel, share, pieces), out_shape=...  6.49 us
    pallas_call x4, Pallas kernels, gram(): pl.pallas_call(functools.partial(gram_kernel, share, run, ranges), out_sh...  4.37 us
    pallas_call x1, Pallas kernels, turn(): pl.pallas_call(functools.partial(turn_kernel, step), out_shape=(pltpu.VME...  3.8 us
  transfers between devices with their start and end apart: 26, of which 11 were waited for; matrix products, arithmetic and copies ran while one was open for 0% of the time, Pallas kernels for 11%

profile of v9, /device:TPU:0, one launch (start us, length us, event | category | flops | bytes accessed | tf_op | source)
XLA Modules:
  0.0 116.7 jit_solution(13370348806433433994)
XLA Ops:
  0.0 4.9 %picks.3 = (bf16[1792,256]{1,0:T(8,128)(2,1)S(1)}, bf16[1792,256]{1,0:T(8,128)(2,1)}, bf16[1792,128]{1,0:T(8,128)(2,1)S(1)}, bf16[768,128]{1,0:T(8,128)(2,1)S(1)}, bf16[1024,128]{1,0:T(8,128)(2,1)S(1)}) custom-call(bf16[2048,768]{1,0:T(8,128)(2,1)} %block.5), custom_call_target="tpu_custom_call" | custom-call | flops 2415919104 | bytes 6291456 | tf_op jit(solution)/shard_map/picks/pallas_call | solution.py:91
  4.9 0.0 copy-start
  4.9 0.7 copy-done
  5.6 3.1 %collective-permute-start.6 = (bf16[1792,256]{1,0:T(8,128)(2,1)}, bf16[1792,256]{1,0:T(8,128)(2,1)S(1)}, u32[]{:S(2)}, u32[]{:S(2)}) collective-permute-start(bf16[1792,256]{1,0:T(8,128)(2,1)} %get-tuple-element.52), channel_id=1, source_target_pairs={{0,8},{8,16},{16,24},{24,0},{1,9},{9,17},{17,25},{25,1},{2,10},{10... | collective-permute-start | bytes 2752520 | tf_op jit(solution)/shard_map/ppermute | solution.py:20
  8.7 1.6 %collective-permute-start.11 = (bf16[1792,256]{1,0:T(8,128)(2,1)S(1)}, bf16[1792,256]{1,0:T(8,128)(2,1)S(1)}, u32[]{:S(2)}, u32[]{:S(2)}) collective-permute-start(bf16[1792,256]{1,0:T(8,128)(2,1)S(1)} %get-tuple-element.60), channel_id=1, source_target_pairs={{0,8},{8,16},{16,24},{24,0},{1,9},{9,17},{17,25},{25,1},{2,10},{10... | collective-permute-start | bytes 2752520 | tf_op jit(solution)/shard_map/ppermute | solution.py:20
  10.2 1.0 top.1
  11.2 1.6 %collective-permute-start = (bf16[256,768]{1,0:T(8,128)(2,1)S(1)}, bf16[256,768]{1,0:T(8,128)(2,1)S(1)}, u32[]{:S(2)}, u32[]{:S(2)}) collective-permute-start(bf16[256,768]{1,0:T(8,128)(2,1)S(1)} %top.1), channel_id=1, source_target_pairs={{0,8},{8,16},{16,24},{24,0},{1,9},{9,17},{17,25},{25,1},{2,10},{10... | collective-permute-start | bytes 1179656 | tf_op jit(solution)/shard_map/ppermute | solution.py:20
  12.9 0.1 collective-permute-start.1
  12.9 1.7 %collective-permute-start.20 = (bf16[1024,128]{1,0:T(8,128)(2,1)S(1)}, bf16[1024,128]{1,0:T(8,128)(2,1)S(1)}, u32[]{:S(2)}, u32[]{:S(2)}) collective-permute-start(bf16[1024,128]{1,0:T(8,128)(2,1)S(1)} %get-tuple-element.70), channel_id=1, source_target_pairs={{0,8},{8,16},{16,24},{24,0},{1,9},{9,17},{17,25},{25,1},{2,10},{10... | collective-permute-start | bytes 786440 | tf_op jit(solution)/shard_map/ppermute | solution.py:20
  14.7 0.7 copy-done.2
  15.3 0.6 flag.1
  15.9 3.8 %turn.1 = (bf16[768,2048]{1,0:T(8,128)(2,1)S(1)}, f32[1,768]{1,0:T(1,128)S(1)}) custom-call(s32[4]{0:T(128)} %onsets.1, bf16[2048,768]{1,0:T(8,128)(2,1)} %block.5), custom_call_target="tpu_custom_call" | custom-call | flops 6291456 | bytes 6291456 | tf_op jit(solution)/shard_map/turn/pallas_call | solution.py:129
  19.7 0.0 copy-start.1
  19.7 40.5 %collective-permute-done.block = bf16[256,768]{1,0:T(8,128)(2,1)S(1)} collective-permute-done((bf16[256,768]{1,0:T(8,128)(2,1)S(1)}, bf16[256,768]{1,0:T(8,128)(2,1)S(1)}, u32[]{:S(2)}, u32[]{:S(2)}) %collective-permute-start) | collective-permute-done | bytes 393248 | tf_op jit(solution)/shard_map/ppermute | solution.py:20
  60.2 0.7 copy-done.3
  60.9 1.6 %picks.2 = (bf16[256,256]{1,0:T(8,128)(2,1)S(1)}, bf16[256,256]{1,0:T(8,128)(2,1)S(1)}, bf16[256,128]{1,0:T(8,128)(2,1)S(1)}, bf16[256,128]{1,0:T(8,128)(2,1)S(1)}) custom-call(bf16[256,768]{1,0:T(8,128)(2,1)} %copy-done.3), custom_call_target="tpu_custom_call" | custom-call | flops 301989888 | bytes 786432 | tf_op jit(solution)/shard_map/picks/pallas_call | solution.py:91
  62.5 0.0 collective-permute-done.6.refs_1_
  62.5 1.2 %gram.5 = (f32[4,32,768]{2,1,0:T(8,128)S(1)}, f32[4,32,768]{2,1,0:T(8,128)S(1)}) custom-call(s32[1]{0:T(128)S(4)} %flag.1, bf16[768,2048]{1,0:T(8,128)(2,1)S(1)} %get-tuple-element.42.own, bf16[256,256]{1,0:T(8,128)(2,1)S(1)} %get-tuple-element.51.refs_0_, bf16[1792,256]{1,0:T(8,128)(2,1)S(1)} %collective-permute-done.6.refs_1_), custom_call_target="tpu_custom_call" | custom-call | flops 805306368 | bytes 3145728 | tf_op jit(solution)/shard_map/gram/pallas_call | solution.py:210
  63.8 0.1 collective-permute-start.7
  63.9 0.1 collective-permute-start.21
  63.9 1.2 %gram.6 = (f32[4,32,768]{2,1,0:T(8,128)S(1)}, f32[4,32,768]{2,1,0:T(8,128)S(1)}) custom-call(s32[1]{0:T(128)S(4)} %flag.1, bf16[768,2048]{1,0:T(8,128)(2,1)S(1)} %get-tuple-element.42.own, bf16[256,256]{1,0:T(8,128)(2,1)S(1)} %get-tuple-element.59.refs_0_, bf16[1792,256]{1,0:T(8,128)(2,1)S(1)} %collective-permute-done.11.refs_1_), custom_call_target="tpu_custom_call" | custom-call | flops 805306368 | bytes 3145728 | tf_op jit(solution)/shard_map/gram/pallas_call | solution.py:210
  65.2 0.5 collective-permute-start.12
  65.7 4.3 %collective-permute-done.1.refs_1_ = bf16[1792,128]{1,0:T(8,128)(2,1)S(1)} collective-permute-done((bf16[1792,128]{1,0:T(8,128)(2,1)S(1)}, bf16[1792,128]{1,0:T(8,128)(2,1)S(1)}, u32[]{:S(2)}, u32[]{:S(2)}) %collective-permute-start.1) | collective-permute-done | bytes 458784 | tf_op jit(solution)/shard_map/ppermute | solution.py:20
  70.0 1.1 gram.4
  71.2 0.1 collective-permute-start.2
  71.2 7.8 %collective-permute-done.21.refs_1_ = bf16[768,128]{1,0:T(8,128)(2,1)S(1)} collective-permute-done((bf16[768,128]{1,0:T(8,128)(2,1)S(1)}, bf16[768,128]{1,0:T(8,128)(2,1)S(1)}, u32[]{:S(2)}, u32[]{:S(2)}) %collective-permute-start.21) | collective-permute-done | bytes 196640 | tf_op jit(solution)/shard_map/ppermute | solution.py:20
  79.0 0.6 early.1.refs_1_
  79.6 0.0 collective-permute-done.20.refs_0_
  79.6 0.7 gram.7
  80.3 0.1 collective-permute-start.22
  80.4 0.0 collective-permute-done.7.arrived
  80.4 0.1 fold.5
  80.5 1.6 %collective-permute-start.8 = (f32[32,768]{1,0:T(8,128)S(1)}, f32[32,768]{1,0:T(8,128)S(1)}, u32[]{:S(2)}, u32[]{:S(2)}) collective-permute-start(f32[32,768]{1,0:T(8,128)S(1)} %get-tuple-element.56), channel_id=1, source_target_pairs={{0,2},{1,3},{2,0},{3,1},{4,6},{5,7},{6,4},{7,5},{8,10},{9,11},{10,... | collective-permute-start | bytes 294920 | tf_op jit(solution)/shard_map/ppermute | solution.py:25
  82.1 0.6 collective-permute-start.3
  82.7 0.0 collective-permute-start.16
  82.7 1.2 collective-permute-done.16.b
  83.8 1.5 %collective-permute-start.17 = (f32[1,768]{1,0:T(1,128)S(1)}, f32[1,768]{1,0:T(1,128)S(1)}, u32[]{:S(2)}, u32[]{:S(2)}) collective-permute-start(f32[1,768]{1,0:T(1,128)S(1)} %plus.3.a), channel_id=1, source_target_pairs={{0,2},{1,3},{2,0},{3,1},{4,6},{5,7},{6,4},{7,5},{8,10},{9,11},{10,... | collective-permute-start | bytes 9224 | tf_op jit(solution)/shard_map/ppermute | solution.py:25
  85.3 2.1 %collective-permute-done.17.b = f32[1,768]{1,0:T(1,128)S(1)} collective-permute-done((f32[1,768]{1,0:T(1,128)S(1)}, f32[1,768]{1,0:T(1,128)S(1)}, u32[]{:S(2)}, u32[]{:S(2)}) %collective-permute-start.17) | collective-permute-done | bytes 3104 | tf_op jit(solution)/shard_map/ppermute | solution.py:25
  87.4 1.5 %collective-permute-start.18 = (f32[1,768]{1,0:T(1,128)S(1)}, f32[1,768]{1,0:T(1,128)S(1)}, u32[]{:S(2)}, u32[]{:S(2)}) collective-permute-start(f32[1,768]{1,0:T(1,128)S(1)} %plus.4.a), channel_id=1, source_target_pairs={{0,4},{1,5},{2,6},{3,7},{4,0},{5,1},{6,2},{7,3},{8,12},{9,13},{10,... | collective-permute-start | bytes 9224 | tf_op jit(solution)/shard_map/ppermute | solution.py:25
  89.0 2.1 %collective-permute-done.18.b = f32[1,768]{1,0:T(1,128)S(1)} collective-permute-done((f32[1,768]{1,0:T(1,128)S(1)}, f32[1,768]{1,0:T(1,128)S(1)}, u32[]{:S(2)}, u32[]{:S(2)}) %collective-permute-start.18) | collective-permute-done | bytes 3104 | tf_op jit(solution)/shard_map/ppermute | solution.py:25
  91.0 0.0 collective-permute-start.19
  91.0 5.4 %collective-permute-done.19.norm_low = f32[1,768]{1,0:T(1,128)S(1)} collective-permute-done((f32[1,768]{1,0:T(1,128)S(1)}, f32[1,768]{1,0:T(1,128)S(1)}, u32[]{:S(2)}, u32[]{:S(2)}) %collective-permute-start.19) | collective-permute-done | bytes 3104 | tf_op jit(solution)/shard_map/ppermute | solution.py:20
  96.4 1.5 %collective-permute-start.9 = (f32[32,768]{1,0:T(8,128)S(1)}, f32[32,768]{1,0:T(8,128)S(1)}, u32[]{:S(2)}, u32[]{:S(2)}) collective-permute-start(f32[32,768]{1,0:T(8,128)S(1)} %get-tuple-element.57), channel_id=1, source_target_pairs={{0,4},{1,5},{2,6},{3,7},{4,0},{5,1},{6,2},{7,3},{8,12},{9,13},{10,... | collective-permute-start | bytes 294920 | tf_op jit(solution)/shard_map/ppermute | solution.py:25
  98.0 0.0 collective-permute-done.12.arrived
  98.0 1.4 %collective-permute-start.10 = (f32[32,768]{1,0:T(8,128)S(1)}, f32[32,768]{1,0:T(8,128)S(1)}, u32[]{:S(2)}, u32[]{:S(2)}) collective-permute-start(f32[32,768]{1,0:T(8,128)S(1)} %get-tuple-element.58), channel_id=1, source_target_pairs={{0,6},{1,7},{2,4},{3,5},{4,2},{5,3},{6,0},{7,1},{8,14},{9,15},{10,... | collective-permute-start | bytes 294920 | tf_op jit(solution)/shard_map/ppermute | solution.py:25
  99.4 0.6 collective-permute-start.13
  100.0 0.0 collective-permute-done.3.refs_1_
  100.0 1.5 %collective-permute-start.14 = (f32[32,768]{1,0:T(8,128)S(1)}, f32[32,768]{1,0:T(8,128)S(1)}, u32[]{:S(2)}, u32[]{:S(2)}) collective-permute-start(f32[32,768]{1,0:T(8,128)S(1)} %get-tuple-element.65), channel_id=1, source_target_pairs={{0,4},{1,5},{2,6},{3,7},{4,0},{5,1},{6,2},{7,3},{8,12},{9,13},{10,... | collective-permute-start | bytes 294920 | tf_op jit(solution)/shard_map/ppermute | solution.py:25
  101.6 1.4 %collective-permute-start.15 = (f32[32,768]{1,0:T(8,128)S(1)}, f32[32,768]{1,0:T(8,128)S(1)}, u32[]{:S(2)}, u32[]{:S(2)}) collective-permute-start(f32[32,768]{1,0:T(8,128)S(1)} %get-tuple-element.66), channel_id=1, source_target_pairs={{0,6},{1,7},{2,4},{3,5},{4,2},{5,3},{6,0},{7,1},{8,14},{9,15},{10,... | collective-permute-start | bytes 294920 | tf_op jit(solution)/shard_map/ppermute | solution.py:25
  103.0 1.3 %collective-permute-done.9.refs_2_ = f32[32,768]{1,0:T(8,128)S(1)} collective-permute-done((f32[32,768]{1,0:T(8,128)S(1)}, f32[32,768]{1,0:T(8,128)S(1)}, u32[]{:S(2)}, u32[]{:S(2)}) %collective-permute-start.9) | collective-permute-done | bytes 98336 | tf_op jit(solution)/shard_map/ppermute | solution.py:25
  104.3 1.6 %collective-permute-start.4 = (f32[16,768]{1,0:T(8,128)S(1)}, f32[16,768]{1,0:T(8,128)S(1)}, u32[]{:S(2)}, u32[]{:S(2)}) collective-permute-start(f32[16,768]{1,0:T(8,128)S(1)} %get-tuple-element.49), channel_id=1, source_target_pairs={{0,4},{1,5},{2,6},{3,7},{4,0},{5,1},{6,2},{7,3},{8,12},{9,13},{10,... | collective-permute-start | bytes 147464 | tf_op jit(solution)/shard_map/ppermute | solution.py:25
  105.9 0.0 collective-permute-done.10.refs_3_
  105.9 2.8 %collective-permute-start.5 = (f32[16,768]{1,0:T(8,128)S(1)}, f32[16,768]{1,0:T(8,128)S(1)}, u32[]{:S(2)}, u32[]{:S(2)}) collective-permute-start(f32[16,768]{1,0:T(8,128)S(1)} %get-tuple-element.50), channel_id=1, source_target_pairs={{0,6},{1,7},{2,4},{3,5},{4,2},{5,3},{6,0},{7,1},{8,14},{9,15},{10,... | collective-permute-start | bytes 147464 | tf_op jit(solution)/shard_map/ppermute | solution.py:25
  108.8 0.6 collective-permute-start.23
  109.4 1.5 %collective-permute-start.24 = (f32[16,768]{1,0:T(8,128)S(1)}, f32[16,768]{1,0:T(8,128)S(1)}, u32[]{:S(2)}, u32[]{:S(2)}) collective-permute-start(f32[16,768]{1,0:T(8,128)S(1)} %get-tuple-element.77), channel_id=1, source_target_pairs={{0,4},{1,5},{2,6},{3,7},{4,0},{5,1},{6,2},{7,3},{8,12},{9,13},{10,... | collective-permute-start | bytes 147464 | tf_op jit(solution)/shard_map/ppermute | solution.py:25
  110.9 0.0 collective-permute-done.15.refs_3_
  110.9 1.4 %collective-permute-start.25 = (f32[16,768]{1,0:T(8,128)S(1)}, f32[16,768]{1,0:T(8,128)S(1)}, u32[]{:S(2)}, u32[]{:S(2)}) collective-permute-start(f32[16,768]{1,0:T(8,128)S(1)} %get-tuple-element.78), channel_id=1, source_target_pairs={{0,6},{1,7},{2,4},{3,5},{4,2},{5,3},{6,0},{7,1},{8,14},{9,15},{10,... | collective-permute-start | bytes 147464 | tf_op jit(solution)/shard_map/ppermute | solution.py:25
  112.4 0.1 shard_map.39
  112.6 0.0 collective-permute-done.4.refs_2_
  112.6 0.1 shard_map.40.base
  112.7 0.2 collective-permute-done.23.refs_1_
  112.9 0.6 collective-permute-done.24.refs_2_
  113.5 2.4 %collective-permute-done.25.refs_3_ = f32[16,768]{1,0:T(8,128)S(1)} collective-permute-done((f32[16,768]{1,0:T(8,128)S(1)}, f32[16,768]{1,0:T(8,128)S(1)}, u32[]{:S(2)}, u32[]{:S(2)}) %collective-permute-start.25) | collective-permute-done | bytes 49184 | tf_op jit(solution)/shard_map/ppermute | solution.py:25
  115.9 0.8 shard_map.41
  (18 shorter events, 0.2 us)
Async XLA Ops:
  4.9 0.7 copy-start
  5.6 56.9 %collective-permute-start.6 = (bf16[1792,256]{1,0:T(8,128)(2,1)}, bf16[1792,256]{1,0:T(8,128)(2,1)S(1)}, u32[]{:S(2)}, u32[]{:S(2)}) collective-permute-start(bf16[1792,256]{1,0:T(8,128)(2,1)} %get-tuple-element.52), channel_id=1, source_target_pairs={{0,8},{8,16},{16,24},{24,0},{1,9},{9,17},{17,25},{25,1},{2,10},{10... | collective-permute-start | bytes 2752520 | tf_op jit(solution)/shard_map/ppermute | solution.py:20
  8.7 55.3 %collective-permute-start.11 = (bf16[1792,256]{1,0:T(8,128)(2,1)S(1)}, bf16[1792,256]{1,0:T(8,128)(2,1)S(1)}, u32[]{:S(2)}, u32[]{:S(2)}) collective-permute-start(bf16[1792,256]{1,0:T(8,128)(2,1)S(1)} %get-tuple-element.60), channel_id=1, source_target_pairs={{0,8},{8,16},{16,24},{24,0},{1,9},{9,17},{17,25},{25,1},{2,10},{10... | collective-permute-start | bytes 2752520 | tf_op jit(solution)/shard_map/ppermute | solution.py:20
  11.2 48.9 %collective-permute-start = (bf16[256,768]{1,0:T(8,128)(2,1)S(1)}, bf16[256,768]{1,0:T(8,128)(2,1)S(1)}, u32[]{:S(2)}, u32[]{:S(2)}) collective-permute-start(bf16[256,768]{1,0:T(8,128)(2,1)S(1)} %top.1), channel_id=1, source_target_pairs={{0,8},{8,16},{16,24},{24,0},{1,9},{9,17},{17,25},{25,1},{2,10},{10... | collective-permute-start | bytes 1179656 | tf_op jit(solution)/shard_map/ppermute | solution.py:20
  12.9 57.1 %collective-permute-start.1 = (bf16[1792,128]{1,0:T(8,128)(2,1)S(1)}, bf16[1792,128]{1,0:T(8,128)(2,1)S(1)}, u32[]{:S(2)}, u32[]{:S(2)}) collective-permute-start(bf16[1792,128]{1,0:T(8,128)(2,1)S(1)} %get-tuple-element.44), channel_id=1, source_target_pairs={{0,8},{8,16},{16,24},{24,0},{1,9},{9,17},{17,25},{25,1},{2,10},{10... | collective-permute-start | bytes 1376264 | tf_op jit(solution)/shard_map/ppermute | solution.py:20
  12.9 66.6 %collective-permute-start.20 = (bf16[1024,128]{1,0:T(8,128)(2,1)S(1)}, bf16[1024,128]{1,0:T(8,128)(2,1)S(1)}, u32[]{:S(2)}, u32[]{:S(2)}) collective-permute-start(bf16[1024,128]{1,0:T(8,128)(2,1)S(1)} %get-tuple-element.70), channel_id=1, source_target_pairs={{0,8},{8,16},{16,24},{24,0},{1,9},{9,17},{17,25},{25,1},{2,10},{10... | collective-permute-start | bytes 786440 | tf_op jit(solution)/shard_map/ppermute | solution.py:20
  14.7 0.7 copy-start.2
  19.7 44.2 %copy-start.1 = (bf16[768,128]{1,0:T(8,128)(2,1)S(1)}, bf16[768,128]{1,0:T(8,128)(2,1)}, u32[]{:S(2)}) copy-start(bf16[768,128]{1,0:T(8,128)(2,1)} %copy-done) | copy-start | bytes 589828
  60.2 0.7 copy-start.3
  63.8 16.6 %collective-permute-start.7 = (f32[4,32,768]{2,1,0:T(8,128)S(1)}, f32[4,32,768]{2,1,0:T(8,128)S(1)}, u32[]{:S(2)}, u32[]{:S(2)}) collective-permute-start(f32[4,32,768]{2,1,0:T(8,128)S(1)} %get-tuple-element.54), channel_id=1, source_target_pairs={{0,1},{1,0},{2,3},{3,2},{4,5},{5,4},{6,7},{7,6},{8,9},{9,8},{10,11... | collective-permute-start | bytes 1179656 | tf_op jit(solution)/shard_map/ppermute | solution.py:25
  63.9 15.1 %collective-permute-start.21 = (bf16[768,128]{1,0:T(8,128)(2,1)S(1)}, bf16[768,128]{1,0:T(8,128)(2,1)S(1)}, u32[]{:S(2)}, u32[]{:S(2)}) collective-permute-start(bf16[768,128]{1,0:T(8,128)(2,1)S(1)} %copy-done.1), channel_id=1, source_target_pairs={{0,8},{8,16},{16,24},{24,0},{1,9},{9,17},{17,25},{25,1},{2,10},{10... | collective-permute-start | bytes 589832 | tf_op jit(solution)/shard_map/ppermute | solution.py:20
  65.2 32.8 %collective-permute-start.12 = (f32[4,32,768]{2,1,0:T(8,128)S(1)}, f32[4,32,768]{2,1,0:T(8,128)S(1)}, u32[]{:S(2)}, u32[]{:S(2)}) collective-permute-start(f32[4,32,768]{2,1,0:T(8,128)S(1)} %get-tuple-element.62), channel_id=1, source_target_pairs={{0,1},{1,0},{2,3},{3,2},{4,5},{5,4},{6,7},{7,6},{8,9},{9,8},{10,11... | collective-permute-start | bytes 1179656 | tf_op jit(solution)/shard_map/ppermute | solution.py:25
  71.2 10.9 %collective-permute-start.2 = (f32[4,16,768]{2,1,0:T(8,128)S(1)}, f32[4,16,768]{2,1,0:T(8,128)S(1)}, u32[]{:S(2)}, u32[]{:S(2)}) collective-permute-start(f32[4,16,768]{2,1,0:T(8,128)S(1)} %get-tuple-element.46), channel_id=1, source_target_pairs={{0,1},{1,0},{2,3},{3,2},{4,5},{5,4},{6,7},{7,6},{8,9},{9,8},{10,11... | collective-permute-start | bytes 589832 | tf_op jit(solution)/shard_map/ppermute | solution.py:25
  80.3 19.1 %collective-permute-start.22 = (f32[4,16,768]{2,1,0:T(8,128)S(1)}, f32[4,16,768]{2,1,0:T(8,128)S(1)}, u32[]{:S(2)}, u32[]{:S(2)}) collective-permute-start(f32[4,16,768]{2,1,0:T(8,128)S(1)} %get-tuple-element.74), channel_id=1, source_target_pairs={{0,1},{1,0},{2,3},{3,2},{4,5},{5,4},{6,7},{7,6},{8,9},{9,8},{10,11... | collective-permute-start | bytes 589832 | tf_op jit(solution)/shard_map/ppermute | solution.py:25
  80.5 21.1 %collective-permute-start.8 = (f32[32,768]{1,0:T(8,128)S(1)}, f32[32,768]{1,0:T(8,128)S(1)}, u32[]{:S(2)}, u32[]{:S(2)}) collective-permute-start(f32[32,768]{1,0:T(8,128)S(1)} %get-tuple-element.56), channel_id=1, source_target_pairs={{0,2},{1,3},{2,0},{3,1},{4,6},{5,7},{6,4},{7,5},{8,10},{9,11},{10,... | collective-permute-start | bytes 294920 | tf_op jit(solution)/shard_map/ppermute | solution.py:25
  82.1 18.0 %collective-permute-start.3 = (f32[16,768]{1,0:T(8,128)S(1)}, f32[16,768]{1,0:T(8,128)S(1)}, u32[]{:S(2)}, u32[]{:S(2)}) collective-permute-start(f32[16,768]{1,0:T(8,128)S(1)} %get-tuple-element.48), channel_id=1, source_target_pairs={{0,2},{1,3},{2,0},{3,1},{4,6},{5,7},{6,4},{7,5},{8,10},{9,11},{10,... | collective-permute-start | bytes 147464 | tf_op jit(solution)/shard_map/ppermute | solution.py:25
  82.7 1.2 collective-permute-start.16
  83.8 3.6 %collective-permute-start.17 = (f32[1,768]{1,0:T(1,128)S(1)}, f32[1,768]{1,0:T(1,128)S(1)}, u32[]{:S(2)}, u32[]{:S(2)}) collective-permute-start(f32[1,768]{1,0:T(1,128)S(1)} %plus.3.a), channel_id=1, source_target_pairs={{0,2},{1,3},{2,0},{3,1},{4,6},{5,7},{6,4},{7,5},{8,10},{9,11},{10,... | collective-permute-start | bytes 9224 | tf_op jit(solution)/shard_map/ppermute | solution.py:25
  87.4 3.6 %collective-permute-start.18 = (f32[1,768]{1,0:T(1,128)S(1)}, f32[1,768]{1,0:T(1,128)S(1)}, u32[]{:S(2)}, u32[]{:S(2)}) collective-permute-start(f32[1,768]{1,0:T(1,128)S(1)} %plus.4.a), channel_id=1, source_target_pairs={{0,4},{1,5},{2,6},{3,7},{4,0},{5,1},{6,2},{7,3},{8,12},{9,13},{10,... | collective-permute-start | bytes 9224 | tf_op jit(solution)/shard_map/ppermute | solution.py:25
  91.0 5.4 %collective-permute-start.19 = (f32[1,768]{1,0:T(1,128)S(1)}, f32[1,768]{1,0:T(1,128)S(1)}, u32[]{:S(2)}, u32[]{:S(2)}) collective-permute-start(f32[1,768]{1,0:T(1,128)S(1)} %plus.5.norm_own), channel_id=1, source_target_pairs={{0,8},{8,16},{16,24},{24,0},{1,9},{9,17},{17,25},{25,1},{2,10},{10... | collective-permute-start | bytes 9224 | tf_op jit(solution)/shard_map/ppermute | solution.py:20
  96.4 7.8 %collective-permute-start.9 = (f32[32,768]{1,0:T(8,128)S(1)}, f32[32,768]{1,0:T(8,128)S(1)}, u32[]{:S(2)}, u32[]{:S(2)}) collective-permute-start(f32[32,768]{1,0:T(8,128)S(1)} %get-tuple-element.57), channel_id=1, source_target_pairs={{0,4},{1,5},{2,6},{3,7},{4,0},{5,1},{6,2},{7,3},{8,12},{9,13},{10,... | collective-permute-start | bytes 294920 | tf_op jit(solution)/shard_map/ppermute | solution.py:25
  98.0 7.9 %collective-permute-start.10 = (f32[32,768]{1,0:T(8,128)S(1)}, f32[32,768]{1,0:T(8,128)S(1)}, u32[]{:S(2)}, u32[]{:S(2)}) collective-permute-start(f32[32,768]{1,0:T(8,128)S(1)} %get-tuple-element.58), channel_id=1, source_target_pairs={{0,6},{1,7},{2,4},{3,5},{4,2},{5,3},{6,0},{7,1},{8,14},{9,15},{10,... | collective-permute-start | bytes 294920 | tf_op jit(solution)/shard_map/ppermute | solution.py:25
  99.4 9.3 %collective-permute-start.13 = (f32[32,768]{1,0:T(8,128)S(1)}, f32[32,768]{1,0:T(8,128)S(1)}, u32[]{:S(2)}, u32[]{:S(2)}) collective-permute-start(f32[32,768]{1,0:T(8,128)S(1)} %get-tuple-element.64), channel_id=1, source_target_pairs={{0,2},{1,3},{2,0},{3,1},{4,6},{5,7},{6,4},{7,5},{8,10},{9,11},{10,... | collective-permute-start | bytes 294920 | tf_op jit(solution)/shard_map/ppermute | solution.py:25
  100.0 9.3 %collective-permute-start.14 = (f32[32,768]{1,0:T(8,128)S(1)}, f32[32,768]{1,0:T(8,128)S(1)}, u32[]{:S(2)}, u32[]{:S(2)}) collective-permute-start(f32[32,768]{1,0:T(8,128)S(1)} %get-tuple-element.65), channel_id=1, source_target_pairs={{0,4},{1,5},{2,6},{3,7},{4,0},{5,1},{6,2},{7,3},{8,12},{9,13},{10,... | collective-permute-start | bytes 294920 | tf_op jit(solution)/shard_map/ppermute | solution.py:25
  101.6 9.4 %collective-permute-start.15 = (f32[32,768]{1,0:T(8,128)S(1)}, f32[32,768]{1,0:T(8,128)S(1)}, u32[]{:S(2)}, u32[]{:S(2)}) collective-permute-start(f32[32,768]{1,0:T(8,128)S(1)} %get-tuple-element.66), channel_id=1, source_target_pairs={{0,6},{1,7},{2,4},{3,5},{4,2},{5,3},{6,0},{7,1},{8,14},{9,15},{10,... | collective-permute-start | bytes 294920 | tf_op jit(solution)/shard_map/ppermute | solution.py:25
  104.3 8.3 %collective-permute-start.4 = (f32[16,768]{1,0:T(8,128)S(1)}, f32[16,768]{1,0:T(8,128)S(1)}, u32[]{:S(2)}, u32[]{:S(2)}) collective-permute-start(f32[16,768]{1,0:T(8,128)S(1)} %get-tuple-element.49), channel_id=1, source_target_pairs={{0,4},{1,5},{2,6},{3,7},{4,0},{5,1},{6,2},{7,3},{8,12},{9,13},{10,... | collective-permute-start | bytes 147464 | tf_op jit(solution)/shard_map/ppermute | solution.py:25
  105.9 6.7 %collective-permute-start.5 = (f32[16,768]{1,0:T(8,128)S(1)}, f32[16,768]{1,0:T(8,128)S(1)}, u32[]{:S(2)}, u32[]{:S(2)}) collective-permute-start(f32[16,768]{1,0:T(8,128)S(1)} %get-tuple-element.50), channel_id=1, source_target_pairs={{0,6},{1,7},{2,4},{3,5},{4,2},{5,3},{6,0},{7,1},{8,14},{9,15},{10,... | collective-permute-start | bytes 147464 | tf_op jit(solution)/shard_map/ppermute | solution.py:25
  108.8 4.2 %collective-permute-start.23 = (f32[16,768]{1,0:T(8,128)S(1)}, f32[16,768]{1,0:T(8,128)S(1)}, u32[]{:S(2)}, u32[]{:S(2)}) collective-permute-start(f32[16,768]{1,0:T(8,128)S(1)} %get-tuple-element.76), channel_id=1, source_target_pairs={{0,2},{1,3},{2,0},{3,1},{4,6},{5,7},{6,4},{7,5},{8,10},{9,11},{10,... | collective-permute-start | bytes 147464 | tf_op jit(solution)/shard_map/ppermute | solution.py:25
  109.4 4.1 %collective-permute-start.24 = (f32[16,768]{1,0:T(8,128)S(1)}, f32[16,768]{1,0:T(8,128)S(1)}, u32[]{:S(2)}, u32[]{:S(2)}) collective-permute-start(f32[16,768]{1,0:T(8,128)S(1)} %get-tuple-element.77), channel_id=1, source_target_pairs={{0,4},{1,5},{2,6},{3,7},{4,0},{5,1},{6,2},{7,3},{8,12},{9,13},{10,... | collective-permute-start | bytes 147464 | tf_op jit(solution)/shard_map/ppermute | solution.py:25
  110.9 5.0 %collective-permute-start.25 = (f32[16,768]{1,0:T(8,128)S(1)}, f32[16,768]{1,0:T(8,128)S(1)}, u32[]{:S(2)}, u32[]{:S(2)}) collective-permute-start(f32[16,768]{1,0:T(8,128)S(1)} %get-tuple-element.78), channel_id=1, source_target_pairs={{0,6},{1,7},{2,4},{3,5},{4,2},{5,3},{6,0},{7,1},{8,14},{9,15},{10,... | collective-permute-start | bytes 147464 | tf_op jit(solution)/shard_map/ppermute | solution.py:25
